TPU v7x, 32 devices: a whole 2x2x4 slice. The times are simulated.
32 devices in a mesh: dp: 4 (over x, core), row: 4 (over z), col: 2 (over y).
Axes of the slice: x: 2, y: 2, z: 4, core: 2. Of those that a mesh axis runs over, the one named last changes fastest.
Arguments:
- block_input: bfloat16 [7168, 2048], P(('dp', 'col'), 'row'), may hold values from -6 to 6
- segment_ids: int32 [7168], P(('dp', 'row')), may hold values from 0 to 111, never falling along the last dimension, each value on 1 to 448 neighbouring positions
- attn_gain: float32 [2048], P('row'), may hold values from 0.25 to 1.75
- mix_weight: bfloat16 [2048, 12288], P('row', 'col'), may hold values from -0.125 to 0.125
- decay_weight: bfloat16 [2048, 32], P('row', 'col'), may hold values from -0.125 to 0.125
- conv_weight: float32 [4, 8192], P(None, 'col'), may hold values from -2.5 to 2.5
- decay_log: float32 [16], P('col'), may hold values from -6.5 to -2.5
- decay_bias: float32 [16], P('col'), may hold values from -1.5 to 1
- out_gain: float32 [256], replicated, may hold values from 0.25 to 1.75
- out_weight: bfloat16 [4096, 2048], P('col', 'row'), may hold values from -0.1875 to 0.1875
- ffn_gain: float32 [2048], P('row'), may hold values from 0.25 to 1.75
- gate_weight: bfloat16 [2048, 5632], P('row', 'col'), may hold values from -0.125 to 0.125
- up_weight: bfloat16 [2048, 5632], P('row', 'col'), may hold values from -0.125 to 0.125
- down_weight: bfloat16 [5632, 2048], P('col', 'row'), may hold values from -0.15625 to 0.15625
- cotangent: bfloat16 [7168, 2048], P(('dp', 'col'), 'row'), may hold values from -6 to 6
Outputs:
- block_output: bfloat16 [7168, 2048], P(('dp', 'col'), 'row')
- input_grad: bfloat16 [7168, 2048], P(('dp', 'col'), 'row')
- attn_gain_grad: float32 [2048], P('row')
- mix_weight_grad: float32 [2048, 12288], P('row', 'col')
- decay_weight_grad: float32 [2048, 32], P('row', 'col')
- conv_weight_grad: float32 [4, 8192], P(None, 'col')
- decay_log_grad: float32 [16], P('col')
- decay_bias_grad: float32 [16], P('col')
- out_gain_grad: float32 [256], replicated
- out_weight_grad: float32 [4096, 2048], P('col', 'row')
- ffn_gain_grad: float32 [2048], P('row')
- gate_weight_grad: float32 [2048, 5632], P('row', 'col')
- up_weight_grad: float32 [2048, 5632], P('row', 'col')
- down_weight_grad: float32 [5632, 2048], P('col', 'row')
Inputs may be any that keep to these rules, and one draw needn't show every extreme that they name: `segment_ids`: segment numbers never fall along the tokens; each document has 1 to 448 tokens and one has exactly 448.
All inputs are finite; a program needn't handle non-finite values.
Results may differ from a plain program's by a relative error of at most 0.025.
Values may be sent and summed in bfloat16 or wider, within the bound.
A program may use at most 320 MiB of HBM per device.

v0:
```python
import jax
import jax.numpy as jnp
from jax import lax
from jax.sharding import PartitionSpec as P

D = 2048
BLOCK = 64
SEQ = 448


def block_step(state, inputs):
    query, key, value, beta, decay, starts = inputs
    highest = lax.Precision.HIGHEST
    total = jnp.cumsum(decay, axis=-1)
    marks = jnp.cumsum(starts, axis=-1)
    position = jnp.arange(BLOCK)
    lower = position[:, None] >= position[None, :]
    strict = (position[:, None] > position[None, :]).astype(key.dtype)
    same = (marks[..., :, None] == marks[..., None, :]) & lower
    spread = total[..., :, None] - total[..., None, :]
    weight = jnp.where(same, jnp.exp(jnp.where(same, spread, 0.0)), 0.0)
    carried = jnp.where(marks == 0.0, jnp.exp(total), 0.0)
    inner = jnp.einsum("chtk,chsk->chts", key, key, precision=highest)
    system = jnp.eye(BLOCK, dtype=key.dtype) + beta[..., None] * weight * strict * inner
    known = jnp.einsum("chtk,chkv->chtv", key, state, precision=highest)
    target = beta[..., None] * (value - carried[..., None] * known)
    fresh = jax.scipy.linalg.solve_triangular(system, target, lower=True, unit_diagonal=True)
    scores = jnp.einsum("chtk,chsk->chts", query, key, precision=highest) * weight
    result = carried[..., None] * jnp.einsum("chtk,chkv->chtv", query, state, precision=highest)
    result = result + jnp.einsum("chts,chsv->chtv", scores, fresh, precision=highest)
    last_row = weight[..., -1, :]
    new_state = carried[..., -1][..., None, None] * state
    new_state = new_state + jnp.einsum(
        "chsk,chsv->chkv", key * last_row[..., None], fresh, precision=highest
    )
    return (new_state, result)


def mix_core(proj, decay_in, conv_w, decay_log, decay_bias, out_gain, segments):
    count, length, width = proj.shape
    heads = decay_log.shape[0]
    value_dim = out_gain.shape[0]
    per_head = width // heads
    key_dim = (per_head - 2 * value_dim) // 2
    inner_width = 2 * key_dim + value_dim
    split = proj.reshape(count, length, heads, per_head)
    conv_in = split[..., :inner_width].reshape(count, length, heads * inner_width)
    gate_out = split[..., inner_width:]
    taps = conv_w.shape[0]
    summed = jnp.zeros_like(conv_in)
    for lag in range(taps):
        moved = jnp.pad(conv_in, ((0, 0), (lag, 0), (0, 0)))[:, :length]
        moved_seg = jnp.pad(segments, ((0, 0), (lag, 0)), constant_values=-1)[:, :length]
        keep = (moved_seg == segments).astype(proj.dtype)[..., None]
        summed = summed + conv_w[taps - 1 - lag] * moved * keep
    active = jax.nn.silu(summed).reshape(count, length, heads, inner_width)
    query = active[..., :key_dim]
    key = active[..., key_dim : 2 * key_dim]
    value = active[..., 2 * key_dim :]
    query = (
        query
        * lax.rsqrt(jnp.sum(query * query, axis=-1, keepdims=True) + 1e-06)
        * key_dim ** (-0.5)
    )
    key = key * lax.rsqrt(jnp.sum(key * key, axis=-1, keepdims=True) + 1e-06)
    paired = decay_in.reshape(count, length, heads, 2)
    beta = jax.nn.sigmoid(paired[..., 0])
    decay = -jnp.exp(decay_log) * jax.nn.softplus(paired[..., 1] + decay_bias)
    prior = jnp.pad(segments, ((0, 0), (1, 0)), constant_values=-1)[:, :length]
    starts = jnp.broadcast_to(
        (prior != segments).astype(proj.dtype)[..., None], (count, length, heads)
    )
    blocks = length // BLOCK

    def to_blocks(values):
        values = values.reshape((count, blocks, BLOCK) + values.shape[2:])
        values = jnp.moveaxis(values, 1, 0)
        return jnp.moveaxis(values, 3, 2)

    inputs = (
        to_blocks(query),
        to_blocks(key),
        to_blocks(value),
        to_blocks(beta),
        to_blocks(decay),
        to_blocks(starts),
    )
    state = jnp.zeros((count, heads, key_dim, value_dim), proj.dtype)
    state, outputs = lax.scan(jax.checkpoint(block_step), state, inputs)
    outputs = jnp.moveaxis(jnp.moveaxis(outputs, 3, 2), 0, 1).reshape(
        count, length, heads, value_dim
    )
    normed = outputs * lax.rsqrt(jnp.mean(outputs * outputs, axis=-1, keepdims=True) + 1e-05)
    normed = normed * out_gain * jax.nn.silu(gate_out)
    return normed.reshape(count, length, heads * value_dim)


def project(left, right):
    return jnp.dot(left, right, preferred_element_type=jnp.float32)


def project_back(left, right):
    return jnp.einsum("tn,kn->tk", left, right, preferred_element_type=jnp.float32)


def weight_grad(left, right):
    return jnp.einsum("tk,tn->kn", left, right, preferred_element_type=jnp.float32)


def norm_forward(values):
    local_sum = jnp.sum(values * values, axis=1)
    total = lax.psum(local_sum, "row")
    scale = lax.rsqrt(total / D + 1e-05)[:, None]
    return (values * scale, scale)


def norm_backward(grad_normed, normed, scale, gain):
    scaled = grad_normed * gain
    local_sum = jnp.sum(scaled * normed, axis=1)
    total = lax.psum(local_sum, "row")
    grad_input = scale * (scaled - normed * (total / D)[:, None])
    return (grad_input, jnp.sum(grad_normed * normed, axis=0))


def gather_tokens(values):
    return lax.all_gather(values, "col", axis=0, tiled=True)


def gather_grads(values):
    return lax.all_gather(values, "col", axis=0, tiled=True)


def split_rows(first, second):
    return (
        lax.psum_scatter(first, "row", scatter_dimension=0, tiled=True),
        lax.psum_scatter(second, "row", scatter_dimension=0, tiled=True),
    )


def join_rows(values):
    return lax.all_gather(values, "row", axis=0, tiled=True)


def join_grads(first, second):
    return (
        lax.all_gather(first, "row", axis=0, tiled=True),
        lax.all_gather(second, "row", axis=0, tiled=True),
    )


def sum_to_tokens(whole, weight, out_rows):

    def term(start, count):
        return project(whole, weight)

    return lax.psum_scatter(
        term(jnp.int32(0), lax.axis_size("col") * out_rows).astype(jnp.bfloat16),
        "col",
        scatter_dimension=0,
        tiled=True,
    ).astype(jnp.float32)


def grads_to_tokens(wholes, weights, out_rows):

    def term(start, count):
        total = project_back(wholes[0], weights[0])
        return total + project_back(wholes[1], weights[1])

    return lax.psum_scatter(
        term(jnp.int32(0), lax.axis_size("col") * out_rows).astype(jnp.bfloat16),
        "col",
        scatter_dimension=0,
        tiled=True,
    ).astype(jnp.float32)


def grads_to_rows(whole, weight, out_rows):

    def term(start, count):
        return project_back(whole, weight)

    return lax.psum_scatter(
        term(jnp.int32(0), lax.axis_size("row") * out_rows).astype(jnp.bfloat16),
        "row",
        scatter_dimension=0,
        tiled=True,
    ).astype(jnp.float32)


def swiglu_back(grad_hidden, gate, up_values):
    sigmoid_gate = jax.nn.sigmoid(gate)
    grad_gate = grad_hidden * up_values * sigmoid_gate * (1.0 + gate * (1.0 - sigmoid_gate))
    grad_up = grad_hidden * gate * sigmoid_gate
    return (grad_gate.astype(jnp.bfloat16), grad_up.astype(jnp.bfloat16))


def on_device(
    block_input,
    segment_ids,
    attn_gain,
    mix_weight,
    decay_weight,
    conv_weight,
    decay_log,
    decay_bias,
    out_gain,
    out_weight,
    ffn_gain,
    gate_weight,
    up_weight,
    down_weight,
    cotangent,
):
    stored = block_input.astype(jnp.float32)
    local_rows = stored.shape[0]
    normed_one, scale_one = norm_forward(stored)
    attn_input = (normed_one * attn_gain).astype(jnp.bfloat16)
    attn_all = gather_tokens(attn_input)
    proj, decay_in = split_rows(project(attn_all, mix_weight), project(attn_all, decay_weight))
    mixer_rows = proj.shape[0]
    sequences = mixer_rows // SEQ
    segments = segment_ids.reshape(sequences, SEQ)

    def mixer(proj_rows, decay_rows, conv_local, log_local, bias_local, gain_local):
        result = mix_core(
            proj_rows.reshape(sequences, SEQ, -1),
            decay_rows.reshape(sequences, SEQ, -1),
            conv_local,
            log_local,
            bias_local,
            gain_local,
            segments,
        )
        return result.reshape(mixer_rows, -1)

    mixed, mixer_back = jax.vjp(mixer, proj, decay_in, conv_weight, decay_log, decay_bias, out_gain)
    mixed_all = join_rows(mixed.astype(jnp.bfloat16))
    residual = stored + sum_to_tokens(mixed_all, out_weight, local_rows)
    normed_two, scale_two = norm_forward(residual)
    ffn_input = (normed_two * ffn_gain).astype(jnp.bfloat16)
    ffn_all = gather_tokens(ffn_input)
    gate, up_values = (
        lax.psum(project(ffn_all, gate_weight).astype(jnp.bfloat16), "row").astype(jnp.float32),
        lax.psum(project(ffn_all, up_weight).astype(jnp.bfloat16), "row").astype(jnp.float32),
    )
    hidden_all = (jax.nn.silu(gate) * up_values).astype(jnp.bfloat16)
    block_output = (residual + sum_to_tokens(hidden_all, down_weight, local_rows)).astype(
        jnp.bfloat16
    )
    out_grads = gather_grads(cotangent)
    down_grad = weight_grad(hidden_all, out_grads)
    grad_hidden = lax.psum(project_back(out_grads, down_weight).astype(jnp.bfloat16), "row").astype(
        jnp.float32
    )
    grad_gate, grad_up = swiglu_back(grad_hidden, gate, up_values)
    gate_grad = weight_grad(ffn_all, grad_gate)
    up_grad = weight_grad(ffn_all, grad_up)
    grad_ffn_in = grads_to_tokens((grad_gate, grad_up), (gate_weight, up_weight), local_rows)
    grad_from_ffn, ffn_gain_part = norm_backward(grad_ffn_in, normed_two, scale_two, ffn_gain)
    grad_residual = cotangent.astype(jnp.float32) + grad_from_ffn
    branch_grads = gather_grads(grad_residual.astype(jnp.bfloat16))
    out_weight_grad = weight_grad(mixed_all, branch_grads)
    grad_mixed = grads_to_rows(branch_grads, out_weight, mixer_rows)
    grad_proj, grad_decay_in, conv_part, log_part, bias_part, gain_part = mixer_back(grad_mixed)
    proj_grads, decay_grads = join_grads(
        grad_proj.astype(jnp.bfloat16), grad_decay_in.astype(jnp.bfloat16)
    )
    mix_grad = weight_grad(attn_all, proj_grads)
    decay_grad = weight_grad(attn_all, decay_grads)
    grad_attn_in = grads_to_tokens(
        (proj_grads, decay_grads), (mix_weight, decay_weight), local_rows
    )
    grad_from_attn, attn_gain_part = norm_backward(grad_attn_in, normed_one, scale_one, attn_gain)
    input_grad = (grad_residual + grad_from_attn).astype(jnp.bfloat16)
    summed = (
        lax.psum(mix_grad.astype(jnp.bfloat16), "dp").astype(jnp.float32),
        lax.psum(decay_grad.astype(jnp.bfloat16), "dp").astype(jnp.float32),
        lax.psum(out_weight_grad.astype(jnp.bfloat16), "dp").astype(jnp.float32),
        lax.psum(gate_grad.astype(jnp.bfloat16), "dp").astype(jnp.float32),
        lax.psum(up_grad.astype(jnp.bfloat16), "dp").astype(jnp.float32),
        lax.psum(down_grad.astype(jnp.bfloat16), "dp").astype(jnp.float32),
    )
    row_index = lax.axis_index("row")
    col_index = lax.axis_index("col")
    row_pick = (jnp.arange(lax.axis_size("row")) == row_index).astype(jnp.float32)
    col_pick = (jnp.arange(lax.axis_size("col")) == col_index).astype(jnp.float32)
    small = lax.psum(
        (
            row_pick[:, None] * attn_gain_part[None, :],
            row_pick[:, None] * ffn_gain_part[None, :],
            col_pick[:, None, None] * conv_part[None],
            col_pick[:, None] * log_part[None, :],
            col_pick[:, None] * bias_part[None, :],
            gain_part,
        ),
        ("dp", "row", "col"),
    )
    attn_gain_grad = lax.dynamic_index_in_dim(small[0], row_index, 0, keepdims=False)
    ffn_gain_grad = lax.dynamic_index_in_dim(small[1], row_index, 0, keepdims=False)
    conv_grad = lax.dynamic_index_in_dim(small[2], col_index, 0, keepdims=False)
    log_grad = lax.dynamic_index_in_dim(small[3], col_index, 0, keepdims=False)
    bias_grad = lax.dynamic_index_in_dim(small[4], col_index, 0, keepdims=False)
    return (
        block_output,
        input_grad,
        attn_gain_grad,
        summed[0],
        summed[1],
        conv_grad,
        log_grad,
        bias_grad,
        small[5],
        summed[2],
        ffn_gain_grad,
        summed[3],
        summed[4],
        summed[5],
    )


def solution(mesh):
    return jax.shard_map(
        on_device,
        mesh=mesh,
        in_specs=(
            P(("dp", "col"), "row"),
            P(("dp", "row")),
            P("row"),
            P("row", "col"),
            P("row", "col"),
            P(None, "col"),
            P("col"),
            P("col"),
            P(),
            P("col", "row"),
            P("row"),
            P("row", "col"),
            P("row", "col"),
            P("col", "row"),
            P(("dp", "col"), "row"),
        ),
        out_specs=(
            P(("dp", "col"), "row"),
            P(("dp", "col"), "row"),
            P("row"),
            P("row", "col"),
            P("row", "col"),
            P(None, "col"),
            P("col"),
            P("col"),
            P(),
            P("col", "row"),
            P("row"),
            P("row", "col"),
            P("row", "col"),
            P("col", "row"),
        ),
        check_vma=False,
    )
```

profile of v0, /device:TPU:13, one launch (start us, length us, event | category | flops | bytes accessed | tf_op | source)
XLA Modules:
  0.0 4327.3 jit_solution(5476020139172058934)
XLA Ops:
  80.7 718.2 %reduce-scatter.10.cloned.1.call-done = f32[448,6144]{1,0:T(8,128)} async-done(((f32[1792,6144]{1,0:T(8,128)}), f32[448,6144]{1,0:T(8,128)}) %reduce-scatter.10.cloned.1.call-update) | async-done | bytes 11010064 | tf_op jit(solution)/shard_map/reduce_scatter | solution.py:135
  869.8 405.6 %while.44 = (s32[]{:T(128)}, f32[1,8,128,256]{3,2,1,0:T(8,128)}, f32[7,1,8,64,256]{4,2,3,0,1:T(8,128)}, f32[7,1,8,128,256]{4,3,2,1,0:T(8,128)}, f32[7,1,8,64]{3,...) while((s32[]{:T(128)}, f32[1,8,128,256]{3,2,1,0:T(8,128)}, ...), condition=%wide.region_9.11_spmd.clone.clone, body=%wide.region_6.10_spmd.clone.clone.sunk | while | flops 908922432 | bytes 18620180 | solution.py:89
  873.0 40.0 custom-call.26
  929.3 40.0 custom-call.26
  987.5 40.0 custom-call.26
  1045.6 40.0 custom-call.26
  1103.8 40.0 custom-call.26
  1162.0 40.0 custom-call.26
  1220.1 40.0 custom-call.26
  1283.9 134.4 %all-gather.10.cloned.1.call-done = bf16[1792,2048]{1,0:T(8,128)(2,1)} async-done(((bf16[448,2048]{1,0:T(8,128)(2,1)}), bf16[1792,2048]{1,0:T(8,128)(2,1)}) %all-gather.10.cloned.1.call-update) | async-done | bytes 7340048 | tf_op jit(solution)/shard_map/all_gather | solution.py:141
  1538.4 999.0 %all-reduce.31.cloned.1.call-done = (bf16[1792,2816]{1,0:T(8,128)(2,1)}, bf16[1792,2816]{1,0:T(8,128)(2,1)}, bf16[1792,2816]{1,0:T(8,128)(2,1)}) async-done(((bf16[1792,2816]{1,0:T(8,128)(2,1)}, bf16[1792,2816]{1,0:T(8,128)(2,1)}, bf16[1792,2816]{1,0:T(8,128)(2,1)}), (bf16[1792,2816]{1,0:T(8,128)(2,1)}, bf16[1792,2816]{1,0:T(8,128)(2,1)}, bf16[1792,2816]{1,0:T(8,128)(2,1)})) %all-reduce.31.cloned.1.call-update) | async-done | bytes 30277648 | tf_op jit(solution)/shard_map/psum | solution.py:245
  2656.2 128.8 %reduce-scatter.18.cloned.1.call-done = bf16[448,2048]{1,0:T(8,128)(2,1)} async-done(((bf16[1792,2048]{1,0:T(8,128)(2,1)}), bf16[448,2048]{1,0:T(8,128)(2,1)}) %reduce-scatter.18.cloned.1.call-update) | async-done | bytes 1835024 | tf_op jit(solution)/shard_map/reduce_scatter | solution.py:183
  2807.3 547.6 %while.43 = (s32[]{:T(128)}, f32[1,8,128,256]{2,3,1,0:T(8,128)}, f32[7,1,8,64,128]{4,2,3,0,1:T(8,128)}, f32[7,1,8,64,128]{4,2,3,0,1:T(8,128)}, f32[7,1,8,64,256]...) while((s32[]{:T(128)}, f32[1,8,128,256]{2,3,1,0:T(8,128)}, ...), condition=%wide.region_35.37_spmd.clone, body=%wide.region_23.36_spmd.clone.sunk | while | flops 2448786944 | bytes 53756548 | solution.py:89
  2817.8 40.7 custom-call.25
  2896.1 40.7 custom-call.25
  2974.5 40.7 custom-call.25
  3052.8 40.7 custom-call.25
  3131.1 40.7 custom-call.25
  3209.5 40.7 custom-call.25
  3287.8 40.7 custom-call.25
  3451.4 357.4 %all-gather.18.cloned.1.call-done = bf16[1792,6144]{1,0:T(8,128)(2,1)} async-done(((bf16[448,6144]{1,0:T(8,128)(2,1)}), bf16[1792,6144]{1,0:T(8,128)(2,1)}) %all-gather.18.cloned.1.call-update) | async-done | bytes 22020112 | tf_op jit(solution)/shard_map/all_gather | solution.py:146
  3903.7 32.6 all-reduce.29.cloned.1.call-done
  3969.5 40.9 all-reduce.22
  4023.7 275.5 %all-reduce.33.cloned.1.call-done = (bf16[512,6144]{1,0:T(8,128)(2,1)}, bf16[2048,512]{1,0:T(8,128)(2,1)}, bf16[512,2816]{1,0:T(8,128)(2,1)}, bf16[512,2816]{1,0:T(8,128)(2,1)}, bf16[2816,512]{1,0:T(8,128)(2,1)}) async-done(((bf16[512,6144]{1,0:T(8,128)(2,1)}, bf16[2048,512]{1,0:T(8,128)(2,1)}, bf16[512,2816]{1,0:T(8,128)(2,1)}, bf16[512,2816]{1,0:T(8,128)(2,1)}, bf16[2816,512]{1,0:T(8,128)(2,1)}), ...) | async-done | bytes 17039376 | tf_op jit(solution)/shard_map/psum | solution.py:277
  (1003 shorter events, 1056.9 us)
Async XLA Ops:
  7.2 1523.4 %copy-start = (bf16[512,2816]{1,0:T(8,128)(2,1)S(1)}, bf16[512,2816]{1,0:T(8,128)(2,1)}, u32[]{:S(2)}) copy-start(bf16[512,2816]{1,0:T(8,128)(2,1)} %param.32) | copy-start | bytes 8650756
  7.2 44.1 %all-gather.8.cloned.1.call-start = ((), (), s32[]{:S(2)}) async-start(), calls=%async_computation.7 | async-start | bytes 2752512 | tf_op jit(solution)/shard_map/all_gather | solution.py:126
  19.1 59.0 %reduce-scatter.22.cloned.1.call-start = ((), (), s32[]{:S(2)}) async-start(), calls=%async_computation.20 | async-start | bytes 1146880
  54.4 744.5 %reduce-scatter.10.cloned.1.call-start = ((), (), s32[]{:S(2)}) async-start(), calls=%async_computation.8 | async-start | bytes 55050240 | tf_op jit(solution)/shard_map/reduce_scatter | solution.py:135
  77.0 1341.4 %all-gather.10.cloned.1.call-start = ((), (), s32[]{:S(2)}) async-start(), calls=%async_computation.9 | async-start | bytes 9175040 | tf_op jit(solution)/shard_map/all_gather | solution.py:141
  77.9 750.4 %copy-start.57 = (f32[1,448]{1,0:T(1,128)}, f32[1,448]{1,0:T(1,128)S(1)}, u32[]{:S(2)}) copy-start(f32[1,448]{1,0:T(1,128)S(1)} %get-tuple-element.925) | copy-start | bytes 5380
  77.9 750.4 %copy-start.59 = (f32[1,448]{1,0:T(1,128)}, f32[1,448]{1,0:T(1,128)S(1)}, u32[]{:S(2)}) copy-start(f32[1,448]{1,0:T(1,128)S(1)} %get-tuple-element.926) | copy-start | bytes 5380
  77.9 750.4 %copy-start.61 = (f32[1,448]{1,0:T(1,128)}, f32[1,448]{1,0:T(1,128)S(1)}, u32[]{:S(2)}) copy-start(f32[1,448]{1,0:T(1,128)S(1)} %get-tuple-element.927) | copy-start | bytes 5380
  78.0 750.3 %copy-start.31 = (f32[1,4096]{1,0:T(1,128)}, f32[1,4096]{1,0:T(1,128)S(1)}, u32[]{:S(2)}) copy-start(f32[1,4096]{1,0:T(1,128)S(1)} %get-tuple-element.917) | copy-start | bytes 49156
  78.0 750.3 %copy-start.33 = (f32[1,4096]{1,0:T(1,128)}, f32[1,4096]{1,0:T(1,128)S(1)}, u32[]{:S(2)}) copy-start(f32[1,4096]{1,0:T(1,128)S(1)} %get-tuple-element.918) | copy-start | bytes 49156
  78.0 750.3 %copy-start.35 = (f32[1,4096]{1,0:T(1,128)}, f32[1,4096]{1,0:T(1,128)S(1)}, u32[]{:S(2)}) copy-start(f32[1,4096]{1,0:T(1,128)S(1)} %get-tuple-element.919) | copy-start | bytes 49156
  1283.9 172.6 %reduce-scatter.12.cloned.1.call-start = ((), (), s32[]{:S(2)}) async-start(), calls=%async_computation.10 | async-start | bytes 2752512 | tf_op jit(solution)/shard_map/reduce_scatter | solution.py:156
  1427.3 60.8 %all-gather.14.cloned.1.call-start = ((), (), s32[]{:S(2)}) async-start(), calls=%async_computation.13 | async-start | bytes 2752512 | tf_op jit(solution)/shard_map/all_gather | solution.py:130
  1427.9 92.5 %all-gather.12.cloned.1.call-start = ((), (), s32[]{:S(2)}) async-start(), calls=%async_computation.11 | async-start | bytes 2752512 | tf_op jit(solution)/shard_map/all_gather | solution.py:126
  1465.5 1146.3 %copy-start.48 = (f32[896]{0:T(1024)}, f32[896]{0:T(1024)S(1)}, u32[]{:S(2)}) copy-start(f32[896]{0:T(1024)S(1)} %add_rsqrt_fusion.2) | copy-start | bytes 10756
  1468.5 1068.9 %all-reduce.31.cloned.1.call-start = ((), (), s32[]{:S(2)}) async-start(), calls=%async_computation.21 | async-start | bytes 60555264 | tf_op jit(solution)/shard_map/psum | solution.py:245
  1538.4 1063.8 %reduce-scatter.16.cloned.1.call-start = ((), (), s32[]{:S(2)}) async-start(), calls=%async_computation.14 | async-start | bytes 2752512 | tf_op jit(solution)/shard_map/reduce_scatter | solution.py:170
  2573.1 73.9 %all-gather.16.cloned.1.call-start = ((), (), s32[]{:S(2)}) async-start(), calls=%async_computation.15 | async-start | bytes 2752512 | tf_op jit(solution)/shard_map/all_gather | solution.py:130
  2614.7 170.2 %reduce-scatter.18.cloned.1.call-start = ((), (), s32[]{:S(2)}) async-start(), calls=%async_computation.16 | async-start | bytes 9175040 | tf_op jit(solution)/shard_map/reduce_scatter | solution.py:183
  2656.1 1152.7 %all-gather.18.cloned.1.call-start = ((), (), s32[]{:S(2)}) async-start(), calls=%async_computation.17 | async-start | bytes 27525120 | tf_op jit(solution)/shard_map/all_gather | solution.py:146
  3436.7 499.6 %all-reduce.29.cloned.1.call-start = ((), (), s32[]{:S(2)}) async-start(), calls=%async_computation.19 | async-start | bytes 262144 | tf_op jit(solution)/shard_map/psum | solution.py:288
  3451.3 516.1 %reduce-scatter.20.cloned.1.call-start = ((), (), s32[]{:S(2)}) async-start(), calls=%async_computation.18 | async-start | bytes 2752512 | tf_op jit(solution)/shard_map/reduce_scatter | solution.py:170
  3828.2 191.7 %reduce-scatter.14.cloned.1.call-start = ((), (), s32[]{:S(2)}) async-start(), calls=%async_computation.12 | async-start | bytes 2752512 | tf_op jit(solution)/shard_map/reduce_scatter | solution.py:156
  3838.1 461.1 %all-reduce.33.cloned.1.call-start = ((), (), s32[]{:S(2)}) async-start(), calls=%async_computation.22 | async-start | bytes 34078720 | tf_op jit(solution)/shard_map/psum | solution.py:277
  (120 other events, 5446.1 us)
Sparse Core Ops, SparseCore 0:
  19.2 32.0 all-gather.7
  54.5 23.5 reduce-scatter.21
  80.5 718.3 reduce-scatter.9
  1284.0 134.3 all-gather.9
  1427.4 28.9 reduce-scatter.11
  1457.9 30.1 all-gather.13
  1490.2 30.1 all-gather.11
  1538.5 998.8 all-reduce.30
  2573.2 28.9 reduce-scatter.15
  2614.8 32.0 all-gather.15
  2656.2 128.7 reduce-scatter.17
  3436.8 371.9 all-gather.17
  3814.9 121.3 all-reduce.28
  3938.4 28.9 reduce-scatter.19
  3969.6 29.6 reduce-scatter.13
  4003.3 295.8 all-reduce.32
where the time goes:
time: 4340 us; the launch traced here: 4330 us
  waiting for transfers between devices  2840 us (65%)
  other arithmetic  776 us (18%)
  matrix products  417 us (10%)
  local copies, waits for them, and re-layouts  184 us (4%)
  blocking collectives  89.1 us (2%)
    psum x1, waiting for transfers between devices, on_device(): lax.psum(project(ffn_all, up_weight).astype(jnp.bfloat16), 'row')  999 us
    reduce_scatter x1, waiting for transfers between devices, split_rows(): lax.psum_scatter(first, 'row', scatter_dimension=0, tiled=True)  718 us
    another operation x56, other arithmetic, block_step(): jax.scipy.linalg.solve_triangular(system, target, lower=True, unit_diagon...  573 us
    all_gather x1, waiting for transfers between devices, join_grads(): lax.all_gather(first, 'row', axis=0, tiled=True)  357 us
    psum x1, waiting for transfers between devices, on_device(): lax.psum(mix_grad.astype(jnp.bfloat16), 'dp').astype(jnp.float32)  276 us
    all_gather x1, waiting for transfers between devices, join_rows(): return lax.all_gather(values, 'row', axis=0, tiled=True)  134 us
    reduce_scatter x1, waiting for transfers between devices, grads_to_rows(): lax.psum_scatter(term(jnp.int32(0), lax.axis_size('row') * out_rows).asty...  129 us
  transfers between devices with their start and end apart: 16, of which 15 were waited for; matrix products, arithmetic and copies ran while one was open for 3% of the time, Pallas kernels for 0%

commit v1 on v0

v1 whole, which is shorter than its diff:
```python
import functools
import jax
import jax.numpy as jnp
from jax import lax
from jax.experimental import pallas as pl
from jax.experimental.pallas import tpu as pltpu
from jax.sharding import Mesh
from jax.sharding import PartitionSpec as P

F32, BF16 = jnp.float32, jnp.bfloat16
DK, DV, TAPS = 128, 256, 4
INNER = 2 * DK + DV
PER_HEAD = INNER + DV
NN = (((1,), (0,)), ((), ()))
NT = (((1,), (1,)), ((), ()))
TN = (((0,), (0,)), ((), ()))


def mm(left, right, dims=NN):
    return lax.dot_general(left.astype(BF16), right.astype(BF16), dims, preferred_element_type=F32)


def sigmoid(values):
    return 1.0 / (1.0 + jnp.exp(-values))


def softplus(values):
    return jnp.maximum(values, 0.0) + jnp.log(1.0 + jnp.exp(-jnp.abs(values)))


def shift_down(values, lag):
    return jnp.concatenate([jnp.zeros_like(values[:lag]), values[: values.shape[0] - lag]], axis=0)


def shift_up(values, lag):
    return jnp.concatenate([values[lag:], jnp.zeros_like(values[:lag])], axis=0)


def cumsum_rows(values):
    step = 1
    while step < values.shape[0]:
        values = values + shift_down(values, step)
        step *= 2
    return values


def reverse_cumsum_rows(values):
    step = 1
    while step < values.shape[0]:
        values = values + shift_up(values, step)
        step *= 2
    return values


def prepare(head, proj, extra, seg_col, seg_row, conv, log_ref, bias_ref):
    length = proj.shape[0]
    summed = conv[TAPS - 1 : TAPS] * proj[:, :INNER]
    keeps = []
    for lag in range(1, TAPS):
        keep = (shift_down(seg_col + 1.0, lag) == seg_col + 1.0).astype(F32)
        keeps.append(keep)
        summed = summed + conv[TAPS - 1 - lag : TAPS - lag] * (shift_down(proj[:, :INNER], lag) * keep)
    gate_conv = sigmoid(summed)
    active = summed * gate_conv
    lane = lax.broadcasted_iota(jnp.int32, extra.shape, 1)
    write = jnp.sum(jnp.where(lane == 2 * head, extra, 0.0), axis=1, keepdims=True)
    drive = jnp.sum(jnp.where(lane == 2 * head + 1, extra, 0.0), axis=1, keepdims=True)
    beta = sigmoid(write)
    drive = drive + bias_ref[head]
    rate = jnp.exp(jnp.full((1, 1), log_ref[head], F32))
    decay = -rate * softplus(drive)
    total = cumsum_rows(decay)
    rows = lax.broadcasted_iota(jnp.int32, (length, length), 0)
    cols = lax.broadcasted_iota(jnp.int32, (length, length), 1)
    total_row = jnp.sum(jnp.where(rows == cols, total, 0.0), axis=0, keepdims=True)
    weight = jnp.exp(jnp.where((rows >= cols) & (seg_col == seg_row), total - total_row, -1e30))
    raw_q, raw_k, value = active[:, :DK], active[:, DK : 2 * DK], active[:, 2 * DK :]
    scale_q = lax.rsqrt(jnp.sum(raw_q * raw_q, axis=1, keepdims=True) + 1e-06)
    scale_k = lax.rsqrt(jnp.sum(raw_k * raw_k, axis=1, keepdims=True) + 1e-06)
    query = (raw_q * scale_q * DK ** (-0.5)).astype(BF16)
    key = (raw_k * scale_k).astype(BF16)
    inner = mm(key, key, NT)
    strict = jnp.where(rows > cols, weight, 0.0)
    return dict(
        summed=summed, keeps=keeps, gate_conv=gate_conv, raw_q=raw_q, raw_k=raw_k, value=value,
        scale_q=scale_q, scale_k=scale_k, query=query, key=key, inner=inner, weight=weight,
        strict=strict, beta=beta, drive=drive, rate=rate, decay=decay, rows=rows, cols=cols,
    )


def forward_kernel(head, proj_ref, extra_ref, segc_ref, segr_ref, conv_ref, log_ref, bias_ref, gain_ref,
                   mixed_ref, solve_ref, work):
    length = proj_ref.shape[0]
    size = work.shape[0]
    p = prepare(head, proj_ref[...], extra_ref[...], segc_ref[...], segr_ref[0], conv_ref[...], log_ref, bias_ref)
    lower = p["beta"] * p["strict"] * p["inner"]
    if size != length:
        work[...] = jnp.zeros_like(work)
    work[0:length, 0:length] = lower
    tile = min(128, size)
    blocks = size // tile
    r = lax.broadcasted_iota(jnp.int32, (tile, tile), 0)
    c = lax.broadcasted_iota(jnp.int32, (tile, tile), 1)
    parts = [work[b * tile : (b + 1) * tile, b * tile : (b + 1) * tile] for b in range(blocks)]
    eye = (r == c).astype(F32)
    inv = [eye - jnp.where((r // 2 == c // 2), part, 0.0) for part in parts]
    step = 2
    while step < tile:
        pick = (r // (2 * step) == c // (2 * step)) & (r // step != c // step)
        lows = [mm(jnp.where(pick, part, 0.0), x) for part, x in zip(parts, inv)]
        inv = [x - mm(x, low) for x, low in zip(inv, lows)]
        step *= 2
    for b in range(blocks):
        work[b * tile : (b + 1) * tile, b * tile : (b + 1) * tile] = inv[b]
    step = tile
    while step < size:
        for start in range(0, size, 2 * step):
            mid, end = start + step, start + 2 * step
            low = mm(work[mid:end, start:mid], work[start:mid, start:mid])
            work[mid:end, start:mid] = -mm(work[mid:end, mid:end], low)
        step *= 2
    solve = work[0:length, 0:length].astype(BF16)
    solve_ref[0] = solve
    fresh = mm(solve, p["beta"] * p["value"])
    out = mm(mm(p["query"], p["key"], NT) * p["weight"], fresh)
    scale = lax.rsqrt(jnp.sum(out * out, axis=1, keepdims=True) * (1.0 / DV) + 1e-05)
    gate = proj_ref[:, INNER:]
    mixed_ref[...] = (out * scale * gain_ref[...] * (gate * sigmoid(gate))).astype(BF16)


def backward_kernel(head, last, *refs):
    if last:
        (proj_ref, extra_ref, segc_ref, segr_ref, conv_ref, log_ref, bias_ref, gain_ref, solve_ref, grad_ref,
         other_ref, gproj_ref, gconv_ref, gsmall_ref) = refs
    else:
        (proj_ref, extra_ref, segc_ref, segr_ref, conv_ref, log_ref, bias_ref, gain_ref, solve_ref, grad_ref,
         gproj_ref, gextra_ref, gconv_ref, gsmall_ref) = refs
    conv = conv_ref[...]
    p = prepare(head, proj_ref[...], extra_ref[...], segc_ref[...], segr_ref[0], conv, log_ref, bias_ref)
    weight, strict, inner, beta, value = p["weight"], p["strict"], p["inner"], p["beta"], p["value"]
    query, key = p["query"], p["key"]
    solve = solve_ref[0]
    fresh = mm(solve, beta * value).astype(BF16)
    scores = mm(query, key, NT)
    probs = (scores * weight).astype(BF16)
    out = mm(probs, fresh)
    scale = lax.rsqrt(jnp.sum(out * out, axis=1, keepdims=True) * (1.0 / DV) + 1e-05)
    normed = out * scale
    gate = proj_ref[:, INNER:]
    gate_sig = sigmoid(gate)
    grad = grad_ref[...].astype(F32)
    gain = gain_ref[...]
    through = grad * normed
    ggate = through * gain * (gate_sig * (1.0 + gate * (1.0 - gate_sig)))
    ggain = jnp.sum(through * (gate * gate_sig), axis=0, keepdims=True)
    gnormed = grad * gain * (gate * gate_sig)
    gout = scale * (gnormed - normed * (jnp.sum(gnormed * normed, axis=1, keepdims=True) * (1.0 / DV)))
    gout = gout.astype(BF16)
    gprobs = mm(gout, fresh, NT)
    gfresh = mm(probs, gout, TN)
    gtarget = mm(solve, gfresh, TN)
    glower = -mm(gtarget, fresh, NT) * strict
    gscores = gprobs * weight
    tilt = glower * inner
    flow = gscores * scores + beta * tilt
    gbeta = jnp.sum(tilt, axis=1, keepdims=True) + jnp.sum(gtarget * value, axis=1, keepdims=True)
    gscores = gscores.astype(BF16)
    ginner = (beta * glower).astype(BF16)
    gquery = mm(gscores, key)
    gkey = mm(gscores, query, TN) + mm(ginner, key) + mm(ginner, key, TN)
    col_flow = jnp.sum(flow, axis=0, keepdims=True)
    col_flow = jnp.sum(jnp.where(p["rows"] == p["cols"], col_flow, 0.0), axis=1, keepdims=True)
    gdecay = reverse_cumsum_rows(jnp.sum(flow, axis=1, keepdims=True) - col_flow)
    raw_q, raw_k, scale_q, scale_k = p["raw_q"], p["raw_k"], p["scale_q"], p["scale_k"]
    gq = (DK ** (-0.5)) * scale_q * (
        gquery - raw_q * (scale_q * scale_q * jnp.sum(gquery * raw_q, axis=1, keepdims=True)))
    gk = scale_k * (gkey - raw_k * (scale_k * scale_k * jnp.sum(gkey * raw_k, axis=1, keepdims=True)))
    gactive = jnp.concatenate([gq, gk, beta * gtarget], axis=1)
    gsummed = gactive * (p["gate_conv"] * (1.0 + p["summed"] * (1.0 - p["gate_conv"])))
    source = proj_ref[:, :INNER]
    gsource = conv[TAPS - 1 : TAPS] * gsummed
    gconv_ref[0, TAPS - 1 : TAPS, :] = jnp.sum(gsummed * source, axis=0, keepdims=True)
    for lag in range(1, TAPS):
        kept = gsummed * p["keeps"][lag - 1]
        gsource = gsource + conv[TAPS - 1 - lag : TAPS - lag] * shift_up(kept, lag)
        gconv_ref[0, TAPS - 1 - lag : TAPS - lag, :] = jnp.sum(kept * shift_down(source, lag), axis=0, keepdims=True)
    gdrive = -p["rate"] * gdecay * sigmoid(p["drive"])
    gwrite = gbeta * beta * (1.0 - beta)
    lane = lax.broadcasted_iota(jnp.int32, extra_ref.shape, 1)
    gextra = jnp.where(lane == 2 * head, gwrite, jnp.where(lane == 2 * head + 1, gdrive, 0.0))
    gproj_ref[:, :INNER] = gsource.astype(BF16)
    gproj_ref[:, INNER:PER_HEAD] = ggate.astype(BF16)
    if last:
        gproj_ref[:, PER_HEAD:] = (gextra + other_ref[...].astype(F32)).astype(BF16)
    else:
        gextra_ref[...] = gextra.astype(BF16)
    glog = jnp.sum(gdecay * p["decay"], axis=0, keepdims=True)
    gbias = jnp.sum(gdrive, axis=0, keepdims=True)
    lane = lax.broadcasted_iota(jnp.int32, (1, 128), 1)
    gsmall_ref[0, :, 0:DV] = ggain
    gsmall_ref[0, :, DV:] = jnp.where(lane == 0, glog, jnp.where(lane == 1, gbias, 0.0))


def common_specs(length, heads, head, extra_block):
    smem = pl.BlockSpec(memory_space=pltpu.SMEM)
    return [
        pl.BlockSpec((length, PER_HEAD), lambda s: (s, 0)),
        pl.BlockSpec((length, 128), lambda s: (s, extra_block)),
        pl.BlockSpec((length, 1), lambda s: (s, 0)),
        pl.BlockSpec((1, 1, length), lambda s: (s, 0, 0)),
        pl.BlockSpec((TAPS, INNER), lambda s: (0, head)),
        smem,
        smem,
        pl.BlockSpec((1, DV), lambda s: (0, 0)),
    ]


def mixer_forward(head, heads, proj, extra, extra_block, seg_col, seg_row, conv, log, bias, gain):
    count, _, length = seg_row.shape
    tokens = count * length
    size = 64
    while size < length:
        size *= 2
    return pl.pallas_call(
        functools.partial(forward_kernel, head),
        grid=(count,),
        in_specs=common_specs(length, heads, head, extra_block),
        out_specs=[
            pl.BlockSpec((length, DV), lambda s: (s, 0)),
            pl.BlockSpec((1, length, length), lambda s: (s, 0, 0)),
        ],
        out_shape=[
            jax.ShapeDtypeStruct((tokens, DV), BF16),
            jax.ShapeDtypeStruct((count, length, length), BF16),
        ],
        scratch_shapes=[pltpu.VMEM((size, size), F32)],
        compiler_params=pltpu.CompilerParams(vmem_limit_bytes=56 << 20),
        name="mixer_forward",
    )(proj, extra, seg_col, seg_row, conv, log, bias, gain)


def mixer_backward(head, heads, proj, extra, extra_block, seg_col, seg_row, conv, log, bias, gain, solve, grad, other):
    count, _, length = seg_row.shape
    tokens = count * length
    last = other is not None
    in_specs = common_specs(length, heads, head, extra_block) + [
        pl.BlockSpec((1, length, length), lambda s: (s, 0, 0)),
        pl.BlockSpec((length, DV), lambda s: (s, head)),
    ]
    args = [proj, extra, seg_col, seg_row, conv, log, bias, gain, solve, grad]
    width = PER_HEAD
    tail_specs = [
        pl.BlockSpec((1, TAPS, INNER), lambda s: (s, 0, 0)),
        pl.BlockSpec((1, 1, DV + 128), lambda s: (s, 0, 0)),
    ]
    tail_shapes = [
        jax.ShapeDtypeStruct((count, TAPS, INNER), F32),
        jax.ShapeDtypeStruct((count, 1, DV + 128), F32),
    ]
    mid_specs, mid_shapes = [], []
    if last:
        width += 128
        in_specs.append(pl.BlockSpec((length, 128), lambda s: (s, 0)))
        args.append(other)
    else:
        mid_specs = [pl.BlockSpec((length, 128), lambda s: (s, 0))]
        mid_shapes = [jax.ShapeDtypeStruct((tokens, 128), BF16)]
    return pl.pallas_call(
        functools.partial(backward_kernel, head, last),
        grid=(count,),
        in_specs=in_specs,
        out_specs=[pl.BlockSpec((length, width), lambda s: (s, 0))] + mid_specs + tail_specs,
        out_shape=[jax.ShapeDtypeStruct((tokens, width), BF16)] + mid_shapes + tail_shapes,
        compiler_params=pltpu.CompilerParams(vmem_limit_bytes=60 << 20),
        name="mixer_backward",
    )(*args)


MESH_ID = pl.DeviceIdType.MESH
ANY_SPEC = pl.BlockSpec(memory_space=pl.ANY)


def meet(targets):
    barrier = pltpu.get_barrier_semaphore()
    for target in targets:
        pl.semaphore_signal(barrier, inc=1, device_id=target, device_id_type=MESH_ID)
    pl.semaphore_wait(barrier, len(targets))


def remote(source, dest, send, recv, index, target):
    return pltpu.make_async_remote_copy(
        src_ref=source,
        dst_ref=dest,
        send_sem=send.at[index],
        recv_sem=recv.at[index],
        device_id=target,
        device_id_type=MESH_ID,
    )


def team_places(part_name):
    part, col = lax.axis_index(part_name), lax.axis_index("col")
    across, twin, other = lax.rem(part + 2, 4), part + 1 - 2 * lax.rem(part, 2), 1 - col
    targets = {
        "x": {part_name: across, "col": col},
        "y": {part_name: part, "col": other},
        "core": {part_name: twin, "col": col},
    }
    slots = [across * 2 + other, across * 2 + col, part * 2 + other, part * 2 + col]
    far = lax.rem(twin + 2, 4)
    twin_slots = [far * 2 + other, far * 2 + col, twin * 2 + other, twin * 2 + col]
    return targets, slots, twin_slots


def gather_kernel(part_name, src, out, keep, send, recv):
    targets, (diag, across, other, own), _ = team_places(part_name)
    half = src.shape[0] // 2
    first, second = pl.ds(0, half), pl.ds(half, half)
    meet(list(targets.values()))
    local = pltpu.make_async_copy(src, out.at[own], keep)
    local.start()
    x_first = remote(src.at[first], out.at[own, first], send, recv, 0, targets["x"])
    x_second = remote(src.at[second], out.at[own, second], send, recv, 1, targets["x"])
    y_second = remote(src.at[second], out.at[own, second], send, recv, 2, targets["y"])
    y_first = remote(src.at[first], out.at[own, first], send, recv, 3, targets["y"])
    core_own = remote(src, out.at[own], send, recv, 4, targets["core"])
    for copy in (x_first, y_second, core_own, x_second, y_first):
        copy.start()
    y_pass = remote(out.at[across, first], out.at[across, first], send, recv, 5, targets["y"])
    x_pass = remote(out.at[other, second], out.at[other, second], send, recv, 6, targets["x"])
    core_x = remote(out.at[across], out.at[across], send, recv, 7, targets["core"])
    core_y = remote(out.at[other], out.at[other], send, recv, 8, targets["core"])
    core_first = remote(out.at[diag, first], out.at[diag, first], send, recv, 9, targets["core"])
    core_second = remote(out.at[diag, second], out.at[diag, second], send, recv, 10, targets["core"])
    x_first.wait_recv()
    y_pass.start()
    y_second.wait_recv()
    x_pass.start()
    x_second.wait_recv()
    core_x.start()
    y_first.wait_recv()
    core_y.start()
    y_pass.wait_recv()
    core_first.start()
    x_pass.wait_recv()
    core_second.start()
    for copy in (core_own, core_x, core_y, core_first, core_second):
        copy.wait_recv()
    for copy in (x_first, x_second, y_second, y_first, core_own, y_pass, x_pass, core_x, core_y, core_first, core_second):
        copy.wait_send()
    local.wait()


def team_gather_kernel(part_name, values, ident):
    rows, width = values.shape
    return pl.pallas_call(
        functools.partial(gather_kernel, part_name),
        in_specs=[ANY_SPEC],
        out_specs=ANY_SPEC,
        out_shape=jax.ShapeDtypeStruct((8, rows, width), values.dtype),
        scratch_shapes=[
            pltpu.SemaphoreType.DMA,
            pltpu.SemaphoreType.DMA((11,)),
            pltpu.SemaphoreType.DMA((11,)),
        ],
        compiler_params=pltpu.CompilerParams(collective_id=ident, has_side_effects=True),
        name="team_gather",
    )(values).reshape(8 * rows, width)


def add_rows(dest, sources, start, count):
    @pl.loop(0, count // 16)
    def _(step):
        rows = pl.ds(pl.multiple_of(start + step * 16, 16), 16)
        total = sources[0][0][rows if sources[0][1] else pl.ds(pl.multiple_of(step * 16, 16), 16), :].astype(F32)
        for ref, whole in sources[1:]:
            total = total + ref[rows if whole else pl.ds(pl.multiple_of(step * 16, 16), 16), :].astype(F32)
        dest[rows, :] = total.astype(dest.dtype)


def scatter_kernel(part_name, src, out, mine, twin, sent, relay, final, keep, send, recv):
    targets, slots, twin_slots = team_places(part_name)
    rows = out.shape[0]
    half = rows // 2
    first, second = pl.ds(0, half), pl.ds(half, half)
    meet(list(targets.values()))
    swaps, loads = [], []
    for item in range(4):
        swaps.append(remote(src.at[twin_slots[item]], twin.at[item], send, recv, item, targets["core"]))
        loads.append(pltpu.make_async_copy(src.at[slots[item]], mine.at[item], keep.at[item]))
        swaps[item].start()
        loads[item].start()

    def arrive(item):
        loads[item].wait()
        swaps[item].wait_recv()

    def both(item):
        return [(mine.at[item], True), (twin.at[item], True)]

    relay_x = remote(sent.at[0, first], relay.at[0], send, recv, 4, targets["x"])
    relay_y = remote(sent.at[0, second], relay.at[1], send, recv, 5, targets["y"])
    x_first = remote(sent.at[1, first], final.at[0, first], send, recv, 6, targets["x"])
    x_second = remote(sent.at[1, second], final.at[0, second], send, recv, 7, targets["x"])
    y_second = remote(sent.at[2, second], final.at[1, second], send, recv, 8, targets["y"])
    y_first = remote(sent.at[2, first], final.at[1, first], send, recv, 9, targets["y"])
    arrive(0)
    add_rows(sent.at[0], both(0), 0, half)
    relay_x.start()
    add_rows(sent.at[0], both(0), half, half)
    relay_y.start()
    arrive(1)
    add_rows(sent.at[1], both(1), 0, half)
    x_first.start()
    arrive(2)
    add_rows(sent.at[2], both(2), half, half)
    y_second.start()
    relay_y.wait_recv()
    add_rows(sent.at[1], both(1) + [(relay.at[1], False)], half, half)
    x_second.start()
    relay_x.wait_recv()
    add_rows(sent.at[2], both(2) + [(relay.at[0], False)], 0, half)
    y_first.start()
    arrive(3)
    x_first.wait_recv()
    y_first.wait_recv()
    ends = both(3) + [(final.at[0], True), (final.at[1], True)]
    add_rows(out, ends, 0, half)
    x_second.wait_recv()
    y_second.wait_recv()
    add_rows(out, ends, half, half)
    for copy in swaps + [relay_x, relay_y, x_first, x_second, y_second, y_first]:
        copy.wait_send()


def team_scatter_kernel(part_name, values, ident):
    rows, width = values.shape[0] // 8, values.shape[1]
    return pl.pallas_call(
        functools.partial(scatter_kernel, part_name),
        in_specs=[ANY_SPEC],
        out_specs=pl.BlockSpec(memory_space=pltpu.VMEM),
        out_shape=jax.ShapeDtypeStruct((rows, width), F32),
        scratch_shapes=[
            pltpu.VMEM((4, rows, width), BF16),
            pltpu.VMEM((4, rows, width), BF16),
            pltpu.VMEM((3, rows, width), BF16),
            pltpu.VMEM((2, rows // 2, width), BF16),
            pltpu.VMEM((2, rows, width), BF16),
            pltpu.SemaphoreType.DMA((4,)),
            pltpu.SemaphoreType.DMA((10,)),
            pltpu.SemaphoreType.DMA((10,)),
        ],
        compiler_params=pltpu.CompilerParams(collective_id=ident, has_side_effects=True, vmem_limit_bytes=40 << 20),
        name="team_scatter",
    )(values.reshape(8, rows, width))


def spread_kernel(src, out, middle, keep, send, recv):
    row, col = lax.axis_index("row"), lax.axis_index("col")
    meet([{"col": 1 - col}] + [{"row": lax.rem(row + hop, 4)} for hop in range(1, 4)])
    hops = []
    for item in range(2):
        hops.append(remote(src.at[2 * item + 1 - col], middle.at[item], send, recv, item, {"col": 1 - col}))
        hops[item].start()

    def pieces(wait_first):
        for side in range(2):
            home = col if side == 0 else 1 - col
            for item in range(2):
                if side == 1 and wait_first:
                    hops[item].wait_recv()
                source = src.at[2 * item + col] if side == 0 else middle.at[item]
                to_row = 2 * home + item
                copy = pltpu.make_async_remote_copy(
                    src_ref=source,
                    dst_ref=out.at[row],
                    send_sem=send.at[2 + 2 * side + item],
                    recv_sem=recv.at[2 + row],
                    device_id={"row": to_row},
                    device_id_type=MESH_ID,
                )
                yield to_row == row, copy, pltpu.make_async_copy(source, out.at[row], keep)

    for here, far, near in pieces(True):
        pl.when(here)(near.start)
        pl.when(jnp.logical_not(here))(far.start)
    for hop in range(1, 4):
        index = lax.rem(row + hop, 4)
        pltpu.make_async_remote_copy(
            src_ref=src.at[0],
            dst_ref=out.at[index],
            send_sem=send.at[0],
            recv_sem=recv.at[2 + index],
            device_id={"row": index},
            device_id_type=MESH_ID,
        ).wait_recv()
    for here, far, near in pieces(False):
        pl.when(here)(near.wait)
        pl.when(jnp.logical_not(here))(far.wait_send)
    for hop in hops:
        hop.wait_send()


def spread_call(values, ident):
    tokens, width = values.shape[0] // 4, values.shape[1]
    return pl.pallas_call(
        spread_kernel,
        in_specs=[ANY_SPEC],
        out_specs=ANY_SPEC,
        out_shape=jax.ShapeDtypeStruct((4, tokens, width), values.dtype),
        scratch_shapes=[
            pltpu.VMEM((2, tokens, width), values.dtype),
            pltpu.SemaphoreType.DMA,
            pltpu.SemaphoreType.DMA((6,)),
            pltpu.SemaphoreType.DMA((6,)),
        ],
        compiler_params=pltpu.CompilerParams(collective_id=ident, has_side_effects=True),
        name="spread",
    )(values.reshape(4, tokens, width))


def deal(count, inward, part_name, rows_n, cols_n, refs):
    srcs, outs = refs[:count], refs[count : 2 * count]
    keep, send, recv = refs[2 * count :]
    row, col = lax.axis_index("row"), lax.axis_index("col")
    spot = row * cols_n + col

    def holder(index):
        return index, spot // rows_n

    def owner(index):
        place = col * rows_n + index
        return place // cols_n, lax.rem(place, cols_n)

    give, take = (owner, holder) if inward else (holder, owner)
    mark = row if inward else lax.rem(spot, rows_n)
    barrier = pltpu.get_barrier_semaphore()
    for index in range(rows_n):
        to_row, to_col = take(index)

        @pl.when((to_row != row) | (to_col != col))
        def _():
            pl.semaphore_signal(barrier, inc=1, device_id={"row": to_row, "col": to_col}, device_id_type=MESH_ID)

    kept = jnp.int32(0)
    for index in range(rows_n):
        to_row, to_col = give(index)
        kept = kept + ((to_row == row) & (to_col == col)).astype(jnp.int32)
    pl.semaphore_wait(barrier, rows_n - kept)

    def each(act_local, act_remote):
        for item in range(count):
            for index in range(rows_n):
                to_row, to_col = give(index)
                here = (to_row == row) & (to_col == col)

                @pl.when(here)
                def _():
                    act_local(pltpu.make_async_copy(srcs[item].at[index], outs[item].at[mark], keep.at[item]))

                @pl.when(jnp.logical_not(here))
                def _():
                    act_remote(
                        pltpu.make_async_remote_copy(
                            src_ref=srcs[item].at[index],
                            dst_ref=outs[item].at[mark],
                            send_sem=send.at[item, index],
                            recv_sem=recv.at[item, mark],
                            device_id={"row": to_row, "col": to_col},
                            device_id_type=MESH_ID,
                        )
                    )

    each(lambda copy: copy.start(), lambda copy: copy.start())
    for item in range(count):
        for index in range(rows_n):
            from_row, from_col = take(index)

            @pl.when((from_row != row) | (from_col != col))
            def _():
                pltpu.make_async_remote_copy(
                    src_ref=srcs[item].at[0],
                    dst_ref=outs[item].at[index],
                    send_sem=send.at[item, 0],
                    recv_sem=recv.at[item, index],
                    device_id={"row": from_row, "col": from_col},
                    device_id_type=MESH_ID,
                ).wait_recv()

    each(lambda copy: copy.wait(), lambda copy: copy.wait_send())


def deal_kernel(lay, inward, values, ident):
    count = len(values)
    shapes = [jax.ShapeDtypeStruct(v.shape, v.dtype) for v in values]

    def body(*refs):
        deal(count, inward, lay.part, lay.rows, lay.cols, refs)

    return pl.pallas_call(
        body,
        in_specs=[ANY_SPEC] * count,
        out_specs=[ANY_SPEC] * count,
        out_shape=shapes,
        scratch_shapes=[
            pltpu.SemaphoreType.DMA((count,)),
            pltpu.SemaphoreType.DMA((count, lay.rows)),
            pltpu.SemaphoreType.DMA((count, lay.rows)),
        ],
        compiler_params=pltpu.CompilerParams(collective_id=ident, has_side_effects=True),
        name="deal",
    )(*values)


SEQ = 448


def project(left, right):
    return jnp.dot(left, right, preferred_element_type=F32)


def project_back(left, right):
    return lax.dot_general(left, right, NT, preferred_element_type=F32)


def weight_grad(left, right):
    return lax.dot_general(left, right, TN, preferred_element_type=F32).astype(BF16)


class Layout:
    def __init__(self, mesh, heads):
        dp, self.rows, self.cols = (mesh.shape[name] for name in ("dp", "row", "col"))
        ways = dp
        while dp % ways or (heads // self.cols) % ways:
            ways -= 1
        self.ways = ways
        if ways == dp:
            self.mesh, self.shared, self.part = mesh, (), "dp"
        else:
            devices = mesh.devices.reshape(dp // ways, ways, self.rows, self.cols)
            self.mesh = Mesh(devices, ("group", "part", "row", "col"))
            self.shared, self.part = ("group",), "part"
        self.data = self.shared + (self.part,)
        self.team = (self.part, "col")
        self.native = (ways, self.rows, self.cols) == (4, 4, 2)
        self.next_id = 0

    def fresh_id(self):
        self.next_id += 1
        return self.next_id


def spread(lay, values):
    if lay.native:
        moved = spread_call(values, lay.fresh_id())
        return jnp.moveaxis(moved, 0, 1).reshape(moved.shape[1], -1)
    local = values.shape[0]
    whole = lax.all_gather(values, "col", axis=0, tiled=True)
    whole = lax.all_to_all(whole, "row", split_axis=0, concat_axis=1, tiled=True)
    mine = local // lay.rows
    return lax.dynamic_slice_in_dim(whole, lax.axis_index("col") * mine, mine, 0)


def unspread(lay, values):
    if lay.native:
        pieces = [jnp.moveaxis(v.reshape(v.shape[0], lay.rows, -1), 1, 0) for v in values]
        return [v.reshape(-1, v.shape[2]) for v in deal_kernel(lay, False, pieces, lay.fresh_id())]
    results = []
    for value in values:
        local = value.shape[0] * lay.rows
        whole = lax.all_gather(value, "col", axis=0, tiled=True)
        whole = lax.all_to_all(whole, "row", split_axis=1, concat_axis=0, tiled=True)
        results.append(lax.dynamic_slice_in_dim(whole, lax.axis_index("col") * local, local, 0))
    return results


def team_gather(lay, values):
    if lay.native:
        return team_gather_kernel(lay.part, values, lay.fresh_id())
    return lax.all_gather(values, lay.team, axis=0, tiled=True)


def team_scatter(lay, values):
    if lay.native:
        return team_scatter_kernel(lay.part, values.astype(BF16), lay.fresh_id())
    return lax.psum_scatter(values.astype(BF16), lay.team, scatter_dimension=0, tiled=True).astype(F32)


def norm_forward(values):
    scale = lax.rsqrt(jnp.mean(values * values, axis=1, keepdims=True) + 1e-05)
    return values * scale, scale


def norm_backward(grad, normed, scale, gain):
    scaled = grad * gain
    inner = jnp.mean(scaled * normed, axis=1, keepdims=True)
    return scale * (scaled - normed * inner), jnp.sum(grad * normed, axis=0)


def on_device(
    lay,
    block_input,
    segment_ids,
    attn_gain,
    mix_weight,
    decay_weight,
    conv_weight,
    decay_log,
    decay_bias,
    out_gain,
    out_weight,
    ffn_gain,
    gate_weight,
    up_weight,
    down_weight,
    cotangent,
):
    part = lax.axis_index(lay.part)
    heads = decay_log.shape[0] // lay.ways
    units = gate_weight.shape[1] // lay.ways
    width = mix_weight.shape[0]

    def mine(values, dim, size):
        return lax.dynamic_slice_in_dim(values, part * size, size, dim)

    def gather_rows(values):
        return lax.all_gather(values, "row", axis=0, tiled=False)

    mix_mine = mine(mix_weight, 1, heads * PER_HEAD)
    decay_mine = mine(decay_weight, 1, heads * 2)
    decay_pad = jnp.pad(decay_mine, ((0, 0), (0, 128 - heads * 2)))
    head_weights = []
    for head in range(heads):
        piece = mix_mine[:, head * PER_HEAD : (head + 1) * PER_HEAD]
        if head == 0:
            piece = jnp.concatenate([piece, decay_pad], axis=1)
        head_weights.append(gather_rows(piece).reshape(lay.rows * width, -1))
    out_all = gather_rows(mine(out_weight, 0, heads * DV))
    pair = jnp.concatenate([mine(gate_weight, 1, units), mine(up_weight, 1, units)], axis=1)
    pair_all = gather_rows(pair).reshape(lay.rows * width, -1)
    down_all = gather_rows(mine(down_weight, 0, units))
    gains = lax.all_gather(jnp.stack([attn_gain, ffn_gain]), "row", axis=1, tiled=True)
    gain_one, gain_two = gains[0], gains[1]
    segments = lax.all_gather(segment_ids, lay.part, axis=0, tiled=True).astype(F32)
    sequences = segments.shape[0] // SEQ
    seg_col = segments.reshape(-1, 1)
    seg_row = segments.reshape(sequences, 1, SEQ)
    conv_mine = mine(conv_weight, 1, heads * INNER)
    log_mine, bias_mine = mine(decay_log, 0, heads), mine(decay_bias, 0, heads)
    gain_row = out_gain.reshape(1, -1)

    stored = spread(lay, block_input).astype(F32)
    normed_one, scale_one = norm_forward(stored)
    attn_all = team_gather(lay, (normed_one * gain_one).astype(BF16))
    projs = [project(attn_all, weight) for weight in head_weights]
    shared = (projs[0], PER_HEAD // 128, seg_col, seg_row, conv_mine, log_mine, bias_mine, gain_row)
    mixed, solves = [], []
    for head in range(heads):
        values, solve = mixer_forward(head, heads, projs[head], *shared)
        mixed.append(values)
        solves.append(solve)
    mixed = jnp.concatenate(mixed, axis=1)
    tokens = mixed.shape[0]

    def wide(left, stack):
        return jnp.einsum("tk,rkn->trn", left, stack, preferred_element_type=F32).reshape(tokens, -1)

    def wide_back(left, stack):
        left = left.reshape(tokens, lay.rows, -1)
        return jnp.einsum("trn,rkn->tk", left, stack, preferred_element_type=F32)

    def wide_grad(left, right):
        right = right.reshape(tokens, lay.rows, -1)
        return jnp.einsum("tk,trn->rkn", left, right, preferred_element_type=F32).astype(BF16)

    def sum_rows(grads):
        grads = lax.psum_scatter(grads, "row", scatter_dimension=0, tiled=False)
        return lax.psum(grads, lay.shared) if lay.shared else grads

    residual = stored + team_scatter(lay, wide(mixed, out_all))

    normed_two, scale_two = norm_forward(residual)
    ffn_all = team_gather(lay, (normed_two * gain_two).astype(BF16))
    both = project(ffn_all, pair_all)
    gate, up_values = both[:, :units], both[:, units:]
    gate_sig = jax.nn.sigmoid(gate)
    hidden = (gate * gate_sig * up_values).astype(BF16)
    block_output = (residual + team_scatter(lay, wide(hidden, down_all))).astype(BF16)

    out_grads = spread(lay, cotangent)
    out_grads_all = team_gather(lay, out_grads)
    grad_hidden = wide_back(out_grads_all, down_all)
    grad_gate = grad_hidden * up_values * gate_sig * (1.0 + gate * (1.0 - gate_sig))
    grad_up = grad_hidden * gate * gate_sig
    grad_both = jnp.concatenate([grad_gate.astype(BF16), grad_up.astype(BF16)], axis=1)
    grad_ffn = team_scatter(lay, project_back(grad_both, pair_all))
    pair_grad = sum_rows(weight_grad(ffn_all, grad_both).reshape(lay.rows, width, -1))
    down_grad = sum_rows(wide_grad(hidden, out_grads_all))
    grad_norm, ffn_gain_part = norm_backward(grad_ffn, normed_two, scale_two, gain_two)
    grad_residual = out_grads.astype(F32) + grad_norm
    branch_all = team_gather(lay, grad_residual.astype(BF16))
    grad_mixed = wide_back(branch_all, out_all)
    out_grad = sum_rows(wide_grad(mixed, branch_all))
    other = jnp.zeros((tokens, 128), BF16)
    proj_grads, mix_grads, conv_parts, small_parts = [], [], [], []
    for head in reversed(range(heads)):
        common = (head, heads, projs[head], *shared, solves[head], grad_mixed)
        if head:
            grad, extra, conv_part, small_part = mixer_backward(*common, None)
            other = other + extra
        else:
            grad, conv_part, small_part = mixer_backward(*common, other)
        proj_grads.insert(0, grad)
        conv_parts.insert(0, conv_part.sum(0))
        small_parts.insert(0, small_part.sum(0)[0])
        mix_grads.insert(0, sum_rows(weight_grad(attn_all, grad).reshape(lay.rows, width, -1)))
    grad_attn = sum(project_back(grad, weight) for grad, weight in zip(proj_grads, head_weights))
    grad_attn = team_scatter(lay, grad_attn)
    grad_norm, attn_gain_part = norm_backward(grad_attn, normed_one, scale_one, gain_one)
    input_grad = (grad_residual + grad_norm).astype(BF16)
    block_output, input_grad = unspread(lay, [block_output, input_grad])

    def join(grads):
        return lax.all_gather(grads, lay.part, axis=0, tiled=False)

    def columns(stack):
        return jnp.moveaxis(stack, 0, 1).reshape(stack.shape[1], -1).astype(F32)

    mix_stack = [join(grads) for grads in mix_grads]
    decay_grad = columns(mix_stack[0][:, :, PER_HEAD : PER_HEAD + 2 * heads])
    mix_grad = columns(jnp.concatenate([stack[:, :, :PER_HEAD] for stack in mix_stack], axis=2))
    pair_stack = join(pair_grad)
    gate_grad, up_grad = columns(pair_stack[:, :, :units]), columns(pair_stack[:, :, units:])
    out_weight_grad = join(out_grad).reshape(-1, width).astype(F32)
    down_weight_grad = join(down_grad).reshape(-1, width).astype(F32)

    everyone = lay.data + ("row", "col")
    place = part * lay.cols + lax.axis_index("col")
    slots = lay.ways * lay.cols
    pick = (jnp.arange(slots) == place).astype(F32)[:, None]
    own = jnp.concatenate(
        [jnp.concatenate(conv_parts, axis=1).reshape(-1)]
        + [jnp.stack([part_of[DV + item] for part_of in small_parts]) for item in range(2)]
    )
    sums, gain_sum, ffn_sum, attn_sum = lax.psum(
        (
            pick * own[None, :],
            sum(part_of[:DV] for part_of in small_parts),
            ffn_gain_part,
            attn_gain_part,
        ),
        everyone,
    )
    sums = sums.reshape(lay.ways, lay.cols, -1)
    sums = lax.dynamic_index_in_dim(sums, lax.axis_index("col"), 1, keepdims=False)
    split = TAPS * heads * INNER
    conv_grad = jnp.moveaxis(sums[:, :split].reshape(lay.ways, TAPS, -1), 0, 1).reshape(TAPS, -1)
    log_grad = sums[:, split : split + heads].reshape(-1)
    bias_grad = sums[:, split + heads :].reshape(-1)
    row = lax.axis_index("row")
    attn_gain_grad = lax.dynamic_slice_in_dim(attn_sum, row * width, width, 0)
    ffn_gain_grad = lax.dynamic_slice_in_dim(ffn_sum, row * width, width, 0)
    return (
        block_output,
        input_grad,
        attn_gain_grad,
        mix_grad,
        decay_grad,
        conv_grad,
        log_grad,
        bias_grad,
        gain_sum,
        out_weight_grad,
        ffn_gain_grad,
        gate_grad,
        up_grad,
        down_weight_grad,
    )


def solution(mesh):
    def run(*args):
        lay = Layout(mesh, args[6].shape[0])
        tokens, grid = P(lay.data + ("col",), "row"), P("row", "col")
        turned, features, inner = P("col", "row"), P("row"), P("col")
        conv = P(None, "col")
        return jax.shard_map(
            functools.partial(on_device, lay),
            mesh=lay.mesh,
            in_specs=(
                tokens, P(lay.data + ("row",)), features, grid, grid, conv, inner, inner, P(),
                turned, features, grid, grid, turned, tokens,
            ),
            out_specs=(
                tokens, tokens, features, grid, grid, conv, inner, inner, P(),
                turned, features, grid, grid, turned,
            ),
            check_vma=False,
        )(*args)

    return run
```

time: 4340 us -> 1290 us (0.30)
  waiting for transfers between devices: 2840 us -> 249 us
  other arithmetic: 776 us -> 45.1 us
  Pallas kernels: 0 us -> 530 us
  matrix products: 417 us -> 176 us
    psum x3 -> x1, waiting for transfers between devices: 1310 us -> 0.02 us  [on_device(): lax.psum((pick * own[None, :], sum((part_of[:DV] for part_of in small_par...]
    reduce_scatter x6 -> x5, waiting for transfers between devices: 934 us -> 144 us  [sum_rows(): grads = lax.psum_scatter(grads, 'row', scatter_dimension=0, tiled=False)]
    another operation x105 -> x1, other arithmetic: 590 us -> 0.01 us  [on_device(): jnp.stack([attn_gain, ffn_gain])]
    pallas_call x0 -> x15, Pallas kernels: none -> 530 us  [the longest x4 155 us: team_gather_kernel(): pl.pallas_call(functools.partial(gather_kernel, part_name), in_specs=[ANY...]
    all_gather x6 -> x10, waiting for transfers between devices: 598 us -> 104 us  [the longest x5 104 us: join(): return lax.all_gather(grads, lay.part, axis=0, tiled=False)]
    dot_general x178 -> x15, matrix products: 380 us -> 176 us  [the longest x3 41.2 us: project(): return jnp.dot(left, right, preferred_element_type=F32)]
    convert_element_type x1 -> x7, local copies, waits for them, and re-layouts: 0.01 us -> 76.3 us  [the longest x4 73.6 us: team_scatter(): return team_scatter_kernel(lay.part, values.astype(BF16), lay.fresh_id())]
    squeeze x53 -> x0, local copies, waits for them, and re-layouts: 44.4 us -> none  [the longest x49 41.8 us: mix_core(): state, outputs = lax.scan(jax.checkpoint(block_step), state, inputs)]
  transfers between devices with their start and end apart: 16 -> 16, of which waited for: 15 -> 8; matrix products, arithmetic and copies ran while one was open for 3% -> 25% of each run, Pallas kernels for 0% -> 36%
where the time goes in v1:
time: 1290 us; the launch traced here: 1280 us
  Pallas kernels  530 us (41%)
  waiting for transfers between devices  249 us (19%)
  local copies, waits for them, and re-layouts  212 us (16%)
  matrix products  176 us (14%)
  blocking collectives  52.1 us (4%)
  other arithmetic  45.1 us (3%)
  between operations  15.7 us (1%)
    pallas_call x4, Pallas kernels, team_gather_kernel(): pl.pallas_call(functools.partial(gather_kernel, part_name), in_specs=[ANY...  155 us
    reduce_scatter x5, waiting for transfers between devices, sum_rows(): grads = lax.psum_scatter(grads, 'row', scatter_dimension=0, tiled=False)  144 us
    pallas_call x4, Pallas kernels, team_scatter_kernel(): pl.pallas_call(functools.partial(scatter_kernel, part_name), in_specs=[AN...  143 us
    pallas_call x2, Pallas kernels, spread_call(): pl.pallas_call(spread_kernel, in_specs=[ANY_SPEC], out_specs=ANY_SPEC, ou...  105 us
    all_gather x5, waiting for transfers between devices, join(): return lax.all_gather(grads, lay.part, axis=0, tiled=False)  104 us
    convert_element_type x4, local copies, waits for them, and re-layouts, team_scatter(): return team_scatter_kernel(lay.part, values.astype(BF16), lay.fresh_id())  73.6 us
    unnamed x105, local copies, waits for them, and re-layouts  54 us
    pallas_call x2, Pallas kernels, mixer_backward(): pl.pallas_call(functools.partial(backward_kernel, head, last), grid=(coun...  45.8 us
  transfers between devices with their start and end apart: 16, of which 8 were waited for; matrix products, arithmetic and copies ran while one was open for 25% of the time, Pallas kernels for 36%

profile of v1, /device:TPU:13, one launch (start us, length us, event | category | flops | bytes accessed | tf_op | source)
XLA Modules:
  0.0 1280.5 jit_solution(5096988641569351337)
XLA Ops:
  27.9 54.9 %spread.2 = bf16[4,224,512]{2,1,0:T(8,128)(2,1)} custom-call(bf16[4,224,512]{2,1,0:T(8,128)(2,1)} %bitcast.157), custom_call_target="tpu_custom_call" | custom-call | tf_op jit(solution)/shard_map/spread/pallas_call | solution.py:506
  98.4 50.5 %spread.3 = bf16[4,224,512]{2,1,0:T(8,128)(2,1)} custom-call(bf16[4,224,512]{2,1,0:T(8,128)(2,1)} %bitcast.158), custom_call_target="tpu_custom_call" | custom-call | tf_op jit(solution)/shard_map/spread/pallas_call | solution.py:506
  152.3 48.0 %team_gather.4 = bf16[8,224,2048]{2,1,0:T(8,128)(2,1)} custom-call(bf16[224,2048]{1,0:T(8,128)(2,1)} %multiply_convert_fusion.2.src), custom_call_target="tpu_custom_call" | custom-call | tf_op jit(solution)/shard_map/team_gather/pallas_call | solution.py:356
  200.3 36.1 %team_gather.6 = bf16[8,224,2048]{2,1,0:T(8,128)(2,1)} custom-call(bf16[224,2048]{1,0:T(8,128)(2,1)} %bitcast.140), custom_call_target="tpu_custom_call" | custom-call | tf_op jit(solution)/shard_map/team_gather/pallas_call | solution.py:356
  274.3 18.3 %mixer_forward.2 = (bf16[1792,256]{1,0:T(8,128)(2,1)}, bf16[4,448,448]{2,1,0:T(8,128)(2,1)}) custom-call(f32[1792,896]{1,0:T(8,128)} %fusion.28.proj_ref.extra_ref.refs_1_.refs_0_, f32[1792,896]{1,0:T(8,128)} %fusion.28.proj_ref.extra_ref.refs_1_.refs_0_, f32[1792,1]{1,0:T(8,128)} %reshape.224.segc_ref.refs_2_, f32[4,1,448]{2,1,0:T(1,128)} %reshape.178.segr_ref.refs_3_, ...), custom_call_target="tpu_custom_call" | custom-call | tf_op jit(solution)/shard_map/mixer_forward/pallas_call | solution.py:224
  292.6 18.5 %mixer_forward.3 = (bf16[1792,256]{1,0:T(8,128)(2,1)}, bf16[4,448,448]{2,1,0:T(8,128)(2,1)}) custom-call(f32[1792,768]{1,0:T(8,128)} %fusion.29.proj_ref.refs_0_, f32[1792,896]{1,0:T(8,128)} %fusion.28.proj_ref.extra_ref.refs_1_.refs_0_, f32[1792,1]{1,0:T(8,128)} %reshape.224.segc_ref.refs_2_, f32[4,1,448]{2,1,0:T(1,128)} %reshape.178.segr_ref.refs_3_, ...), custom_call_target="tpu_custom_call" | custom-call | tf_op jit(solution)/shard_map/mixer_forward/pallas_call | solution.py:224
  317.0 24.1 %copy.90 = bf16[1792,4,512]{2,1,0:T(4,128)(2,1)} copy(bf16[1792,4,512]{2,0,1:T(8,128)(2,1)S(1)} %convolution_convert_fusion.3) | data formatting | bytes 14680064 | tf_op jit(solution)/shard_map/convert_element_type | solution.py:685
  357.0 35.5 %team_scatter.4 = f32[224,2048]{1,0:T(8,128)S(1)} custom-call(bf16[8,224,2048]{2,1,0:T(8,128)(2,1)S(1)} %copy-done.2), custom_call_target="tpu_custom_call" | custom-call | tf_op jit(solution)/shard_map/team_scatter/pallas_call | solution.py:438
  395.2 35.4 %team_gather.5 = bf16[8,224,2048]{2,1,0:T(8,128)(2,1)} custom-call(bf16[224,2048]{1,0:T(8,128)(2,1)} %multiply_convert_fusion.1.src), custom_call_target="tpu_custom_call" | custom-call | tf_op jit(solution)/shard_map/team_gather/pallas_call | solution.py:356
  479.1 35.4 %team_scatter.6 = f32[224,2048]{1,0:T(8,128)S(1)} custom-call(bf16[8,224,2048]{2,1,0:T(8,128)(2,1)S(1)} %bitcast.132), custom_call_target="tpu_custom_call" | custom-call | tf_op jit(solution)/shard_map/team_scatter/pallas_call | solution.py:438
  517.8 35.4 %team_gather.7 = bf16[8,224,2048]{2,1,0:T(8,128)(2,1)} custom-call(bf16[224,2048]{1,0:T(8,128)(2,1)} %fusion.22.src), custom_call_target="tpu_custom_call" | custom-call | tf_op jit(solution)/shard_map/team_gather/pallas_call | solution.py:356
  606.0 22.8 %mixer_backward.2 = (bf16[1792,768]{1,0:T(8,128)(2,1)}, bf16[1792,128]{1,0:T(8,128)(2,1)}, f32[4,4,512]{2,1,0:T(4,128)}, f32[4,1,384]{2,1,0:T(1,128)}) custom-call(f32[1792,768]{1,0:T(8,128)} %fusion.29.proj_ref.refs_0_, f32[1792,896]{1,0:T(8,128)} %fusion.28.proj_ref.extra_ref.refs_1_.refs_0_, f32[1792,1]{1,0:T(8,128)} %reshape.224.segc_ref.refs_2_, ...), custom_call_target="tpu_custom_call" | custom-call | tf_op jit(solution)/shard_map/mixer_backward/pallas_call | solution.py:268
  639.1 23.1 %mixer_backward.3 = (bf16[1792,896]{1,0:T(8,128)(2,1)}, f32[4,4,512]{2,1,0:T(4,128)}, f32[4,1,384]{2,1,0:T(1,128)}) custom-call(f32[1792,896]{1,0:T(8,128)} %fusion.28.proj_ref.extra_ref.refs_1_.refs_0_, f32[1792,896]{1,0:T(8,128)} %fusion.28.proj_ref.extra_ref.refs_1_.refs_0_, f32[1792,1]{1,0:T(8,128)} %reshape.224.segc_ref.refs_2_, ...), custom_call_target="tpu_custom_call" | custom-call | tf_op jit(solution)/shard_map/mixer_backward/pallas_call | solution.py:268
  701.3 50.3 %reduce-scatter.8.cloned.1.call-done = bf16[1,512,768]{2,1,0:T(8,128)(2,1)} async-done(((bf16[4,512,768]{2,1,0:T(8,128)(2,1)}), bf16[1,512,768]{2,1,0:T(8,128)(2,1)}) %reduce-scatter.8.cloned.1.call-update) | async-done | bytes 786448 | tf_op jit(solution)/shard_map/reduce_scatter | solution.py:777
  751.6 71.7 %reduce-scatter.6.cloned.1.call-done = bf16[1,512,896]{2,1,0:T(8,128)(2,1)} async-done(((bf16[4,512,896]{2,1,0:T(8,128)(2,1)}), bf16[1,512,896]{2,1,0:T(8,128)(2,1)}) %reduce-scatter.6.cloned.1.call-update) | async-done | bytes 917520 | tf_op jit(solution)/shard_map/reduce_scatter | solution.py:777
  831.6 24.1 %copy.91 = bf16[1792,4,512]{2,1,0:T(4,128)(2,1)} copy(bf16[1792,4,512]{2,0,1:T(8,128)(2,1)S(1)} %convolution_convert_fusion.2) | data formatting | bytes 14680064 | tf_op jit(solution)/shard_map/convert_element_type | solution.py:685
  871.5 36.0 %team_scatter.5 = f32[224,2048]{1,0:T(8,128)S(1)} custom-call(bf16[8,224,2048]{2,1,0:T(8,128)(2,1)S(1)} %copy-done.3), custom_call_target="tpu_custom_call" | custom-call | tf_op jit(solution)/shard_map/team_scatter/pallas_call | solution.py:438
  907.5 21.5 %reduce-scatter.12.cloned.1.call-done = bf16[1,512,1408]{2,1,0:T(8,128)(2,1)} async-done(((bf16[4,512,1408]{2,1,0:T(8,128)(2,1)}), bf16[1,512,1408]{2,1,0:T(8,128)(2,1)}) %reduce-scatter.12.cloned.1.call-update) | async-done | bytes 1441808 | tf_op jit(solution)/shard_map/reduce_scatter | solution.py:777
  952.9 36.3 %team_scatter.7 = f32[224,2048]{1,0:T(8,128)S(1)} custom-call(bf16[8,224,2048]{2,1,0:T(8,128)(2,1)S(1)} %bitcast.131), custom_call_target="tpu_custom_call" | custom-call | tf_op jit(solution)/shard_map/team_scatter/pallas_call | solution.py:438
  991.1 39.1 %all-reduce.2 = (f32[2048]{0:T(1024)S(1)}, f32[256]{0:T(256)}, f32[2048]{0:T(1024)S(1)}) all-reduce(f32[2048]{0:T(1024)S(1)} %get-tuple-element.84, f32[256]{0:T(256)S(1)} %bitcast.177, f32[2048]{0:T(1024)S(1)} %copy-done.19), channel_id=1, replica_groups=mesh['dp'=4,'row'=4,'col'=2] {'dp','row','col'}, use_global_device_ids=true, to_apply=%region_5.6 | all-reduce | flops 4352 | bytes 34816 | tf_op jit(solution)/shard_map/psum | solution.py:845
  1037.8 44.1 %deal.1 = (bf16[4,224,512]{2,1,0:T(8,128)(2,1)}, bf16[4,224,512]{2,1,0:T(8,128)(2,1)}) custom-call(bf16[4,224,512]{2,1,0:T(8,128)(2,1)} %bitcast.152, bf16[4,224,512]{2,1,0:T(8,128)(2,1)} %bitcast.151), custom_call_target="tpu_custom_call" | custom-call | tf_op jit(solution)/shard_map/deal/pallas_call | solution.py:600
  1104.2 24.5 %all-gather.24.cloned.1.call-done = bf16[4,704,512]{2,1,0:T(8,128)(2,1)} async-done(((bf16[1,704,512]{2,1,0:T(8,128)(2,1)}), bf16[4,704,512]{2,1,0:T(8,128)(2,1)}) %all-gather.24.cloned.1.call-update) | async-done | bytes 2883600 | tf_op jit(solution)/shard_map/all_gather | solution.py:824
  1133.9 24.9 %all-gather.18.cloned.1.call-done = bf16[4,512,768]{2,1,0:T(8,128)(2,1)} async-done(((bf16[1,512,768]{2,1,0:T(8,128)(2,1)}), bf16[4,512,768]{2,1,0:T(8,128)(2,1)}) %all-gather.18.cloned.1.call-update) | async-done | bytes 3145744 | tf_op jit(solution)/shard_map/all_gather | solution.py:824
  1163.7 28.1 %all-gather.16.cloned.1.call-done = bf16[4,512,896]{2,1,0:T(8,128)(2,1)} async-done(((bf16[1,512,896]{2,1,0:T(8,128)(2,1)}), bf16[4,512,896]{2,1,0:T(8,128)(2,1)}) %all-gather.16.cloned.1.call-update) | async-done | bytes 3670032 | tf_op jit(solution)/shard_map/all_gather | solution.py:824
  (234 shorter events, 426.2 us)
Async XLA Ops:
  7.2 243.8 %all-gather.28.cloned.1.call-start = ((), (), s32[]{:S(2)}) async-start(), calls=%async_computation.17 | async-start | bytes 3932160 | tf_op jit(solution)/shard_map/all_gather | solution.py:727
  10.0 251.5 %all-gather.26.cloned.1.call-start = ((), (), s32[]{:S(2)}) async-start(), calls=%async_computation.16 | async-start | bytes 4587520 | tf_op jit(solution)/shard_map/all_gather | solution.py:727
  13.1 298.0 %all-gather.30.cloned.1.call-start = ((), (), s32[]{:S(2)}) async-start(), calls=%async_computation.18 | async-start | bytes 2621440 | tf_op jit(solution)/shard_map/all_gather | solution.py:727
  15.1 415.6 %all-gather.32.cloned.1.call-start = ((), (), s32[]{:S(2)}) async-start(), calls=%async_computation.19 | async-start | bytes 7208960 | tf_op jit(solution)/shard_map/all_gather | solution.py:727
  18.9 429.6 %all-gather.34.cloned.1.call-start = ((), (), s32[]{:S(2)}) async-start(), calls=%async_computation.20 | async-start | bytes 3604480 | tf_op jit(solution)/shard_map/all_gather | solution.py:727
  19.9 678.3 %reduce-scatter.10.cloned.1.call-start = ((), (), s32[]{:S(2)}) async-start(), calls=%async_computation.10 | async-start | bytes 2621440 | tf_op jit(solution)/shard_map/reduce_scatter | solution.py:777
  26.7 60.2 %copy-start.38 = (f32[8]{0:T(128)S(1)}, f32[8]{0:T(128)}, u32[]{:S(2)}) copy-start(f32[8]{0:T(128)} %param.21) | copy-start | bytes 100
  26.7 60.8 %copy-start.39 = (f32[8]{0:T(128)S(1)}, f32[8]{0:T(128)}, u32[]{:S(2)}) copy-start(f32[8]{0:T(128)} %param.22) | copy-start | bytes 100
  26.7 61.4 %copy-start.31 = (f32[512]{0:T(512)S(1)}, f32[512]{0:T(512)}, u32[]{:S(2)}) copy-start(f32[512]{0:T(512)} %param.25) | copy-start | bytes 6148
  26.7 61.4 %copy-start.32 = (f32[512]{0:T(512)S(1)}, f32[512]{0:T(512)}, u32[]{:S(2)}) copy-start(f32[512]{0:T(512)} %param.17) | copy-start | bytes 6148
  96.6 54.5 %copy-start.17 = (f32[1,2048]{1,0:T(1,128)}, f32[1,2048]{1,0:T(1,128)S(1)}, u32[]{:S(2)}) copy-start(f32[1,2048]{1,0:T(1,128)S(1)} %get-tuple-element.103) | copy-start | bytes 24580
  96.6 419.0 %copy-start.15 = (f32[1,2048]{1,0:T(1,128)}, f32[1,2048]{1,0:T(1,128)S(1)}, u32[]{:S(2)}) copy-start(f32[1,2048]{1,0:T(1,128)S(1)} %get-tuple-element.102) | copy-start | bytes 24580
  392.9 122.7 %copy-start.22 = (f32[224]{0:T(256)}, f32[224]{0:T(256)S(1)}, u32[]{:S(2)}) copy-start(f32[224]{0:T(256)S(1)} %add_rsqrt_fusion) | copy-start | bytes 2692
  586.9 113.6 %reduce-scatter.14.cloned.1.call-start = ((), (), s32[]{:S(2)}) async-start(), calls=%async_computation.14 | async-start | bytes 3604480 | tf_op jit(solution)/shard_map/reduce_scatter | solution.py:777
  596.9 154.6 %reduce-scatter.8.cloned.1.call-start = ((), (), s32[]{:S(2)}) async-start(), calls=%async_computation.7 | async-start | bytes 3932160 | tf_op jit(solution)/shard_map/reduce_scatter | solution.py:777
  639.1 184.3 %reduce-scatter.6.cloned.1.call-start = ((), (), s32[]{:S(2)}) async-start(), calls=%async_computation.5 | async-start | bytes 4587520 | tf_op jit(solution)/shard_map/reduce_scatter | solution.py:777
  674.5 254.5 %reduce-scatter.12.cloned.1.call-start = ((), (), s32[]{:S(2)}) async-start(), calls=%async_computation.12 | async-start | bytes 7208960 | tf_op jit(solution)/shard_map/reduce_scatter | solution.py:777
  692.7 130.8 %copy-start.41 = (bf16[1792,704]{0,1:T(8,128)(2,1)S(1)}, bf16[1792,704]{0,1:T(8,128)(2,1)}, u32[]{:S(2)}) copy-start(bf16[1792,704]{0,1:T(8,128)(2,1)} %get-tuple-element.93) | copy-start | bytes 7569412
  692.7 389.3 %all-reduce.5.cloned.1.call-start = ((), (), s32[]{:S(2)}) async-start(), calls=%async_computation.9 | async-start | bytes 270336 | tf_op jit(solution)/shard_map/psum | solution.py:845
  698.2 401.8 %all-gather.20.cloned.1.call-start = ((), (), s32[]{:S(2)}) async-start(), calls=%async_computation.11 | async-start | bytes 2621440 | tf_op jit(solution)/shard_map/all_gather | solution.py:824
  700.5 428.2 %all-gather.24.cloned.1.call-start = ((), (), s32[]{:S(2)}) async-start(), calls=%async_computation.15 | async-start | bytes 3604480 | tf_op jit(solution)/shard_map/all_gather | solution.py:824
  701.2 457.5 %all-gather.18.cloned.1.call-start = ((), (), s32[]{:S(2)}) async-start(), calls=%async_computation.8 | async-start | bytes 3932160 | tf_op jit(solution)/shard_map/all_gather | solution.py:824
  751.6 440.2 %all-gather.16.cloned.1.call-start = ((), (), s32[]{:S(2)}) async-start(), calls=%async_computation.6 | async-start | bytes 4587520 | tf_op jit(solution)/shard_map/all_gather | solution.py:824
  823.4 413.4 %all-gather.22.cloned.1.call-start = ((), (), s32[]{:S(2)}) async-start(), calls=%async_computation.13 | async-start | bytes 7208960 | tf_op jit(solution)/shard_map/all_gather | solution.py:824
  (37 other events, 716.6 us)
Sparse Core Ops, SparseCore 0:
  10.2 80.5 all-gather.27
  92.9 87.2 all-gather.25
  182.4 48.3 all-gather.29
  232.8 104.5 all-gather.31
  338.8 57.8 all-gather.33
  587.0 40.9 reduce-scatter.9
  631.0 57.1 reduce-scatter.13
  691.3 60.2 reduce-scatter.7
  754.5 68.7 reduce-scatter.5
  826.2 102.7 reduce-scatter.11
  935.5 140.1 all-reduce.4
  1077.2 22.7 all-gather.19
  1101.6 27.0 all-gather.23
  1130.2 28.5 all-gather.17
  1160.2 31.4 all-gather.15
  1193.3 43.4 all-gather.21

commit v2 on v1

v2 whole, which is shorter than its diff:
```python
import functools
import jax
import jax.numpy as jnp
from jax import lax
from jax.experimental import pallas as pl
from jax.experimental.pallas import tpu as pltpu
from jax.sharding import Mesh
from jax.sharding import PartitionSpec as P

F32, BF16 = jnp.float32, jnp.bfloat16
DK, DV, TAPS = 128, 256, 4
INNER = 2 * DK + DV
PER_HEAD = INNER + DV
NN = (((1,), (0,)), ((), ()))
NT = (((1,), (1,)), ((), ()))
TN = (((0,), (0,)), ((), ()))


def mm(left, right, dims=NN):
    return lax.dot_general(left.astype(BF16), right.astype(BF16), dims, preferred_element_type=F32)


def sigmoid(values):
    return 1.0 / (1.0 + jnp.exp(-values))


def softplus(values):
    return jnp.maximum(values, 0.0) + jnp.log(1.0 + jnp.exp(-jnp.abs(values)))


def shift_down(values, lag):
    return jnp.concatenate([jnp.zeros_like(values[:lag]), values[: values.shape[0] - lag]], axis=0)


def shift_up(values, lag):
    return jnp.concatenate([values[lag:], jnp.zeros_like(values[:lag])], axis=0)


def cumsum_rows(values):
    step = 1
    while step < values.shape[0]:
        values = values + shift_down(values, step)
        step *= 2
    return values


def reverse_cumsum_rows(values):
    step = 1
    while step < values.shape[0]:
        values = values + shift_up(values, step)
        step *= 2
    return values


def prepare(head, proj, extra, seg_col, seg_row, conv, log_ref, bias_ref):
    length = proj.shape[0]
    summed = conv[TAPS - 1 : TAPS] * proj[:, :INNER]
    keeps = []
    for lag in range(1, TAPS):
        keep = (shift_down(seg_col + 1.0, lag) == seg_col + 1.0).astype(F32)
        keeps.append(keep)
        summed = summed + conv[TAPS - 1 - lag : TAPS - lag] * (shift_down(proj[:, :INNER], lag) * keep)
    gate_conv = sigmoid(summed)
    active = summed * gate_conv
    lane = lax.broadcasted_iota(jnp.int32, extra.shape, 1)
    write = jnp.sum(jnp.where(lane == 2 * head, extra, 0.0), axis=1, keepdims=True)
    drive = jnp.sum(jnp.where(lane == 2 * head + 1, extra, 0.0), axis=1, keepdims=True)
    beta = sigmoid(write)
    drive = drive + bias_ref[head]
    rate = jnp.exp(jnp.full((1, 1), log_ref[head], F32))
    decay = -rate * softplus(drive)
    total = cumsum_rows(decay)
    rows = lax.broadcasted_iota(jnp.int32, (length, length), 0)
    cols = lax.broadcasted_iota(jnp.int32, (length, length), 1)
    total_row = jnp.sum(jnp.where(rows == cols, total, 0.0), axis=0, keepdims=True)
    weight = jnp.exp(jnp.where((rows >= cols) & (seg_col == seg_row), total - total_row, -1e30))
    raw_q, raw_k, value = active[:, :DK], active[:, DK : 2 * DK], active[:, 2 * DK :]
    scale_q = lax.rsqrt(jnp.sum(raw_q * raw_q, axis=1, keepdims=True) + 1e-06)
    scale_k = lax.rsqrt(jnp.sum(raw_k * raw_k, axis=1, keepdims=True) + 1e-06)
    query = (raw_q * scale_q * DK ** (-0.5)).astype(BF16)
    key = (raw_k * scale_k).astype(BF16)
    inner = mm(key, key, NT)
    strict = jnp.where(rows > cols, weight, 0.0)
    return dict(
        summed=summed, keeps=keeps, gate_conv=gate_conv, raw_q=raw_q, raw_k=raw_k, value=value,
        scale_q=scale_q, scale_k=scale_k, query=query, key=key, inner=inner, weight=weight,
        strict=strict, beta=beta, drive=drive, rate=rate, decay=decay, rows=rows, cols=cols,
    )


def forward_kernel(head, proj_ref, extra_ref, segc_ref, segr_ref, conv_ref, log_ref, bias_ref, gain_ref,
                   mixed_ref, solve_ref, work):
    length = proj_ref.shape[0]
    size = work.shape[0]
    p = prepare(head, proj_ref[...], extra_ref[...], segc_ref[...], segr_ref[0], conv_ref[...], log_ref, bias_ref)
    lower = p["beta"] * p["strict"] * p["inner"]
    if size != length:
        work[...] = jnp.zeros_like(work)
    work[0:length, 0:length] = lower
    tile = min(128, size)
    blocks = size // tile
    r = lax.broadcasted_iota(jnp.int32, (tile, tile), 0)
    c = lax.broadcasted_iota(jnp.int32, (tile, tile), 1)
    parts = [work[b * tile : (b + 1) * tile, b * tile : (b + 1) * tile] for b in range(blocks)]
    eye = (r == c).astype(F32)
    inv = [eye - jnp.where((r // 2 == c // 2), part, 0.0) for part in parts]
    step = 2
    while step < tile:
        pick = (r // (2 * step) == c // (2 * step)) & (r // step != c // step)
        lows = [mm(jnp.where(pick, part, 0.0), x) for part, x in zip(parts, inv)]
        inv = [x - mm(x, low) for x, low in zip(inv, lows)]
        step *= 2
    for b in range(blocks):
        work[b * tile : (b + 1) * tile, b * tile : (b + 1) * tile] = inv[b]
    step = tile
    while step < size:
        for start in range(0, size, 2 * step):
            mid, end = start + step, start + 2 * step
            low = mm(work[mid:end, start:mid], work[start:mid, start:mid])
            work[mid:end, start:mid] = -mm(work[mid:end, mid:end], low)
        step *= 2
    solve = work[0:length, 0:length].astype(BF16)
    solve_ref[0] = solve
    fresh = mm(solve, p["beta"] * p["value"])
    out = mm(mm(p["query"], p["key"], NT) * p["weight"], fresh)
    scale = lax.rsqrt(jnp.sum(out * out, axis=1, keepdims=True) * (1.0 / DV) + 1e-05)
    gate = proj_ref[:, INNER:]
    mixed_ref[...] = (out * scale * gain_ref[...] * (gate * sigmoid(gate))).astype(BF16)


def backward_kernel(head, last, *refs):
    if last:
        (proj_ref, extra_ref, segc_ref, segr_ref, conv_ref, log_ref, bias_ref, gain_ref, solve_ref, grad_ref,
         turn_ref, other_ref, gproj_ref, gconv_ref, gsmall_ref) = refs
    else:
        (proj_ref, extra_ref, segc_ref, segr_ref, conv_ref, log_ref, bias_ref, gain_ref, solve_ref, grad_ref,
         turn_ref, gproj_ref, gextra_ref, gconv_ref, gsmall_ref) = refs
    conv = conv_ref[...]
    p = prepare(head, proj_ref[...], extra_ref[...], segc_ref[...], segr_ref[0], conv, log_ref, bias_ref)
    weight, strict, inner, beta, value = p["weight"], p["strict"], p["inner"], p["beta"], p["value"]
    query, key = p["query"], p["key"]
    solve = solve_ref[0]
    fresh = mm(solve, beta * value).astype(BF16)
    scores = mm(query, key, NT)
    probs = (scores * weight).astype(BF16)
    out = mm(probs, fresh)
    scale = lax.rsqrt(jnp.sum(out * out, axis=1, keepdims=True) * (1.0 / DV) + 1e-05)
    normed = out * scale
    gate = proj_ref[:, INNER:]
    gate_sig = sigmoid(gate)
    grad, width = 0.0, turn_ref.shape[2]
    for index in range(turn_ref.shape[0]):
        grad = grad + mm(grad_ref[:, index * width : (index + 1) * width], turn_ref[index], NT)
    gain = gain_ref[...]
    through = grad * normed
    ggate = through * gain * (gate_sig * (1.0 + gate * (1.0 - gate_sig)))
    ggain = jnp.sum(through * (gate * gate_sig), axis=0, keepdims=True)
    gnormed = grad * gain * (gate * gate_sig)
    gout = scale * (gnormed - normed * (jnp.sum(gnormed * normed, axis=1, keepdims=True) * (1.0 / DV)))
    gout = gout.astype(BF16)
    gprobs = mm(gout, fresh, NT)
    gfresh = mm(probs, gout, TN)
    gtarget = mm(solve, gfresh, TN)
    glower = -mm(gtarget, fresh, NT) * strict
    gscores = gprobs * weight
    tilt = glower * inner
    flow = gscores * scores + beta * tilt
    gbeta = jnp.sum(tilt, axis=1, keepdims=True) + jnp.sum(gtarget * value, axis=1, keepdims=True)
    gscores = gscores.astype(BF16)
    ginner = (beta * glower).astype(BF16)
    gquery = mm(gscores, key)
    gkey = mm(gscores, query, TN) + mm(ginner, key) + mm(ginner, key, TN)
    col_flow = jnp.sum(flow, axis=0, keepdims=True)
    col_flow = jnp.sum(jnp.where(p["rows"] == p["cols"], col_flow, 0.0), axis=1, keepdims=True)
    gdecay = reverse_cumsum_rows(jnp.sum(flow, axis=1, keepdims=True) - col_flow)
    raw_q, raw_k, scale_q, scale_k = p["raw_q"], p["raw_k"], p["scale_q"], p["scale_k"]
    gq = (DK ** (-0.5)) * scale_q * (
        gquery - raw_q * (scale_q * scale_q * jnp.sum(gquery * raw_q, axis=1, keepdims=True)))
    gk = scale_k * (gkey - raw_k * (scale_k * scale_k * jnp.sum(gkey * raw_k, axis=1, keepdims=True)))
    gactive = jnp.concatenate([gq, gk, beta * gtarget], axis=1)
    gsummed = gactive * (p["gate_conv"] * (1.0 + p["summed"] * (1.0 - p["gate_conv"])))
    source = proj_ref[:, :INNER]
    gsource = conv[TAPS - 1 : TAPS] * gsummed
    gconv_ref[0, TAPS - 1 : TAPS, :] = jnp.sum(gsummed * source, axis=0, keepdims=True)
    for lag in range(1, TAPS):
        kept = gsummed * p["keeps"][lag - 1]
        gsource = gsource + conv[TAPS - 1 - lag : TAPS - lag] * shift_up(kept, lag)
        gconv_ref[0, TAPS - 1 - lag : TAPS - lag, :] = jnp.sum(kept * shift_down(source, lag), axis=0, keepdims=True)
    gdrive = -p["rate"] * gdecay * sigmoid(p["drive"])
    gwrite = gbeta * beta * (1.0 - beta)
    lane = lax.broadcasted_iota(jnp.int32, extra_ref.shape, 1)
    gextra = jnp.where(lane == 2 * head, gwrite, jnp.where(lane == 2 * head + 1, gdrive, 0.0))
    gproj_ref[:, :INNER] = gsource.astype(BF16)
    gproj_ref[:, INNER:PER_HEAD] = ggate.astype(BF16)
    if last:
        gproj_ref[:, PER_HEAD:] = (gextra + other_ref[...].astype(F32)).astype(BF16)
    else:
        gextra_ref[...] = gextra.astype(BF16)
    glog = jnp.sum(gdecay * p["decay"], axis=0, keepdims=True)
    gbias = jnp.sum(gdrive, axis=0, keepdims=True)
    lane = lax.broadcasted_iota(jnp.int32, (1, 128), 1)
    gsmall_ref[0, :, 0:DV] = ggain
    gsmall_ref[0, :, DV:] = jnp.where(lane == 0, glog, jnp.where(lane == 1, gbias, 0.0))


def common_specs(length, heads, head, extra_block):
    smem = pl.BlockSpec(memory_space=pltpu.SMEM)
    return [
        pl.BlockSpec((length, PER_HEAD), lambda s: (s, 0)),
        pl.BlockSpec((length, 128), lambda s: (s, extra_block)),
        pl.BlockSpec((length, 1), lambda s: (s, 0)),
        pl.BlockSpec((1, 1, length), lambda s: (s, 0, 0)),
        pl.BlockSpec((TAPS, INNER), lambda s: (0, head)),
        smem,
        smem,
        pl.BlockSpec((1, DV), lambda s: (0, 0)),
    ]


def mixer_forward(head, heads, proj, extra, extra_block, seg_col, seg_row, conv, log, bias, gain):
    count, _, length = seg_row.shape
    tokens = count * length
    size = 64
    while size < length:
        size *= 2
    return pl.pallas_call(
        functools.partial(forward_kernel, head),
        grid=(count,),
        in_specs=common_specs(length, heads, head, extra_block),
        out_specs=[
            pl.BlockSpec((length, DV), lambda s: (s, 0)),
            pl.BlockSpec((1, length, length), lambda s: (s, 0, 0)),
        ],
        out_shape=[
            jax.ShapeDtypeStruct((tokens, DV), BF16),
            jax.ShapeDtypeStruct((count, length, length), BF16),
        ],
        scratch_shapes=[pltpu.VMEM((size, size), F32)],
        compiler_params=pltpu.CompilerParams(vmem_limit_bytes=56 << 20),
        name="mixer_forward",
    )(proj, extra, seg_col, seg_row, conv, log, bias, gain)


def mixer_backward(head, heads, proj, extra, extra_block, seg_col, seg_row, conv, log, bias, gain, solve, grad, turned, other):
    count, _, length = seg_row.shape
    tokens = count * length
    last = other is not None
    in_specs = common_specs(length, heads, head, extra_block) + [
        pl.BlockSpec((1, length, length), lambda s: (s, 0, 0)),
        pl.BlockSpec((length, grad.shape[1]), lambda s: (s, 0)),
        pl.BlockSpec((turned.shape[0], DV, turned.shape[2]), lambda s: (0, head, 0)),
    ]
    args = [proj, extra, seg_col, seg_row, conv, log, bias, gain, solve, grad, turned]
    width = PER_HEAD
    tail_specs = [
        pl.BlockSpec((1, TAPS, INNER), lambda s: (s, 0, 0)),
        pl.BlockSpec((1, 1, DV + 128), lambda s: (s, 0, 0)),
    ]
    tail_shapes = [
        jax.ShapeDtypeStruct((count, TAPS, INNER), F32),
        jax.ShapeDtypeStruct((count, 1, DV + 128), F32),
    ]
    mid_specs, mid_shapes = [], []
    if last:
        width += 128
        in_specs.append(pl.BlockSpec((length, 128), lambda s: (s, 0)))
        args.append(other)
    else:
        mid_specs = [pl.BlockSpec((length, 128), lambda s: (s, 0))]
        mid_shapes = [jax.ShapeDtypeStruct((tokens, 128), BF16)]
    return pl.pallas_call(
        functools.partial(backward_kernel, head, last),
        grid=(count,),
        in_specs=in_specs,
        out_specs=[pl.BlockSpec((length, width), lambda s: (s, 0))] + mid_specs + tail_specs,
        out_shape=[jax.ShapeDtypeStruct((tokens, width), BF16)] + mid_shapes + tail_shapes,
        compiler_params=pltpu.CompilerParams(vmem_limit_bytes=60 << 20),
        name="mixer_backward",
    )(*args)


MESH_ID = pl.DeviceIdType.MESH
ANY_SPEC = pl.BlockSpec(memory_space=pl.ANY)
VMEM_SPEC = pl.BlockSpec(memory_space=pltpu.VMEM)
STRIP = 16
DECAY_ROWS = 16


def meet(targets):
    barrier = pltpu.get_barrier_semaphore()
    for target in targets:
        pl.semaphore_signal(barrier, inc=1, device_id=target, device_id_type=MESH_ID)
    pl.semaphore_wait(barrier, len(targets))


def remote(source, dest, send, recv, index, target):
    return pltpu.make_async_remote_copy(
        src_ref=source,
        dst_ref=dest,
        send_sem=send.at[index],
        recv_sem=recv.at[index],
        device_id=target,
        device_id_type=MESH_ID,
    )


class Team:
    def __init__(self, name):
        self.name, self.part, self.col = name, lax.axis_index(name), lax.axis_index("col")
        self.across, self.twin = lax.rem(self.part + 2, 4), self.part + 1 - 2 * lax.rem(self.part, 2)
        self.far, self.other = lax.rem(self.twin + 2, 4), 1 - self.col
        self.x, self.y, self.core = {name: self.across}, {"col": self.other}, {name: self.twin}

    def partners(self):
        return [self.x, self.y, self.core]


def gather_phase(team, src, out, keep, send, recv):
    half = src.shape[0] // 2
    first, second = pl.ds(0, half), pl.ds(half, half)
    own, across = team.part * 2 + team.col, team.across * 2 + team.col
    other, diag = team.part * 2 + team.other, team.across * 2 + team.other
    local = pltpu.make_async_copy(src, out.at[own], keep)
    local.start()
    x_first = remote(src.at[first], out.at[own, first], send, recv, 0, team.x)
    x_second = remote(src.at[second], out.at[own, second], send, recv, 1, team.x)
    y_second = remote(src.at[second], out.at[own, second], send, recv, 2, team.y)
    y_first = remote(src.at[first], out.at[own, first], send, recv, 3, team.y)
    core_own = remote(src, out.at[own], send, recv, 4, team.core)
    for copy in (x_first, y_second, core_own, x_second, y_first):
        copy.start()
    y_pass = remote(out.at[across, first], out.at[across, first], send, recv, 5, team.y)
    x_pass = remote(out.at[other, second], out.at[other, second], send, recv, 6, team.x)
    core_x = remote(out.at[across], out.at[across], send, recv, 7, team.core)
    core_y = remote(out.at[other], out.at[other], send, recv, 8, team.core)
    core_first = remote(out.at[diag, first], out.at[diag, first], send, recv, 9, team.core)
    core_second = remote(out.at[diag, second], out.at[diag, second], send, recv, 10, team.core)
    x_first.wait_recv()
    y_pass.start()
    y_second.wait_recv()
    x_pass.start()
    x_second.wait_recv()
    core_x.start()
    y_first.wait_recv()
    core_y.start()
    y_pass.wait_recv()
    core_first.start()
    x_pass.wait_recv()
    core_second.start()
    for copy in (core_own, core_x, core_y, core_first, core_second):
        copy.wait_recv()
    for copy in (
        x_first, x_second, y_second, y_first, core_own, y_pass, x_pass, core_x, core_y, core_first, core_second,
    ):
        copy.wait_send()
    local.wait()


GATHER_SEMS = [pltpu.SemaphoreType.DMA, pltpu.SemaphoreType.DMA((11,)), pltpu.SemaphoreType.DMA((11,))]


def spread_phase(src, out, middle, keep, send, recv):
    row, col = lax.axis_index("row"), lax.axis_index("col")
    hops = []
    for item in range(2):
        hops.append(remote(src.at[2 * item + 1 - col], middle.at[item], send, recv, item, {"col": 1 - col}))
        hops[item].start()

    def pieces(wait_first):
        for side in range(2):
            home = col if side == 0 else 1 - col
            for item in range(2):
                if side == 1 and wait_first:
                    hops[item].wait_recv()
                source = src.at[2 * item + col] if side == 0 else middle.at[item]
                to_row = 2 * home + item
                copy = pltpu.make_async_remote_copy(
                    src_ref=source,
                    dst_ref=out.at[row],
                    send_sem=send.at[2 + 2 * side + item],
                    recv_sem=recv.at[2 + row],
                    device_id={"row": to_row},
                    device_id_type=MESH_ID,
                )
                yield to_row == row, copy, pltpu.make_async_copy(source, out.at[row], keep)

    for here, far, near in pieces(True):
        pl.when(here)(near.start)
        pl.when(jnp.logical_not(here))(far.start)
    for hop in range(1, 4):
        index = lax.rem(row + hop, 4)
        pltpu.make_async_remote_copy(
            src_ref=src.at[0],
            dst_ref=out.at[index],
            send_sem=send.at[0],
            recv_sem=recv.at[2 + index],
            device_id={"row": index},
            device_id_type=MESH_ID,
        ).wait_recv()
    for here, far, near in pieces(False):
        pl.when(here)(near.wait)
        pl.when(jnp.logical_not(here))(far.wait_send)
    for hop in hops:
        hop.wait_send()


def share(source, dest, mark, others, keep, send, recv):
    near = pltpu.make_async_copy(source, dest.at[mark], keep)
    near.start()
    copies = []
    for item, (target, _) in enumerate(others):
        copies.append(
            pltpu.make_async_remote_copy(
                src_ref=source,
                dst_ref=dest.at[mark],
                send_sem=send.at[item],
                recv_sem=recv.at[mark],
                device_id=target,
                device_id_type=MESH_ID,
            )
        )
        copies[item].start()

    def finish():
        near.wait()
        for target, index in others:
            pltpu.make_async_remote_copy(
                src_ref=source,
                dst_ref=dest.at[index],
                send_sem=send.at[0],
                recv_sem=recv.at[index],
                device_id=target,
                device_id_type=MESH_ID,
            ).wait_recv()
        for copy in copies:
            copy.wait_send()

    return finish


def enter_kernel(part_name, normed, *refs):
    if normed:
        (src, gains, segs, tok, everyone, gains_all, segs_all, stage, middle, ready, spread_keep, spread_send,
         spread_recv, keep, send, recv, small_keep, gain_send, gain_recv, seg_send, seg_recv) = refs
    else:
        (src, tok, everyone, stage, middle, ready, spread_keep, spread_send, spread_recv, keep, send, recv) = refs
    team = Team(part_name)
    row = lax.axis_index("row")
    rows = [({"row": lax.rem(row + hop, 4)}, lax.rem(row + hop, 4)) for hop in range(1, 4)]
    targets = team.partners() + [target for target, _ in rows]
    if normed:
        targets.append({part_name: team.far})
    meet(targets)
    if normed:
        done_gains = share(gains, gains_all, row, rows, small_keep.at[0], gain_send, gain_recv)
        parts = [({part_name: index}, index) for index in (team.across, team.twin, team.far)]
        done_segs = share(segs, segs_all, team.part, parts, small_keep.at[1], seg_send, seg_recv)
    spread_phase(src, stage, middle, spread_keep, spread_send, spread_recv)
    if normed:
        done_gains()
        done_segs()
    tokens, width = src.shape[1], src.shape[2]

    @pl.loop(0, tokens // STRIP)
    def _(step):
        strip = pl.ds(pl.multiple_of(step * STRIP, STRIP), STRIP)
        pieces = [stage[index, strip, :] for index in range(4)]
        if normed:
            wides = [piece.astype(F32) for piece in pieces]
            square = sum(jnp.sum(wide * wide, axis=1, keepdims=True) for wide in wides)
            scale = lax.rsqrt(square * (1.0 / (4 * width)) + 1e-05)
        for index in range(4):
            cols = slice(index * width, (index + 1) * width)
            tok[strip, cols] = pieces[index]
            if normed:
                ready[strip, cols] = (wides[index] * scale * gains_all[index, 0:1, :]).astype(BF16)
            else:
                ready[strip, cols] = pieces[index]

    gather_phase(team, ready, everyone, keep, send, recv)


def enter_call(lay, values, gains, segs):
    tokens, width = values.shape[0] // 4, values.shape[1]
    wide = 4 * width
    normed = gains is not None
    args = [values.reshape(4, tokens, width)]
    in_specs, out_specs = [ANY_SPEC], [VMEM_SPEC, ANY_SPEC]
    out_shape = [jax.ShapeDtypeStruct((tokens, wide), BF16), jax.ShapeDtypeStruct((8, tokens, wide), BF16)]
    scratch = [
        pltpu.VMEM((4, tokens, width), BF16),
        pltpu.VMEM((2, tokens, width), BF16),
        pltpu.VMEM((tokens, wide), BF16),
        pltpu.SemaphoreType.DMA,
        pltpu.SemaphoreType.DMA((6,)),
        pltpu.SemaphoreType.DMA((6,)),
    ] + GATHER_SEMS
    if normed:
        args += [gains, segs]
        in_specs += [VMEM_SPEC, VMEM_SPEC]
        out_specs += [VMEM_SPEC, VMEM_SPEC]
        out_shape += [
            jax.ShapeDtypeStruct((4,) + gains.shape, gains.dtype),
            jax.ShapeDtypeStruct((4,) + segs.shape, segs.dtype),
        ]
        scratch += [
            pltpu.SemaphoreType.DMA((2,)),
            pltpu.SemaphoreType.DMA((3,)),
            pltpu.SemaphoreType.DMA((4,)),
            pltpu.SemaphoreType.DMA((3,)),
            pltpu.SemaphoreType.DMA((4,)),
        ]
    results = list(pl.pallas_call(
        functools.partial(enter_kernel, lay.part, normed),
        in_specs=in_specs,
        out_specs=out_specs,
        out_shape=out_shape,
        scratch_shapes=scratch,
        compiler_params=pltpu.CompilerParams(
            collective_id=lay.fresh_id(), has_side_effects=True, vmem_limit_bytes=16 << 20
        ),
        name="enter",
    )(*args))
    results[1] = results[1].reshape(8 * tokens, wide)
    return results


def strips(start, count, body):
    @pl.loop(0, count // STRIP)
    def _(step):
        body(pl.ds(pl.multiple_of(start + step * STRIP, STRIP), STRIP), pl.ds(pl.multiple_of(step * STRIP, STRIP), STRIP))


def scatter_phase(team, dots, finish, work, twin, sent, relay, final, send, recv):
    rows, chunk_size = twin.shape[1], twin.shape[2] // 4
    half = rows // 2
    first, second = pl.ds(0, half), pl.ds(half, half)

    def swap(item):
        return remote(work.at[item, 0], twin.at[item], send, recv, item, team.core)

    relay_x = remote(sent.at[0, first], relay.at[0], send, recv, 4, team.x)
    relay_y = remote(sent.at[0, second], relay.at[1], send, recv, 5, team.y)
    x_first = remote(sent.at[1, first], final.at[0, first], send, recv, 6, team.x)
    x_second = remote(sent.at[1, second], final.at[0, second], send, recv, 7, team.x)
    y_second = remote(sent.at[2, second], final.at[1, second], send, recv, 8, team.y)
    y_first = remote(sent.at[2, first], final.at[1, first], send, recv, 9, team.y)

    def total(item, start, passed=None):
        def add(rows, local):
            value = work[item, 1, rows, :].astype(F32) + twin[item, rows, :].astype(F32)
            if passed is not None:
                value = value + relay[passed, local, :].astype(F32)
            sent[item, rows, :] = value.astype(BF16)

        strips(start, half, add)

    @pl.loop(0, 4)
    def _(item):
        @pl.loop(0, 8)
        def _(step):
            which, chunk = step // 4, lax.rem(step, 4)
            base = team.part * which + team.twin * (1 - which)
            slot = lax.rem(base + 2 * (1 - item // 2), 4) * 2 + lax.rem(team.col + 1 + item, 2)
            columns = pl.ds(pl.multiple_of(chunk * chunk_size, chunk_size), chunk_size)
            work[item, which, :, columns] = dots(
                pl.ds(pl.multiple_of(slot * rows, STRIP), rows), chunk, columns
            ).astype(BF16)

        swap(item).start()

        @pl.when(item == 1)
        def _():
            swap(0).wait_recv()
            total(0, 0)
            relay_x.start()
            total(0, half)
            relay_y.start()

        @pl.when(item == 2)
        def _():
            swap(1).wait_recv()
            total(1, 0)
            x_first.start()

        @pl.when(item == 3)
        def _():
            swap(2).wait_recv()
            total(2, half)
            y_second.start()

    relay_y.wait_recv()
    total(1, half, 1)
    x_second.start()
    relay_x.wait_recv()
    total(2, 0, 0)
    y_first.start()
    swap(3).wait_recv()

    def last(rows, _):
        value = work[3, 1, rows, :].astype(F32) + twin[3, rows, :].astype(F32)
        finish(rows, value + final[0, rows, :].astype(F32) + final[1, rows, :].astype(F32))

    x_first.wait_recv()
    y_first.wait_recv()
    strips(0, half, last)
    x_second.wait_recv()
    y_second.wait_recv()
    strips(half, half, last)
    for copy in [swap(item) for item in range(4)] + [relay_x, relay_y, x_first, x_second, y_second, y_first]:
        copy.wait_send()


def team_kernel(part_name, kind, starts, *refs):
    extras, outs = {"mid": (2, 2), "end": (1, 1), "branch": (3, 3), "input": (3, 2)}[kind]
    count = len(starts)
    lefts, right, refs = refs[:count], refs[count], refs[count + 1 :]
    extra, out, scratch = refs[:extras], refs[extras : extras + outs], refs[extras + outs :]
    scatter_refs, scratch = scratch[:7], scratch[7:]
    team = Team(part_name)
    meet(team.partners())

    def dots(rows, chunk, columns):
        value = 0.0
        for left, start in zip(lefts, starts):
            depth = slice(start, start + left.shape[1])
            if len(right.shape) == 3:
                value = value + lax.dot_general(left[rows, :], right[chunk, depth, :], NN, preferred_element_type=F32)
            else:
                value = value + lax.dot_general(left[rows, :], right[columns, depth], NT, preferred_element_type=F32)
        return value

    if kind in ("branch", "input"):
        gain_sum, scratch = scratch[0], scratch[1:]
        gain_sum[...] = jnp.zeros_like(gain_sum)
    if kind in ("mid", "branch"):
        ready, scratch = scratch[0], scratch[1:]

    def deal_out(rows, value):
        width = value.shape[1] // 4
        for index in range(4):
            out[0][index, rows, :] = value[:, index * width : (index + 1) * width].astype(BF16)

    def finish(rows, total):
        width = total.shape[1]
        if kind == "mid":
            stored, gain = extra
            value = stored[rows, :].astype(F32) + total
            out[0][rows, :] = value
            scale = lax.rsqrt(jnp.sum(value * value, axis=1, keepdims=True) * (1.0 / width) + 1e-05)
            ready[rows, :] = (value * scale * gain[...]).astype(BF16)
        elif kind == "end":
            deal_out(rows, extra[0][rows, :] + total)
        else:
            before, through, gain = extra
            value = before[rows, :].astype(F32)
            scale = lax.rsqrt(jnp.sum(value * value, axis=1, keepdims=True) * (1.0 / width) + 1e-05)
            normed = value * scale
            gain_sum[...] += total * normed
            scaled = total * gain[...]
            inner = jnp.sum(scaled * normed, axis=1, keepdims=True) * (1.0 / width)
            value = through[rows, :].astype(F32) + scale * (scaled - normed * inner)
            if kind == "branch":
                out[0][rows, :] = value
                ready[rows, :] = value.astype(BF16)
            else:
                deal_out(rows, value)

    scatter_phase(team, dots, finish, *scatter_refs)
    if kind == "branch":
        out[2][...] = jnp.sum(gain_sum[...], axis=0, keepdims=True)
    if kind == "input":
        out[1][...] = jnp.sum(gain_sum[...], axis=0, keepdims=True)
    if kind in ("mid", "branch"):
        gather_phase(team, ready, out[1], *scratch)


def team_call(lay, kind, lefts, right, starts, extra):
    tokens = lefts[0].shape[0] // 8
    wide = extra[0].shape[1]
    whole = jax.ShapeDtypeStruct((tokens, wide), F32)
    if kind in ("end", "input"):
        whole = jax.ShapeDtypeStruct((4, tokens, wide // 4), BF16)
    everyone = jax.ShapeDtypeStruct((8, tokens, wide), BF16)
    gain = jax.ShapeDtypeStruct((1, wide), F32)
    shapes = {"mid": [whole, everyone], "end": [whole], "branch": [whole, everyone, gain], "input": [whole, gain]}[kind]
    specs = [VMEM_SPEC if shape is not everyone else ANY_SPEC for shape in shapes]
    scratch = [
        pltpu.VMEM((4, 2, tokens, wide), BF16),
        pltpu.VMEM((4, tokens, wide), BF16),
        pltpu.VMEM((3, tokens, wide), BF16),
        pltpu.VMEM((2, tokens // 2, wide), BF16),
        pltpu.VMEM((2, tokens, wide), BF16),
        pltpu.SemaphoreType.DMA((10,)),
        pltpu.SemaphoreType.DMA((10,)),
    ]
    if kind in ("branch", "input"):
        scratch.append(pltpu.VMEM((STRIP, wide), F32))
    if kind in ("mid", "branch"):
        scratch.append(pltpu.VMEM((tokens, wide), BF16))
        scratch += GATHER_SEMS
    flops = 2 * 8 * tokens * wide * sum(left.shape[1] for left in lefts)
    results = list(pl.pallas_call(
        functools.partial(team_kernel, lay.part, kind, tuple(starts)),
        in_specs=[VMEM_SPEC] * (len(lefts) + 1 + len(extra)),
        out_specs=specs,
        out_shape=shapes,
        scratch_shapes=scratch,
        compiler_params=pltpu.CompilerParams(
            collective_id=lay.fresh_id(), has_side_effects=True, vmem_limit_bytes=56 << 20
        ),
        cost_estimate=pl.CostEstimate(flops=flops, bytes_accessed=200 << 20, transcendentals=0),
        name="team_" + kind,
    )(*lefts, right, *extra))
    if kind in ("mid", "branch"):
        results[1] = results[1].reshape(8 * tokens, wide)
    return results


def leave_kernel(part_name, rows_n, cols_n, count, *refs):
    srcs, src = refs[:count], refs[count]
    outs, out = refs[count + 1 : 2 * count + 1], refs[2 * count + 1]
    keep, send, recv, rows_in, summed, near, row_send, row_recv, team_send, team_recv = refs[2 * count + 2 :]
    team = Team(part_name)
    row, col = lax.axis_index("row"), lax.axis_index("col")
    rows = [({"row": lax.rem(row + hop, 4)}, lax.rem(row + hop, 4)) for hop in range(1, 4)]
    mates = []
    for part in (team.part, team.across, team.twin, team.far):
        for side in (team.col, team.other):
            mates.append(({part_name: part, "col": side}, part * 2 + side))
    mates = mates[1:]
    spot = row * cols_n + col
    mark = lax.rem(spot, rows_n)
    home = spot // rows_n

    def owner(index):
        place = col * rows_n + index
        return place // cols_n, lax.rem(place, cols_n)

    barrier = pltpu.get_barrier_semaphore()
    for target, _ in rows + mates:
        pl.semaphore_signal(barrier, inc=1, device_id=target, device_id_type=MESH_ID)
    for index in range(rows_n):
        from_row, from_col = owner(index)

        @pl.when((from_row != row) | (from_col != col))
        def _():
            pl.semaphore_signal(barrier, inc=1, device_id={"row": from_row, "col": from_col}, device_id_type=MESH_ID)

    pl.semaphore_wait(barrier, len(rows + mates) + rows_n - (home == col).astype(jnp.int32))
    finish_rows = share(src, rows_in, row, rows, near.at[0], row_send, row_recv)

    def each(act_local, act_remote):
        for item in range(count):
            for index in range(rows_n):
                here = (row == index) & (home == col)

                @pl.when(here)
                def _():
                    act_local(pltpu.make_async_copy(srcs[item].at[index], outs[item].at[mark], keep.at[item]))

                @pl.when(jnp.logical_not(here))
                def _():
                    act_remote(
                        pltpu.make_async_remote_copy(
                            src_ref=srcs[item].at[index],
                            dst_ref=outs[item].at[mark],
                            send_sem=send.at[item, index],
                            recv_sem=recv.at[item, mark],
                            device_id={"row": index, "col": home},
                            device_id_type=MESH_ID,
                        )
                    )

    each(lambda copy: copy.start(), lambda copy: copy.start())
    finish_rows()
    summed[...] = (rows_in[0] + rows_in[1]) + (rows_in[2] + rows_in[3])
    finish_team = share(summed, out, team.part * 2 + team.col, mates, near.at[1], team_send, team_recv)
    for item in range(count):
        for index in range(rows_n):
            from_row, from_col = owner(index)

            @pl.when((from_row != row) | (from_col != col))
            def _():
                pltpu.make_async_remote_copy(
                    src_ref=srcs[item].at[0],
                    dst_ref=outs[item].at[index],
                    send_sem=send.at[item, 0],
                    recv_sem=recv.at[item, index],
                    device_id={"row": from_row, "col": from_col},
                    device_id_type=MESH_ID,
                ).wait_recv()

    each(lambda copy: copy.wait(), lambda copy: copy.wait_send())
    finish_team()


def leave_call(lay, values, small):
    count = len(values)
    return pl.pallas_call(
        functools.partial(leave_kernel, lay.part, lay.rows, lay.cols, count),
        in_specs=[ANY_SPEC] * count + [VMEM_SPEC],
        out_specs=[ANY_SPEC] * count + [VMEM_SPEC],
        out_shape=[jax.ShapeDtypeStruct(value.shape, value.dtype) for value in values]
        + [jax.ShapeDtypeStruct((8,) + small.shape, F32)],
        scratch_shapes=[
            pltpu.SemaphoreType.DMA((count,)),
            pltpu.SemaphoreType.DMA((count, lay.rows)),
            pltpu.SemaphoreType.DMA((count, lay.rows)),
            pltpu.VMEM((4,) + small.shape, F32),
            pltpu.VMEM(small.shape, F32),
            pltpu.SemaphoreType.DMA((2,)),
            pltpu.SemaphoreType.DMA((3,)),
            pltpu.SemaphoreType.DMA((4,)),
            pltpu.SemaphoreType.DMA((7,)),
            pltpu.SemaphoreType.DMA((8,)),
        ],
        compiler_params=pltpu.CompilerParams(collective_id=lay.fresh_id(), has_side_effects=True),
        name="leave",
    )(*values, small)


def permute_join(lay, value):
    across = lax.ppermute(value, lay.part, [(0, 2), (2, 0), (1, 3), (3, 1)])
    pairs = [(0, 1), (1, 0), (2, 3), (3, 2)]
    return [value, across, lax.ppermute(value, lay.part, pairs), lax.ppermute(across, lay.part, pairs)]


def part_order(lay):
    part = lax.axis_index(lay.part)
    twin = part + 1 - 2 * (part % 2)
    return jnp.stack([part, (part + 2) % 4, twin, (twin + 2) % 4]).astype(jnp.int32)


def rows_kernel(order, *refs):
    for index, ref in enumerate(refs[:4]):

        @pl.when(pl.program_id(0) == index)
        def _():
            refs[4][...] = ref[...].astype(F32)


def place_rows(order, pieces, start, rows):
    width = pieces[0].shape[1]
    return pl.pallas_call(
        rows_kernel,
        grid_spec=pltpu.PrefetchScalarGridSpec(
            num_scalar_prefetch=1,
            grid=(4,),
            in_specs=[pl.BlockSpec((rows, width), lambda i, order: (start // rows, 0))] * 4,
            out_specs=pl.BlockSpec((rows, width), lambda i, order: (order[i], 0)),
        ),
        out_shape=jax.ShapeDtypeStruct((4 * rows, width), F32),
        compiler_params=pltpu.CompilerParams(vmem_limit_bytes=24 << 20),
        name="place_rows",
    )(order, *pieces)


def heads_kernel(heads, order, *refs):
    ins, decays, (out, decay) = refs[: 4 * heads], refs[4 * heads : -2], refs[-2:]
    for index in range(4):
        for head in range(heads):
            start = pl.multiple_of((order[index] * heads + head) * PER_HEAD, 128)
            out[:, pl.ds(start, PER_HEAD)] = ins[head * 4 + index][...].astype(F32).T
        small = decays[index][...].astype(F32).T[:, : 2 * heads]
        for part in range(4):

            @pl.when(order[index] == part)
            def _():
                decay[:, part * 2 * heads : (part + 1) * 2 * heads] = small


def place_heads(order, pieces):
    heads = len(pieces)
    flat = [piece for group in pieces for piece in group]
    features = flat[0].shape[1]
    wide = 4 * heads * PER_HEAD
    return pl.pallas_call(
        functools.partial(heads_kernel, heads),
        grid_spec=pltpu.PrefetchScalarGridSpec(
            num_scalar_prefetch=1,
            grid=(features // 128,),
            in_specs=[pl.BlockSpec((PER_HEAD, 128), lambda i, order: (0, i))] * len(flat)
            + [pl.BlockSpec((DECAY_ROWS, 128), lambda i, order: (PER_HEAD // DECAY_ROWS, i))] * 4,
            out_specs=[
                pl.BlockSpec((128, wide), lambda i, order: (i, 0)),
                pl.BlockSpec((128, 8 * heads), lambda i, order: (i, 0)),
            ],
        ),
        out_shape=[
            jax.ShapeDtypeStruct((features, wide), F32),
            jax.ShapeDtypeStruct((features, 8 * heads), F32),
        ],
        compiler_params=pltpu.CompilerParams(vmem_limit_bytes=40 << 20),
        name="place_heads",
    )(order, *flat, *pieces[0])


def pair_kernel(units, order, *refs):
    srcs, gate, up = refs[:4], refs[4], refs[5]
    for index in range(4):
        gate_part = srcs[index][:units, :].astype(F32).T
        up_part = srcs[index][units:, :].astype(F32).T
        for part in range(4):

            @pl.when(order[index] == part)
            def _():
                gate[:, part * units : (part + 1) * units] = gate_part
                up[:, part * units : (part + 1) * units] = up_part


def place_pair(order, pieces, units):
    features = pieces[0].shape[1]
    shape = jax.ShapeDtypeStruct((features, 4 * units), F32)
    return pl.pallas_call(
        functools.partial(pair_kernel, units),
        grid_spec=pltpu.PrefetchScalarGridSpec(
            num_scalar_prefetch=1,
            grid=(features // 128,),
            in_specs=[pl.BlockSpec((2 * units, 128), lambda i, order: (0, i))] * 4,
            out_specs=[pl.BlockSpec((128, 4 * units), lambda i, order: (i, 0))] * 2,
        ),
        out_shape=[shape, shape],
        compiler_params=pltpu.CompilerParams(vmem_limit_bytes=24 << 20),
        name="place_pair",
    )(order, *pieces)


def stack_kernel(counts, *refs):
    grads, values, out = refs[: len(counts)], refs[len(counts) : -1], refs[-1]
    base = 0
    for grad, value, count in zip(grads, values, counts):
        for start in range(0, count, 256):
            size = min(256, grad.shape[1] - start)
            part = lax.dot_general(grad[:, start : start + size], value[...], TN, preferred_element_type=F32)
            size = min(size, count - start)
            out[0, base + start : base + start + size, :] = part[:size].astype(BF16)
        base += count


def stack_call(rows_n, pairs, counts):
    tokens, wide = pairs[0][1].shape
    width = wide // rows_n
    total = sum(counts)
    flops = 2 * tokens * wide * sum(grad.shape[1] for grad, _ in pairs)
    return pl.pallas_call(
        functools.partial(stack_kernel, counts),
        grid=(rows_n,),
        in_specs=[
            pl.BlockSpec(grad.shape, lambda i: (0, 0), pipeline_mode=pl.Buffered(1)) for grad, _ in pairs
        ]
        + [pl.BlockSpec((tokens, width), lambda i: (0, i)) for _ in pairs],
        out_specs=pl.BlockSpec((1, total, width), lambda i: (i, 0, 0)),
        out_shape=jax.ShapeDtypeStruct((rows_n, total, width), BF16),
        compiler_params=pltpu.CompilerParams(vmem_limit_bytes=48 << 20),
        cost_estimate=pl.CostEstimate(flops=flops, bytes_accessed=40 << 20, transcendentals=0),
        name="weight_grads",
    )(*[grad for grad, _ in pairs], *[value for _, value in pairs])


def ffn_kernel(start, values, grads, pair, turned, hidden, both_grad):
    units = hidden.shape[1]
    both = lax.dot_general(values[...], pair[...], NN, preferred_element_type=F32)
    grad, width = 0.0, turned.shape[2]
    for index in range(turned.shape[0]):
        left = grads[:, index * width : (index + 1) * width]
        grad = grad + lax.dot_general(left, turned[index, start : start + units, :], NT, preferred_element_type=F32)
    gate, up = both[:, :units], both[:, units:]
    sig = sigmoid(gate)
    act = gate * sig
    hidden[...] = (act * up).astype(BF16)
    both_grad[:, :units] = (grad * up * (sig + act * (1.0 - sig))).astype(BF16)
    both_grad[:, units:] = (grad * act).astype(BF16)


def ffn_call(values, grads, pair, turned, start):
    tokens, width = values.shape
    units = pair.shape[1] // 2
    block = 256
    while tokens % block:
        block //= 2
    row = pl.BlockSpec((block, width), lambda i: (i, 0))
    return pl.pallas_call(
        functools.partial(ffn_kernel, start),
        grid=(tokens // block,),
        in_specs=[
            row,
            row,
            pl.BlockSpec(pair.shape, lambda i: (0, 0)),
            pl.BlockSpec(turned.shape, lambda i: (0, 0, 0)),
        ],
        out_specs=[
            pl.BlockSpec((block, units), lambda i: (i, 0)),
            pl.BlockSpec((block, 2 * units), lambda i: (i, 0)),
        ],
        out_shape=[
            jax.ShapeDtypeStruct((tokens, units), BF16),
            jax.ShapeDtypeStruct((tokens, 2 * units), BF16),
        ],
        compiler_params=pltpu.CompilerParams(vmem_limit_bytes=48 << 20),
        cost_estimate=pl.CostEstimate(
            flops=6 * tokens * width * units, bytes_accessed=30 << 20, transcendentals=tokens * units
        ),
        name="ffn",
    )(values, grads, pair, turned)


SEQ = 448


def project(left, right):
    return jnp.dot(left, right, preferred_element_type=F32)


def project_back(left, right):
    return lax.dot_general(left, right, NT, preferred_element_type=F32)


def weight_grads(lay, *pairs):
    if lay.native:
        return stack_call(lay.rows, [pair[:2] for pair in pairs], [count for _, _, count in pairs])
    stacks = []
    for grad, value, count in pairs:
        whole = lax.dot_general(grad, value, TN, preferred_element_type=F32)[:count].astype(BF16)
        stacks.append(jnp.moveaxis(whole.reshape(count, lay.rows, -1), 1, 0))
    return jnp.concatenate(stacks, axis=1)


def after(value, *others):
    return lax.optimization_barrier((value,) + others)[0]


class Layout:
    def __init__(self, mesh, heads):
        dp, self.rows, self.cols = (mesh.shape[name] for name in ("dp", "row", "col"))
        ways = dp
        while dp % ways or (heads // self.cols) % ways:
            ways -= 1
        self.ways = ways
        if ways == dp:
            self.mesh, self.shared, self.part = mesh, (), "dp"
        else:
            devices = mesh.devices.reshape(dp // ways, ways, self.rows, self.cols)
            self.mesh = Mesh(devices, ("group", "part", "row", "col"))
            self.shared, self.part = ("group",), "part"
        self.data = self.shared + (self.part,)
        self.team = (self.part, "col")
        self.native = (ways, self.rows, self.cols) == (4, 4, 2)
        self.next_id = 0

    def fresh_id(self):
        self.next_id += 1
        return self.next_id


def spread(lay, values):
    local = values.shape[0]
    whole = lax.all_gather(values, "col", axis=0, tiled=True)
    whole = lax.all_to_all(whole, "row", split_axis=0, concat_axis=1, tiled=True)
    mine = local // lay.rows
    return lax.dynamic_slice_in_dim(whole, lax.axis_index("col") * mine, mine, 0)


def unspread(lay, value):
    local = value.shape[0] * lay.rows
    whole = lax.all_gather(value, "col", axis=0, tiled=True)
    whole = lax.all_to_all(whole, "row", split_axis=1, concat_axis=0, tiled=True)
    return lax.dynamic_slice_in_dim(whole, lax.axis_index("col") * local, local, 0)


def team_gather(lay, values):
    return lax.all_gather(values, lay.team, axis=0, tiled=True)


def team_scatter(lay, values):
    return lax.psum_scatter(values.astype(BF16), lay.team, scatter_dimension=0, tiled=True).astype(F32)


def norm_forward(values):
    scale = lax.rsqrt(jnp.mean(values * values, axis=1, keepdims=True) + 1e-05)
    return values * scale, scale


def norm_backward(grad, values, gain):
    normed, scale = norm_forward(values)
    scaled = grad * gain
    inner = jnp.mean(scaled * normed, axis=1, keepdims=True)
    return scale * (scaled - normed * inner), jnp.sum(grad * normed, axis=0, keepdims=True)


def enter(lay, values, gains, segments):
    if lay.native:
        return enter_call(lay, values, gains, segments)
    mine = spread(lay, values)
    if gains is None:
        return mine, team_gather(lay, mine)
    gains = lax.all_gather(gains, "row", axis=0, tiled=False)
    segments = lax.all_gather(segments, lay.part, axis=0, tiled=False)
    normed, _ = norm_forward(mine.astype(F32))
    everyone = team_gather(lay, (normed * gains[:, 0].reshape(1, -1)).astype(BF16))
    return mine, everyone, gains, segments


def beside(stack, start, size):
    return jnp.moveaxis(stack[:, start : start + size], 0, 1).reshape(size, -1)


def mid_step(lay, mixed, turned, stored, gain):
    starts = [head * DV for head in range(len(mixed))]
    if lay.native:
        return team_call(lay, "mid", mixed, turned, starts, [stored, gain])
    total = sum(project(left, beside(turned, start, DV)) for left, start in zip(mixed, starts))
    residual = stored.astype(F32) + team_scatter(lay, total)
    normed, _ = norm_forward(residual)
    return residual, team_gather(lay, (normed * gain).astype(BF16))


def feed_forward(lay, values, grads, pair, turned, start):
    if lay.native:
        return ffn_call(values, grads, pair, turned, start)
    units = pair.shape[1] // 2
    both = project(values, pair)
    gate, up = both[:, :units], both[:, units:]
    sig = jax.nn.sigmoid(gate)
    grad = project_back(grads, beside(turned, start, units))
    grad_gate = grad * up * sig * (1.0 + gate * (1.0 - sig))
    both = jnp.concatenate([grad_gate.astype(BF16), (grad * gate * sig).astype(BF16)], axis=1)
    return (gate * sig * up).astype(BF16), both


def end_step(lay, hidden, turned, start, residual):
    if lay.native:
        return team_call(lay, "end", [hidden], turned, [start], [residual])[0]
    total = project(hidden, beside(turned, start, hidden.shape[1]))
    return (residual + team_scatter(lay, total)).astype(BF16)


def branch_step(lay, left, right, residual, out_grads, gain):
    if lay.native:
        return team_call(lay, "branch", [left], right, [0], [residual, out_grads, gain])
    grad, gain_part = norm_backward(team_scatter(lay, project_back(left, right)), residual, gain)
    grad = out_grads.astype(F32) + grad
    return grad, team_gather(lay, grad.astype(BF16)), gain_part


def input_step(lay, lefts, right, starts, stored, grad_residual, gain):
    if lay.native:
        return team_call(lay, "input", lefts, right, starts, [stored, grad_residual, gain])
    total = sum(project_back(left, right[:, start : start + left.shape[1]]) for left, start in zip(lefts, starts))
    grad, gain_part = norm_backward(team_scatter(lay, total), stored.astype(F32), gain)
    return (grad_residual + grad).astype(BF16), gain_part


def columns(stack):
    return jnp.moveaxis(stack, 2, 0).reshape(stack.shape[2], -1).astype(F32)


def on_device(
    lay,
    block_input,
    segment_ids,
    attn_gain,
    mix_weight,
    decay_weight,
    conv_weight,
    decay_log,
    decay_bias,
    out_gain,
    out_weight,
    ffn_gain,
    gate_weight,
    up_weight,
    down_weight,
    cotangent,
):
    part = lax.axis_index(lay.part)
    heads = decay_log.shape[0] // lay.ways
    units = gate_weight.shape[1] // lay.ways
    width = mix_weight.shape[0]

    def mine(values, dim, size):
        return lax.dynamic_slice_in_dim(values, part * size, size, dim)

    def gather_rows(values):
        return lax.all_gather(values, "row", axis=0, tiled=False)

    mix_mine = mine(mix_weight, 1, heads * PER_HEAD)
    decay_mine = mine(decay_weight, 1, heads * 2)
    decay_pad = jnp.pad(decay_mine, ((0, 0), (0, 128 - heads * 2)))
    splits = [0, PER_HEAD + 128]
    for head in range(1, heads):
        splits.append(splits[-1] + PER_HEAD)
    mix_pad = jnp.concatenate([mix_mine[:, :PER_HEAD], decay_pad, mix_mine[:, PER_HEAD:]], axis=1)
    mix_all = gather_rows(mix_pad).reshape(lay.rows * width, -1)
    turned = jnp.concatenate([mine(out_weight, 0, heads * DV), mine(down_weight, 0, units)], axis=0)
    turned_all = gather_rows(turned)
    pair = jnp.concatenate([mine(gate_weight, 1, units), mine(up_weight, 1, units)], axis=1)
    pair_all = gather_rows(pair).reshape(lay.rows * width, -1)
    conv_mine = mine(conv_weight, 1, heads * INNER)
    log_mine, bias_mine = mine(decay_log, 0, heads), mine(decay_bias, 0, heads)

    gains = jnp.stack([attn_gain, ffn_gain])
    stored, attn_all, gains, segments = enter(lay, block_input, gains, segment_ids.reshape(1, -1))
    gain_one, gain_two = gains[:, 0].reshape(1, -1), gains[:, 1].reshape(1, -1)
    segments = segments.astype(F32)
    seg_col, seg_row = segments.reshape(-1, 1), segments.reshape(-1, 1, SEQ)
    tokens = attn_all.shape[0]
    head_weights = [mix_all[:, start:end] for start, end in zip(splits[:-1], splits[1:])]
    shared, mixed, solves, projs = (), [], [], []
    for head in range(heads):
        projs.append(project(attn_all, head_weights[head]))
        if not head:
            shared = (
                projs[0], PER_HEAD // 128, seg_col, seg_row, conv_mine, log_mine, bias_mine, out_gain.reshape(1, -1),
            )
        values, solve = mixer_forward(head, heads, projs[head], *shared)
        mixed.append(values)
        solves.append(solve)
    out_grads, out_grads_all = enter(lay, after(cotangent, *mixed), None, None)
    mixed[0] = after(mixed[0], out_grads)
    residual, ffn_all = mid_step(lay, mixed, turned_all, stored, gain_two)

    hidden, grad_both = feed_forward(lay, ffn_all, out_grads_all, pair_all, turned_all, heads * DV)

    def sum_rows(grads):
        grads = lax.psum_scatter(grads, "row", scatter_dimension=0, tiled=False)
        return lax.psum(grads, lay.shared) if lay.shared else grads

    ffn_part = weight_grads(lay, (grad_both, ffn_all, 2 * units), (hidden, out_grads_all, units))
    grad_both, hidden = lax.optimization_barrier((grad_both, hidden, ffn_part))[:2]
    ffn_grad = sum_rows(ffn_part)
    grad_residual, branch_all, ffn_gain_part = branch_step(lay, grad_both, pair_all, residual, out_grads, gain_two)

    branch = branch_all
    other = jnp.zeros((tokens, 128), BF16)
    proj_grads, mix_grads, conv_parts, small_parts = [], [], [], []
    for head in reversed(range(heads)):
        common = (head, heads, projs[head], *shared, solves[head], branch, turned_all)
        if head:
            grad, extra, conv_part, small_part = mixer_backward(*common, None)
            other = other + extra
        else:
            grad, conv_part, small_part = mixer_backward(*common, other)
        triples = [(grad, attn_all, PER_HEAD if head else PER_HEAD + DECAY_ROWS)]
        if head == heads - 1:
            triples += [(values, branch_all, DV) for values in mixed]
        mix_part = weight_grads(lay, *triples)
        branch, grad = lax.optimization_barrier((branch, grad, mix_part))[:2]
        proj_grads.insert(0, grad)
        conv_parts.insert(0, conv_part.sum(0))
        small_parts.insert(0, small_part.sum(0)[0])
        mix_grads.insert(0, sum_rows(mix_part))
    input_grad, attn_gain_part = input_step(lay, proj_grads, mix_all, splits[:-1], stored, grad_residual, gain_one)
    hidden, ffn_grad = lax.optimization_barrier((hidden, ffn_grad, input_grad))[:2]
    block_output = end_step(lay, hidden, turned_all, heads * DV, residual)
    own = jnp.concatenate(
        [jnp.concatenate(conv_parts, axis=1).reshape(-1)]
        + [jnp.stack([part_of[DV + item] for part_of in small_parts]) for item in range(2)]
    )
    split = TAPS * heads * INNER
    gain_part = sum(part_of[:DV] for part_of in small_parts)
    col = lax.axis_index("col")
    if lay.native:
        flat = jnp.concatenate([own, gain_part, attn_gain_part[0], ffn_gain_part[0]])
        size = flat.shape[0]
        flat = jnp.pad(flat, (0, -size % 1024)).reshape(-1, 128)
        block_output, input_grad, sums = leave_call(lay, [block_output, input_grad], flat)
        block_output, input_grad = (value.reshape(-1, value.shape[2]) for value in (block_output, input_grad))
        sums = sums.reshape(8, -1)
        gain_sum, attn_sum, ffn_sum = jnp.split(
            jnp.sum(sums[:, own.shape[0] : size], axis=0), [DV, DV + lay.rows * width]
        )
        sums = sums[:, : own.shape[0]].reshape(lay.ways, lay.cols, -1)
    else:
        block_output, input_grad = unspread(lay, block_output), unspread(lay, input_grad)
        slots = lay.ways * lay.cols
        pick = (jnp.arange(slots) == part * lay.cols + col).astype(F32)[:, None]
        sums, gain_sum, ffn_sum, attn_sum = lax.psum(
            (pick * own[None, :], gain_part, ffn_gain_part[0], attn_gain_part[0]), lay.data + ("row", "col")
        )
        sums = sums.reshape(lay.ways, lay.cols, -1)
    sums = lax.dynamic_index_in_dim(sums, col, 1, keepdims=False)
    conv_grad = jnp.moveaxis(sums[:, :split].reshape(lay.ways, TAPS, -1), 0, 1).reshape(TAPS, -1)
    log_grad = sums[:, split : split + heads].reshape(-1)
    bias_grad = sums[:, split + heads :].reshape(-1)
    row = lax.axis_index("row")
    attn_gain_grad = lax.dynamic_slice_in_dim(attn_sum, row * width, width, 0)
    ffn_gain_grad = lax.dynamic_slice_in_dim(ffn_sum, row * width, width, 0)

    out_start = PER_HEAD if heads > 1 else PER_HEAD + DECAY_ROWS
    if lay.native:
        order = part_order(lay)
        pieces = [permute_join(lay, ffn_grad)]
        for grads in reversed(mix_grads):
            pieces.append(permute_join(lay, after(grads, input_grad)))
        gate_grad, up_grad = place_pair(order, pieces[0], units)
        down_weight_grad = place_rows(order, pieces[0], 2 * units, units)
        mix_grad, decay_grad = place_heads(order, pieces[:0:-1])
        out_weight_grad = place_rows(order, [piece[out_start:] for piece in pieces[1]], 0, heads * DV)
    else:
        ffn_stack, *mix_stacks = (
            lax.all_gather(value, lay.part, axis=0, tiled=False) for value in [ffn_grad] + mix_grads
        )
        decay_grad = columns(mix_stacks[0][:, PER_HEAD : PER_HEAD + 2 * heads])
        mix_grad = columns(jnp.concatenate([stack[:, :PER_HEAD] for stack in mix_stacks], axis=1))
        gate_grad, up_grad = columns(ffn_stack[:, :units]), columns(ffn_stack[:, units : 2 * units])
        down_weight_grad = ffn_stack[:, 2 * units :].reshape(-1, width).astype(F32)
        out_weight_grad = mix_stacks[-1][:, out_start : out_start + heads * DV].reshape(-1, width).astype(F32)
    return (
        block_output,
        input_grad,
        attn_gain_grad,
        mix_grad,
        decay_grad,
        conv_grad,
        log_grad,
        bias_grad,
        gain_sum,
        out_weight_grad,
        ffn_gain_grad,
        gate_grad,
        up_grad,
        down_weight_grad,
    )


def solution(mesh):
    def run(*args):
        lay = Layout(mesh, args[6].shape[0])
        tokens, grid = P(lay.data + ("col",), "row"), P("row", "col")
        turned, features, inner = P("col", "row"), P("row"), P("col")
        conv = P(None, "col")
        return jax.shard_map(
            functools.partial(on_device, lay),
            mesh=lay.mesh,
            in_specs=(
                tokens, P(lay.data + ("row",)), features, grid, grid, conv, inner, inner, P(),
                turned, features, grid, grid, turned, tokens,
            ),
            out_specs=(
                tokens, tokens, features, grid, grid, conv, inner, inner, P(),
                turned, features, grid, grid, turned,
            ),
            check_vma=False,
        )(*args)

    return run
```

time: 1290 us -> 895 us (0.69)
  Pallas kernels: 530 us -> 714 us
  waiting for transfers between devices: 249 us -> 72.5 us
  local copies, waits for them, and re-layouts: 212 us -> 45.8 us
  matrix products: 176 us -> 22.1 us
  blocking collectives: 52.1 us -> 0 us
  other arithmetic: 45.1 us -> 5.9 us
    pallas_call x11 -> x15, Pallas kernels: 448 us -> 627 us  [the longest x4 293 us: team_call(): pl.pallas_call(functools.partial(team_kernel, lay.part, kind, tuple(start...]
    reduce_scatter x5 -> x3, waiting for transfers between devices: 144 us -> 0.04 us  [sum_rows(): grads = lax.psum_scatter(grads, 'row', scatter_dimension=0, tiled=False)]
    dot_general x12 -> x0, matrix products: 135 us -> none  [the longest x3 39.4 us: project_back(): return lax.dot_general(left, right, NT, preferred_element_type=F32)]
    all_gather x5 -> x0, waiting for transfers between devices: 104 us -> none  [join(): return lax.all_gather(grads, lay.part, axis=0, tiled=False)]
    convert_element_type x7 -> x0, local copies, waits for them, and re-layouts: 76.3 us -> none  [the longest x4 73.6 us: team_scatter(): return team_scatter_kernel(lay.part, values.astype(BF16), lay.fresh_id())]
    psum x1 -> x0, blocking collectives: 39.1 us -> none  [on_device(): lax.psum((pick * own[None, :], sum((part_of[:DV] for part_of in small_par...]
    ppermute x0 -> x9, waiting for transfers between devices: none -> 38.8 us  [the longest x3 38.8 us: permute_join(): across = lax.ppermute(value, lay.part, [(0, 2), (2, 0), (1, 3), (3, 1)])]
    another operation x3 -> x0, local copies, waits for them, and re-layouts: 38.4 us -> none  [wide_back(): left = left.reshape(tokens, lay.rows, -1)]
  transfers between devices with their start and end apart: 16 -> 15, of which waited for: 8 -> 3; matrix products, arithmetic and copies ran while one was open for 25% -> 6% of each run, Pallas kernels for 36% -> 74%
where the time goes in v2:
time: 895 us; the launch traced here: 884 us
  Pallas kernels  714 us (80%)
  waiting for transfers between devices  72.5 us (8%)
  local copies, waits for them, and re-layouts  45.8 us (5%)
  matrix products  22.1 us (2%)
  between operations  14.9 us (2%)
  starting transfers between devices  9.15 us (1%)
    pallas_call x4, Pallas kernels, team_call(): pl.pallas_call(functools.partial(team_kernel, lay.part, kind, tuple(start...  293 us
    pallas_call x2, Pallas kernels, enter_call(): pl.pallas_call(functools.partial(enter_kernel, lay.part, normed), in_spec...  179 us
    pallas_call x1, Pallas kernels, leave_call(): pl.pallas_call(functools.partial(leave_kernel, lay.part, lay.rows, lay.co...  55 us
    pallas_call x2, Pallas kernels, mixer_backward(): pl.pallas_call(functools.partial(backward_kernel, head, last), grid=(coun...  49.5 us
    pallas_call x3, Pallas kernels, stack_call(): pl.pallas_call(functools.partial(stack_kernel, counts), grid=(rows_n,), i...  47 us
    ppermute x3, waiting for transfers between devices, permute_join(): across = lax.ppermute(value, lay.part, [(0, 2), (2, 0), (1, 3), (3, 1)])  38.8 us
    pallas_call x2, Pallas kernels, mixer_forward(): pl.pallas_call(functools.partial(forward_kernel, head), grid=(count,), in...  37.2 us
    all_gather x3, waiting for transfers between devices, gather_rows(): return lax.all_gather(values, 'row', axis=0, tiled=False)  33.6 us
  transfers between devices with their start and end apart: 15, of which 3 were waited for; matrix products, arithmetic and copies ran while one was open for 6% of the time, Pallas kernels for 74%

profile of v2, /device:TPU:13, one launch (start us, length us, event | category | flops | bytes accessed | tf_op | source)
XLA Modules:
  0.0 884.4 jit_solution(16357515230779952592)
XLA Ops:
  18.7 91.2 %enter.2 = (bf16[224,2048]{1,0:T(8,128)(2,1)S(1)}, bf16[8,224,2048]{2,1,0:T(8,128)(2,1)S(1)}, f32[4,2,512]{2,1,0:T(2,128)S(1)}, s32[4,1,448]{2,1,0:T(1,128)S(1)}) custom-call(bf16[4,224,512]{2,1,0:T(8,128)(2,1)S(1)} %bitcast.62, f32[2,512]{1,0:T(2,128)S(1)} %pad_maximum_fusion.2.refs_1_, s32[1,448]{1,0:T(1,128)S(1)} %bitcast.64), custom_call_target="tpu_custom_call" | custom-call | tf_op jit(solution)/shard_map/enter/pallas_call | solution.py:513
  118.0 33.6 %all-gather.7.cloned.1.call-done.refs_2_ = bf16[2048,1664]{1,0:T(8,128)(2,1)} async-done(((bf16[512,1664]{1,0:T(8,128)(2,1)}), bf16[2048,1664]{1,0:T(8,128)(2,1)}) %all-gather.7.cloned.1.call-update) | async-done | bytes 6815760 | tf_op jit(solution)/shard_map/all_gather | solution.py:1185
  151.6 12.7 %fusion.proj_ref.extra_ref.refs_1_.refs_0_ = f32[1792,896]{1,0:T(8,128)} fusion(bf16[1792,2048]{1,0:T(8,128)(2,1)} %bitcast.65, bf16[2048,1664]{1,0:T(8,128)(2,1)} %all-gather.7.cloned.1.call-done.refs_2_), kind=kOutput, calls=%fused_computation.2 | convolution fusion | flops 6576668672 | bytes 17432576 | tf_op jit(solution)/shard_map/dot_general | solution.py:1012
  164.3 18.6 %mixer_forward.2 = (bf16[1792,256]{1,0:T(8,128)(2,1)}, bf16[4,448,448]{2,1,0:T(8,128)(2,1)}) custom-call(f32[1792,896]{1,0:T(8,128)} %fusion.proj_ref.extra_ref.refs_1_.refs_0_, f32[1792,896]{1,0:T(8,128)} %fusion.proj_ref.extra_ref.refs_1_.refs_0_, f32[1792,1]{1,0:T(8,128)} %reshape.126.segc_ref.refs_2_, f32[4,1,448]{2,1,0:T(1,128)} %convert_element_type.7.segr_ref.refs_3_, ...), custom_call_target="tpu_custom_call" | custom-call | tf_op jit(solution)/shard_map/mixer_forward/pallas_call | solution.py:226
  182.9 9.5 %fusion.4.proj_ref.refs_0_ = f32[1792,768]{1,0:T(8,128)} fusion(bf16[1792,2048]{1,0:T(8,128)(2,1)S(1)} %bitcast.68, bf16[2048,1664]{1,0:T(8,128)(2,1)} %all-gather.7.cloned.1.call-done.refs_2_), kind=kOutput, calls=%fused_computation.6 | convolution fusion | flops 5637144576 | bytes 15990784 | tf_op jit(solution)/shard_map/dot_general | solution.py:1012
  192.4 18.5 %mixer_forward.3 = (bf16[1792,256]{1,0:T(8,128)(2,1)}, bf16[4,448,448]{2,1,0:T(8,128)(2,1)}) custom-call(f32[1792,768]{1,0:T(8,128)} %fusion.4.proj_ref.refs_0_, f32[1792,896]{1,0:T(8,128)} %fusion.proj_ref.extra_ref.refs_1_.refs_0_, f32[1792,1]{1,0:T(8,128)} %reshape.126.segc_ref.refs_2_, f32[4,1,448]{2,1,0:T(1,128)} %convert_element_type.7.segr_ref.refs_3_, ...), custom_call_target="tpu_custom_call" | custom-call | tf_op jit(solution)/shard_map/mixer_forward/pallas_call | solution.py:226
  210.9 87.8 %enter.3 = (bf16[224,2048]{1,0:T(8,128)(2,1)S(1)}, bf16[8,224,2048]{2,1,0:T(8,128)(2,1)S(1)}) custom-call(bf16[4,224,512]{2,1,0:T(8,128)(2,1)S(1)} %bitcast.63), custom_call_target="tpu_custom_call" | custom-call | tf_op jit(solution)/shard_map/enter/pallas_call | solution.py:513
  302.7 78.2 %team_mid.1 = (f32[224,2048]{1,0:T(8,128)}, bf16[8,224,2048]{2,1,0:T(8,128)(2,1)}) custom-call(bf16[1792,256]{1,0:T(8,128)(2,1)} %get-tuple-element.64.refs_0_.refs_1_, bf16[1792,256]{1,0:T(8,128)(2,1)} %get-tuple-element.61.refs_1_.refs_2_, bf16[4,1216,512]{2,1,0:T(8,128)(2,1)} %bitcast.75, bf16[224,2048]{1,0:T(8,128)(2,1)} %copy-done.16, f32[1,2048]{1,0:T(1,128)} %bitcast.97), custom_call_target="tpu_custom_call" | custom-call | flops 3758096384 | bytes 209715200 | tf_op jit(solution)/shard_map/team_mid/pallas_call | solution.py:703
  380.9 24.7 %ffn.1 = (bf16[1792,704]{1,0:T(8,128)(2,1)S(1)}, bf16[1792,1408]{1,0:T(8,128)(2,1)}) custom-call(bf16[1792,2048]{1,0:T(8,128)(2,1)} %bitcast.102, bf16[1792,2048]{1,0:T(8,128)(2,1)} %bitcast.69, bf16[2048,1408]{1,0:T(8,128)(2,1)} %all-gather.11.cloned.1.call-done.pair.refs_1_, bf16[4,1216,512]{2,1,0:T(8,128)(2,1)} %bitcast.76), custom_call_target="tpu_custom_call" | custom-call | flops 15502147584 | bytes 31457280 | tf_op jit(solution)/shard_map/ffn/pallas_call | solution.py:983
  405.7 21.4 %weight_grads.3 = bf16[4,2112,512]{2,1,0:T(8,128)(2,1)} custom-call(bf16[1792,1408]{1,0:T(8,128)(2,1)} %get-tuple-element.72.refs_0_, bf16[1792,704]{1,0:T(8,128)(2,1)S(1)} %get-tuple-element.85.refs_1_.refs_0_, bf16[1792,2048]{1,0:T(8,128)(2,1)} %bitcast.103, bf16[1792,2048]{1,0:T(8,128)(2,1)} %bitcast.70), custom_call_target="tpu_custom_call" | custom-call | flops 15502147584 | bytes 41943040 | tf_op jit(solution)/shard_map/weight_grads/pallas_call | solution.py:946
  428.7 87.4 %team_branch.1 = (f32[224,2048]{1,0:T(8,128)}, bf16[8,224,2048]{2,1,0:T(8,128)(2,1)}, f32[1,2048]{1,0:T(1,128)}) custom-call(bf16[1792,1408]{1,0:T(8,128)(2,1)} %get-tuple-element.72.refs_0_, bf16[2048,1408]{1,0:T(8,128)(2,1)} %all-gather.11.cloned.1.call-done.pair.refs_1_, f32[224,2048]{1,0:T(8,128)} %get-tuple-element.73.refs_2_, ...), custom_call_target="tpu_custom_call" | custom-call | flops 10334765056 | bytes 209715200 | tf_op jit(solution)/shard_map/team_branch/pallas_call | solution.py:703
  516.1 24.7 %mixer_backward.2 = (bf16[1792,768]{1,0:T(8,128)(2,1)}, bf16[1792,128]{1,0:T(8,128)(2,1)}, f32[4,4,512]{2,1,0:T(4,128)}, f32[4,1,384]{2,1,0:T(1,128)}) custom-call(f32[1792,768]{1,0:T(8,128)} %fusion.4.proj_ref.refs_0_, f32[1792,896]{1,0:T(8,128)} %fusion.proj_ref.extra_ref.refs_1_.refs_0_, f32[1792,1]{1,0:T(8,128)} %reshape.126.segc_ref.refs_2_, ...), custom_call_target="tpu_custom_call" | custom-call | tf_op jit(solution)/shard_map/mixer_backward/pallas_call | solution.py:271
  542.6 14.7 %weight_grads.4 = bf16[4,1280,512]{2,1,0:T(8,128)(2,1)} custom-call(bf16[1792,768]{1,0:T(8,128)(2,1)S(1)} %copy-done.15, bf16[1792,256]{1,0:T(8,128)(2,1)S(1)} %copy-done.17, bf16[1792,256]{1,0:T(8,128)(2,1)S(1)} %copy-done.18, bf16[1792,2048]{1,0:T(8,128)(2,1)} %bitcast.66, bf16[1792,2048]{1,0:T(8,128)(2,1)} %bitcast.72, bf16[1792,2048]{1,0:T(8,128)(2,1)} %bitcast.73), custom_call_target="tpu_custom_call" | custom-call | flops 9395240960 | bytes 41943040 | tf_op jit(solution)/shard_map/weight_grads/pallas_call | solution.py:946
  557.4 24.8 %mixer_backward.3 = (bf16[1792,896]{1,0:T(8,128)(2,1)}, f32[4,4,512]{2,1,0:T(4,128)}, f32[4,1,384]{2,1,0:T(1,128)}) custom-call(f32[1792,896]{1,0:T(8,128)} %fusion.proj_ref.extra_ref.refs_1_.refs_0_, f32[1792,896]{1,0:T(8,128)} %fusion.proj_ref.extra_ref.refs_1_.refs_0_, f32[1792,1]{1,0:T(8,128)} %reshape.126.segc_ref.refs_2_, ...), custom_call_target="tpu_custom_call" | custom-call | tf_op jit(solution)/shard_map/mixer_backward/pallas_call | solution.py:271
  582.2 10.9 %weight_grads.5 = bf16[4,784,512]{2,1,0:T(8,128)(2,1)} custom-call(bf16[1792,896]{1,0:T(8,128)(2,1)} %get-tuple-element.81.refs_0_, bf16[1792,2048]{1,0:T(8,128)(2,1)} %bitcast.67), custom_call_target="tpu_custom_call" | custom-call | flops 6576668672 | bytes 41943040 | tf_op jit(solution)/shard_map/weight_grads/pallas_call | solution.py:946
  593.2 54.7 %team_input.1 = (bf16[4,224,512]{2,1,0:T(8,128)(2,1)}, f32[1,2048]{1,0:T(1,128)}) custom-call(bf16[1792,896]{1,0:T(8,128)(2,1)} %get-tuple-element.81.refs_0_, bf16[1792,768]{1,0:T(8,128)(2,1)} %get-tuple-element.82.refs_0_.refs_1_, bf16[2048,1664]{1,0:T(8,128)(2,1)} %all-gather.7.cloned.1.call-done.refs_2_, bf16[224,2048]{1,0:T(8,128)(2,1)} %copy-done.16, ...), custom_call_target="tpu_custom_call" | custom-call | flops 12213813248 | bytes 209715200 | tf_op jit(solution)/shard_map/team_input/pallas_call | solution.py:703
  650.1 3.4 concatenate.19
  654.1 72.9 %team_end.1.refs_0_ = bf16[4,224,512]{2,1,0:T(8,128)(2,1)} custom-call(bf16[1792,704]{1,0:T(8,128)(2,1)} %copy-done.20, bf16[4,1216,512]{2,1,0:T(8,128)(2,1)} %bitcast.79, f32[224,2048]{1,0:T(8,128)} %get-tuple-element.73.refs_2_), custom_call_target="tpu_custom_call" | custom-call | flops 5167382528 | bytes 209715200 | tf_op jit(solution)/shard_map/team_end/pallas_call | solution.py:703
  727.0 55.0 %leave.1 = (bf16[4,224,512]{2,1,0:T(8,128)(2,1)}, bf16[4,224,512]{2,1,0:T(8,128)(2,1)}, f32[8,72,128]{2,1,0:T(8,128)}) custom-call(bf16[4,224,512]{2,1,0:T(8,128)(2,1)} %team_end.1.refs_0_, bf16[4,224,512]{2,1,0:T(8,128)(2,1)} %get-tuple-element.84.refs_1_, f32[72,128]{1,0:T(8,128)} %pad_bitcast_fusion.refs_2_), custom_call_target="tpu_custom_call" | custom-call | tf_op jit(solution)/shard_map/leave/pallas_call | solution.py:800
  785.3 26.6 %collective-permute-done.3.refs_5_ = bf16[1280,512]{1,0:T(8,128)(2,1)} collective-permute-done((bf16[1280,512]{1,0:T(8,128)(2,1)}, bf16[1280,512]{1,0:T(8,128)(2,1)}, u32[]{:S(2)}, u32[]{:S(2)}) %collective-permute-start.3) | collective-permute-done | bytes 1310752 | tf_op jit(solution)/shard_map/ppermute | solution.py:824
  816.9 12.2 %collective-permute-done.refs_1_.refs_9_ = bf16[784,512]{1,0:T(8,128)(2,1)} collective-permute-done((bf16[784,512]{1,0:T(8,128)(2,1)}, bf16[784,512]{1,0:T(8,128)(2,1)}, u32[]{:S(2)}, u32[]{:S(2)}) %collective-permute-start) | collective-permute-done | bytes 802848 | tf_op jit(solution)/shard_map/ppermute | solution.py:824
  841.6 9.9 %place_heads.1 = (f32[512,6144]{1,0:T(8,128)}, f32[512,16]{1,0:T(8,128)S(1)}) custom-call(s32[4]{0:T(128)S(1)} %pad_add_fusion.order, bf16[784,512]{1,0:T(8,128)(2,1)S(1)} %bitcast.56, bf16[784,512]{1,0:T(8,128)(2,1)} %collective-permute-done.refs_1_.refs_9_, bf16[784,512]{1,0:T(8,128)(2,1)} %collective-permute-done.1.refs_2_.refs_10_, ...), custom_call_target="tpu_custom_call" | custom-call | tf_op jit(solution)/shard_map/place_heads/pallas_call | solution.py:878
  860.1 5.1 place_rows.3
  865.2 10.3 %place_pair.1 = (f32[512,2816]{1,0:T(8,128)}, f32[512,2816]{1,0:T(8,128)}) custom-call(s32[4]{0:T(128)S(1)} %pad_add_fusion.order, bf16[2112,512]{1,0:T(8,128)(2,1)S(1)} %bitcast.53, bf16[2112,512]{1,0:T(8,128)(2,1)} %collective-permute-done.6.refs_1_, bf16[2112,512]{1,0:T(8,128)(2,1)} %collective-permute-done.7.refs_2_, ...), custom_call_target="tpu_custom_call" | custom-call | tf_op jit(solution)/shard_map/place_pair/pallas_call | solution.py:915
  (152 shorter events, 60.7 us)
Async XLA Ops:
  7.2 144.4 %all-gather.7.cloned.1.call-start = ((), (), s32[]{:S(2)}) async-start(), calls=%async_computation.6 | async-start | bytes 8519680 | tf_op jit(solution)/shard_map/all_gather | solution.py:1185
  11.1 291.6 %all-gather.9.cloned.1.call-start = ((), (), s32[]{:S(2)}) async-start(), calls=%async_computation.7 | async-start | bytes 6225920 | tf_op jit(solution)/shard_map/all_gather | solution.py:1185
  13.5 367.4 %all-gather.11.cloned.1.call-start = ((), (), s32[]{:S(2)}) async-start(), calls=%async_computation.8 | async-start | bytes 7208960 | tf_op jit(solution)/shard_map/all_gather | solution.py:1185
  17.4 630.5 %reduce-scatter.4.cloned.1.call-start = ((), (), s32[]{:S(2)}) async-start(), calls=%async_computation.3 | async-start | bytes 10813440 | tf_op jit(solution)/shard_map/reduce_scatter | solution.py:1226
  428.6 353.4 %reduce-scatter.8.cloned.1.call-start = ((), (), s32[]{:S(2)}) async-start(), calls=%async_computation.5 | async-start | bytes 6553600 | tf_op jit(solution)/shard_map/reduce_scatter | solution.py:1226
  516.1 24.8 %copy-start.17 = (bf16[1792,256]{1,0:T(8,128)(2,1)S(1)}, bf16[1792,256]{1,0:T(8,128)(2,1)}, u32[]{:S(2)}) copy-start(bf16[1792,256]{1,0:T(8,128)(2,1)} %get-tuple-element.64.refs_0_.refs_1_) | copy-start | bytes 2752516
  516.1 24.7 %copy-start.18 = (bf16[1792,256]{1,0:T(8,128)(2,1)S(1)}, bf16[1792,256]{1,0:T(8,128)(2,1)}, u32[]{:S(2)}) copy-start(bf16[1792,256]{1,0:T(8,128)(2,1)} %get-tuple-element.61.refs_1_.refs_2_) | copy-start | bytes 2752516
  557.4 227.8 %reduce-scatter.6.cloned.1.call-start = ((), (), s32[]{:S(2)}) async-start(), calls=%async_computation.4 | async-start | bytes 4014080 | tf_op jit(solution)/shard_map/reduce_scatter | solution.py:1226
  593.1 55.6 %copy-start.28 = (f32[4,1,384]{2,1,0:T(1,128)S(1)}, f32[4,1,384]{2,1,0:T(1,128)}, u32[]{:S(2)}) copy-start(f32[4,1,384]{2,1,0:T(1,128)} %get-tuple-element.88) | copy-start | bytes 18436
  593.1 55.6 %copy-start.27 = (f32[4,1,384]{2,1,0:T(1,128)S(1)}, f32[4,1,384]{2,1,0:T(1,128)}, u32[]{:S(2)}) copy-start(f32[4,1,384]{2,1,0:T(1,128)} %get-tuple-element.89) | copy-start | bytes 18436
  593.1 55.7 %copy-start.25 = (f32[4,4,512]{2,1,0:T(4,128)S(1)}, f32[4,4,512]{2,1,0:T(4,128)}, u32[]{:S(2)}) copy-start(f32[4,4,512]{2,1,0:T(4,128)} %get-tuple-element.86) | copy-start | bytes 98308
  593.2 55.7 %copy-start.24 = (f32[4,4,512]{2,1,0:T(4,128)S(1)}, f32[4,4,512]{2,1,0:T(4,128)}, u32[]{:S(2)}) copy-start(f32[4,4,512]{2,1,0:T(4,128)} %get-tuple-element.87) | copy-start | bytes 98308
  593.2 56.9 %copy-start.26 = (f32[1,2048]{1,0:T(1,128)S(1)}, f32[1,2048]{1,0:T(1,128)}, u32[]{:S(2)}) copy-start(f32[1,2048]{1,0:T(1,128)} %get-tuple-element.91) | copy-start | bytes 24580
  648.0 136.7 %collective-permute-start.6 = (bf16[2112,512]{1,0:T(8,128)(2,1)}, bf16[2112,512]{1,0:T(8,128)(2,1)}, u32[]{:S(2)}, u32[]{:S(2)}) collective-permute-start(bf16[2112,512]{1,0:T(8,128)(2,1)} %bitcast.50), channel_id=1, source_target_pairs={{0,16},{16,0},{8,24},{24,8},{1,17},{17,1},{9,25},{25,9},{2,18},{18... | collective-permute-start | bytes 6488072 | tf_op jit(solution)/shard_map/ppermute | solution.py:824
  654.1 130.6 %copy-start.2 = (bf16[1,2112,512]{2,1,0:T(8,128)(2,1)S(1)}, bf16[1,2112,512]{2,1,0:T(8,128)(2,1)}, u32[]{:S(2)}) copy-start(bf16[1,2112,512]{2,1,0:T(8,128)(2,1)} %reduce-scatter.4.cloned.1.call-done) | copy-start | bytes 6488068
  782.1 29.8 %collective-permute-start.3 = (bf16[1280,512]{1,0:T(8,128)(2,1)}, bf16[1280,512]{1,0:T(8,128)(2,1)}, u32[]{:S(2)}, u32[]{:S(2)}) collective-permute-start(bf16[1280,512]{1,0:T(8,128)(2,1)} %bitcast.58), channel_id=1, source_target_pairs={{0,16},{16,0},{8,24},{24,8},{1,17},{17,1},{9,25},{25,9},{2,18},{18... | collective-permute-start | bytes 3932168 | tf_op jit(solution)/shard_map/ppermute | solution.py:824
  783.4 47.5 %collective-permute-start.4 = (bf16[1280,512]{1,0:T(8,128)(2,1)}, bf16[1280,512]{1,0:T(8,128)(2,1)}, u32[]{:S(2)}, u32[]{:S(2)}) collective-permute-start(bf16[1280,512]{1,0:T(8,128)(2,1)} %bitcast.59), channel_id=1, source_target_pairs={{0,8},{8,0},{16,24},{24,16},{1,9},{9,1},{17,25},{25,17},{2,10},{10... | collective-permute-start | bytes 3932168 | tf_op jit(solution)/shard_map/ppermute | solution.py:826
  784.6 75.5 %collective-permute-start.7 = (bf16[2112,512]{1,0:T(8,128)(2,1)S(1)}, bf16[2112,512]{1,0:T(8,128)(2,1)}, u32[]{:S(2)}, u32[]{:S(2)}) collective-permute-start(bf16[2112,512]{1,0:T(8,128)(2,1)S(1)} %bitcast.51), channel_id=1, source_target_pairs={{0,8},{8,0},{16,24},{24,16},{1,9},{9,1},{17,25},{25,17},{2,10},{10... | collective-permute-start | bytes 6488072 | tf_op jit(solution)/shard_map/ppermute | solution.py:826
  784.6 75.5 %collective-permute-start.8 = (bf16[2112,512]{1,0:T(8,128)(2,1)}, bf16[2112,512]{1,0:T(8,128)(2,1)}, u32[]{:S(2)}, u32[]{:S(2)}) collective-permute-start(bf16[2112,512]{1,0:T(8,128)(2,1)} %collective-permute-done.6.refs_1_), channel_id=1, source_target_pairs={{0,8},{8,0},{16,24},{24,16},{1,9},{9,1},{17,25},{25,17},{2,10},{10... | collective-permute-start | bytes 6488072 | tf_op jit(solution)/shard_map/ppermute | solution.py:826
  785.1 56.5 %copy-start.4 = (bf16[1,784,512]{2,1,0:T(8,128)(2,1)S(1)}, bf16[1,784,512]{2,1,0:T(8,128)(2,1)}, u32[]{:S(2)}) copy-start(bf16[1,784,512]{2,1,0:T(8,128)(2,1)} %reduce-scatter.6.cloned.1.call-done) | copy-start | bytes 2408452
  785.2 43.9 %collective-permute-start = (bf16[784,512]{1,0:T(8,128)(2,1)}, bf16[784,512]{1,0:T(8,128)(2,1)}, u32[]{:S(2)}, u32[]{:S(2)}) collective-permute-start(bf16[784,512]{1,0:T(8,128)(2,1)} %bitcast.54), channel_id=1, source_target_pairs={{0,16},{16,0},{8,24},{24,8},{1,17},{17,1},{9,25},{25,9},{2,18},{18... | collective-permute-start | bytes 2408456 | tf_op jit(solution)/shard_map/ppermute | solution.py:824
  811.9 29.8 %collective-permute-start.5 = (bf16[1280,512]{1,0:T(8,128)(2,1)}, bf16[1280,512]{1,0:T(8,128)(2,1)}, u32[]{:S(2)}, u32[]{:S(2)}) collective-permute-start(bf16[1280,512]{1,0:T(8,128)(2,1)} %collective-permute-done.3.refs_5_), channel_id=1, source_target_pairs={{0,8},{8,0},{16,24},{24,16},{1,9},{9,1},{17,25},{25,17},{2,10},{10... | collective-permute-start | bytes 3932168 | tf_op jit(solution)/shard_map/ppermute | solution.py:826
  829.1 12.6 %collective-permute-start.1 = (bf16[784,512]{1,0:T(8,128)(2,1)}, bf16[784,512]{1,0:T(8,128)(2,1)}, u32[]{:S(2)}, u32[]{:S(2)}) collective-permute-start(bf16[784,512]{1,0:T(8,128)(2,1)} %bitcast.55), channel_id=1, source_target_pairs={{0,8},{8,0},{16,24},{24,16},{1,9},{9,1},{17,25},{25,17},{2,10},{10... | collective-permute-start | bytes 2408456 | tf_op jit(solution)/shard_map/ppermute | solution.py:826
  830.8 10.8 %collective-permute-start.2 = (bf16[784,512]{1,0:T(8,128)(2,1)}, bf16[784,512]{1,0:T(8,128)(2,1)}, u32[]{:S(2)}, u32[]{:S(2)}) collective-permute-start(bf16[784,512]{1,0:T(8,128)(2,1)} %collective-permute-done.refs_1_.refs_9_), channel_id=1, source_target_pairs={{0,8},{8,0},{16,24},{24,16},{1,9},{9,1},{17,25},{25,17},{2,10},{10... | collective-permute-start | bytes 2408456 | tf_op jit(solution)/shard_map/ppermute | solution.py:826
  (24 other events, 145.6 us)
Sparse Core Ops, SparseCore 0:
  11.2 140.3 all-gather.6
  153.7 112.0 all-gather.8
  268.0 105.8 all-gather.10
  428.8 149.0 reduce-scatter.3
  580.6 94.7 reduce-scatter.7
  678.2 67.3 reduce-scatter.5

commit v3 on v2

v3 whole, which is shorter than its diff:
```python
import functools
import jax
import jax.numpy as jnp
from jax import lax
from jax.experimental import pallas as pl
from jax.experimental.pallas import tpu as pltpu
from jax.sharding import Mesh
from jax.sharding import PartitionSpec as P

F32, BF16 = jnp.float32, jnp.bfloat16
DK, DV, TAPS = 128, 256, 4
INNER = 2 * DK + DV
PER_HEAD = INNER + DV
NN = (((1,), (0,)), ((), ()))
NT = (((1,), (1,)), ((), ()))
TN = (((0,), (0,)), ((), ()))


def mm(left, right, dims=NN):
    return lax.dot_general(left.astype(BF16), right.astype(BF16), dims, preferred_element_type=F32)


def sigmoid(values):
    return 1.0 / (1.0 + jnp.exp(-values))


def softplus(values):
    return jnp.maximum(values, 0.0) + jnp.log(1.0 + jnp.exp(-jnp.abs(values)))


def shift_down(values, lag):
    return jnp.concatenate([jnp.zeros_like(values[:lag]), values[: values.shape[0] - lag]], axis=0)


def shift_up(values, lag):
    return jnp.concatenate([values[lag:], jnp.zeros_like(values[:lag])], axis=0)


def cumsum_rows(values):
    step = 1
    while step < values.shape[0]:
        values = values + shift_down(values, step)
        step *= 2
    return values


def reverse_cumsum_rows(values):
    step = 1
    while step < values.shape[0]:
        values = values + shift_up(values, step)
        step *= 2
    return values


def prepare(head, proj, extra, seg_col, seg_row, conv, log_ref, bias_ref):
    length = proj.shape[0]
    summed = conv[TAPS - 1 : TAPS] * proj[:, :INNER]
    keeps = []
    for lag in range(1, TAPS):
        keep = (shift_down(seg_col + 1.0, lag) == seg_col + 1.0).astype(F32)
        keeps.append(keep)
        summed = summed + conv[TAPS - 1 - lag : TAPS - lag] * (shift_down(proj[:, :INNER], lag) * keep)
    gate_conv = sigmoid(summed)
    active = summed * gate_conv
    lane = lax.broadcasted_iota(jnp.int32, extra.shape, 1)
    write = jnp.sum(jnp.where(lane == 2 * head, extra, 0.0), axis=1, keepdims=True)
    drive = jnp.sum(jnp.where(lane == 2 * head + 1, extra, 0.0), axis=1, keepdims=True)
    beta = sigmoid(write)
    drive = drive + bias_ref[head]
    rate = jnp.exp(jnp.full((1, 1), log_ref[head], F32))
    decay = -rate * softplus(drive)
    total = cumsum_rows(decay)
    rows = lax.broadcasted_iota(jnp.int32, (length, length), 0)
    cols = lax.broadcasted_iota(jnp.int32, (length, length), 1)
    total_row = jnp.sum(jnp.where(rows == cols, total, 0.0), axis=0, keepdims=True)
    weight = jnp.exp(jnp.where((rows >= cols) & (seg_col == seg_row), total - total_row, -1e30))
    raw_q, raw_k, value = active[:, :DK], active[:, DK : 2 * DK], active[:, 2 * DK :]
    scale_q = lax.rsqrt(jnp.sum(raw_q * raw_q, axis=1, keepdims=True) + 1e-06)
    scale_k = lax.rsqrt(jnp.sum(raw_k * raw_k, axis=1, keepdims=True) + 1e-06)
    query = (raw_q * scale_q * DK ** (-0.5)).astype(BF16)
    key = (raw_k * scale_k).astype(BF16)
    inner = mm(key, key, NT)
    strict = jnp.where(rows > cols, weight, 0.0)
    return dict(
        summed=summed, keeps=keeps, gate_conv=gate_conv, raw_q=raw_q, raw_k=raw_k, value=value,
        scale_q=scale_q, scale_k=scale_k, query=query, key=key, inner=inner, weight=weight,
        strict=strict, beta=beta, drive=drive, rate=rate, decay=decay, rows=rows, cols=cols,
    )


def forward_kernel(head, proj_ref, extra_ref, segc_ref, segr_ref, conv_ref, log_ref, bias_ref, gain_ref,
                   mixed_ref, solve_ref, work):
    length = proj_ref.shape[0]
    size = work.shape[0]
    p = prepare(head, proj_ref[...], extra_ref[...], segc_ref[...], segr_ref[0], conv_ref[...], log_ref, bias_ref)
    lower = p["beta"] * p["strict"] * p["inner"]
    if size != length:
        work[...] = jnp.zeros_like(work)
    work[0:length, 0:length] = lower
    tile = min(128, size)
    blocks = size // tile
    r = lax.broadcasted_iota(jnp.int32, (tile, tile), 0)
    c = lax.broadcasted_iota(jnp.int32, (tile, tile), 1)
    parts = [work[b * tile : (b + 1) * tile, b * tile : (b + 1) * tile] for b in range(blocks)]
    eye = (r == c).astype(F32)
    inv = [eye - jnp.where((r // 2 == c // 2), part, 0.0) for part in parts]
    step = 2
    while step < tile:
        pick = (r // (2 * step) == c // (2 * step)) & (r // step != c // step)
        lows = [mm(jnp.where(pick, part, 0.0), x) for part, x in zip(parts, inv)]
        inv = [x - mm(x, low) for x, low in zip(inv, lows)]
        step *= 2
    for b in range(blocks):
        work[b * tile : (b + 1) * tile, b * tile : (b + 1) * tile] = inv[b]
    step = tile
    while step < size:
        for start in range(0, size, 2 * step):
            mid, end = start + step, start + 2 * step
            low = mm(work[mid:end, start:mid], work[start:mid, start:mid])
            work[mid:end, start:mid] = -mm(work[mid:end, mid:end], low)
        step *= 2
    solve = work[0:length, 0:length].astype(BF16)
    solve_ref[0] = solve
    fresh = mm(solve, p["beta"] * p["value"])
    out = mm(mm(p["query"], p["key"], NT) * p["weight"], fresh)
    scale = lax.rsqrt(jnp.sum(out * out, axis=1, keepdims=True) * (1.0 / DV) + 1e-05)
    gate = proj_ref[:, INNER:]
    mixed_ref[...] = (out * scale * gain_ref[...] * (gate * sigmoid(gate))).astype(BF16)


def backward_kernel(head, last, *refs):
    if last:
        (proj_ref, extra_ref, segc_ref, segr_ref, conv_ref, log_ref, bias_ref, gain_ref, solve_ref, grad_ref,
         turn_ref, other_ref, gproj_ref, gconv_ref, gsmall_ref) = refs
    else:
        (proj_ref, extra_ref, segc_ref, segr_ref, conv_ref, log_ref, bias_ref, gain_ref, solve_ref, grad_ref,
         turn_ref, gproj_ref, gextra_ref, gconv_ref, gsmall_ref) = refs
    conv = conv_ref[...]
    p = prepare(head, proj_ref[...], extra_ref[...], segc_ref[...], segr_ref[0], conv, log_ref, bias_ref)
    weight, strict, inner, beta, value = p["weight"], p["strict"], p["inner"], p["beta"], p["value"]
    query, key = p["query"], p["key"]
    solve = solve_ref[0]
    fresh = mm(solve, beta * value).astype(BF16)
    scores = mm(query, key, NT)
    probs = (scores * weight).astype(BF16)
    out = mm(probs, fresh)
    scale = lax.rsqrt(jnp.sum(out * out, axis=1, keepdims=True) * (1.0 / DV) + 1e-05)
    normed = out * scale
    gate = proj_ref[:, INNER:]
    gate_sig = sigmoid(gate)
    grad, width = 0.0, turn_ref.shape[2]
    for index in range(turn_ref.shape[0]):
        grad = grad + mm(grad_ref[:, index * width : (index + 1) * width], turn_ref[index], NT)
    gain = gain_ref[...]
    through = grad * normed
    ggate = through * gain * (gate_sig * (1.0 + gate * (1.0 - gate_sig)))
    ggain = jnp.sum(through * (gate * gate_sig), axis=0, keepdims=True)
    gnormed = grad * gain * (gate * gate_sig)
    gout = scale * (gnormed - normed * (jnp.sum(gnormed * normed, axis=1, keepdims=True) * (1.0 / DV)))
    gout = gout.astype(BF16)
    gprobs = mm(gout, fresh, NT)
    gfresh = mm(probs, gout, TN)
    gtarget = mm(solve, gfresh, TN)
    glower = -mm(gtarget, fresh, NT) * strict
    gscores = gprobs * weight
    tilt = glower * inner
    flow = gscores * scores + beta * tilt
    gbeta = jnp.sum(tilt, axis=1, keepdims=True) + jnp.sum(gtarget * value, axis=1, keepdims=True)
    gscores = gscores.astype(BF16)
    ginner = (beta * glower).astype(BF16)
    gquery = mm(gscores, key)
    gkey = mm(gscores, query, TN) + mm(ginner, key) + mm(ginner, key, TN)
    col_flow = jnp.sum(flow, axis=0, keepdims=True)
    col_flow = jnp.sum(jnp.where(p["rows"] == p["cols"], col_flow, 0.0), axis=1, keepdims=True)
    gdecay = reverse_cumsum_rows(jnp.sum(flow, axis=1, keepdims=True) - col_flow)
    raw_q, raw_k, scale_q, scale_k = p["raw_q"], p["raw_k"], p["scale_q"], p["scale_k"]
    gq = (DK ** (-0.5)) * scale_q * (
        gquery - raw_q * (scale_q * scale_q * jnp.sum(gquery * raw_q, axis=1, keepdims=True)))
    gk = scale_k * (gkey - raw_k * (scale_k * scale_k * jnp.sum(gkey * raw_k, axis=1, keepdims=True)))
    gactive = jnp.concatenate([gq, gk, beta * gtarget], axis=1)
    gsummed = gactive * (p["gate_conv"] * (1.0 + p["summed"] * (1.0 - p["gate_conv"])))
    source = proj_ref[:, :INNER]
    gsource = conv[TAPS - 1 : TAPS] * gsummed
    gconv_ref[0, TAPS - 1 : TAPS, :] = jnp.sum(gsummed * source, axis=0, keepdims=True)
    for lag in range(1, TAPS):
        kept = gsummed * p["keeps"][lag - 1]
        gsource = gsource + conv[TAPS - 1 - lag : TAPS - lag] * shift_up(kept, lag)
        gconv_ref[0, TAPS - 1 - lag : TAPS - lag, :] = jnp.sum(kept * shift_down(source, lag), axis=0, keepdims=True)
    gdrive = -p["rate"] * gdecay * sigmoid(p["drive"])
    gwrite = gbeta * beta * (1.0 - beta)
    lane = lax.broadcasted_iota(jnp.int32, extra_ref.shape, 1)
    gextra = jnp.where(lane == 2 * head, gwrite, jnp.where(lane == 2 * head + 1, gdrive, 0.0))
    gproj_ref[:, :INNER] = gsource.astype(BF16)
    gproj_ref[:, INNER:PER_HEAD] = ggate.astype(BF16)
    if last:
        gproj_ref[:, PER_HEAD:] = (gextra + other_ref[...].astype(F32)).astype(BF16)
    else:
        gextra_ref[...] = gextra.astype(BF16)
    glog = jnp.sum(gdecay * p["decay"], axis=0, keepdims=True)
    gbias = jnp.sum(gdrive, axis=0, keepdims=True)
    lane = lax.broadcasted_iota(jnp.int32, (1, 128), 1)
    gsmall_ref[0, :, 0:DV] = ggain
    gsmall_ref[0, :, DV:] = jnp.where(lane == 0, glog, jnp.where(lane == 1, gbias, 0.0))


def common_specs(length, heads, head, extra_block):
    smem = pl.BlockSpec(memory_space=pltpu.SMEM)
    return [
        pl.BlockSpec((length, PER_HEAD), lambda s: (s, 0)),
        pl.BlockSpec((length, 128), lambda s: (s, extra_block)),
        pl.BlockSpec((length, 1), lambda s: (s, 0)),
        pl.BlockSpec((1, 1, length), lambda s: (s, 0, 0)),
        pl.BlockSpec((TAPS, INNER), lambda s: (0, head)),
        smem,
        smem,
        pl.BlockSpec((1, DV), lambda s: (0, 0)),
    ]


def mixer_cost(count, passes):
    return pl.CostEstimate(flops=passes * count * (3 << 30), bytes_accessed=passes * count << 23, transcendentals=0)


def mixer_forward(head, heads, proj, extra, extra_block, seg_col, seg_row, conv, log, bias, gain):
    count, _, length = seg_row.shape
    tokens = count * length
    size = 64
    while size < length:
        size *= 2
    return pl.pallas_call(
        functools.partial(forward_kernel, head),
        grid=(count,),
        in_specs=common_specs(length, heads, head, extra_block),
        out_specs=[
            pl.BlockSpec((length, DV), lambda s: (s, 0)),
            pl.BlockSpec((1, length, length), lambda s: (s, 0, 0)),
        ],
        out_shape=[
            jax.ShapeDtypeStruct((tokens, DV), BF16),
            jax.ShapeDtypeStruct((count, length, length), BF16),
        ],
        scratch_shapes=[pltpu.VMEM((size, size), F32)],
        compiler_params=pltpu.CompilerParams(vmem_limit_bytes=56 << 20),
        cost_estimate=mixer_cost(count, 1),
        name="mixer_forward",
    )(proj, extra, seg_col, seg_row, conv, log, bias, gain)


def mixer_backward(head, heads, proj, extra, extra_block, seg_col, seg_row, conv, log, bias, gain, solve, grad, turned, other):
    count, _, length = seg_row.shape
    tokens = count * length
    last = other is not None
    in_specs = common_specs(length, heads, head, extra_block) + [
        pl.BlockSpec((1, length, length), lambda s: (s, 0, 0)),
        pl.BlockSpec((length, grad.shape[1]), lambda s: (s, 0)),
        pl.BlockSpec((turned.shape[0], DV, turned.shape[2]), lambda s: (0, head, 0)),
    ]
    args = [proj, extra, seg_col, seg_row, conv, log, bias, gain, solve, grad, turned]
    width = PER_HEAD
    tail_specs = [
        pl.BlockSpec((1, TAPS, INNER), lambda s: (s, 0, 0)),
        pl.BlockSpec((1, 1, DV + 128), lambda s: (s, 0, 0)),
    ]
    tail_shapes = [
        jax.ShapeDtypeStruct((count, TAPS, INNER), F32),
        jax.ShapeDtypeStruct((count, 1, DV + 128), F32),
    ]
    mid_specs, mid_shapes = [], []
    if last:
        width += 128
        in_specs.append(pl.BlockSpec((length, 128), lambda s: (s, 0)))
        args.append(other)
    else:
        mid_specs = [pl.BlockSpec((length, 128), lambda s: (s, 0))]
        mid_shapes = [jax.ShapeDtypeStruct((tokens, 128), BF16)]
    return pl.pallas_call(
        functools.partial(backward_kernel, head, last),
        grid=(count,),
        in_specs=in_specs,
        out_specs=[pl.BlockSpec((length, width), lambda s: (s, 0))] + mid_specs + tail_specs,
        out_shape=[jax.ShapeDtypeStruct((tokens, width), BF16)] + mid_shapes + tail_shapes,
        compiler_params=pltpu.CompilerParams(vmem_limit_bytes=60 << 20),
        cost_estimate=mixer_cost(count, 2),
        name="mixer_backward",
    )(*args)


MESH_ID = pl.DeviceIdType.MESH
HBM_SPEC = pl.BlockSpec(memory_space=pltpu.HBM)
VMEM_SPEC = pl.BlockSpec(memory_space=pltpu.VMEM)
STRIP = 16
DECAY_ROWS = 16


def meet(targets):
    barrier = pltpu.get_barrier_semaphore()
    for target in targets:
        pl.semaphore_signal(barrier, inc=1, device_id=target, device_id_type=MESH_ID)
    pl.semaphore_wait(barrier, len(targets))


def remote(source, dest, send, recv, index, target):
    return pltpu.make_async_remote_copy(
        src_ref=source,
        dst_ref=dest,
        send_sem=send.at[index],
        recv_sem=recv.at[index],
        device_id=target,
        device_id_type=MESH_ID,
    )


class Team:
    def __init__(self, name):
        self.name, self.part, self.col = name, lax.axis_index(name), lax.axis_index("col")
        self.across, self.twin = lax.rem(self.part + 2, 4), self.part + 1 - 2 * lax.rem(self.part, 2)
        self.far, self.other = lax.rem(self.twin + 2, 4), 1 - self.col
        self.x, self.y, self.core = {name: self.across}, {"col": self.other}, {name: self.twin}

    def partners(self):
        return [self.x, self.y, self.core]


def gather_phase(team, src, out, keep, send, recv):
    half = src.shape[0] // 2
    first, second = pl.ds(0, half), pl.ds(half, half)
    own, across = team.part * 2 + team.col, team.across * 2 + team.col
    other, diag = team.part * 2 + team.other, team.across * 2 + team.other
    local = pltpu.make_async_copy(src, out.at[own], keep)
    local.start()
    x_first = remote(src.at[first], out.at[own, first], send, recv, 0, team.x)
    x_second = remote(src.at[second], out.at[own, second], send, recv, 1, team.x)
    y_second = remote(src.at[second], out.at[own, second], send, recv, 2, team.y)
    y_first = remote(src.at[first], out.at[own, first], send, recv, 3, team.y)
    core_own = remote(src, out.at[own], send, recv, 4, team.core)
    for copy in (x_first, y_second, core_own, x_second, y_first):
        copy.start()
    y_pass = remote(out.at[across, first], out.at[across, first], send, recv, 5, team.y)
    x_pass = remote(out.at[other, second], out.at[other, second], send, recv, 6, team.x)
    core_x = remote(out.at[across], out.at[across], send, recv, 7, team.core)
    core_y = remote(out.at[other], out.at[other], send, recv, 8, team.core)
    core_first = remote(out.at[diag, first], out.at[diag, first], send, recv, 9, team.core)
    core_second = remote(out.at[diag, second], out.at[diag, second], send, recv, 10, team.core)
    x_first.wait_recv()
    y_pass.start()
    y_second.wait_recv()
    x_pass.start()
    x_second.wait_recv()
    core_x.start()
    y_first.wait_recv()
    core_y.start()
    y_pass.wait_recv()
    core_first.start()
    x_pass.wait_recv()
    core_second.start()
    for copy in (core_own, core_x, core_y, core_first, core_second):
        copy.wait_recv()
    for copy in (
        x_first, x_second, y_second, y_first, core_own, y_pass, x_pass, core_x, core_y, core_first, core_second,
    ):
        copy.wait_send()
    local.wait()


GATHER_SEMS = [pltpu.SemaphoreType.DMA, pltpu.SemaphoreType.DMA((11,)), pltpu.SemaphoreType.DMA((11,))]


class Spread:
    def __init__(self, src, out, middle, keep, send, recv):
        self.src, self.out, self.middle, self.keep, self.send, self.recv = src, out, middle, keep, send, recv
        self.row, self.col = lax.axis_index("row"), lax.axis_index("col")
        self.hops = [
            remote(src.at[2 * item + 1 - self.col], middle.at[item], send, recv, item, {"col": 1 - self.col})
            for item in range(2)
        ]

    def pieces(self, side):
        home = self.col if side == 0 else 1 - self.col
        for item in range(2):
            source = self.src.at[2 * item + self.col] if side == 0 else self.middle.at[item]
            to_row = 2 * home + item
            copy = pltpu.make_async_remote_copy(
                src_ref=source,
                dst_ref=self.out.at[self.row],
                send_sem=self.send.at[2 + 2 * side + item],
                recv_sem=self.recv.at[2 + self.row],
                device_id={"row": to_row},
                device_id_type=MESH_ID,
            )
            yield to_row == self.row, copy, pltpu.make_async_copy(source, self.out.at[self.row], self.keep)

    def start(self):
        for hop in self.hops:
            hop.start()
        self.send_side(0)

    def send_side(self, side):
        for here, far, near in self.pieces(side):
            pl.when(here)(near.start)
            pl.when(jnp.logical_not(here))(far.start)

    def turn(self):
        for hop in self.hops:
            hop.wait_recv()
        self.send_side(1)

    def finish(self):
        for hop in range(1, 4):
            index = lax.rem(self.row + hop, 4)
            pltpu.make_async_remote_copy(
                src_ref=self.src.at[0],
                dst_ref=self.out.at[index],
                send_sem=self.send.at[0],
                recv_sem=self.recv.at[2 + index],
                device_id={"row": index},
                device_id_type=MESH_ID,
            ).wait_recv()
        for side in range(2):
            for here, far, near in self.pieces(side):
                pl.when(here)(near.wait)
                pl.when(jnp.logical_not(here))(far.wait_send)
        for hop in self.hops:
            hop.wait_send()


class Line:
    def __init__(self, src, out, keep, send, recv):
        self.src, self.out, self.send, self.recv = src, out, send, recv
        self.row = lax.axis_index("row")
        self.near = pltpu.make_async_copy(src, out.at[self.row], keep)

    def copy(self, hops, up):
        step = 1 if up else -1
        mark = self.row - hops * step
        return pltpu.make_async_remote_copy(
            src_ref=self.src if hops == 0 else self.out.at[mark],
            dst_ref=self.out.at[mark],
            send_sem=self.send.at[hops if up else 3 + hops],
            recv_sem=self.recv.at[mark],
            device_id={"row": self.row + step},
            device_id_type=MESH_ID,
        )

    def sends(self, hops, up):
        return (self.row >= hops) & (self.row < 3) if up else (self.row + hops <= 3) & (self.row > 0)

    def start(self):
        self.near.start()
        for up in (True, False):
            pl.when(self.sends(0, up))(lambda: self.copy(0, up).start())

    def arrive(self, hops):
        for up in (True, False):
            mark = self.row - hops if up else self.row + hops

            @pl.when((self.row >= hops) if up else (self.row + hops <= 3))
            def _():
                pltpu.make_async_remote_copy(
                    src_ref=self.src,
                    dst_ref=self.out.at[mark],
                    send_sem=self.send.at[0],
                    recv_sem=self.recv.at[mark],
                    device_id={"row": self.row - 1 if up else self.row + 1},
                    device_id_type=MESH_ID,
                ).wait_recv()

    def pass_on(self, hops):
        self.arrive(hops)
        for up in (True, False):
            pl.when(self.sends(hops, up))(lambda: self.copy(hops, up).start())

    def finish(self):
        self.arrive(3)
        for hops in range(3):
            for up in (True, False):
                pl.when(self.sends(hops, up))(lambda: self.copy(hops, up).wait_send())
        self.near.wait()


def share(source, dest, mark, others, keep, send, recv):
    near = pltpu.make_async_copy(source, dest.at[mark], keep)
    near.start()
    copies = []
    for item, (target, _) in enumerate(others):
        copies.append(
            pltpu.make_async_remote_copy(
                src_ref=source,
                dst_ref=dest.at[mark],
                send_sem=send.at[item],
                recv_sem=recv.at[mark],
                device_id=target,
                device_id_type=MESH_ID,
            )
        )
        copies[item].start()

    def finish():
        near.wait()
        for target, index in others:
            pltpu.make_async_remote_copy(
                src_ref=source,
                dst_ref=dest.at[index],
                send_sem=send.at[0],
                recv_sem=recv.at[index],
                device_id=target,
                device_id_type=MESH_ID,
            ).wait_recv()
        for copy in copies:
            copy.wait_send()

    return finish


def enter_kernel(part_name, *refs):
    sources, outs, scratch = refs[:5], refs[5:12], refs[12:]
    first, second, gains, segs, weight = sources
    first_tok, first_all, second_tok, second_all, gains_all, segs_all, weight_all = outs
    (stage_one, middle_one, stage_two, middle_two, ready_one, ready_two, line_keep, line_send, line_recv, small_keep,
     gain_send, gain_recv, seg_send, seg_recv) = scratch[:14]
    spread_one, spread_two, gather_one, gather_two = (scratch[14 + 3 * index : 17 + 3 * index] for index in range(4))
    team = Team(part_name)
    row = lax.axis_index("row")
    rows = [({"row": lax.rem(row + hop, 4)}, lax.rem(row + hop, 4)) for hop in range(1, 4)]
    meet(team.partners() + [target for target, _ in rows] + [{part_name: team.far}])
    one = Spread(first, stage_one, middle_one, *spread_one)
    two = Spread(second, stage_two, middle_two, *spread_two)
    line = Line(weight, weight_all, line_keep, line_send, line_recv)
    one.start()
    done_gains = share(gains, gains_all, row, rows, small_keep.at[0], gain_send, gain_recv)
    parts = [({part_name: index}, index) for index in (team.across, team.twin, team.far)]
    done_segs = share(segs, segs_all, team.part, parts, small_keep.at[1], seg_send, seg_recv)
    line.start()
    one.turn()
    two.start()
    one.finish()
    done_gains()
    done_segs()
    tokens, width = first.shape[1], first.shape[2]

    def norm(rows, _):
        wides = [stage_one[index, rows, :].astype(F32) for index in range(4)]
        square = sum(jnp.sum(wide * wide, axis=1, keepdims=True) for wide in wides)
        scale = lax.rsqrt(square * (1.0 / (4 * width)) + 1e-05)
        for index in range(4):
            cols = slice(index * width, (index + 1) * width)
            first_tok[rows, cols] = stage_one[index, rows, :]
            ready_one[rows, cols] = (wides[index] * scale * gains_all[index, 0:1, :]).astype(BF16)

    strips(0, tokens, norm)
    two.turn()
    line.pass_on(1)
    gather_phase(team, ready_one, first_all, *gather_one)
    two.finish()

    def join_blocks(rows, _):
        for index in range(4):
            cols = slice(index * width, (index + 1) * width)
            second_tok[rows, cols] = stage_two[index, rows, :]
            ready_two[rows, cols] = stage_two[index, rows, :]

    strips(0, tokens, join_blocks)
    line.pass_on(2)
    gather_phase(team, ready_two, second_all, *gather_two)
    line.finish()


def enter_call(lay, first, second, gains, segs, weight):
    tokens, width = first.shape[0] // 4, first.shape[1]
    wide = 4 * width
    tok, everyone = jax.ShapeDtypeStruct((tokens, wide), BF16), jax.ShapeDtypeStruct((8, tokens, wide), BF16)
    stage = [pltpu.VMEM((4, tokens, width), BF16), pltpu.VMEM((2, tokens, width), BF16)]
    line_sems = [pltpu.SemaphoreType.DMA, pltpu.SemaphoreType.DMA((6,)), pltpu.SemaphoreType.DMA((4,))]
    small_sems = [pltpu.SemaphoreType.DMA((count,)) for count in (2, 3, 4, 3, 4)]
    spread_sems = [pltpu.SemaphoreType.DMA, pltpu.SemaphoreType.DMA((6,)), pltpu.SemaphoreType.DMA((6,))]
    results = pl.pallas_call(
        functools.partial(enter_kernel, lay.part),
        in_specs=[HBM_SPEC, HBM_SPEC, VMEM_SPEC, VMEM_SPEC, HBM_SPEC],
        out_specs=[VMEM_SPEC, HBM_SPEC, VMEM_SPEC, HBM_SPEC, VMEM_SPEC, VMEM_SPEC, HBM_SPEC],
        out_shape=[
            tok,
            everyone,
            tok,
            everyone,
            jax.ShapeDtypeStruct((4,) + gains.shape, gains.dtype),
            jax.ShapeDtypeStruct((4,) + segs.shape, segs.dtype),
            jax.ShapeDtypeStruct((4,) + weight.shape, weight.dtype),
        ],
        scratch_shapes=stage
        + stage
        + [pltpu.VMEM((tokens, wide), BF16)] * 2
        + line_sems
        + small_sems
        + spread_sems
        + spread_sems
        + GATHER_SEMS
        + GATHER_SEMS,
        compiler_params=pltpu.CompilerParams(
            collective_id=lay.fresh_id(), has_side_effects=True, vmem_limit_bytes=60 << 20
        ),
        cost_estimate=pl.CostEstimate(flops=1 << 30, bytes_accessed=400 << 20, transcendentals=0),
        name="enter",
    )(first.reshape(4, tokens, width), second.reshape(4, tokens, width), gains, segs, weight)
    first_tok, first_all, second_tok, second_all, gains, segs, weight = results
    return (
        first_tok, first_all.reshape(-1, wide), second_tok, second_all.reshape(-1, wide), gains, segs, weight,
    )


def strips(start, count, body):
    @pl.loop(0, count // STRIP)
    def _(step):
        body(pl.ds(pl.multiple_of(start + step * STRIP, STRIP), STRIP), pl.ds(pl.multiple_of(step * STRIP, STRIP), STRIP))


class Scatter:
    def __init__(self, team, dots, finish, refs):
        self.team, self.dots, self.finish = team, dots, finish
        self.work, self.twin, self.sent, self.relay, self.final, self.send, self.recv = refs
        self.rows, self.chunk = self.twin.shape[1], self.twin.shape[2] // 4
        self.half = self.rows // 2
        first, second = pl.ds(0, self.half), pl.ds(self.half, self.half)
        sent, relay, final = self.sent, self.relay, self.final
        self.relay_x = self.copy(sent.at[0, first], relay.at[0], 4, team.x)
        self.relay_y = self.copy(sent.at[0, second], relay.at[1], 5, team.y)
        self.x_first = self.copy(sent.at[1, first], final.at[0, first], 6, team.x)
        self.x_second = self.copy(sent.at[1, second], final.at[0, second], 7, team.x)
        self.y_second = self.copy(sent.at[2, second], final.at[1, second], 8, team.y)
        self.y_first = self.copy(sent.at[2, first], final.at[1, first], 9, team.y)

    def copy(self, source, dest, index, target):
        return remote(source, dest, self.send, self.recv, index, target)

    def swap(self, item):
        return self.copy(self.work.at[item, 0], self.twin.at[item], item, self.team.core)

    def total(self, item, start, passed=None):
        def add(rows, local):
            value = self.work[item, 1, rows, :].astype(F32) + self.twin[item, rows, :].astype(F32)
            if passed is not None:
                value = value + self.relay[passed, local, :].astype(F32)
            self.sent[item, rows, :] = value.astype(BF16)

        strips(start, self.half, add)

    def begin(self):
        team = self.team

        @pl.loop(0, 4)
        def _(item):
            @pl.loop(0, 8)
            def _(step):
                which, chunk = step // 4, lax.rem(step, 4)
                base = team.part * which + team.twin * (1 - which)
                slot = lax.rem(base + 2 * (1 - item // 2), 4) * 2 + lax.rem(team.col + 1 + item, 2)
                columns = pl.ds(pl.multiple_of(chunk * self.chunk, self.chunk), self.chunk)
                rows = pl.ds(pl.multiple_of(slot * self.rows, STRIP), self.rows)
                self.work[item, which, :, columns] = self.dots(rows, chunk, columns).astype(BF16)

            self.swap(item).start()

            @pl.when(item == 1)
            def _():
                self.swap(0).wait_recv()
                self.total(0, 0)
                self.relay_x.start()
                self.total(0, self.half)
                self.relay_y.start()

            @pl.when(item == 2)
            def _():
                self.swap(1).wait_recv()
                self.total(1, 0)
                self.x_first.start()

            @pl.when(item == 3)
            def _():
                self.swap(2).wait_recv()
                self.total(2, self.half)
                self.y_second.start()

    def pass_on(self):
        self.relay_y.wait_recv()
        self.total(1, self.half, 1)
        self.x_second.start()
        self.relay_x.wait_recv()
        self.total(2, 0, 0)
        self.y_first.start()

    def conclude(self):
        self.swap(3).wait_recv()

        def last(rows, _):
            value = self.work[3, 1, rows, :].astype(F32) + self.twin[3, rows, :].astype(F32)
            self.finish(rows, value + self.final[0, rows, :].astype(F32) + self.final[1, rows, :].astype(F32))

        self.x_first.wait_recv()
        self.y_first.wait_recv()
        strips(0, self.half, last)
        self.x_second.wait_recv()
        self.y_second.wait_recv()
        strips(self.half, self.half, last)
        for copy in [self.swap(item) for item in range(4)]:
            copy.wait_send()
        for copy in (self.relay_x, self.relay_y, self.x_first, self.x_second, self.y_second, self.y_first):
            copy.wait_send()


def scatter_scratch(tokens, wide):
    return [
        pltpu.VMEM((4, 2, tokens, wide), BF16),
        pltpu.VMEM((4, tokens, wide), BF16),
        pltpu.VMEM((3, tokens, wide), BF16),
        pltpu.VMEM((2, tokens // 2, wide), BF16),
        pltpu.VMEM((2, tokens, wide), BF16),
        pltpu.SemaphoreType.DMA((10,)),
        pltpu.SemaphoreType.DMA((10,)),
    ]


def make_dots(lefts, rights, starts):
    def dots(rows, chunk, columns):
        value = 0.0
        for left, (index, start) in zip(lefts, starts):
            right, depth = rights[index], slice(start, start + left.shape[1])
            if len(right.shape) == 3:
                value = value + lax.dot_general(left[rows, :], right[chunk, depth, :], NN, preferred_element_type=F32)
            else:
                value = value + lax.dot_general(left[rows, :], right[columns, depth], NT, preferred_element_type=F32)
        return value

    return dots


def norm_back(value, total, gain, gain_sum):
    scale = lax.rsqrt(jnp.sum(value * value, axis=1, keepdims=True) * (1.0 / value.shape[1]) + 1e-05)
    normed = value * scale
    gain_sum[...] += total * normed
    scaled = total * gain
    inner = jnp.sum(scaled * normed, axis=1, keepdims=True) * (1.0 / value.shape[1])
    return scale * (scaled - normed * inner)


def deal_out(out, rows, value):
    width = value.shape[1] // 4
    for index in range(4):
        out[index, rows, :] = value[:, index * width : (index + 1) * width].astype(BF16)


def fetch(sources, places, sems):
    copies = []
    for index, (source, place) in enumerate(zip(sources, places)):
        if isinstance(source, tuple):
            ref, start = source
            source = ref.at[:, pl.ds(start, place.shape[1]), :]
        copies.append(pltpu.make_async_copy(source, place, sems.at[index]))
        copies[index].start()
    return copies


def fetched(shapes):
    return [pltpu.VMEM(shape, dtype) for shape, dtype in shapes] + [pltpu.SemaphoreType.DMA((len(shapes),))]


def whole(values):
    return values.shape, values.dtype


def mid_kernel(part_name, starts, *refs):
    count = len(starts)
    sources, (out, everyone), scratch = refs[: count + 3], refs[count + 3 : count + 5], refs[count + 5 :]
    places, sems, scratch = scratch[: count + 3], scratch[count + 3], scratch[count + 4 :]
    loads = fetch(sources, places, sems)
    lefts, (right, stored, gain) = places[:count], places[count:]
    ready = scratch[7]
    team = Team(part_name)
    meet(team.partners())
    for load in loads:
        load.wait()

    def finish(rows, total):
        value = stored[rows, :].astype(F32) + total
        out[rows, :] = value
        scale = lax.rsqrt(jnp.sum(value * value, axis=1, keepdims=True) * (1.0 / value.shape[1]) + 1e-05)
        ready[rows, :] = (value * scale * gain[...]).astype(BF16)

    scatter = Scatter(team, make_dots(lefts, [right], starts), finish, scratch[:7])
    scatter.begin()
    scatter.pass_on()
    scatter.conclude()
    gather_phase(team, ready, everyone, *scratch[8:])


def mid_call(lay, lefts, right, starts, stored, gain):
    tokens, wide = stored.shape
    residual, everyone = pl.pallas_call(
        functools.partial(mid_kernel, lay.part, starts),
        in_specs=[HBM_SPEC] * (len(lefts) + 3),
        out_specs=[VMEM_SPEC, HBM_SPEC],
        out_shape=[jax.ShapeDtypeStruct((tokens, wide), F32), jax.ShapeDtypeStruct((8, tokens, wide), BF16)],
        scratch_shapes=fetched([whole(values) for values in (*lefts, right, stored, gain)])
        + scatter_scratch(tokens, wide) + [pltpu.VMEM((tokens, wide), BF16)] + GATHER_SEMS,
        compiler_params=pltpu.CompilerParams(
            collective_id=lay.fresh_id(), has_side_effects=True, vmem_limit_bytes=60 << 20
        ),
        cost_estimate=pl.CostEstimate(flops=1 << 35, bytes_accessed=200 << 20, transcendentals=0),
        name="team_mid",
    )(*lefts, right, stored, gain)
    return residual, everyone.reshape(8 * tokens, wide)


def branch_kernel(part_name, count, *refs):
    total = 2 * count + 3
    sources, (out, everyone, gain_out), scratch = refs[:total], refs[total : total + 3], refs[total + 3 :]
    places, sems, scratch = scratch[:total], scratch[total], scratch[total + 1 :]
    sources = [(ref, 0) if count <= index < 2 * count else ref for index, ref in enumerate(sources)]
    loads = fetch(sources, places, sems)
    lefts, rights, (residual, through, gain) = places[:count], places[count : 2 * count], places[2 * count :]
    gain_sum, ready = scratch[7:9]
    team = Team(part_name)
    meet(team.partners())
    for load in loads:
        load.wait()
    gain_sum[...] = jnp.zeros_like(gain_sum)

    def finish(rows, total):
        value = through[rows, :].astype(F32) + norm_back(residual[rows, :], total, gain[...], gain_sum)
        out[rows, :] = value
        ready[rows, :] = value.astype(BF16)

    scatter = Scatter(team, make_dots(lefts, rights, [(index, 0) for index in range(count)]), finish, scratch[:7])
    scatter.begin()
    scatter.pass_on()
    scatter.conclude()
    gain_out[...] = jnp.sum(gain_sum[...], axis=0, keepdims=True)
    gather_phase(team, ready, everyone, *scratch[9:])


def branch_call(lay, lefts, rights, residual, through, gain):
    tokens, wide = residual.shape
    width = rights[0].shape[2]
    out, everyone, gain_part = pl.pallas_call(
        functools.partial(branch_kernel, lay.part, len(lefts)),
        in_specs=[HBM_SPEC] * (2 * len(lefts) + 3),
        out_specs=[VMEM_SPEC, HBM_SPEC, VMEM_SPEC],
        out_shape=[
            jax.ShapeDtypeStruct((tokens, wide), F32),
            jax.ShapeDtypeStruct((8, tokens, wide), BF16),
            jax.ShapeDtypeStruct((1, wide), F32),
        ],
        scratch_shapes=fetched(
            [whole(left) for left in lefts]
            + [((4, left.shape[1], width), BF16) for left in lefts]
            + [whole(values) for values in (residual, through, gain)]
        )
        + scatter_scratch(tokens, wide)
        + [pltpu.VMEM((STRIP, wide), F32), pltpu.VMEM((tokens, wide), BF16)]
        + GATHER_SEMS,
        compiler_params=pltpu.CompilerParams(
            collective_id=lay.fresh_id(), has_side_effects=True, vmem_limit_bytes=60 << 20
        ),
        cost_estimate=pl.CostEstimate(flops=1 << 35, bytes_accessed=250 << 20, transcendentals=0),
        name="team_branch",
    )(*lefts, *rights, residual, through, gain)
    return out, everyone.reshape(8 * tokens, wide), gain_part


def finish_kernel(part_name, count, starts, *refs):
    total = 2 * count + len(starts) + 5
    sources, (block_out, input_out, gain_out), scratch = refs[:total], refs[total : total + 3], refs[total + 3 :]
    places, sems, scratch = scratch[:total], scratch[total], scratch[total + 1 :]
    hidden, downs, grads = places[:count], places[count : 2 * count], places[2 * count : -5]
    mix, residual, stored, through, gain = places[-5:]
    downs_from = [(ref, 2 * values.shape[1]) for ref, values in zip(sources[count : 2 * count], hidden)]
    loads = fetch([*sources[:count], *downs_from, *sources[2 * count :]], places, sems)
    gain_sum = scratch[14]
    team = Team(part_name)
    meet(team.partners())
    for load in loads[: 2 * count]:
        load.wait()
    gain_sum[...] = jnp.zeros_like(gain_sum)

    def finish_block(rows, total):
        deal_out(block_out, rows, residual[rows, :] + total)

    def finish_input(rows, total):
        value = norm_back(stored[rows, :].astype(F32), total, gain[...], gain_sum)
        deal_out(input_out, rows, through[rows, :] + value)

    block = Scatter(
        team, make_dots(hidden, downs, [(index, 0) for index in range(count)]), finish_block, scratch[:7]
    )
    inputs = Scatter(team, make_dots(grads, [mix], [(0, start) for start in starts]), finish_input, scratch[7:14])
    block.begin()
    for load in loads[2 * count :]:
        load.wait()
    inputs.begin()
    block.pass_on()
    inputs.pass_on()
    block.conclude()
    inputs.conclude()
    gain_out[...] = jnp.sum(gain_sum[...], axis=0, keepdims=True)


def finish_call(lay, hidden, stacks, grads, mix, starts, residual, stored, through, gain):
    tokens, wide = residual.shape
    width = stacks[0].shape[2]
    pieces = jax.ShapeDtypeStruct((4, tokens, width), BF16)
    return pl.pallas_call(
        functools.partial(finish_kernel, lay.part, len(hidden), starts),
        in_specs=[HBM_SPEC] * (2 * len(hidden) + len(grads) + 5),
        out_specs=[VMEM_SPEC] * 3,
        out_shape=[pieces, pieces, jax.ShapeDtypeStruct((1, wide), F32)],
        scratch_shapes=fetched(
            [whole(values) for values in hidden]
            + [((4, values.shape[1], width), BF16) for values in hidden]
            + [whole(values) for values in (*grads, mix, residual, stored, through, gain)]
        )
        + scatter_scratch(tokens, wide)
        + scatter_scratch(tokens, wide)
        + [pltpu.VMEM((STRIP, wide), F32)],
        compiler_params=pltpu.CompilerParams(
            collective_id=lay.fresh_id(), has_side_effects=True, vmem_limit_bytes=60 << 20
        ),
        cost_estimate=pl.CostEstimate(flops=1 << 35, bytes_accessed=250 << 20, transcendentals=0),
        name="team_finish",
    )(*hidden, *stacks, *grads, mix, residual, stored, through, gain)


class Deal:
    def __init__(self, src, out, keep, send, recv):
        self.src, self.out, self.keep, self.send, self.recv = src, out, keep, send, recv
        self.row, self.col = lax.axis_index("row"), lax.axis_index("col")
        spot = self.row * 2 + self.col
        self.mark, self.home = lax.rem(spot, 4), spot // 4

    def owner(self, index):
        place = self.col * 4 + index
        return {"row": place // 2, "col": lax.rem(place, 2)}

    def apart(self, index):
        owner = self.owner(index)
        return (owner["row"] != self.row) | (owner["col"] != self.col)

    def greet(self, barrier):
        for index in range(4):

            @pl.when(self.apart(index))
            def _():
                pl.semaphore_signal(barrier, inc=1, device_id=self.owner(index), device_id_type=MESH_ID)

        return 4 - (self.home == self.col).astype(jnp.int32)

    def each(self, act_near, act_far):
        for index in range(4):
            here = (self.row == index) & (self.home == self.col)

            @pl.when(here)
            def _():
                act_near(pltpu.make_async_copy(self.src.at[index], self.out.at[self.mark], self.keep))

            @pl.when(jnp.logical_not(here))
            def _():
                act_far(
                    pltpu.make_async_remote_copy(
                        src_ref=self.src.at[index],
                        dst_ref=self.out.at[self.mark],
                        send_sem=self.send.at[index],
                        recv_sem=self.recv.at[self.mark],
                        device_id={"row": index, "col": self.home},
                        device_id_type=MESH_ID,
                    )
                )

    def start(self):
        self.each(lambda copy: copy.start(), lambda copy: copy.start())

    def finish(self):
        for index in range(4):

            @pl.when(self.apart(index))
            def _():
                pltpu.make_async_remote_copy(
                    src_ref=self.src.at[0],
                    dst_ref=self.out.at[index],
                    send_sem=self.send.at[0],
                    recv_sem=self.recv.at[index],
                    device_id=self.owner(index),
                    device_id_type=MESH_ID,
                ).wait_recv()

        self.each(lambda copy: copy.wait(), lambda copy: copy.wait_send())


DEAL_SEMS = [pltpu.SemaphoreType.DMA, pltpu.SemaphoreType.DMA((4,)), pltpu.SemaphoreType.DMA((4,))]


def leave_kernel(part_name, *refs):
    first, second, block, src, first_out, second_out, blocks, out = refs[:8]
    deals = [Deal(first, first_out, *refs[8:11]), Deal(second, second_out, *refs[11:14])]
    rows_in, summed, near, row_send, row_recv, team_send, team_recv, join_send, join_recv = refs[14:]
    team = Team(part_name)
    row = lax.axis_index("row")
    rows = [({"row": lax.rem(row + hop, 4)}, lax.rem(row + hop, 4)) for hop in range(1, 4)]
    mates = []
    for part in (team.part, team.across, team.twin, team.far):
        for side in (team.col, team.other):
            mates.append(({part_name: part, "col": side}, part * 2 + side))
    mates = mates[1:]
    barrier = pltpu.get_barrier_semaphore()
    for target, _ in rows + mates:
        pl.semaphore_signal(barrier, inc=1, device_id=target, device_id_type=MESH_ID)
    pl.semaphore_wait(barrier, len(rows + mates) + deals[0].greet(barrier))
    own, across = blocks.at[team.part], blocks.at[team.across]
    join_x = remote(block, own, join_send, join_recv, 0, team.x)
    join_core = remote(block, own, join_send, join_recv, 1, team.core)
    join_pass = remote(across, across, join_send, join_recv, 2, team.core)
    join_near = pltpu.make_async_copy(block, own, near.at[2])
    finish_rows = share(src, rows_in, row, rows, near.at[0], row_send, row_recv)
    for copy in (join_x, join_core, join_near):
        copy.start()
    for deal in deals:
        deal.start()
    finish_rows()
    summed[...] = (rows_in[0] + rows_in[1]) + (rows_in[2] + rows_in[3])
    finish_team = share(summed, out, team.part * 2 + team.col, mates, near.at[1], team_send, team_recv)
    join_x.wait_recv()
    join_pass.start()
    for deal in deals:
        deal.finish()
    finish_team()
    join_core.wait_recv()
    join_pass.wait_recv()
    for copy in (join_x, join_core, join_pass):
        copy.wait_send()
    join_near.wait()


def leave_call(lay, first, second, block, small):
    whole_array = jax.ShapeDtypeStruct(first.shape, first.dtype)
    return pl.pallas_call(
        functools.partial(leave_kernel, lay.part),
        in_specs=[HBM_SPEC, HBM_SPEC, HBM_SPEC, VMEM_SPEC],
        out_specs=[HBM_SPEC, HBM_SPEC, HBM_SPEC, VMEM_SPEC],
        out_shape=[
            whole_array,
            whole_array,
            jax.ShapeDtypeStruct((4,) + block.shape, block.dtype),
            jax.ShapeDtypeStruct((8,) + small.shape, F32),
        ],
        scratch_shapes=DEAL_SEMS
        + DEAL_SEMS
        + [pltpu.VMEM((4,) + small.shape, F32), pltpu.VMEM(small.shape, F32)]
        + [pltpu.SemaphoreType.DMA((count,)) for count in (3, 3, 4, 7, 8, 3, 3)],
        compiler_params=pltpu.CompilerParams(
            collective_id=lay.fresh_id(), has_side_effects=True, vmem_limit_bytes=60 << 20
        ),
        cost_estimate=pl.CostEstimate(flops=1 << 30, bytes_accessed=120 << 20, transcendentals=0),
        name="leave",
    )(first, second, block, small)


def cross(lay, value):
    return lax.ppermute(value, lay.part, [(0, 2), (2, 0), (1, 3), (3, 1)])


def link(lay, value):
    return lax.ppermute(value, lay.part, [(0, 1), (1, 0), (2, 3), (3, 2)])


def part_order(lay):
    part = lax.axis_index(lay.part)
    twin = part + 1 - 2 * (part % 2)
    return jnp.stack([part, (part + 2) % 4, twin, (twin + 2) % 4]).astype(jnp.int32)


def rows_kernel(order, *refs):
    for index, ref in enumerate(refs[:4]):

        @pl.when(pl.program_id(1) == index)
        def _():
            refs[4][...] = ref[...].astype(F32)


def place_rows(order, pieces, start, rows):
    width = pieces[0].shape[1]
    block = rows
    while start % block:
        block //= 2
    steps = rows // block
    return pl.pallas_call(
        rows_kernel,
        grid_spec=pltpu.PrefetchScalarGridSpec(
            num_scalar_prefetch=1,
            grid=(steps, 4),
            in_specs=[pl.BlockSpec((block, width), lambda j, i, order: (start // block + j, 0))] * 4,
            out_specs=pl.BlockSpec((block, width), lambda j, i, order: (order[i] * steps + j, 0)),
        ),
        out_shape=jax.ShapeDtypeStruct((4 * rows, width), F32),
        compiler_params=pltpu.CompilerParams(vmem_limit_bytes=60 << 20),
        name="place_rows",
    )(order, *pieces)


def late_head_kernel(order, *refs):
    for index, ref in enumerate(refs[:4]):

        @pl.when(pl.program_id(0) == index)
        def _():
            refs[4][...] = ref[...].T.astype(F32)


def place_late_head(order, heads, head, pieces):
    features = pieces[0].shape[1]
    return pl.pallas_call(
        late_head_kernel,
        grid_spec=pltpu.PrefetchScalarGridSpec(
            num_scalar_prefetch=1,
            grid=(4,),
            in_specs=[pl.BlockSpec((PER_HEAD, features), lambda i, order: (0, 0))] * 4,
            out_specs=pl.BlockSpec((features, PER_HEAD), lambda i, order: (0, order[i] * heads + head)),
        ),
        out_shape=jax.ShapeDtypeStruct((features, 4 * heads * PER_HEAD), F32),
        compiler_params=pltpu.CompilerParams(vmem_limit_bytes=60 << 20),
        name="place_late_head",
    )(order, *pieces)


def first_head_kernel(heads, src, tail, _, out, decay):
    out[...] = src[0].T.astype(F32)
    small = tail[0].astype(F32).T[:, : 2 * heads]
    for part in range(4):

        @pl.when(pl.program_id(0) == part)
        def _():
            decay[:, part * 2 * heads : (part + 1) * 2 * heads] = small


def place_first_head(heads, stack, whole_grad):
    features = stack.shape[2]
    return pl.pallas_call(
        functools.partial(first_head_kernel, heads),
        grid=(4,),
        in_specs=[
            pl.BlockSpec((1, PER_HEAD, features), lambda i: (i, 0, 0)),
            pl.BlockSpec((1, DECAY_ROWS, features), lambda i: (i, PER_HEAD // DECAY_ROWS, 0)),
            HBM_SPEC,
        ],
        out_specs=[
            pl.BlockSpec((features, PER_HEAD), lambda i: (0, i * heads)),
            pl.BlockSpec((features, 8 * heads), lambda i: (0, 0)),
        ],
        out_shape=[
            jax.ShapeDtypeStruct((features, 4 * heads * PER_HEAD), F32),
            jax.ShapeDtypeStruct((features, 8 * heads), F32),
        ],
        input_output_aliases={2: 0},
        compiler_params=pltpu.CompilerParams(vmem_limit_bytes=60 << 20),
        name="place_first_head",
    )(stack, stack, whole_grad)


def place_ffn_kernel(counts, order, *refs):
    units = sum(counts)
    blocks = len(counts)
    pairs, downs = refs[: 4 * blocks], refs[4 * blocks : 8 * blocks]
    gate, up, down = refs[8 * blocks : 8 * blocks + 3]
    turned = refs[8 * blocks + 3 :]
    base = 0
    for block, count in enumerate(counts):
        for index in range(4):
            turned[block][order[index]] = pairs[4 * block + index][...].T.astype(F32)
            start = pl.multiple_of(order[index] * units + base, 64)
            down[pl.ds(start, count), :] = downs[4 * block + index][...].astype(F32)
        for part in range(4):
            place = slice(part * units + base, part * units + base + count)
            gate[:, place] = turned[block][part, :, :count]
            up[:, place] = turned[block][part, :, count:]
        base += count


def place_ffn(order, pieces):
    counts = [group[0].shape[0] // 3 for group in pieces]
    flat = [piece for group in pieces for piece in group]
    features, units = flat[0].shape[1], sum(counts)
    wide = jax.ShapeDtypeStruct((features, 4 * units), F32)
    return pl.pallas_call(
        functools.partial(place_ffn_kernel, counts),
        grid_spec=pltpu.PrefetchScalarGridSpec(
            num_scalar_prefetch=1,
            grid=(features // 128,),
            in_specs=[pl.BlockSpec((2 * (p.shape[0] // 3), 128), lambda i, order: (0, i)) for p in flat]
            + [pl.BlockSpec((p.shape[0] // 3, 128), lambda i, order: (2, i)) for p in flat],
            out_specs=[
                pl.BlockSpec((128, 4 * units), lambda i, order: (i, 0)),
                pl.BlockSpec((128, 4 * units), lambda i, order: (i, 0)),
                pl.BlockSpec((4 * units, 128), lambda i, order: (0, i)),
            ],
            scratch_shapes=[pltpu.VMEM((4, 128, 2 * count), F32) for count in counts],
        ),
        out_shape=[wide, wide, jax.ShapeDtypeStruct((4 * units, features), F32)],
        compiler_params=pltpu.CompilerParams(vmem_limit_bytes=60 << 20),
        cost_estimate=pl.CostEstimate(flops=1 << 30, bytes_accessed=30 << 20, transcendentals=0),
        name="place_ffn",
    )(order, *flat, *flat)


def stack_kernel(counts, *refs):
    grads, values, out = refs[: len(counts)], refs[len(counts) : -1], refs[-1]
    base = 0
    for grad, value, count in zip(grads, values, counts):
        for start in range(0, count, 256):
            size = min(256, grad.shape[1] - start)
            part = lax.dot_general(grad[:, start : start + size], value[...], TN, preferred_element_type=F32)
            size = min(size, count - start)
            out[0, base + start : base + start + size, :] = part[:size].astype(BF16)
        base += count


def stack_call(rows_n, pairs, counts):
    tokens, wide = pairs[0][1].shape
    width = wide // rows_n
    total = sum(counts)
    flops = 2 * tokens * wide * sum(grad.shape[1] for grad, _ in pairs)
    return pl.pallas_call(
        functools.partial(stack_kernel, counts),
        grid=(rows_n,),
        in_specs=[
            pl.BlockSpec(grad.shape, lambda i: (0, 0), pipeline_mode=pl.Buffered(1)) for grad, _ in pairs
        ]
        + [pl.BlockSpec((tokens, width), lambda i: (0, i)) for _ in pairs],
        out_specs=pl.BlockSpec((1, total, width), lambda i: (i, 0, 0)),
        out_shape=jax.ShapeDtypeStruct((rows_n, total, width), BF16),
        compiler_params=pltpu.CompilerParams(vmem_limit_bytes=60 << 20),
        cost_estimate=pl.CostEstimate(flops=flops, bytes_accessed=40 << 20, transcendentals=0),
        name="weight_grads",
    )(*[grad for grad, _ in pairs], *[value for _, value in pairs])


def units_kernel(part_name, cuts, gate, up, down, *outs):
    part, units = lax.axis_index(part_name), cuts[-1]
    for index in range(gate.shape[1] // units):

        @pl.when(part == index)
        def _():
            base = index * units
            for which, ref in enumerate((gate, up)):
                turned = ref[:, base : base + units].T
                for out, start, end in zip(outs, cuts[:-1], cuts[1:]):
                    out[which * (end - start) : (which + 1) * (end - start), :] = turned[start:end]
            for out, start, end in zip(outs, cuts[:-1], cuts[1:]):
                out[2 * (end - start) :, :] = down[base + start : base + end, :]


def units_call(lay, cuts, gate, up, down):
    features, wide = gate.shape
    rows = [3 * (end - start) for start, end in zip(cuts[:-1], cuts[1:])]
    return pl.pallas_call(
        functools.partial(units_kernel, lay.part, cuts),
        grid=(features // 128,),
        in_specs=[pl.BlockSpec((128, wide), lambda i: (i, 0))] * 2 + [pl.BlockSpec((wide, 128), lambda i: (0, i))],
        out_specs=[pl.BlockSpec((count, 128), lambda i: (0, i)) for count in rows],
        out_shape=[jax.ShapeDtypeStruct((count, features), BF16) for count in rows],
        compiler_params=pltpu.CompilerParams(vmem_limit_bytes=60 << 20),
        name="own_units",
    )(gate, up, down)


def ffn_kernel(values, grads, stack, hidden, both_grad):
    units, width = hidden.shape[1], stack.shape[2]
    both, grad = 0.0, 0.0
    for index in range(stack.shape[0]):
        cols = slice(index * width, (index + 1) * width)
        both = both + lax.dot_general(
            values[:, cols], stack[index, : 2 * units, :], NT, preferred_element_type=F32
        )
        grad = grad + lax.dot_general(grads[:, cols], stack[index, 2 * units :, :], NT, preferred_element_type=F32)
    gate, up = both[:, :units], both[:, units:]
    sig = sigmoid(gate)
    act = gate * sig
    hidden[...] = (act * up).astype(BF16)
    both_grad[:, :units] = (grad * up * (sig + act * (1.0 - sig))).astype(BF16)
    both_grad[:, units:] = (grad * act).astype(BF16)


def ffn_call(values, grads, stack):
    tokens, width = values.shape
    units = stack.shape[1] // 3
    block = 256
    while tokens % block:
        block //= 2
    row = pl.BlockSpec((block, width), lambda i: (i, 0))
    return pl.pallas_call(
        ffn_kernel,
        grid=(tokens // block,),
        in_specs=[row, row, pl.BlockSpec(stack.shape, lambda i: (0, 0, 0))],
        out_specs=[
            pl.BlockSpec((block, units), lambda i: (i, 0)),
            pl.BlockSpec((block, 2 * units), lambda i: (i, 0)),
        ],
        out_shape=[
            jax.ShapeDtypeStruct((tokens, units), BF16),
            jax.ShapeDtypeStruct((tokens, 2 * units), BF16),
        ],
        compiler_params=pltpu.CompilerParams(vmem_limit_bytes=60 << 20),
        cost_estimate=pl.CostEstimate(
            flops=6 * tokens * width * units, bytes_accessed=30 << 20, transcendentals=tokens * units
        ),
        name="ffn",
    )(values, grads, stack)


SEQ = 448


def project(left, right):
    return jnp.dot(left, right, preferred_element_type=F32)


def project_back(left, right):
    return lax.dot_general(left, right, NT, preferred_element_type=F32)


def weight_grads(lay, *pairs):
    if lay.native:
        return stack_call(lay.rows, [pair[:2] for pair in pairs], [count for _, _, count in pairs])
    stacks = []
    for grad, value, count in pairs:
        whole = lax.dot_general(grad, value, TN, preferred_element_type=F32)[:count].astype(BF16)
        stacks.append(jnp.moveaxis(whole.reshape(count, lay.rows, -1), 1, 0))
    return jnp.concatenate(stacks, axis=1)


def after(value, *others):
    return lax.optimization_barrier((value,) + others)[0]


class Plan:
    def __init__(self, mesh, heads):
        dp, self.rows, self.cols = (mesh.shape[name] for name in ("dp", "row", "col"))
        ways = dp
        while dp % ways or (heads // self.cols) % ways:
            ways -= 1
        self.ways = ways
        if ways == dp:
            self.mesh, self.shared, self.part = mesh, (), "dp"
        else:
            devices = mesh.devices.reshape(dp // ways, ways, self.rows, self.cols)
            self.mesh = Mesh(devices, ("group", "part", "row", "col"))
            self.shared, self.part = ("group",), "part"
        self.data = self.shared + (self.part,)
        self.team = (self.part, "col")
        self.native = (ways, self.rows, self.cols) == (4, 4, 2) and heads == 2 * ways * self.cols
        self.next_id = 0

    def fresh_id(self):
        self.next_id += 1
        return self.next_id


def spread(lay, values):
    local = values.shape[0]
    whole = lax.all_gather(values, "col", axis=0, tiled=True)
    whole = lax.all_to_all(whole, "row", split_axis=0, concat_axis=1, tiled=True)
    mine = local // lay.rows
    return lax.dynamic_slice_in_dim(whole, lax.axis_index("col") * mine, mine, 0)


def unspread(lay, value):
    local = value.shape[0] * lay.rows
    whole = lax.all_gather(value, "col", axis=0, tiled=True)
    whole = lax.all_to_all(whole, "row", split_axis=1, concat_axis=0, tiled=True)
    return lax.dynamic_slice_in_dim(whole, lax.axis_index("col") * local, local, 0)


def team_gather(lay, values):
    return lax.all_gather(values, lay.team, axis=0, tiled=True)


def team_scatter(lay, values):
    return lax.psum_scatter(values.astype(BF16), lay.team, scatter_dimension=0, tiled=True).astype(F32)


def norm_forward(values):
    scale = lax.rsqrt(jnp.mean(values * values, axis=1, keepdims=True) + 1e-05)
    return values * scale, scale


def norm_backward(grad, values, gain):
    normed, scale = norm_forward(values)
    scaled = grad * gain
    inner = jnp.mean(scaled * normed, axis=1, keepdims=True)
    return scale * (scaled - normed * inner), jnp.sum(grad * normed, axis=0, keepdims=True)


def enter(lay, values, grads, gains, segments, weight):
    if lay.native:
        return enter_call(lay, values, grads, gains, segments, weight)
    mine, grads = spread(lay, values), spread(lay, grads)
    gains, weight = (lax.all_gather(value, "row", axis=0, tiled=False) for value in (gains, weight))
    segments = lax.all_gather(segments, lay.part, axis=0, tiled=False)
    normed, _ = norm_forward(mine.astype(F32))
    everyone = team_gather(lay, (normed * gains[:, 0].reshape(1, -1)).astype(BF16))
    return mine, everyone, grads, team_gather(lay, grads), gains, segments, weight


def beside(stack, start, size):
    return jnp.moveaxis(stack[:, start : start + size], 0, 1).reshape(size, -1)


def own_units(lay, cuts, gate, up, down):
    if lay.native:
        return units_call(lay, cuts, gate, up, down)
    start, size = lax.axis_index(lay.part) * cuts[-1], cuts[-1]
    gate, up = (lax.dynamic_slice_in_dim(values, start, size, 1).T for values in (gate, up))
    down = lax.dynamic_slice_in_dim(down, start, size, 0)
    return [
        jnp.concatenate([values[first:last] for values in (gate, up, down)], axis=0)
        for first, last in zip(cuts[:-1], cuts[1:])
    ]


def mid_step(lay, mixed, out_all, stored, gain):
    starts = [head * DV for head in range(len(mixed))]
    if lay.native:
        return mid_call(lay, mixed, out_all, [(0, start) for start in starts], stored, gain)
    total = sum(project(left, beside(out_all, start, DV)) for left, start in zip(mixed, starts))
    residual = stored.astype(F32) + team_scatter(lay, total)
    normed, _ = norm_forward(residual)
    return residual, team_gather(lay, (normed * gain).astype(BF16))


def feed_forward(lay, values, grads, stack):
    if lay.native:
        return ffn_call(values, grads, stack)
    units = stack.shape[1] // 3
    gate, up = (project_back(values, beside(stack, start, units)) for start in (0, units))
    sig = jax.nn.sigmoid(gate)
    grad = project_back(grads, beside(stack, 2 * units, units))
    grad_gate = grad * up * sig * (1.0 + gate * (1.0 - sig))
    both = jnp.concatenate([grad_gate.astype(BF16), (grad * gate * sig).astype(BF16)], axis=1)
    return (gate * sig * up).astype(BF16), both


def branch_step(lay, lefts, stacks, residual, out_grads, gain):
    if lay.native:
        return branch_call(lay, lefts, stacks, residual, out_grads, gain)
    total = sum(project(left, beside(stack, 0, left.shape[1])) for left, stack in zip(lefts, stacks))
    grad, gain_part = norm_backward(team_scatter(lay, total), residual, gain)
    grad = out_grads.astype(F32) + grad
    return grad, team_gather(lay, grad.astype(BF16)), gain_part


def finish_step(lay, hidden, stacks, grads, mix, starts, residual, stored, grad_residual, gain):
    if lay.native:
        return finish_call(lay, hidden, stacks, grads, mix, starts, residual, stored, grad_residual, gain)
    total = sum(
        project(left, beside(stack, 2 * left.shape[1], left.shape[1])) for left, stack in zip(hidden, stacks)
    )
    block_output = (residual + team_scatter(lay, total)).astype(BF16)
    total = sum(project_back(left, mix[:, start : start + left.shape[1]]) for left, start in zip(grads, starts))
    grad, gain_part = norm_backward(team_scatter(lay, total), stored.astype(F32), gain)
    return block_output, (grad_residual + grad).astype(BF16), gain_part


def columns(stack):
    return jnp.moveaxis(stack, 2, 0).reshape(stack.shape[2], -1).astype(F32)


def on_device(
    lay,
    block_input,
    segment_ids,
    attn_gain,
    mix_weight,
    decay_weight,
    conv_weight,
    decay_log,
    decay_bias,
    out_gain,
    out_weight,
    ffn_gain,
    gate_weight,
    up_weight,
    down_weight,
    cotangent,
):
    part = lax.axis_index(lay.part)
    heads = decay_log.shape[0] // lay.ways
    units = gate_weight.shape[1] // lay.ways
    width = mix_weight.shape[0]

    def mine(values, dim, size):
        return lax.dynamic_slice_in_dim(values, part * size, size, dim)

    def gather_rows(values):
        return lax.all_gather(values, "row", axis=0, tiled=False)

    mix_mine = mine(mix_weight, 1, heads * PER_HEAD)
    decay_mine = mine(decay_weight, 1, heads * 2)
    decay_pad = jnp.pad(decay_mine, ((0, 0), (0, 128 - heads * 2)))
    splits = [0, PER_HEAD + 128]
    for head in range(1, heads):
        splits.append(splits[-1] + PER_HEAD)
    mix_pad = jnp.concatenate([mix_mine[:, :PER_HEAD], decay_pad, mix_mine[:, PER_HEAD:]], axis=1)
    out_all = gather_rows(mine(out_weight, 0, heads * DV))
    cuts = [0, min(units, -(-units // 256) * 128), units]
    unit_blocks = own_units(lay, cuts, gate_weight, up_weight, down_weight)
    conv_mine = mine(conv_weight, 1, heads * INNER)
    log_mine, bias_mine = mine(decay_log, 0, heads), mine(decay_bias, 0, heads)

    gains = jnp.stack([attn_gain, ffn_gain])
    stored, attn_all, out_grads, out_grads_all, gains, segments, mix_all = enter(
        lay, block_input, cotangent, gains, segment_ids.reshape(1, -1), after(mix_pad, *unit_blocks)
    )
    mix_all = mix_all.reshape(lay.rows * width, -1)
    gain_one, gain_two = gains[:, 0].reshape(1, -1), gains[:, 1].reshape(1, -1)
    segments = segments.astype(F32)
    seg_col, seg_row = segments.reshape(-1, 1), segments.reshape(-1, 1, SEQ)
    waiting = lax.optimization_barrier((*unit_blocks, attn_all))[:-1]
    stacks = [gather_rows(values) for values in waiting]
    tokens = attn_all.shape[0]
    head_weights = [mix_all[:, start:end] for start, end in zip(splits[:-1], splits[1:])]
    shared, mixed, solves, projs = (), [], [], []
    for head in range(heads):
        projs.append(project(after(attn_all, *mixed), head_weights[head]))
        if not head:
            shared = (
                projs[0], PER_HEAD // 128, seg_col, seg_row, conv_mine, log_mine, bias_mine, out_gain.reshape(1, -1),
            )
        values, solve = mixer_forward(head, heads, projs[head], *shared)
        mixed.append(values)
        solves.append(solve)
    residual, ffn_all = mid_step(lay, mixed, out_all, stored, gain_two)

    def sum_rows(grads):
        grads = lax.psum_scatter(grads, "row", scatter_dimension=0, tiled=False)
        return lax.psum(grads, lay.shared) if lay.shared else grads

    hidden, grad_both, ffn_grads = [], [], []
    for stack in stacks:
        values, grads = feed_forward(lay, ffn_all, out_grads_all, stack)
        count = values.shape[1]
        ffn_part = weight_grads(lay, (grads, ffn_all, 2 * count), (values, out_grads_all, count))
        ffn_all, values, grads = lax.optimization_barrier((ffn_all, values, grads, ffn_part))[:3]
        hidden.append(values)
        grad_both.append(grads)
        ffn_grads.append(sum_rows(ffn_part))
    grad_residual, branch_all, ffn_gain_part = branch_step(lay, grad_both, stacks, residual, out_grads, gain_two)

    branch = branch_all
    if lay.native:
        branch = after(branch, ffn_grads[0])
        crossed = [cross(lay, grads) for grads in ffn_grads]
    other = jnp.zeros((tokens, 128), BF16)
    proj_grads, mix_grads, conv_parts, small_parts = [], [], [], []
    for head in reversed(range(heads)):
        common = (head, heads, projs[head], *shared, solves[head], branch, out_all)
        if head:
            grad, extra, conv_part, small_part = mixer_backward(*common, None)
            if lay.native:
                grad = after(grad, crossed[0])
            other = other + extra
        else:
            grad, conv_part, small_part = mixer_backward(*common, other)
            if lay.native:
                grad = after(grad, *crossed)
        triples = [(grad, attn_all, PER_HEAD if head else PER_HEAD + DECAY_ROWS)]
        if head == heads - 1:
            triples += [(values, branch_all, DV) for values in mixed]
        mix_part = weight_grads(lay, *triples)
        branch, grad = lax.optimization_barrier((branch, grad, mix_part))[:2]
        if lay.native:
            branch = after(branch, *ffn_grads[1:])
        proj_grads.insert(0, grad)
        conv_parts.insert(0, conv_part.sum(0))
        small_parts.insert(0, small_part.sum(0)[0])
        mix_grads.insert(0, sum_rows(mix_part))
    if lay.native:
        ffn_pieces = [[ffn_grads[0], crossed[0], link(lay, ffn_grads[0]), link(lay, crossed[0])]]
        hidden[0] = after(hidden[0], *ffn_pieces[0])
    block_output, input_grad, attn_gain_part = finish_step(
        lay, hidden, stacks, proj_grads, mix_all, splits[:-1], residual, stored, grad_residual, gain_one
    )

    own = jnp.concatenate(
        [jnp.concatenate(conv_parts, axis=1).reshape(-1)]
        + [jnp.stack([part_of[DV + item] for part_of in small_parts]) for item in range(2)]
    )
    split = TAPS * heads * INNER
    gain_part = sum(part_of[:DV] for part_of in small_parts)
    col = lax.axis_index("col")
    if lay.native:
        flat = jnp.concatenate([own, gain_part, attn_gain_part[0], ffn_gain_part[0]])
        size = flat.shape[0]
        flat = jnp.pad(flat, (0, -size % 1024)).reshape(-1, 128)
        order = part_order(lay)
        for grads, passed in zip(ffn_grads[1:], crossed[1:]):
            ffn_pieces.append([grads, passed, link(lay, grads), link(lay, passed)])
        late = after(mix_grads[1], block_output)
        late_passed = cross(lay, late)
        ffn_pieces[0][0] = after(ffn_pieces[0][0], block_output)
        gate_grad, up_grad, down_weight_grad = place_ffn(order, ffn_pieces)
        passed = after(late_passed, gate_grad)
        late_pieces = [late, passed, link(lay, late), link(lay, passed)]
        out_weight_grad = place_rows(order, late_pieces, PER_HEAD, heads * DV)
        mix_grad = place_late_head(order, heads, 1, late_pieces)
        first = after(mix_grads[0], mix_grad)
        flat = after(flat, mix_grad, out_weight_grad)
        block_output, input_grad, first_stack, sums = leave_call(lay, block_output, input_grad, first, flat)
        mix_grad, decay_grad = place_first_head(heads, first_stack, mix_grad)
        block_output, input_grad = (value.reshape(-1, value.shape[2]) for value in (block_output, input_grad))
        sums = sums.reshape(8, -1)
        gain_sum, attn_sum, ffn_sum = jnp.split(
            jnp.sum(sums[:, own.shape[0] : size], axis=0), [DV, DV + lay.rows * width]
        )
        sums = sums[:, : own.shape[0]].reshape(lay.ways, lay.cols, -1)
    else:
        block_output, input_grad = unspread(lay, block_output), unspread(lay, input_grad)
        slots = lay.ways * lay.cols
        pick = (jnp.arange(slots) == part * lay.cols + col).astype(F32)[:, None]
        sums, gain_sum, ffn_sum, attn_sum = lax.psum(
            (pick * own[None, :], gain_part, ffn_gain_part[0], attn_gain_part[0]), lay.data + ("row", "col")
        )
        sums = sums.reshape(lay.ways, lay.cols, -1)
    sums = lax.dynamic_index_in_dim(sums, col, 1, keepdims=False)
    conv_grad = jnp.moveaxis(sums[:, :split].reshape(lay.ways, TAPS, -1), 0, 1).reshape(TAPS, -1)
    log_grad = sums[:, split : split + heads].reshape(-1)
    bias_grad = sums[:, split + heads :].reshape(-1)
    row = lax.axis_index("row")
    attn_gain_grad = lax.dynamic_slice_in_dim(attn_sum, row * width, width, 0)
    ffn_gain_grad = lax.dynamic_slice_in_dim(ffn_sum, row * width, width, 0)

    out_start = PER_HEAD if heads > 1 else PER_HEAD + DECAY_ROWS
    if not lay.native:
        mix_stacks = [lax.all_gather(value, lay.part, axis=0, tiled=False) for value in mix_grads]
        ffn_stacks = [lax.all_gather(value, lay.part, axis=0, tiled=False) for value in ffn_grads]
        decay_grad = columns(mix_stacks[0][:, PER_HEAD : PER_HEAD + 2 * heads])
        mix_grad = columns(jnp.concatenate([stack[:, :PER_HEAD] for stack in mix_stacks], axis=1))
        gate_grad, up_grad, down_weight_grad = (
            jnp.concatenate([jnp.split(stack, 3, axis=1)[item] for stack in ffn_stacks], axis=1) for item in range(3)
        )
        gate_grad, up_grad = columns(gate_grad), columns(up_grad)
        down_weight_grad = down_weight_grad.reshape(-1, width).astype(F32)
        out_weight_grad = mix_stacks[-1][:, out_start : out_start + heads * DV].reshape(-1, width).astype(F32)
    return (
        block_output,
        input_grad,
        attn_gain_grad,
        mix_grad,
        decay_grad,
        conv_grad,
        log_grad,
        bias_grad,
        gain_sum,
        out_weight_grad,
        ffn_gain_grad,
        gate_grad,
        up_grad,
        down_weight_grad,
    )


def solution(mesh):
    def run(*args):
        lay = Plan(mesh, args[6].shape[0])
        tokens, grid = P(lay.data + ("col",), "row"), P("row", "col")
        turned, features, inner = P("col", "row"), P("row"), P("col")
        conv = P(None, "col")
        return jax.shard_map(
            functools.partial(on_device, lay),
            mesh=lay.mesh,
            in_specs=(
                tokens, P(lay.data + ("row",)), features, grid, grid, conv, inner, inner, P(),
                turned, features, grid, grid, turned, tokens,
            ),
            out_specs=(
                tokens, tokens, features, grid, grid, conv, inner, inner, P(),
                turned, features, grid, grid, turned,
            ),
            check_vma=False,
        )(*args)

    return run
```

time: 895 us -> 784 us (0.88)
  waiting for transfers between devices: 72.5 us -> 20.9 us
  Pallas kernels: 714 us -> 684 us
  local copies, waits for them, and re-layouts: 45.8 us -> 23.9 us
    pallas_call x10 -> x11, Pallas kernels: 572 us -> 537 us  [the longest x1 188 us: enter_call(): pl.pallas_call(functools.partial(enter_kernel, lay.part), in_specs=[HBM_S...]
    all_gather x3, waiting for transfers between devices: 33.6 us -> 0.06 us  [gather_rows(): return lax.all_gather(values, 'row', axis=0, tiled=False)]
    ppermute x9, waiting for transfers between devices: 38.8 us -> 17.5 us  [the longest x3 14.2 us: cross(): return lax.ppermute(value, lay.part, [(0, 2), (2, 0), (1, 3), (3, 1)])]
    unnamed x74 -> x46, local copies, waits for them, and re-layouts: 19.4 us -> 8.26 us
    pallas_call x3 -> x4, Pallas kernels: 47 us -> 54.8 us  [stack_call(): pl.pallas_call(functools.partial(stack_kernel, counts), grid=(rows_n,), i...]
  transfers between devices with their start and end apart: 15 -> 16, of which waited for: 3 -> 5; matrix products, arithmetic and copies ran while one was open for 6% -> 5% of each run, Pallas kernels for 74% -> 80%
where the time goes in v3:
time: 784 us; the launch traced here: 779 us
  Pallas kernels  684 us (87%)
  local copies, waits for them, and re-layouts  23.9 us (3%)
  matrix products  23.9 us (3%)
  waiting for transfers between devices  20.9 us (3%)
  between operations  14.7 us (2%)
    pallas_call x1, Pallas kernels, enter_call(): pl.pallas_call(functools.partial(enter_kernel, lay.part), in_specs=[HBM_S...  188 us
    pallas_call x1, Pallas kernels, branch_call(): pl.pallas_call(functools.partial(branch_kernel, lay.part, len(lefts)), in...  84.4 us
    pallas_call x1, Pallas kernels, mid_call(): pl.pallas_call(functools.partial(mid_kernel, lay.part, starts), in_specs=...  77.5 us
    pallas_call x1, Pallas kernels, finish_call(): pl.pallas_call(functools.partial(finish_kernel, lay.part, len(hidden), st...  74.9 us
    pallas_call x4, Pallas kernels, stack_call(): pl.pallas_call(functools.partial(stack_kernel, counts), grid=(rows_n,), i...  54.8 us
    pallas_call x1, Pallas kernels, leave_call(): pl.pallas_call(functools.partial(leave_kernel, lay.part), in_specs=[HBM_S...  51.4 us
    pallas_call x2, Pallas kernels, mixer_backward(): pl.pallas_call(functools.partial(backward_kernel, head, last), grid=(coun...  49.4 us
    pallas_call x2, Pallas kernels, mixer_forward(): pl.pallas_call(functools.partial(forward_kernel, head), grid=(count,), in...  36.6 us
  transfers between devices with their start and end apart: 16, of which 5 were waited for; matrix products, arithmetic and copies ran while one was open for 5% of the time, Pallas kernels for 80%

profile of v3, /device:TPU:13, one launch (start us, length us, event | category | flops | bytes accessed | tf_op | source)
XLA Modules:
  0.0 779.5 jit_solution(13258951347925551922)
XLA Ops:
  10.6 5.8 own_units.1
  19.8 188.5 %enter.1 = (bf16[224,2048]{1,0:T(8,128)(2,1)}, bf16[8,224,2048]{2,1,0:T(8,128)(2,1)}, bf16[224,2048]{1,0:T(8,128)(2,1)}, bf16[8,224,2048]{2,1,0:T(8,128)(2,1)}, ...) custom-call(bf16[4,224,512]{2,1,0:T(8,128)(2,1)} %bitcast.89, ...), custom_call_target="tpu_custom_call" | custom-call | flops 1073741824 | bytes 419430400 | tf_op jit(solution)/shard_map/enter/pallas_call | solution.py:575
  214.0 13.3 %fusion.proj_ref.extra_ref.refs_1_.refs_0_ = f32[1792,896]{1,0:T(8,128)} fusion(bf16[1792,2048]{1,0:T(8,128)(2,1)} %bitcast.97, bf16[2048,1664]{1,0:T(8,128)(2,1)} %bitcast.113), kind=kOutput, calls=%fused_computation.2 | convolution fusion | flops 6576668672 | bytes 17432576 | tf_op jit(solution)/shard_map/dot_general | solution.py:1316
  228.7 18.3 %mixer_forward.2 = (bf16[1792,256]{1,0:T(8,128)(2,1)}, bf16[4,448,448]{2,1,0:T(8,128)(2,1)}) custom-call(f32[1792,896]{1,0:T(8,128)} %fusion.proj_ref.extra_ref.refs_1_.refs_0_, f32[1792,896]{1,0:T(8,128)} %fusion.proj_ref.extra_ref.refs_1_.refs_0_, f32[1792,1]{1,0:T(8,128)} %reshape.120.segc_ref.refs_2_, f32[4,1,448]{2,1,0:T(1,128)} %convert_element_type.7.segr_ref.refs_3_, ...), custom_call_target="tpu_custom_call" | custom-call | flops 12884901888 | bytes 33554432 | tf_op jit(solution)/shard_map/mixer_forward/pallas_call | solution.py:230
  247.0 10.6 %fusion.4.proj_ref.refs_0_ = f32[1792,768]{1,0:T(8,128)} fusion(bf16[1792,2048]{1,0:T(8,128)(2,1)} %bitcast.98, bf16[2048,1664]{1,0:T(8,128)(2,1)} %bitcast.114), kind=kOutput, calls=%fused_computation.6 | convolution fusion | flops 5637144576 | bytes 15990784 | tf_op jit(solution)/shard_map/dot_general | solution.py:1316
  258.2 18.3 %mixer_forward.3 = (bf16[1792,256]{1,0:T(8,128)(2,1)}, bf16[4,448,448]{2,1,0:T(8,128)(2,1)}) custom-call(f32[1792,768]{1,0:T(8,128)} %fusion.4.proj_ref.refs_0_, f32[1792,896]{1,0:T(8,128)} %fusion.proj_ref.extra_ref.refs_1_.refs_0_, f32[1792,1]{1,0:T(8,128)} %reshape.120.segc_ref.refs_2_, f32[4,1,448]{2,1,0:T(1,128)} %convert_element_type.7.segr_ref.refs_3_, ...), custom_call_target="tpu_custom_call" | custom-call | flops 12884901888 | bytes 33554432 | tf_op jit(solution)/shard_map/mixer_forward/pallas_call | solution.py:230
  276.5 77.5 %team_mid.1 = (f32[224,2048]{1,0:T(8,128)}, bf16[8,224,2048]{2,1,0:T(8,128)(2,1)}) custom-call(bf16[1792,256]{1,0:T(8,128)(2,1)} %get-tuple-element.83.refs_0_.refs_1_, bf16[1792,256]{1,0:T(8,128)(2,1)} %get-tuple-element.85.refs_1_.refs_2_, bf16[4,512,512]{2,1,0:T(8,128)(2,1)} %bitcast.86, bf16[224,2048]{1,0:T(8,128)(2,1)} %get-tuple-element.86.refs_3_.refs_8_, ...), custom_call_target="tpu_custom_call" | custom-call | flops 34359738368 | bytes 209715200 | tf_op jit(solution)/shard_map/team_mid/pallas_call | solution.py:795
  354.0 15.4 %ffn.2 = (bf16[1792,384]{1,0:T(8,128)(2,1)}, bf16[1792,768]{1,0:T(8,128)(2,1)}) custom-call(bf16[1792,2048]{1,0:T(8,128)(2,1)} %bitcast.109, bf16[1792,2048]{1,0:T(8,128)(2,1)} %bitcast.101, bf16[4,1152,512]{2,1,0:T(8,128)(2,1)} %bitcast.80), custom_call_target="tpu_custom_call" | custom-call | flops 8455716864 | bytes 31457280 | tf_op jit(solution)/shard_map/ffn/pallas_call | solution.py:1292
  369.4 13.9 %weight_grads.4 = bf16[4,1152,512]{2,1,0:T(8,128)(2,1)} custom-call(bf16[1792,768]{1,0:T(8,128)(2,1)} %get-tuple-element.100.refs_0_, bf16[1792,384]{1,0:T(8,128)(2,1)} %get-tuple-element.94.refs_1_.refs_0_, bf16[1792,2048]{1,0:T(8,128)(2,1)} %bitcast.110, bf16[1792,2048]{1,0:T(8,128)(2,1)} %bitcast.102), custom_call_target="tpu_custom_call" | custom-call | flops 8455716864 | bytes 41943040 | tf_op jit(solution)/shard_map/weight_grads/pallas_call | solution.py:1224
  383.4 15.8 %ffn.3 = (bf16[1792,320]{1,0:T(8,128)(2,1)}, bf16[1792,640]{1,0:T(8,128)(2,1)}) custom-call(bf16[1792,2048]{1,0:T(8,128)(2,1)} %bitcast.111, bf16[1792,2048]{1,0:T(8,128)(2,1)} %bitcast.103, bf16[4,960,512]{2,1,0:T(8,128)(2,1)} %bitcast.83), custom_call_target="tpu_custom_call" | custom-call | flops 7046430720 | bytes 31457280 | tf_op jit(solution)/shard_map/ffn/pallas_call | solution.py:1292
  399.2 13.1 %weight_grads.5 = bf16[4,960,512]{2,1,0:T(8,128)(2,1)} custom-call(bf16[1792,640]{1,0:T(8,128)(2,1)} %get-tuple-element.101.refs_0_.refs_1_, bf16[1792,320]{1,0:T(8,128)(2,1)} %get-tuple-element.99.refs_1_, bf16[1792,2048]{1,0:T(8,128)(2,1)} %bitcast.112, bf16[1792,2048]{1,0:T(8,128)(2,1)} %bitcast.104), custom_call_target="tpu_custom_call" | custom-call | flops 7046430720 | bytes 41943040 | tf_op jit(solution)/shard_map/weight_grads/pallas_call | solution.py:1224
  412.4 84.4 %team_branch.1 = (f32[224,2048]{1,0:T(8,128)}, bf16[8,224,2048]{2,1,0:T(8,128)(2,1)}, f32[1,2048]{1,0:T(1,128)}) custom-call(bf16[1792,768]{1,0:T(8,128)(2,1)} %get-tuple-element.100.refs_0_, bf16[1792,640]{1,0:T(8,128)(2,1)} %get-tuple-element.101.refs_0_.refs_1_, bf16[4,1152,512]{2,1,0:T(8,128)(2,1)} %bitcast.81, bf16[4,960,512]{2,1,0:T(8,128)(2,1)} %bitcast.84, ...), custom_call_target="tpu_custom_call" | custom-call | flops 34359738368 | bytes 262144000 | tf_op jit(solution)/shard_map/team_branch/pallas_call | solution.py:841
  498.1 24.6 %mixer_backward.2 = (bf16[1792,768]{1,0:T(8,128)(2,1)}, bf16[1792,128]{1,0:T(8,128)(2,1)}, f32[4,4,512]{2,1,0:T(4,128)}, f32[4,1,384]{2,1,0:T(1,128)}) custom-call(f32[1792,768]{1,0:T(8,128)} %fusion.4.proj_ref.refs_0_, f32[1792,896]{1,0:T(8,128)} %fusion.proj_ref.extra_ref.refs_1_.refs_0_, f32[1792,1]{1,0:T(8,128)} %reshape.120.segc_ref.refs_2_, ...), custom_call_target="tpu_custom_call" | custom-call | flops 25769803776 | bytes 67108864 | tf_op jit(solution)/shard_map/mixer_backward/pallas_call | solution.py:276
  524.6 17.0 %weight_grads.6 = bf16[4,1280,512]{2,1,0:T(8,128)(2,1)} custom-call(bf16[1792,768]{1,0:T(8,128)(2,1)} %get-tuple-element.116.refs_0_.refs_5_, bf16[1792,256]{1,0:T(8,128)(2,1)} %get-tuple-element.83.refs_0_.refs_1_, bf16[1792,256]{1,0:T(8,128)(2,1)} %get-tuple-element.85.refs_1_.refs_2_, bf16[1792,2048]{1,0:T(8,128)(2,1)} %bitcast.99, ...), custom_call_target="tpu_custom_call" | custom-call | flops 9395240960 | bytes 41943040 | tf_op jit(solution)/shard_map/weight_grads/pallas_call | solution.py:1224
  546.3 24.8 %mixer_backward.3 = (bf16[1792,896]{1,0:T(8,128)(2,1)}, f32[4,4,512]{2,1,0:T(4,128)}, f32[4,1,384]{2,1,0:T(1,128)}) custom-call(f32[1792,896]{1,0:T(8,128)} %fusion.proj_ref.extra_ref.refs_1_.refs_0_, f32[1792,896]{1,0:T(8,128)} %fusion.proj_ref.extra_ref.refs_1_.refs_0_, f32[1792,1]{1,0:T(8,128)} %reshape.120.segc_ref.refs_2_, ...), custom_call_target="tpu_custom_call" | custom-call | flops 25769803776 | bytes 67108864 | tf_op jit(solution)/shard_map/mixer_backward/pallas_call | solution.py:276
  571.2 10.8 %weight_grads.7 = bf16[4,784,512]{2,1,0:T(8,128)(2,1)} custom-call(bf16[1792,896]{1,0:T(8,128)(2,1)} %get-tuple-element.115.refs_0_.refs_4_, bf16[1792,2048]{1,0:T(8,128)(2,1)} %bitcast.100), custom_call_target="tpu_custom_call" | custom-call | flops 6576668672 | bytes 41943040 | tf_op jit(solution)/shard_map/weight_grads/pallas_call | solution.py:1224
  582.1 74.9 %team_finish.1 = (bf16[4,224,512]{2,1,0:T(8,128)(2,1)}, bf16[4,224,512]{2,1,0:T(8,128)(2,1)}, f32[1,2048]{1,0:T(1,128)}) custom-call(bf16[1792,384]{1,0:T(8,128)(2,1)} %get-tuple-element.94.refs_1_.refs_0_, bf16[1792,320]{1,0:T(8,128)(2,1)} %get-tuple-element.99.refs_1_, bf16[4,1152,512]{2,1,0:T(8,128)(2,1)} %bitcast.82, bf16[4,960,512]{2,1,0:T(8,128)(2,1)} %bitcast.85, ...), custom_call_target="tpu_custom_call" | custom-call | flops 34359738368 | bytes 262144000 | tf_op jit(solution)/shard_map/team_finish/pallas_call | solution.py:908
  662.6 11.5 %place_ffn.1 = (f32[512,2816]{1,0:T(8,128)}, f32[512,2816]{1,0:T(8,128)}, f32[2816,512]{1,0:T(8,128)}) custom-call(s32[4]{0:T(128)} %pad_add_fusion.order, bf16[1152,512]{1,0:T(8,128)(2,1)} %bitcast.59, bf16[1152,512]{1,0:T(8,128)(2,1)} %copy-done.5, bf16[1152,512]{1,0:T(8,128)(2,1)} %copy-done.6, bf16[1152,512]{1,0:T(8,128)(2,1)} %collective-permute-done.2.refs_3_.refs_11_, ...), custom_call_target="tpu_custom_call" | custom-call | flops 1073741824 | bytes 31457280 | tf_op jit(solution)/shard_map/place_ffn/pallas_call | solution.py:1186
  674.5 12.2 %collective-permute-done.4.refs_1_ = bf16[1280,512]{1,0:T(8,128)(2,1)S(1)} collective-permute-done((bf16[1280,512]{1,0:T(8,128)(2,1)}, bf16[1280,512]{1,0:T(8,128)(2,1)S(1)}, u32[]{:S(2)}, u32[]{:S(2)}) %collective-permute-start.4) | collective-permute-done | bytes 1310752 | tf_op jit(solution)/shard_map/ppermute | solution.py:1063
  689.8 2.7 concatenate.11
  693.1 6.2 place_rows.1
  699.3 5.9 place_late_head.1._
  705.2 51.4 %leave.1 = (bf16[4,224,512]{2,1,0:T(8,128)(2,1)}, bf16[4,224,512]{2,1,0:T(8,128)(2,1)}, bf16[4,784,512]{2,1,0:T(8,128)(2,1)}, f32[8,72,128]{2,1,0:T(8,128)}) custom-call(bf16[4,224,512]{2,1,0:T(8,128)(2,1)} %get-tuple-element.118.refs_0_, bf16[4,224,512]{2,1,0:T(8,128)(2,1)} %get-tuple-element.119.refs_1_, bf16[784,512]{1,0:T(8,128)(2,1)} %bitcast.91, ...), custom_call_target="tpu_custom_call" | custom-call | flops 1073741824 | bytes 125829120 | tf_op jit(solution)/shard_map/leave/pallas_call | solution.py:1040
  758.6 5.9 place_first_head.1
  (120 shorter events, 42.1 us)
Async XLA Ops:
  7.2 269.3 %all-gather.7.cloned.1.call-start = ((), (), s32[]{:S(2)}) async-start(), calls=%async_computation.8 | async-start | bytes 2621440 | tf_op jit(solution)/shard_map/all_gather | solution.py:1496
  9.6 344.4 %all-gather.9.cloned.1.call-start = ((), (), s32[]{:S(2)}) async-start(), calls=%async_computation.9 | async-start | bytes 5898240 | tf_op jit(solution)/shard_map/all_gather | solution.py:1496
  19.8 193.0 %copy-start.17 = (f32[8]{0:T(128)S(1)}, f32[8]{0:T(128)}, u32[]{:S(2)}) copy-start(f32[8]{0:T(128)} %param.21) | copy-start | bytes 100
  19.8 193.6 %copy-start.18 = (f32[8]{0:T(128)S(1)}, f32[8]{0:T(128)}, u32[]{:S(2)}) copy-start(f32[8]{0:T(128)} %param.22) | copy-start | bytes 100
  208.3 175.1 %all-gather.11.cloned.1.call-start = ((), (), s32[]{:S(2)}) async-start(), calls=%async_computation.10 | async-start | bytes 4915200 | tf_op jit(solution)/shard_map/all_gather | solution.py:1496
  209.1 287.7 %reduce-scatter.5.cloned.1.call-start = ((), (), s32[]{:S(2)}) async-start(), calls=%async_computation.4 | async-start | bytes 5898240 | tf_op jit(solution)/shard_map/reduce_scatter | solution.py:1536
  383.4 160.9 %reduce-scatter.7.cloned.1.call-start = ((), (), s32[]{:S(2)}) async-start(), calls=%async_computation.5 | async-start | bytes 4915200 | tf_op jit(solution)/shard_map/reduce_scatter | solution.py:1536
  412.4 244.6 %reduce-scatter.11.cloned.1.call-start = ((), (), s32[]{:S(2)}) async-start(), calls=%async_computation.7 | async-start | bytes 6553600 | tf_op jit(solution)/shard_map/reduce_scatter | solution.py:1536
  496.8 27.8 %collective-permute-start = (bf16[1152,512]{1,0:T(8,128)(2,1)}, bf16[1152,512]{1,0:T(8,128)(2,1)S(1)}, u32[]{:S(2)}, u32[]{:S(2)}) collective-permute-start(bf16[1152,512]{1,0:T(8,128)(2,1)} %bitcast.58), channel_id=1, source_target_pairs={{0,16},{16,0},{8,24},{24,8},{1,17},{17,1},{9,25},{25,9},{2,18},{18... | collective-permute-start | bytes 3538952 | tf_op jit(solution)/shard_map/ppermute | solution.py:1063
  524.6 46.5 %copy-start.5 = (bf16[1152,512]{1,0:T(8,128)(2,1)}, bf16[1152,512]{1,0:T(8,128)(2,1)S(1)}, u32[]{:S(2)}) copy-start(bf16[1152,512]{1,0:T(8,128)(2,1)S(1)} %collective-permute-done.refs_1_.refs_9_) | copy-start | bytes 3538948
  541.6 163.6 %reduce-scatter.9.cloned.1.call-start = ((), (), s32[]{:S(2)}) async-start(), calls=%async_computation.6 | async-start | bytes 4014080 | tf_op jit(solution)/shard_map/reduce_scatter | solution.py:1536
  544.3 26.8 %collective-permute-start.3 = (bf16[960,512]{1,0:T(8,128)(2,1)}, bf16[960,512]{1,0:T(8,128)(2,1)}, u32[]{:S(2)}, u32[]{:S(2)}) collective-permute-start(bf16[960,512]{1,0:T(8,128)(2,1)} %bitcast.16.refs_4_.refs_12_), channel_id=1, source_target_pairs={{0,16},{16,0},{8,24},{24,8},{1,17},{17,1},{9,25},{25,9},{2,18},{18... | collective-permute-start | bytes 2949128 | tf_op jit(solution)/shard_map/ppermute | solution.py:1063
  545.4 36.6 %collective-permute-start.1 = (bf16[1152,512]{1,0:T(8,128)(2,1)S(1)}, bf16[1152,512]{1,0:T(8,128)(2,1)S(1)}, u32[]{:S(2)}, u32[]{:S(2)}) collective-permute-start(bf16[1152,512]{1,0:T(8,128)(2,1)S(1)} %bitcast.61), channel_id=1, source_target_pairs={{0,8},{8,0},{16,24},{24,16},{1,9},{9,1},{17,25},{25,17},{2,10},{10... | collective-permute-start | bytes 3538952 | tf_op jit(solution)/shard_map/ppermute | solution.py:1067
  571.1 10.9 %collective-permute-start.2 = (bf16[1152,512]{1,0:T(8,128)(2,1)S(1)}, bf16[1152,512]{1,0:T(8,128)(2,1)}, u32[]{:S(2)}, u32[]{:S(2)}) collective-permute-start(bf16[1152,512]{1,0:T(8,128)(2,1)S(1)} %collective-permute-done.refs_1_.refs_9_), channel_id=1, source_target_pairs={{0,8},{8,0},{16,24},{24,16},{1,9},{9,1},{17,25},{25,17},{2,10},{10... | collective-permute-start | bytes 3538952 | tf_op jit(solution)/shard_map/ppermute | solution.py:1067
  582.0 74.9 %copy-start.6 = (bf16[1152,512]{1,0:T(8,128)(2,1)}, bf16[1152,512]{1,0:T(8,128)(2,1)S(1)}, u32[]{:S(2)}) copy-start(bf16[1152,512]{1,0:T(8,128)(2,1)S(1)} %collective-permute-done.1.refs_2_.refs_10_) | copy-start | bytes 3538948
  657.0 29.7 %collective-permute-start.4 = (bf16[1280,512]{1,0:T(8,128)(2,1)}, bf16[1280,512]{1,0:T(8,128)(2,1)S(1)}, u32[]{:S(2)}, u32[]{:S(2)}) collective-permute-start(bf16[1280,512]{1,0:T(8,128)(2,1)} %bitcast.54), channel_id=1, source_target_pairs={{0,16},{16,0},{8,24},{24,8},{1,17},{17,1},{9,25},{25,9},{2,18},{18... | collective-permute-start | bytes 3932168 | tf_op jit(solution)/shard_map/ppermute | solution.py:1063
  657.3 3.9 collective-permute-start.5
  658.6 3.9 collective-permute-start.6
  659.2 29.9 %copy-start.14 = (f32[4,1,384]{2,1,0:T(1,128)S(1)}, f32[4,1,384]{2,1,0:T(1,128)}, u32[]{:S(2)}) copy-start(f32[4,1,384]{2,1,0:T(1,128)} %get-tuple-element.127) | copy-start | bytes 18436
  659.2 29.9 %copy-start.9 = (f32[4,4,512]{2,1,0:T(4,128)S(1)}, f32[4,4,512]{2,1,0:T(4,128)}, u32[]{:S(2)}) copy-start(f32[4,4,512]{2,1,0:T(4,128)} %get-tuple-element.125) | copy-start | bytes 98308
  659.2 30.6 %copy-start.11 = (f32[1,2048]{1,0:T(1,128)S(1)}, f32[1,2048]{1,0:T(1,128)}, u32[]{:S(2)}) copy-start(f32[1,2048]{1,0:T(1,128)} %get-tuple-element.130) | copy-start | bytes 24580
  659.3 30.5 %copy-start.12 = (f32[1,2048]{1,0:T(1,128)S(1)}, f32[1,2048]{1,0:T(1,128)}, u32[]{:S(2)}) copy-start(f32[1,2048]{1,0:T(1,128)} %get-tuple-element.129) | copy-start | bytes 24580
  674.1 19.1 %collective-permute-start.7 = (bf16[1280,512]{1,0:T(8,128)(2,1)S(1)}, bf16[1280,512]{1,0:T(8,128)(2,1)}, u32[]{:S(2)}, u32[]{:S(2)}) collective-permute-start(bf16[1280,512]{1,0:T(8,128)(2,1)S(1)} %bitcast.57), channel_id=1, source_target_pairs={{0,8},{8,0},{16,24},{24,16},{1,9},{9,1},{17,25},{25,17},{2,10},{10... | collective-permute-start | bytes 3932168 | tf_op jit(solution)/shard_map/ppermute | solution.py:1067
  686.7 6.4 collective-permute-start.8
  (11 other events, 128.0 us)
Sparse Core Ops, SparseCore 0:
  10.2 74.3 all-gather.6
  208.5 87.2 all-gather.8
  297.4 75.0 all-gather.10
  383.5 84.9 reduce-scatter.4
  471.2 73.0 reduce-scatter.6
  547.0 94.2 reduce-scatter.10
  643.6 61.3 reduce-scatter.8

commit v4 on v3

--- a/solution.py
+++ b/solution.py
@@ -52,8 +52,12 @@
     return values
 
 
-def prepare(head, proj, extra, seg_col, seg_row, conv, log_ref, bias_ref):
+def prepare(head, proj, extra, seg_row, conv, log_ref, bias_ref):
     length = proj.shape[0]
+    seg_row = seg_row.astype(F32)
+    rows = lax.broadcasted_iota(jnp.int32, (length, length), 0)
+    cols = lax.broadcasted_iota(jnp.int32, (length, length), 1)
+    seg_col = jnp.sum(jnp.where(rows == cols, seg_row, 0.0), axis=1, keepdims=True)
     summed = conv[TAPS - 1 : TAPS] * proj[:, :INNER]
     keeps = []
     for lag in range(1, TAPS):
@@ -70,8 +74,6 @@
     rate = jnp.exp(jnp.full((1, 1), log_ref[head], F32))
     decay = -rate * softplus(drive)
     total = cumsum_rows(decay)
-    rows = lax.broadcasted_iota(jnp.int32, (length, length), 0)
-    cols = lax.broadcasted_iota(jnp.int32, (length, length), 1)
     total_row = jnp.sum(jnp.where(rows == cols, total, 0.0), axis=0, keepdims=True)
     weight = jnp.exp(jnp.where((rows >= cols) & (seg_col == seg_row), total - total_row, -1e30))
     raw_q, raw_k, value = active[:, :DK], active[:, DK : 2 * DK], active[:, 2 * DK :]
@@ -88,21 +90,27 @@
     )
 
 
-def forward_kernel(head, proj_ref, extra_ref, segc_ref, segr_ref, conv_ref, log_ref, bias_ref, gain_ref,
+def forward_kernel(head, proj_ref, extra_ref, segr_ref, conv_ref, log_ref, bias_ref, gain_ref,
                    mixed_ref, solve_ref, work):
-    length = proj_ref.shape[0]
-    size = work.shape[0]
-    p = prepare(head, proj_ref[...], extra_ref[...], segc_ref[...], segr_ref[0], conv_ref[...], log_ref, bias_ref)
-    lower = p["beta"] * p["strict"] * p["inner"]
-    if size != length:
-        work[...] = jnp.zeros_like(work)
-    work[0:length, 0:length] = lower
+    count, size = work.shape[:2]
+    length = proj_ref.shape[0] // count
+    spans = [slice(item * length, (item + 1) * length) for item in range(count)]
     tile = min(128, size)
-    blocks = size // tile
+    starts = range(0, size, tile)
     r = lax.broadcasted_iota(jnp.int32, (tile, tile), 0)
     c = lax.broadcasted_iota(jnp.int32, (tile, tile), 1)
-    parts = [work[b * tile : (b + 1) * tile, b * tile : (b + 1) * tile] for b in range(blocks)]
     eye = (r == c).astype(F32)
+    ready, parts = [], []
+    for item, span in enumerate(spans):
+        p = prepare(
+            head, proj_ref[span, :], extra_ref[span, :], segr_ref[item], conv_ref[...], log_ref, bias_ref
+        )
+        if size != length:
+            work[item] = jnp.zeros(work.shape[1:], F32)
+        work[item, 0:length, 0:length] = p["beta"] * p["strict"] * p["inner"]
+        scores = (mm(p["query"], p["key"], NT) * p["weight"]).astype(BF16)
+        ready.append((scores, (p["beta"] * p["value"]).astype(BF16)))
+        parts += [work[item, start : start + tile, start : start + tile] for start in starts]
     inv = [eye - jnp.where((r // 2 == c // 2), part, 0.0) for part in parts]
     step = 2
     while step < tile:
@@ -110,33 +118,40 @@
         lows = [mm(jnp.where(pick, part, 0.0), x) for part, x in zip(parts, inv)]
         inv = [x - mm(x, low) for x, low in zip(inv, lows)]
         step *= 2
-    for b in range(blocks):
-        work[b * tile : (b + 1) * tile, b * tile : (b + 1) * tile] = inv[b]
+    for index, values in enumerate(inv):
+        item, start = index // len(starts), starts[index % len(starts)]
+        work[item, start : start + tile, start : start + tile] = values
     step = tile
     while step < size:
-        for start in range(0, size, 2 * step):
+        places = [(item, start) for item in range(count) for start in range(0, size, 2 * step)]
+        lows = [
+            mm(work[item, start + step : start + 2 * step, start : start + step],
+               work[item, start : start + step, start : start + step])
+            for item, start in places
+        ]
+        for (item, start), low in zip(places, lows):
             mid, end = start + step, start + 2 * step
-            low = mm(work[mid:end, start:mid], work[start:mid, start:mid])
-            work[mid:end, start:mid] = -mm(work[mid:end, mid:end], low)
+            work[item, mid:end, start:mid] = -mm(work[item, mid:end, mid:end], low)
         step *= 2
-    solve = work[0:length, 0:length].astype(BF16)
-    solve_ref[0] = solve
-    fresh = mm(solve, p["beta"] * p["value"])
-    out = mm(mm(p["query"], p["key"], NT) * p["weight"], fresh)
-    scale = lax.rsqrt(jnp.sum(out * out, axis=1, keepdims=True) * (1.0 / DV) + 1e-05)
-    gate = proj_ref[:, INNER:]
-    mixed_ref[...] = (out * scale * gain_ref[...] * (gate * sigmoid(gate))).astype(BF16)
+    for item, span in enumerate(spans):
+        solve = work[item, 0:length, 0:length].astype(BF16)
+        solve_ref[item] = solve
+        scores, target = ready[item]
+        out = mm(scores, mm(solve, target))
+        scale = lax.rsqrt(jnp.sum(out * out, axis=1, keepdims=True) * (1.0 / DV) + 1e-05)
+        gate = proj_ref[span, INNER:PER_HEAD]
+        mixed_ref[span, :] = (out * scale * gain_ref[...] * (gate * sigmoid(gate))).astype(BF16)
 
 
 def backward_kernel(head, last, *refs):
     if last:
-        (proj_ref, extra_ref, segc_ref, segr_ref, conv_ref, log_ref, bias_ref, gain_ref, solve_ref, grad_ref,
+        (proj_ref, extra_ref, segr_ref, conv_ref, log_ref, bias_ref, gain_ref, solve_ref, grad_ref,
          turn_ref, other_ref, gproj_ref, gconv_ref, gsmall_ref) = refs
     else:
-        (proj_ref, extra_ref, segc_ref, segr_ref, conv_ref, log_ref, bias_ref, gain_ref, solve_ref, grad_ref,
+        (proj_ref, extra_ref, segr_ref, conv_ref, log_ref, bias_ref, gain_ref, solve_ref, grad_ref,
          turn_ref, gproj_ref, gextra_ref, gconv_ref, gsmall_ref) = refs
     conv = conv_ref[...]
-    p = prepare(head, proj_ref[...], extra_ref[...], segc_ref[...], segr_ref[0], conv, log_ref, bias_ref)
+    p = prepare(head, proj_ref[...], extra_ref[...], segr_ref[0], conv, log_ref, bias_ref)
     weight, strict, inner, beta, value = p["weight"], p["strict"], p["inner"], p["beta"], p["value"]
     query, key = p["query"], p["key"]
     solve = solve_ref[0]
@@ -203,13 +218,13 @@
     gsmall_ref[0, :, DV:] = jnp.where(lane == 0, glog, jnp.where(lane == 1, gbias, 0.0))
 
 
-def common_specs(length, heads, head, extra_block):
+def common_specs(length, head, extra_block, group):
     smem = pl.BlockSpec(memory_space=pltpu.SMEM)
+    rows = length * group
     return [
-        pl.BlockSpec((length, PER_HEAD), lambda s: (s, 0)),
-        pl.BlockSpec((length, 128), lambda s: (s, extra_block)),
-        pl.BlockSpec((length, 1), lambda s: (s, 0)),
-        pl.BlockSpec((1, 1, length), lambda s: (s, 0, 0)),
+        pl.BlockSpec((rows, PER_HEAD), lambda s: (s, 0)),
+        pl.BlockSpec((rows, 128), lambda s: (s, extra_block)),
+        pl.BlockSpec((group, 1, length), lambda s: (s, 0, 0)),
         pl.BlockSpec((TAPS, INNER), lambda s: (0, head)),
         smem,
         smem,
@@ -221,41 +236,42 @@
     return pl.CostEstimate(flops=passes * count * (3 << 30), bytes_accessed=passes * count << 23, transcendentals=0)
 
 
-def mixer_forward(head, heads, proj, extra, extra_block, seg_col, seg_row, conv, log, bias, gain):
+def mixer_forward(head, heads, proj, extra, extra_block, seg_row, conv, log, bias, gain):
     count, _, length = seg_row.shape
     tokens = count * length
     size = 64
     while size < length:
         size *= 2
+    group = 2 if count % 2 == 0 else 1
     return pl.pallas_call(
         functools.partial(forward_kernel, head),
-        grid=(count,),
-        in_specs=common_specs(length, heads, head, extra_block),
+        grid=(count // group,),
+        in_specs=common_specs(length, head, extra_block, group),
         out_specs=[
-            pl.BlockSpec((length, DV), lambda s: (s, 0)),
-            pl.BlockSpec((1, length, length), lambda s: (s, 0, 0)),
+            pl.BlockSpec((group * length, DV), lambda s: (s, 0)),
+            pl.BlockSpec((group, length, length), lambda s: (s, 0, 0)),
         ],
         out_shape=[
             jax.ShapeDtypeStruct((tokens, DV), BF16),
             jax.ShapeDtypeStruct((count, length, length), BF16),
         ],
-        scratch_shapes=[pltpu.VMEM((size, size), F32)],
+        scratch_shapes=[pltpu.VMEM((group, size, size), F32)],
         compiler_params=pltpu.CompilerParams(vmem_limit_bytes=56 << 20),
         cost_estimate=mixer_cost(count, 1),
         name="mixer_forward",
-    )(proj, extra, seg_col, seg_row, conv, log, bias, gain)
-
-
-def mixer_backward(head, heads, proj, extra, extra_block, seg_col, seg_row, conv, log, bias, gain, solve, grad, turned, other):
+    )(proj, extra, seg_row, conv, log, bias, gain)
+
+
+def mixer_backward(head, heads, proj, extra, extra_block, seg_row, conv, log, bias, gain, solve, grad, turned, other):
     count, _, length = seg_row.shape
     tokens = count * length
     last = other is not None
-    in_specs = common_specs(length, heads, head, extra_block) + [
+    in_specs = common_specs(length, head, extra_block, 1) + [
         pl.BlockSpec((1, length, length), lambda s: (s, 0, 0)),
         pl.BlockSpec((length, grad.shape[1]), lambda s: (s, 0)),
         pl.BlockSpec((turned.shape[0], DV, turned.shape[2]), lambda s: (0, head, 0)),
     ]
-    args = [proj, extra, seg_col, seg_row, conv, log, bias, gain, solve, grad, turned]
+    args = [proj, extra, seg_row, conv, log, bias, gain, solve, grad, turned]
     width = PER_HEAD
     tail_specs = [
         pl.BlockSpec((1, TAPS, INNER), lambda s: (s, 0, 0)),
@@ -290,6 +306,7 @@
 VMEM_SPEC = pl.BlockSpec(memory_space=pltpu.VMEM)
 STRIP = 16
 DECAY_ROWS = 16
+GAIN_ROW, ATTN_ROW, FFN_ROW, REST_ROW, SMALL_ROWS = 32, 34, 50, 66, 72
 
 
 def meet(targets):
@@ -321,45 +338,63 @@
         return [self.x, self.y, self.core]
 
 
-def gather_phase(team, src, out, keep, send, recv):
-    half = src.shape[0] // 2
-    first, second = pl.ds(0, half), pl.ds(half, half)
-    own, across = team.part * 2 + team.col, team.across * 2 + team.col
-    other, diag = team.part * 2 + team.other, team.across * 2 + team.other
-    local = pltpu.make_async_copy(src, out.at[own], keep)
-    local.start()
-    x_first = remote(src.at[first], out.at[own, first], send, recv, 0, team.x)
-    x_second = remote(src.at[second], out.at[own, second], send, recv, 1, team.x)
-    y_second = remote(src.at[second], out.at[own, second], send, recv, 2, team.y)
-    y_first = remote(src.at[first], out.at[own, first], send, recv, 3, team.y)
-    core_own = remote(src, out.at[own], send, recv, 4, team.core)
-    for copy in (x_first, y_second, core_own, x_second, y_first):
-        copy.start()
-    y_pass = remote(out.at[across, first], out.at[across, first], send, recv, 5, team.y)
-    x_pass = remote(out.at[other, second], out.at[other, second], send, recv, 6, team.x)
-    core_x = remote(out.at[across], out.at[across], send, recv, 7, team.core)
-    core_y = remote(out.at[other], out.at[other], send, recv, 8, team.core)
-    core_first = remote(out.at[diag, first], out.at[diag, first], send, recv, 9, team.core)
-    core_second = remote(out.at[diag, second], out.at[diag, second], send, recv, 10, team.core)
-    x_first.wait_recv()
-    y_pass.start()
-    y_second.wait_recv()
-    x_pass.start()
-    x_second.wait_recv()
-    core_x.start()
-    y_first.wait_recv()
-    core_y.start()
-    y_pass.wait_recv()
-    core_first.start()
-    x_pass.wait_recv()
-    core_second.start()
-    for copy in (core_own, core_x, core_y, core_first, core_second):
-        copy.wait_recv()
-    for copy in (
-        x_first, x_second, y_second, y_first, core_own, y_pass, x_pass, core_x, core_y, core_first, core_second,
-    ):
-        copy.wait_send()
-    local.wait()
+class Gather:
+    def __init__(self, team, src, out, keep, send, recv):
+        self.out, self.send, self.recv = out, send, recv
+        half = src.shape[0] // 2
+        first, second = pl.ds(0, half), pl.ds(half, half)
+        own, across = team.part * 2 + team.col, team.across * 2 + team.col
+        other, diag = team.part * 2 + team.other, team.across * 2 + team.other
+        self.local = pltpu.make_async_copy(src, out.at[own], keep)
+        self.x_first = self.copy(src.at[first], out.at[own, first], 0, team.x)
+        self.x_second = self.copy(src.at[second], out.at[own, second], 1, team.x)
+        self.y_second = self.copy(src.at[second], out.at[own, second], 2, team.y)
+        self.y_first = self.copy(src.at[first], out.at[own, first], 3, team.y)
+        self.core_own = self.copy(src, out.at[own], 4, team.core)
+        self.y_pass = self.copy(out.at[across, first], out.at[across, first], 5, team.y)
+        self.x_pass = self.copy(out.at[other, second], out.at[other, second], 6, team.x)
+        self.core_x = self.copy(out.at[across], out.at[across], 7, team.core)
+        self.core_y = self.copy(out.at[other], out.at[other], 8, team.core)
+        self.core_first = self.copy(out.at[diag, first], out.at[diag, first], 9, team.core)
+        self.core_second = self.copy(out.at[diag, second], out.at[diag, second], 10, team.core)
+
+    def copy(self, source, dest, index, target):
+        return remote(source, dest, self.send, self.recv, index, target)
+
+    def start_first(self):
+        self.x_first.start()
+        self.y_first.start()
+
+    def start_second(self):
+        for copy in (self.y_second, self.x_second, self.core_own, self.local):
+            copy.start()
+
+    def finish(self):
+        self.x_first.wait_recv()
+        self.y_pass.start()
+        self.y_first.wait_recv()
+        self.y_second.wait_recv()
+        self.x_pass.start()
+        self.core_y.start()
+        self.x_second.wait_recv()
+        self.core_x.start()
+        self.y_pass.wait_recv()
+        self.core_first.start()
+        self.x_pass.wait_recv()
+        self.core_second.start()
+        cores = (self.core_own, self.core_x, self.core_y, self.core_first, self.core_second)
+        for copy in cores:
+            copy.wait_recv()
+        for copy in (self.x_first, self.x_second, self.y_second, self.y_first, self.y_pass, self.x_pass) + cores:
+            copy.wait_send()
+        self.local.wait()
+
+
+def gather_phase(team, src, out, *sems):
+    gather = Gather(team, src, out, *sems)
+    gather.start_first()
+    gather.start_second()
+    gather.finish()
 
 
 GATHER_SEMS = [pltpu.SemaphoreType.DMA, pltpu.SemaphoreType.DMA((11,)), pltpu.SemaphoreType.DMA((11,))]
@@ -574,7 +609,7 @@
     spread_sems = [pltpu.SemaphoreType.DMA, pltpu.SemaphoreType.DMA((6,)), pltpu.SemaphoreType.DMA((6,))]
     results = pl.pallas_call(
         functools.partial(enter_kernel, lay.part),
-        in_specs=[HBM_SPEC, HBM_SPEC, VMEM_SPEC, VMEM_SPEC, HBM_SPEC],
+        in_specs=[VMEM_SPEC] * 5,
         out_specs=[VMEM_SPEC, HBM_SPEC, VMEM_SPEC, HBM_SPEC, VMEM_SPEC, VMEM_SPEC, HBM_SPEC],
         out_shape=[
             tok,
@@ -686,19 +721,20 @@
         self.total(2, 0, 0)
         self.y_first.start()
 
-    def conclude(self):
+    def last(self, rows, _):
+        value = self.work[3, 1, rows, :].astype(F32) + self.twin[3, rows, :].astype(F32)
+        self.finish(rows, value + self.final[0, rows, :].astype(F32) + self.final[1, rows, :].astype(F32))
+
+    def conclude(self, between=None):
         self.swap(3).wait_recv()
-
-        def last(rows, _):
-            value = self.work[3, 1, rows, :].astype(F32) + self.twin[3, rows, :].astype(F32)
-            self.finish(rows, value + self.final[0, rows, :].astype(F32) + self.final[1, rows, :].astype(F32))
-
         self.x_first.wait_recv()
         self.y_first.wait_recv()
-        strips(0, self.half, last)
+        strips(0, self.half, self.last)
+        if between:
+            between()
         self.x_second.wait_recv()
         self.y_second.wait_recv()
-        strips(self.half, self.half, last)
+        strips(self.half, self.half, self.last)
         for copy in [self.swap(item) for item in range(4)]:
             copy.wait_send()
         for copy in (self.relay_x, self.relay_y, self.x_first, self.x_second, self.y_second, self.y_first):
@@ -786,8 +822,10 @@
     scatter = Scatter(team, make_dots(lefts, [right], starts), finish, scratch[:7])
     scatter.begin()
     scatter.pass_on()
-    scatter.conclude()
-    gather_phase(team, ready, everyone, *scratch[8:])
+    gather = Gather(team, ready, everyone, *scratch[8:])
+    scatter.conclude(gather.start_first)
+    gather.start_second()
+    gather.finish()
 
 
 def mid_call(lay, lefts, right, starts, stored, gain):
@@ -830,9 +868,11 @@
     scatter = Scatter(team, make_dots(lefts, rights, [(index, 0) for index in range(count)]), finish, scratch[:7])
     scatter.begin()
     scatter.pass_on()
-    scatter.conclude()
+    gather = Gather(team, ready, everyone, *scratch[9:])
+    scatter.conclude(gather.start_first)
+    gather.start_second()
     gain_out[...] = jnp.sum(gain_sum[...], axis=0, keepdims=True)
-    gather_phase(team, ready, everyone, *scratch[9:])
+    gather.finish()
 
 
 def branch_call(lay, lefts, rights, residual, through, gain):
@@ -1039,7 +1079,7 @@
     whole_array = jax.ShapeDtypeStruct(first.shape, first.dtype)
     return pl.pallas_call(
         functools.partial(leave_kernel, lay.part),
-        in_specs=[HBM_SPEC, HBM_SPEC, HBM_SPEC, VMEM_SPEC],
+        in_specs=[VMEM_SPEC] * 4,
         out_specs=[HBM_SPEC, HBM_SPEC, HBM_SPEC, VMEM_SPEC],
         out_shape=[
             whole_array,
@@ -1125,38 +1165,86 @@
     )(order, *pieces)
 
 
-def first_head_kernel(heads, src, tail, _, out, decay):
+def close_kernel(heads, src, tail, _, sums, first, second, out, decay, conv, gain, attn, ffn, rest, first_out,
+                 second_out):
+    step = pl.program_id(0)
+    first_out[...] = first[...]
+    second_out[...] = second[...]
     out[...] = src[0].T.astype(F32)
-    small = tail[0].astype(F32).T[:, : 2 * heads]
     for part in range(4):
 
-        @pl.when(pl.program_id(0) == part)
+        @pl.when(step == part)
         def _():
-            decay[:, part * 2 * heads : (part + 1) * 2 * heads] = small
-
-
-def place_first_head(heads, stack, whole_grad):
+            decay[part * 2 * heads : (part + 1) * 2 * heads, :] = tail[0, : 2 * heads, :].astype(F32)
+
+    @pl.when(step == 1)
+    def _():
+        row, col = lax.axis_index("row"), lax.axis_index("col")
+        blocks = conv.shape[1] // 512
+        for part in range(4):
+            own = sums[2 * part + col]
+            for tap in range(TAPS):
+                for block in range(blocks):
+                    start = (part * blocks + block) * 128
+                    conv[tap : tap + 1, start : start + 128] = own[tap * blocks + block : tap * blocks + block + 1]
+            rest[part : part + 1, :] = own[REST_ROW : REST_ROW + 1]
+        total = sums[0]
+        for slot in range(1, 8):
+            total = total + sums[slot]
+        gain[...] = total[GAIN_ROW:ATTN_ROW]
+        for index in range(4):
+
+            @pl.when(row == index)
+            def _():
+                attn[...] = total[ATTN_ROW + 4 * index : ATTN_ROW + 4 * index + 4]
+                ffn[...] = total[FFN_ROW + 4 * index : FFN_ROW + 4 * index + 4]
+
+
+def close_call(heads, stack, whole_grad, sums, first, second):
     features = stack.shape[2]
+    channels = 4 * heads * INNER
+
+    def fixed(*shape):
+        return pl.BlockSpec(shape, lambda i: (0,) * len(shape))
+
+    piece = pl.BlockSpec((1,) + first.shape[1:], lambda i: (i, 0, 0))
     return pl.pallas_call(
-        functools.partial(first_head_kernel, heads),
+        functools.partial(close_kernel, heads),
         grid=(4,),
         in_specs=[
             pl.BlockSpec((1, PER_HEAD, features), lambda i: (i, 0, 0)),
             pl.BlockSpec((1, DECAY_ROWS, features), lambda i: (i, PER_HEAD // DECAY_ROWS, 0)),
             HBM_SPEC,
+            fixed(*sums.shape),
+            piece,
+            piece,
         ],
         out_specs=[
             pl.BlockSpec((features, PER_HEAD), lambda i: (0, i * heads)),
-            pl.BlockSpec((features, 8 * heads), lambda i: (0, 0)),
+            fixed(8 * heads, features),
+            fixed(TAPS, channels),
+            fixed(DV // 128, 128),
+            fixed(4, 128),
+            fixed(4, 128),
+            fixed(4, 128),
+            piece,
+            piece,
         ],
         out_shape=[
             jax.ShapeDtypeStruct((features, 4 * heads * PER_HEAD), F32),
-            jax.ShapeDtypeStruct((features, 8 * heads), F32),
+            jax.ShapeDtypeStruct((8 * heads, features), F32),
+            jax.ShapeDtypeStruct((TAPS, channels), F32),
+            jax.ShapeDtypeStruct((DV // 128, 128), F32),
+            jax.ShapeDtypeStruct((4, 128), F32),
+            jax.ShapeDtypeStruct((4, 128), F32),
+            jax.ShapeDtypeStruct((4, 128), F32),
+            jax.ShapeDtypeStruct(first.shape, first.dtype),
+            jax.ShapeDtypeStruct(second.shape, second.dtype),
         ],
         input_output_aliases={2: 0},
         compiler_params=pltpu.CompilerParams(vmem_limit_bytes=60 << 20),
-        name="place_first_head",
-    )(stack, stack, whole_grad)
+        name="close",
+    )(stack, stack, whole_grad, sums, first, second)
 
 
 def place_ffn_kernel(counts, order, *refs):
@@ -1503,7 +1591,7 @@
         splits.append(splits[-1] + PER_HEAD)
     mix_pad = jnp.concatenate([mix_mine[:, :PER_HEAD], decay_pad, mix_mine[:, PER_HEAD:]], axis=1)
     out_all = gather_rows(mine(out_weight, 0, heads * DV))
-    cuts = [0, min(units, -(-units // 256) * 128), units]
+    cuts = [0, min(units, 320), units]
     unit_blocks = own_units(lay, cuts, gate_weight, up_weight, down_weight)
     conv_mine = mine(conv_weight, 1, heads * INNER)
     log_mine, bias_mine = mine(decay_log, 0, heads), mine(decay_bias, 0, heads)
@@ -1514,8 +1602,7 @@
     )
     mix_all = mix_all.reshape(lay.rows * width, -1)
     gain_one, gain_two = gains[:, 0].reshape(1, -1), gains[:, 1].reshape(1, -1)
-    segments = segments.astype(F32)
-    seg_col, seg_row = segments.reshape(-1, 1), segments.reshape(-1, 1, SEQ)
+    seg_row = segments.reshape(-1, 1, SEQ)
     waiting = lax.optimization_barrier((*unit_blocks, attn_all))[:-1]
     stacks = [gather_rows(values) for values in waiting]
     tokens = attn_all.shape[0]
@@ -1525,7 +1612,7 @@
         projs.append(project(after(attn_all, *mixed), head_weights[head]))
         if not head:
             shared = (
-                projs[0], PER_HEAD // 128, seg_col, seg_row, conv_mine, log_mine, bias_mine, out_gain.reshape(1, -1),
+                projs[0], PER_HEAD // 128, seg_row, conv_mine, log_mine, bias_mine, out_gain.reshape(1, -1),
             )
         values, solve = mixer_forward(head, heads, projs[head], *shared)
         mixed.append(values)
@@ -1582,17 +1669,14 @@
         lay, hidden, stacks, proj_grads, mix_all, splits[:-1], residual, stored, grad_residual, gain_one
     )
 
-    own = jnp.concatenate(
-        [jnp.concatenate(conv_parts, axis=1).reshape(-1)]
-        + [jnp.stack([part_of[DV + item] for part_of in small_parts]) for item in range(2)]
-    )
-    split = TAPS * heads * INNER
+    conv_part = jnp.concatenate(conv_parts, axis=1)
+    rest_part = jnp.concatenate([part_of[DV + item : DV + item + 1] for item in range(2) for part_of in small_parts])
     gain_part = sum(part_of[:DV] for part_of in small_parts)
-    col = lax.axis_index("col")
+    row, col = lax.axis_index("row"), lax.axis_index("col")
     if lay.native:
-        flat = jnp.concatenate([own, gain_part, attn_gain_part[0], ffn_gain_part[0]])
-        size = flat.shape[0]
-        flat = jnp.pad(flat, (0, -size % 1024)).reshape(-1, 128)
+        lines = [conv_part, gain_part, attn_gain_part, ffn_gain_part, jnp.pad(rest_part, (0, 128 - rest_part.size))]
+        flat = jnp.concatenate([values.reshape(-1, 128) for values in lines])
+        flat = jnp.pad(flat, ((0, SMALL_ROWS - flat.shape[0]), (0, 0)))
         order = part_order(lay)
         for grads, passed in zip(ffn_grads[1:], crossed[1:]):
             ffn_pieces.append([grads, passed, link(lay, grads), link(lay, passed)])
@@ -1607,28 +1691,27 @@
         first = after(mix_grads[0], mix_grad)
         flat = after(flat, mix_grad, out_weight_grad)
         block_output, input_grad, first_stack, sums = leave_call(lay, block_output, input_grad, first, flat)
-        mix_grad, decay_grad = place_first_head(heads, first_stack, mix_grad)
+        mix_grad, decay_grad, conv_grad, gain_sum, attn_sum, ffn_sum, rest, block_output, input_grad = close_call(
+            heads, first_stack, mix_grad, sums, block_output, input_grad
+        )
         block_output, input_grad = (value.reshape(-1, value.shape[2]) for value in (block_output, input_grad))
-        sums = sums.reshape(8, -1)
-        gain_sum, attn_sum, ffn_sum = jnp.split(
-            jnp.sum(sums[:, own.shape[0] : size], axis=0), [DV, DV + lay.rows * width]
-        )
-        sums = sums[:, : own.shape[0]].reshape(lay.ways, lay.cols, -1)
+        decay_grad, gain_sum = decay_grad.T, gain_sum.reshape(-1)
+        attn_gain_grad, ffn_gain_grad = attn_sum.reshape(-1), ffn_sum.reshape(-1)
+        log_grad, bias_grad = rest[:, :heads].reshape(-1), rest[:, heads : 2 * heads].reshape(-1)
     else:
         block_output, input_grad = unspread(lay, block_output), unspread(lay, input_grad)
-        slots = lay.ways * lay.cols
-        pick = (jnp.arange(slots) == part * lay.cols + col).astype(F32)[:, None]
+        own = jnp.concatenate([conv_part.reshape(-1), rest_part])
+        pick = (jnp.arange(lay.ways * lay.cols) == part * lay.cols + col).astype(F32)[:, None]
         sums, gain_sum, ffn_sum, attn_sum = lax.psum(
             (pick * own[None, :], gain_part, ffn_gain_part[0], attn_gain_part[0]), lay.data + ("row", "col")
         )
-        sums = sums.reshape(lay.ways, lay.cols, -1)
-    sums = lax.dynamic_index_in_dim(sums, col, 1, keepdims=False)
-    conv_grad = jnp.moveaxis(sums[:, :split].reshape(lay.ways, TAPS, -1), 0, 1).reshape(TAPS, -1)
-    log_grad = sums[:, split : split + heads].reshape(-1)
-    bias_grad = sums[:, split + heads :].reshape(-1)
-    row = lax.axis_index("row")
-    attn_gain_grad = lax.dynamic_slice_in_dim(attn_sum, row * width, width, 0)
-    ffn_gain_grad = lax.dynamic_slice_in_dim(ffn_sum, row * width, width, 0)
+        sums = lax.dynamic_index_in_dim(sums.reshape(lay.ways, lay.cols, -1), col, 1, keepdims=False)
+        split = conv_part.size
+        conv_grad = jnp.moveaxis(sums[:, :split].reshape(lay.ways, TAPS, -1), 0, 1).reshape(TAPS, -1)
+        log_grad = sums[:, split : split + heads].reshape(-1)
+        bias_grad = sums[:, split + heads :].reshape(-1)
+        attn_gain_grad = lax.dynamic_slice_in_dim(attn_sum, row * width, width, 0)
+        ffn_gain_grad = lax.dynamic_slice_in_dim(ffn_sum, row * width, width, 0)
 
     out_start = PER_HEAD if heads > 1 else PER_HEAD + DECAY_ROWS
     if not lay.native:

time: 784 us -> 770 us (0.982)
  local copies, waits for them, and re-layouts: 23.9 us -> 13.9 us
  transfers between devices with their start and end apart: 16 -> 16, of which waited for: 5 -> 6; matrix products, arithmetic and copies ran while one was open for 5% -> 5% of each run, Pallas kernels for 80% -> 81%
where the time goes in v4:
time: 770 us; the launch traced here: 766 us
  Pallas kernels  678 us (88%)
  matrix products  23.4 us (3%)
  waiting for transfers between devices  21.9 us (3%)
  between operations  14.6 us (2%)
  local copies, waits for them, and re-layouts  13.9 us (2%)
  starting transfers between devices  9.15 us (1%)
    pallas_call x1, Pallas kernels, enter_call(): pl.pallas_call(functools.partial(enter_kernel, lay.part), in_specs=[VMEM_...  188 us
    pallas_call x1, Pallas kernels, branch_call(): pl.pallas_call(functools.partial(branch_kernel, lay.part, len(lefts)), in...  83.2 us
    pallas_call x1, Pallas kernels, mid_call(): pl.pallas_call(functools.partial(mid_kernel, lay.part, starts), in_specs=...  77.4 us
    pallas_call x1, Pallas kernels, finish_call(): pl.pallas_call(functools.partial(finish_kernel, lay.part, len(hidden), st...  74.1 us
    pallas_call x4, Pallas kernels, stack_call(): pl.pallas_call(functools.partial(stack_kernel, counts), grid=(rows_n,), i...  54.7 us
    pallas_call x1, Pallas kernels, leave_call(): pl.pallas_call(functools.partial(leave_kernel, lay.part), in_specs=[VMEM_...  52.5 us
    pallas_call x2, Pallas kernels, mixer_backward(): pl.pallas_call(functools.partial(backward_kernel, head, last), grid=(coun...  50.4 us
    pallas_call x2, Pallas kernels, ffn_call(): pl.pallas_call(ffn_kernel, grid=(tokens // block,), in_specs=[row, row, p...  31.5 us
  transfers between devices with their start and end apart: 16, of which 6 were waited for; matrix products, arithmetic and copies ran while one was open for 5% of the time, Pallas kernels for 81%

profile of v4, /device:TPU:13, one launch (start us, length us, event | category | flops | bytes accessed | tf_op | source)
XLA Modules:
  0.0 766.4 jit_solution(8299337483722988535)
XLA Ops:
  10.6 5.8 own_units.1
  19.8 188.1 %enter.1 = (bf16[224,2048]{1,0:T(8,128)(2,1)}, bf16[8,224,2048]{2,1,0:T(8,128)(2,1)}, bf16[224,2048]{1,0:T(8,128)(2,1)}, bf16[8,224,2048]{2,1,0:T(8,128)(2,1)}, ...) custom-call(bf16[4,224,512]{2,1,0:T(8,128)(2,1)} %bitcast.66, ...), custom_call_target="tpu_custom_call" | custom-call | flops 1073741824 | bytes 419430400 | tf_op jit(solution)/shard_map/enter/pallas_call | solution.py:610
  212.8 12.8 %fusion.proj_ref.extra_ref.refs_1_.refs_0_ = f32[1792,896]{1,0:T(8,128)} fusion(bf16[1792,2048]{1,0:T(8,128)(2,1)} %bitcast.80, bf16[2048,1664]{1,0:T(8,128)(2,1)} %bitcast.96), kind=kOutput, calls=%fused_computation.2 | convolution fusion | flops 6576668672 | bytes 17432576 | tf_op jit(solution)/shard_map/dot_general | solution.py:1404
  225.7 14.9 %mixer_forward.2 = (bf16[1792,256]{1,0:T(8,128)(2,1)}, bf16[4,448,448]{2,1,0:T(8,128)(2,1)}) custom-call(f32[1792,896]{1,0:T(8,128)} %fusion.proj_ref.extra_ref.refs_1_.refs_0_, f32[1792,896]{1,0:T(8,128)} %fusion.proj_ref.extra_ref.refs_1_.refs_0_, s32[4,1,448]{2,1,0:T(1,128)} %get-tuple-element.89.segr_ref.refs_2_, ...), custom_call_target="tpu_custom_call" | custom-call | flops 12884901888 | bytes 33554432 | tf_op jit(solution)/shard_map/mixer_forward/pallas_call | solution.py:246
  240.5 10.6 %fusion.4.proj_ref.refs_0_ = f32[1792,768]{1,0:T(8,128)} fusion(bf16[1792,2048]{1,0:T(8,128)(2,1)} %bitcast.81, bf16[2048,1664]{1,0:T(8,128)(2,1)} %bitcast.97), kind=kOutput, calls=%fused_computation.6 | convolution fusion | flops 5637144576 | bytes 15990784 | tf_op jit(solution)/shard_map/dot_general | solution.py:1404
  251.1 15.1 %mixer_forward.3 = (bf16[1792,256]{1,0:T(8,128)(2,1)}, bf16[4,448,448]{2,1,0:T(8,128)(2,1)}) custom-call(f32[1792,768]{1,0:T(8,128)} %fusion.4.proj_ref.refs_0_, f32[1792,896]{1,0:T(8,128)} %fusion.proj_ref.extra_ref.refs_1_.refs_0_, s32[4,1,448]{2,1,0:T(1,128)} %get-tuple-element.89.segr_ref.refs_2_, ...), custom_call_target="tpu_custom_call" | custom-call | flops 12884901888 | bytes 33554432 | tf_op jit(solution)/shard_map/mixer_forward/pallas_call | solution.py:246
  266.2 77.4 %team_mid.1 = (f32[224,2048]{1,0:T(8,128)}, bf16[8,224,2048]{2,1,0:T(8,128)(2,1)}) custom-call(bf16[1792,256]{1,0:T(8,128)(2,1)} %get-tuple-element.90.refs_0_.refs_1_, bf16[1792,256]{1,0:T(8,128)(2,1)} %get-tuple-element.92.refs_1_.refs_2_, bf16[4,512,512]{2,1,0:T(8,128)(2,1)} %bitcast.63, bf16[224,2048]{1,0:T(8,128)(2,1)} %get-tuple-element.93.refs_3_.refs_8_, ...), custom_call_target="tpu_custom_call" | custom-call | flops 34359738368 | bytes 209715200 | tf_op jit(solution)/shard_map/team_mid/pallas_call | solution.py:833
  343.7 15.5 %ffn.2 = (bf16[1792,320]{1,0:T(8,128)(2,1)}, bf16[1792,640]{1,0:T(8,128)(2,1)}) custom-call(bf16[1792,2048]{1,0:T(8,128)(2,1)} %bitcast.92, bf16[1792,2048]{1,0:T(8,128)(2,1)} %bitcast.84, bf16[4,960,512]{2,1,0:T(8,128)(2,1)} %bitcast.60), custom_call_target="tpu_custom_call" | custom-call | flops 7046430720 | bytes 31457280 | tf_op jit(solution)/shard_map/ffn/pallas_call | solution.py:1380
  359.2 13.1 %weight_grads.4 = bf16[4,960,512]{2,1,0:T(8,128)(2,1)} custom-call(bf16[1792,640]{1,0:T(8,128)(2,1)} %get-tuple-element.107.refs_0_, bf16[1792,320]{1,0:T(8,128)(2,1)} %get-tuple-element.101.refs_1_.refs_0_, bf16[1792,2048]{1,0:T(8,128)(2,1)} %bitcast.93, bf16[1792,2048]{1,0:T(8,128)(2,1)} %bitcast.85), custom_call_target="tpu_custom_call" | custom-call | flops 7046430720 | bytes 41943040 | tf_op jit(solution)/shard_map/weight_grads/pallas_call | solution.py:1312
  372.6 16.0 %ffn.3 = (bf16[1792,384]{1,0:T(8,128)(2,1)}, bf16[1792,768]{1,0:T(8,128)(2,1)}) custom-call(bf16[1792,2048]{1,0:T(8,128)(2,1)} %bitcast.94, bf16[1792,2048]{1,0:T(8,128)(2,1)} %bitcast.86, bf16[4,1152,512]{2,1,0:T(8,128)(2,1)} %bitcast.57), custom_call_target="tpu_custom_call" | custom-call | flops 8455716864 | bytes 31457280 | tf_op jit(solution)/shard_map/ffn/pallas_call | solution.py:1380
  388.6 14.0 %weight_grads.5 = bf16[4,1152,512]{2,1,0:T(8,128)(2,1)} custom-call(bf16[1792,768]{1,0:T(8,128)(2,1)} %get-tuple-element.108.refs_0_.refs_1_, bf16[1792,384]{1,0:T(8,128)(2,1)} %get-tuple-element.106.refs_1_, bf16[1792,2048]{1,0:T(8,128)(2,1)} %bitcast.95, bf16[1792,2048]{1,0:T(8,128)(2,1)} %bitcast.87), custom_call_target="tpu_custom_call" | custom-call | flops 8455716864 | bytes 41943040 | tf_op jit(solution)/shard_map/weight_grads/pallas_call | solution.py:1312
  402.7 83.2 %team_branch.1 = (f32[224,2048]{1,0:T(8,128)}, bf16[8,224,2048]{2,1,0:T(8,128)(2,1)}, f32[1,2048]{1,0:T(1,128)}) custom-call(bf16[1792,640]{1,0:T(8,128)(2,1)} %get-tuple-element.107.refs_0_, bf16[1792,768]{1,0:T(8,128)(2,1)} %get-tuple-element.108.refs_0_.refs_1_, bf16[4,960,512]{2,1,0:T(8,128)(2,1)} %bitcast.61, bf16[4,1152,512]{2,1,0:T(8,128)(2,1)} %bitcast.58, ...), custom_call_target="tpu_custom_call" | custom-call | flops 34359738368 | bytes 262144000 | tf_op jit(solution)/shard_map/team_branch/pallas_call | solution.py:881
  486.3 25.1 %mixer_backward.2 = (bf16[1792,768]{1,0:T(8,128)(2,1)}, bf16[1792,128]{1,0:T(8,128)(2,1)}, f32[4,4,512]{2,1,0:T(4,128)}, f32[4,1,384]{2,1,0:T(1,128)}) custom-call(f32[1792,768]{1,0:T(8,128)} %fusion.4.proj_ref.refs_0_, f32[1792,896]{1,0:T(8,128)} %fusion.proj_ref.extra_ref.refs_1_.refs_0_, s32[4,1,448]{2,1,0:T(1,128)} %get-tuple-element.89.segr_ref.refs_2_, ...), custom_call_target="tpu_custom_call" | custom-call | flops 25769803776 | bytes 67108864 | tf_op jit(solution)/shard_map/mixer_backward/pallas_call | solution.py:292
  511.5 16.8 %weight_grads.6 = bf16[4,1280,512]{2,1,0:T(8,128)(2,1)} custom-call(bf16[1792,768]{1,0:T(8,128)(2,1)} %get-tuple-element.123.refs_0_.refs_5_, bf16[1792,256]{1,0:T(8,128)(2,1)} %get-tuple-element.90.refs_0_.refs_1_, bf16[1792,256]{1,0:T(8,128)(2,1)} %get-tuple-element.92.refs_1_.refs_2_, bf16[1792,2048]{1,0:T(8,128)(2,1)} %bitcast.82, ...), custom_call_target="tpu_custom_call" | custom-call | flops 9395240960 | bytes 41943040 | tf_op jit(solution)/shard_map/weight_grads/pallas_call | solution.py:1312
  530.1 7.4 reduce-scatter.7.cloned.1.call-done
  538.6 25.3 %mixer_backward.3 = (bf16[1792,896]{1,0:T(8,128)(2,1)}, f32[4,4,512]{2,1,0:T(4,128)}, f32[4,1,384]{2,1,0:T(1,128)}) custom-call(f32[1792,896]{1,0:T(8,128)} %fusion.proj_ref.extra_ref.refs_1_.refs_0_, f32[1792,896]{1,0:T(8,128)} %fusion.proj_ref.extra_ref.refs_1_.refs_0_, s32[4,1,448]{2,1,0:T(1,128)} %get-tuple-element.89.segr_ref.refs_2_, ...), custom_call_target="tpu_custom_call" | custom-call | flops 25769803776 | bytes 67108864 | tf_op jit(solution)/shard_map/mixer_backward/pallas_call | solution.py:292
  564.6 10.8 %weight_grads.7 = bf16[4,784,512]{2,1,0:T(8,128)(2,1)} custom-call(bf16[1792,896]{1,0:T(8,128)(2,1)} %get-tuple-element.122.refs_0_.refs_4_, bf16[1792,2048]{1,0:T(8,128)(2,1)} %bitcast.83), custom_call_target="tpu_custom_call" | custom-call | flops 6576668672 | bytes 41943040 | tf_op jit(solution)/shard_map/weight_grads/pallas_call | solution.py:1312
  575.5 74.1 %team_finish.1 = (bf16[4,224,512]{2,1,0:T(8,128)(2,1)}, bf16[4,224,512]{2,1,0:T(8,128)(2,1)}, f32[1,2048]{1,0:T(1,128)}) custom-call(bf16[1792,320]{1,0:T(8,128)(2,1)} %get-tuple-element.101.refs_1_.refs_0_, bf16[1792,384]{1,0:T(8,128)(2,1)} %get-tuple-element.106.refs_1_, bf16[4,960,512]{2,1,0:T(8,128)(2,1)} %bitcast.62, bf16[4,1152,512]{2,1,0:T(8,128)(2,1)} %bitcast.59, ...), custom_call_target="tpu_custom_call" | custom-call | flops 34359738368 | bytes 262144000 | tf_op jit(solution)/shard_map/team_finish/pallas_call | solution.py:948
  657.6 11.5 %place_ffn.1 = (f32[512,2816]{1,0:T(8,128)}, f32[512,2816]{1,0:T(8,128)}, f32[2816,512]{1,0:T(8,128)}) custom-call(s32[4]{0:T(128)} %pad_add_fusion.order, bf16[960,512]{1,0:T(8,128)(2,1)} %bitcast.46, bf16[960,512]{1,0:T(8,128)(2,1)} %copy-done.5, bf16[960,512]{1,0:T(8,128)(2,1)} %copy-done.6, bf16[960,512]{1,0:T(8,128)(2,1)} %collective-permute-done.2.refs_3_.refs_11_, ...), custom_call_target="tpu_custom_call" | custom-call | flops 1073741824 | bytes 31457280 | tf_op jit(solution)/shard_map/place_ffn/pallas_call | solution.py:1274
  669.5 8.8 %collective-permute-done.4.refs_1_ = bf16[1280,512]{1,0:T(8,128)(2,1)S(1)} collective-permute-done((bf16[1280,512]{1,0:T(8,128)(2,1)}, bf16[1280,512]{1,0:T(8,128)(2,1)S(1)}, u32[]{:S(2)}, u32[]{:S(2)}) %collective-permute-start.4) | collective-permute-done | bytes 1310752 | tf_op jit(solution)/shard_map/ppermute | solution.py:1103
  686.0 6.2 place_rows.1
  692.2 5.9 place_late_head.1._
  698.2 52.5 %leave.1 = (bf16[4,224,512]{2,1,0:T(8,128)(2,1)}, bf16[4,224,512]{2,1,0:T(8,128)(2,1)}, bf16[4,784,512]{2,1,0:T(8,128)(2,1)}, f32[8,72,128]{2,1,0:T(8,128)}) custom-call(bf16[4,224,512]{2,1,0:T(8,128)(2,1)} %get-tuple-element.125.refs_0_, bf16[4,224,512]{2,1,0:T(8,128)(2,1)} %get-tuple-element.126.refs_1_, bf16[784,512]{1,0:T(8,128)(2,1)} %bitcast.70, ...), custom_call_target="tpu_custom_call" | custom-call | flops 1073741824 | bytes 125829120 | tf_op jit(solution)/shard_map/leave/pallas_call | solution.py:1080
  750.7 6.7 close.1
  (99 shorter events, 34.1 us)
Async XLA Ops:
  7.2 259.0 %all-gather.7.cloned.1.call-start = ((), (), s32[]{:S(2)}) async-start(), calls=%async_computation.8 | async-start | bytes 2621440 | tf_op jit(solution)/shard_map/all_gather | solution.py:1584
  9.6 334.0 %all-gather.9.cloned.1.call-start = ((), (), s32[]{:S(2)}) async-start(), calls=%async_computation.9 | async-start | bytes 4915200 | tf_op jit(solution)/shard_map/all_gather | solution.py:1584
  19.2 189.7 %copy-start.15 = (f32[8]{0:T(128)S(1)}, f32[8]{0:T(128)}, u32[]{:S(2)}) copy-start(f32[8]{0:T(128)} %param.21) | copy-start | bytes 100
  19.2 190.3 %copy-start.16 = (f32[8]{0:T(128)S(1)}, f32[8]{0:T(128)}, u32[]{:S(2)}) copy-start(f32[8]{0:T(128)} %param.22) | copy-start | bytes 100
  208.0 164.6 %all-gather.11.cloned.1.call-start = ((), (), s32[]{:S(2)}) async-start(), calls=%async_computation.10 | async-start | bytes 5898240 | tf_op jit(solution)/shard_map/all_gather | solution.py:1584
  208.7 277.3 %reduce-scatter.5.cloned.1.call-start = ((), (), s32[]{:S(2)}) async-start(), calls=%async_computation.4 | async-start | bytes 4915200 | tf_op jit(solution)/shard_map/reduce_scatter | solution.py:1623
  372.3 165.1 %reduce-scatter.7.cloned.1.call-start = ((), (), s32[]{:S(2)}) async-start(), calls=%async_computation.5 | async-start | bytes 5898240 | tf_op jit(solution)/shard_map/reduce_scatter | solution.py:1623
  402.7 247.0 %reduce-scatter.11.cloned.1.call-start = ((), (), s32[]{:S(2)}) async-start(), calls=%async_computation.7 | async-start | bytes 6553600 | tf_op jit(solution)/shard_map/reduce_scatter | solution.py:1623
  486.0 25.5 %collective-permute-start = (bf16[960,512]{1,0:T(8,128)(2,1)}, bf16[960,512]{1,0:T(8,128)(2,1)S(1)}, u32[]{:S(2)}, u32[]{:S(2)}) collective-permute-start(bf16[960,512]{1,0:T(8,128)(2,1)} %bitcast.45), channel_id=1, source_target_pairs={{0,16},{16,0},{8,24},{24,8},{1,17},{17,1},{9,25},{25,9},{2,18},{18... | collective-permute-start | bytes 2949128 | tf_op jit(solution)/shard_map/ppermute | solution.py:1103
  528.4 169.8 %reduce-scatter.9.cloned.1.call-start = ((), (), s32[]{:S(2)}) async-start(), calls=%async_computation.6 | async-start | bytes 4014080 | tf_op jit(solution)/shard_map/reduce_scatter | solution.py:1623
  529.5 45.9 %collective-permute-start.1 = (bf16[960,512]{1,0:T(8,128)(2,1)S(1)}, bf16[960,512]{1,0:T(8,128)(2,1)S(1)}, u32[]{:S(2)}, u32[]{:S(2)}) collective-permute-start(bf16[960,512]{1,0:T(8,128)(2,1)S(1)} %bitcast.48), channel_id=1, source_target_pairs={{0,8},{8,0},{16,24},{24,16},{1,9},{9,1},{17,25},{25,17},{2,10},{10... | collective-permute-start | bytes 2949128 | tf_op jit(solution)/shard_map/ppermute | solution.py:1107
  530.0 45.5 %collective-permute-start.2 = (bf16[960,512]{1,0:T(8,128)(2,1)S(1)}, bf16[960,512]{1,0:T(8,128)(2,1)}, u32[]{:S(2)}, u32[]{:S(2)}) collective-permute-start(bf16[960,512]{1,0:T(8,128)(2,1)S(1)} %collective-permute-done.refs_1_.refs_9_), channel_id=1, source_target_pairs={{0,8},{8,0},{16,24},{24,16},{1,9},{9,1},{17,25},{25,17},{2,10},{10... | collective-permute-start | bytes 2949128 | tf_op jit(solution)/shard_map/ppermute | solution.py:1107
  537.4 27.2 %collective-permute-start.3 = (bf16[1152,512]{1,0:T(8,128)(2,1)}, bf16[1152,512]{1,0:T(8,128)(2,1)}, u32[]{:S(2)}, u32[]{:S(2)}) collective-permute-start(bf16[1152,512]{1,0:T(8,128)(2,1)} %bitcast.16.refs_4_.refs_12_), channel_id=1, source_target_pairs={{0,16},{16,0},{8,24},{24,8},{1,17},{17,1},{9,25},{25,9},{2,18},{18... | collective-permute-start | bytes 3538952 | tf_op jit(solution)/shard_map/ppermute | solution.py:1103
  575.4 74.1 %copy-start.6 = (bf16[960,512]{1,0:T(8,128)(2,1)}, bf16[960,512]{1,0:T(8,128)(2,1)S(1)}, u32[]{:S(2)}) copy-start(bf16[960,512]{1,0:T(8,128)(2,1)S(1)} %collective-permute-done.1.refs_2_.refs_10_) | copy-start | bytes 2949124
  649.6 28.7 %collective-permute-start.4 = (bf16[1280,512]{1,0:T(8,128)(2,1)}, bf16[1280,512]{1,0:T(8,128)(2,1)S(1)}, u32[]{:S(2)}, u32[]{:S(2)}) collective-permute-start(bf16[1280,512]{1,0:T(8,128)(2,1)} %bitcast.41), channel_id=1, source_target_pairs={{0,16},{16,0},{8,24},{24,8},{1,17},{17,1},{9,25},{25,9},{2,18},{18... | collective-permute-start | bytes 3932168 | tf_op jit(solution)/shard_map/ppermute | solution.py:1103
  650.9 5.0 collective-permute-start.5
  653.1 4.5 collective-permute-start.6
  653.7 27.4 %copy-start.7 = (f32[4,4,512]{2,1,0:T(4,128)S(1)}, f32[4,4,512]{2,1,0:T(4,128)}, u32[]{:S(2)}) copy-start(f32[4,4,512]{2,1,0:T(4,128)} %get-tuple-element.133) | copy-start | bytes 98308
  653.7 28.0 %copy-start.12 = (f32[4,1,384]{2,1,0:T(1,128)S(1)}, f32[4,1,384]{2,1,0:T(1,128)}, u32[]{:S(2)}) copy-start(f32[4,1,384]{2,1,0:T(1,128)} %get-tuple-element.134) | copy-start | bytes 18436
  653.7 28.1 %copy-start.8 = (f32[4,4,512]{2,1,0:T(4,128)S(1)}, f32[4,4,512]{2,1,0:T(4,128)}, u32[]{:S(2)}) copy-start(f32[4,4,512]{2,1,0:T(4,128)} %get-tuple-element.132) | copy-start | bytes 98308
  653.7 31.4 %copy-start.9 = (f32[1,2048]{1,0:T(1,128)S(1)}, f32[1,2048]{1,0:T(1,128)}, u32[]{:S(2)}) copy-start(f32[1,2048]{1,0:T(1,128)} %get-tuple-element.137) | copy-start | bytes 24580
  653.7 31.4 %copy-start.10 = (f32[1,2048]{1,0:T(1,128)S(1)}, f32[1,2048]{1,0:T(1,128)}, u32[]{:S(2)}) copy-start(f32[1,2048]{1,0:T(1,128)} %get-tuple-element.136) | copy-start | bytes 24580
  669.1 16.9 %collective-permute-start.7 = (bf16[1280,512]{1,0:T(8,128)(2,1)S(1)}, bf16[1280,512]{1,0:T(8,128)(2,1)}, u32[]{:S(2)}, u32[]{:S(2)}) collective-permute-start(bf16[1280,512]{1,0:T(8,128)(2,1)S(1)} %bitcast.44), channel_id=1, source_target_pairs={{0,8},{8,0},{16,24},{24,16},{1,9},{9,1},{17,25},{25,17},{2,10},{10... | collective-permute-start | bytes 3932168 | tf_op jit(solution)/shard_map/ppermute | solution.py:1107
  678.3 7.7 %collective-permute-start.8 = (bf16[1280,512]{1,0:T(8,128)(2,1)S(1)}, bf16[1280,512]{1,0:T(8,128)(2,1)}, u32[]{:S(2)}, u32[]{:S(2)}) collective-permute-start(bf16[1280,512]{1,0:T(8,128)(2,1)S(1)} %collective-permute-done.4.refs_1_), channel_id=1, source_target_pairs={{0,8},{8,0},{16,24},{24,16},{1,9},{9,1},{17,25},{25,17},{2,10},{10... | collective-permute-start | bytes 3932168 | tf_op jit(solution)/shard_map/ppermute | solution.py:1107
  (9 other events, 86.1 us)
Sparse Core Ops, SparseCore 0:
  9.8 72.7 all-gather.6
  208.1 74.4 all-gather.8
  284.7 87.8 all-gather.10
  375.3 73.5 reduce-scatter.4
  451.6 85.7 reduce-scatter.6
  540.1 94.2 reduce-scatter.10
  636.8 61.3 reduce-scatter.8

commit v5 on v4

--- a/solution.py
+++ b/solution.py
@@ -9,6 +9,7 @@
 
 F32, BF16 = jnp.float32, jnp.bfloat16
 DK, DV, TAPS = 128, 256, 4
+DECAY_ROWS = 16
 INNER = 2 * DK + DV
 PER_HEAD = INNER + DV
 NN = (((1,), (0,)), ((), ()))
@@ -25,7 +26,7 @@
 
 
 def softplus(values):
-    return jnp.maximum(values, 0.0) + jnp.log(1.0 + jnp.exp(-jnp.abs(values)))
+    return jnp.maximum(values, 0.0) + jnp.log1p(jnp.exp(-jnp.abs(values)))
 
 
 def shift_down(values, lag):
@@ -90,10 +91,15 @@
     )
 
 
-def forward_kernel(head, proj_ref, extra_ref, segr_ref, conv_ref, log_ref, bias_ref, gain_ref,
-                   mixed_ref, solve_ref, work):
+def forward_kernel(head, start, *refs):
+    if head:
+        (attn_ref, stack_ref, extra_ref, segr_ref, conv_ref, log_ref, bias_ref, gain_ref, mixed_ref, solve_ref,
+         proj_ref, work) = refs
+    else:
+        (attn_ref, stack_ref, segr_ref, conv_ref, log_ref, bias_ref, gain_ref, mixed_ref, solve_ref, proj_ref,
+         extra_ref, work) = refs
     count, size = work.shape[:2]
-    length = proj_ref.shape[0] // count
+    length, width = proj_ref.shape[0] // count, stack_ref.shape[2]
     spans = [slice(item * length, (item + 1) * length) for item in range(count)]
     tile = min(128, size)
     starts = range(0, size, tile)
@@ -101,6 +107,18 @@
     c = lax.broadcasted_iota(jnp.int32, (tile, tile), 1)
     eye = (r == c).astype(F32)
     ready, parts = [], []
+
+    def product(span, first, rows):
+        value = 0.0
+        for index in range(stack_ref.shape[0]):
+            left = attn_ref[span, index * width : (index + 1) * width]
+            value = value + mm(left, stack_ref[index, first : first + rows, :], NT)
+        return value
+
+    for span in spans:
+        proj_ref[span, :] = product(span, start, PER_HEAD)
+        if not head:
+            extra_ref[span, :] = product(span, start + PER_HEAD, DECAY_ROWS)
     for item, span in enumerate(spans):
         p = prepare(
             head, proj_ref[span, :], extra_ref[span, :], segr_ref[item], conv_ref[...], log_ref, bias_ref
@@ -139,7 +157,7 @@
         scores, target = ready[item]
         out = mm(scores, mm(solve, target))
         scale = lax.rsqrt(jnp.sum(out * out, axis=1, keepdims=True) * (1.0 / DV) + 1e-05)
-        gate = proj_ref[span, INNER:PER_HEAD]
+        gate = proj_ref[span, INNER:]
         mixed_ref[span, :] = (out * scale * gain_ref[...] * (gate * sigmoid(gate))).astype(BF16)
 
 
@@ -203,7 +221,7 @@
         gconv_ref[0, TAPS - 1 - lag : TAPS - lag, :] = jnp.sum(kept * shift_down(source, lag), axis=0, keepdims=True)
     gdrive = -p["rate"] * gdecay * sigmoid(p["drive"])
     gwrite = gbeta * beta * (1.0 - beta)
-    lane = lax.broadcasted_iota(jnp.int32, extra_ref.shape, 1)
+    lane = lax.broadcasted_iota(jnp.int32, (extra_ref.shape[0], 128), 1)
     gextra = jnp.where(lane == 2 * head, gwrite, jnp.where(lane == 2 * head + 1, gdrive, 0.0))
     gproj_ref[:, :INNER] = gsource.astype(BF16)
     gproj_ref[:, INNER:PER_HEAD] = ggate.astype(BF16)
@@ -218,12 +236,9 @@
     gsmall_ref[0, :, DV:] = jnp.where(lane == 0, glog, jnp.where(lane == 1, gbias, 0.0))
 
 
-def common_specs(length, head, extra_block, group):
+def small_specs(length, head, group):
     smem = pl.BlockSpec(memory_space=pltpu.SMEM)
-    rows = length * group
     return [
-        pl.BlockSpec((rows, PER_HEAD), lambda s: (s, 0)),
-        pl.BlockSpec((rows, 128), lambda s: (s, extra_block)),
         pl.BlockSpec((group, 1, length), lambda s: (s, 0, 0)),
         pl.BlockSpec((TAPS, INNER), lambda s: (0, head)),
         smem,
@@ -236,37 +251,51 @@
     return pl.CostEstimate(flops=passes * count * (3 << 30), bytes_accessed=passes * count << 23, transcendentals=0)
 
 
-def mixer_forward(head, heads, proj, extra, extra_block, seg_row, conv, log, bias, gain):
+def mixer_forward(head, start, attn, stack, extra, seg_row, conv, log, bias, gain):
     count, _, length = seg_row.shape
     tokens = count * length
     size = 64
     while size < length:
         size *= 2
     group = 2 if count % 2 == 0 else 1
+    extra_spec = pl.BlockSpec((group * length, DECAY_ROWS), lambda s: (s, 0))
+    extra_shape = jax.ShapeDtypeStruct((tokens, DECAY_ROWS), F32)
     return pl.pallas_call(
-        functools.partial(forward_kernel, head),
+        functools.partial(forward_kernel, head, start),
         grid=(count // group,),
-        in_specs=common_specs(length, head, extra_block, group),
+        in_specs=[
+            pl.BlockSpec((group * length, attn.shape[1]), lambda s: (s, 0)),
+            pl.BlockSpec(stack.shape, lambda s: (0, 0, 0), pipeline_mode=pl.Buffered(1)),
+        ]
+        + ([extra_spec] if head else [])
+        + small_specs(length, head, group),
         out_specs=[
             pl.BlockSpec((group * length, DV), lambda s: (s, 0)),
             pl.BlockSpec((group, length, length), lambda s: (s, 0, 0)),
-        ],
+            pl.BlockSpec((group * length, PER_HEAD), lambda s: (s, 0)),
+        ]
+        + ([] if head else [extra_spec]),
         out_shape=[
             jax.ShapeDtypeStruct((tokens, DV), BF16),
             jax.ShapeDtypeStruct((count, length, length), BF16),
-        ],
+            jax.ShapeDtypeStruct((tokens, PER_HEAD), F32),
+        ]
+        + ([] if head else [extra_shape]),
         scratch_shapes=[pltpu.VMEM((group, size, size), F32)],
-        compiler_params=pltpu.CompilerParams(vmem_limit_bytes=56 << 20),
+        compiler_params=pltpu.CompilerParams(vmem_limit_bytes=60 << 20),
         cost_estimate=mixer_cost(count, 1),
         name="mixer_forward",
-    )(proj, extra, seg_row, conv, log, bias, gain)
-
-
-def mixer_backward(head, heads, proj, extra, extra_block, seg_row, conv, log, bias, gain, solve, grad, turned, other):
+    )(attn, stack, *([extra] if head else []), seg_row, conv, log, bias, gain)
+
+
+def mixer_backward(head, proj, extra, seg_row, conv, log, bias, gain, solve, grad, turned, other):
     count, _, length = seg_row.shape
     tokens = count * length
     last = other is not None
-    in_specs = common_specs(length, head, extra_block, 1) + [
+    in_specs = [
+        pl.BlockSpec((length, PER_HEAD), lambda s: (s, 0)),
+        pl.BlockSpec((length, DECAY_ROWS), lambda s: (s, 0)),
+        *small_specs(length, head, 1),
         pl.BlockSpec((1, length, length), lambda s: (s, 0, 0)),
         pl.BlockSpec((length, grad.shape[1]), lambda s: (s, 0)),
         pl.BlockSpec((turned.shape[0], DV, turned.shape[2]), lambda s: (0, head, 0)),
@@ -305,7 +334,6 @@
 HBM_SPEC = pl.BlockSpec(memory_space=pltpu.HBM)
 VMEM_SPEC = pl.BlockSpec(memory_space=pltpu.VMEM)
 STRIP = 16
-DECAY_ROWS = 16
 GAIN_ROW, ATTN_ROW, FFN_ROW, REST_ROW, SMALL_ROWS = 32, 34, 50, 66, 72
 
 
@@ -689,7 +717,7 @@
                 slot = lax.rem(base + 2 * (1 - item // 2), 4) * 2 + lax.rem(team.col + 1 + item, 2)
                 columns = pl.ds(pl.multiple_of(chunk * self.chunk, self.chunk), self.chunk)
                 rows = pl.ds(pl.multiple_of(slot * self.rows, STRIP), self.rows)
-                self.work[item, which, :, columns] = self.dots(rows, chunk, columns).astype(BF16)
+                self.work[item, which, :, columns] = self.dots(rows, chunk).astype(BF16)
 
             self.swap(item).start()
 
@@ -753,15 +781,16 @@
     ]
 
 
+def whole_rights(rights):
+    return [(index, 0, right.shape[1]) for index, right in enumerate(rights)]
+
+
 def make_dots(lefts, rights, starts):
-    def dots(rows, chunk, columns):
+    def dots(rows, chunk):
         value = 0.0
-        for left, (index, start) in zip(lefts, starts):
-            right, depth = rights[index], slice(start, start + left.shape[1])
-            if len(right.shape) == 3:
-                value = value + lax.dot_general(left[rows, :], right[chunk, depth, :], NN, preferred_element_type=F32)
-            else:
-                value = value + lax.dot_general(left[rows, :], right[columns, depth], NT, preferred_element_type=F32)
+        for left, (index, start, size) in zip(lefts, starts):
+            part = rights[index][chunk, start : start + size, :]
+            value = value + lax.dot_general(left[rows, :size], part, NN, preferred_element_type=F32)
         return value
 
     return dots
@@ -819,7 +848,7 @@
         scale = lax.rsqrt(jnp.sum(value * value, axis=1, keepdims=True) * (1.0 / value.shape[1]) + 1e-05)
         ready[rows, :] = (value * scale * gain[...]).astype(BF16)
 
-    scatter = Scatter(team, make_dots(lefts, [right], starts), finish, scratch[:7])
+    scatter = Scatter(team, make_dots(lefts, [right], [(0, *place) for place in starts]), finish, scratch[:7])
     scatter.begin()
     scatter.pass_on()
     gather = Gather(team, ready, everyone, *scratch[8:])
@@ -865,7 +894,7 @@
         out[rows, :] = value
         ready[rows, :] = value.astype(BF16)
 
-    scatter = Scatter(team, make_dots(lefts, rights, [(index, 0) for index in range(count)]), finish, scratch[:7])
+    scatter = Scatter(team, make_dots(lefts, rights, whole_rights(rights)), finish, scratch[:7])
     scatter.begin()
     scatter.pass_on()
     gather = Gather(team, ready, everyone, *scratch[9:])
@@ -927,9 +956,9 @@
         deal_out(input_out, rows, through[rows, :] + value)
 
     block = Scatter(
-        team, make_dots(hidden, downs, [(index, 0) for index in range(count)]), finish_block, scratch[:7]
+        team, make_dots(hidden, downs, whole_rights(downs)), finish_block, scratch[:7]
     )
-    inputs = Scatter(team, make_dots(grads, [mix], [(0, start) for start in starts]), finish_input, scratch[7:14])
+    inputs = Scatter(team, make_dots(grads, [mix], [(0, *place) for place in starts]), finish_input, scratch[7:14])
     block.begin()
     for load in loads[2 * count :]:
         load.wait()
@@ -1353,6 +1382,42 @@
     )(gate, up, down)
 
 
+def own_mix_kernel(heads, ways, part, mix, decay, out):
+    turned = mix[...].T
+    out[:PER_HEAD, :] = turned[:PER_HEAD]
+    if heads > 1:
+        out[PER_HEAD + DECAY_ROWS :, :] = turned[PER_HEAD:]
+    small = decay[...].astype(F32).T
+    empty = jnp.zeros((DECAY_ROWS - 2 * heads, small.shape[1]), F32)
+    for index in range(ways):
+
+        @pl.when(part[0] == index)
+        def _():
+            rows = small[index * 2 * heads : (index + 1) * 2 * heads]
+            out[PER_HEAD : PER_HEAD + DECAY_ROWS, :] = jnp.concatenate([rows, empty]).astype(BF16)
+
+
+def own_mix_call(lay, heads, mix, decay):
+    features = mix.shape[0]
+    rows = heads * PER_HEAD + DECAY_ROWS
+    part = lax.axis_index(lay.part).astype(jnp.int32).reshape(1)
+    return pl.pallas_call(
+        functools.partial(own_mix_kernel, heads, lay.ways),
+        grid_spec=pltpu.PrefetchScalarGridSpec(
+            num_scalar_prefetch=1,
+            grid=(features // 128,),
+            in_specs=[
+                pl.BlockSpec((128, heads * PER_HEAD), lambda i, part: (i, part[0])),
+                pl.BlockSpec((128, decay.shape[1]), lambda i, part: (i, 0)),
+            ],
+            out_specs=pl.BlockSpec((rows, 128), lambda i, part: (0, i)),
+        ),
+        out_shape=jax.ShapeDtypeStruct((rows, features), BF16),
+        compiler_params=pltpu.CompilerParams(vmem_limit_bytes=60 << 20),
+        name="own_mix",
+    )(part, mix, decay)
+
+
 def ffn_kernel(values, grads, stack, hidden, both_grad):
     units, width = hidden.shape[1], stack.shape[2]
     both, grad = 0.0, 0.0
@@ -1495,6 +1560,16 @@
     return jnp.moveaxis(stack[:, start : start + size], 0, 1).reshape(size, -1)
 
 
+def own_mix(lay, heads, mix, decay):
+    if lay.native:
+        return own_mix_call(lay, heads, mix, decay)
+    part = lax.axis_index(lay.part)
+    mix = lax.dynamic_slice_in_dim(mix, part * heads * PER_HEAD, heads * PER_HEAD, 1).T
+    decay = lax.dynamic_slice_in_dim(decay, part * 2 * heads, 2 * heads, 1).T
+    decay = jnp.pad(decay, ((0, DECAY_ROWS - 2 * heads), (0, 0)))
+    return jnp.concatenate([mix[:PER_HEAD], decay, mix[PER_HEAD:]], axis=0)
+
+
 def own_units(lay, cuts, gate, up, down):
     if lay.native:
         return units_call(lay, cuts, gate, up, down)
@@ -1510,7 +1585,7 @@
 def mid_step(lay, mixed, out_all, stored, gain):
     starts = [head * DV for head in range(len(mixed))]
     if lay.native:
-        return mid_call(lay, mixed, out_all, [(0, start) for start in starts], stored, gain)
+        return mid_call(lay, mixed, out_all, [(start, DV) for start in starts], stored, gain)
     total = sum(project(left, beside(out_all, start, DV)) for left, start in zip(mixed, starts))
     residual = stored.astype(F32) + team_scatter(lay, total)
     normed, _ = norm_forward(residual)
@@ -1538,14 +1613,14 @@
     return grad, team_gather(lay, grad.astype(BF16)), gain_part
 
 
-def finish_step(lay, hidden, stacks, grads, mix, starts, residual, stored, grad_residual, gain):
+def finish_step(lay, hidden, stacks, grads, mix, places, residual, stored, grad_residual, gain):
     if lay.native:
-        return finish_call(lay, hidden, stacks, grads, mix, starts, residual, stored, grad_residual, gain)
+        return finish_call(lay, hidden, stacks, grads, mix, places, residual, stored, grad_residual, gain)
     total = sum(
         project(left, beside(stack, 2 * left.shape[1], left.shape[1])) for left, stack in zip(hidden, stacks)
     )
     block_output = (residual + team_scatter(lay, total)).astype(BF16)
-    total = sum(project_back(left, mix[:, start : start + left.shape[1]]) for left, start in zip(grads, starts))
+    total = sum(project(left[:, :size], beside(mix, start, size)) for left, (start, size) in zip(grads, places))
     grad, gain_part = norm_backward(team_scatter(lay, total), stored.astype(F32), gain)
     return block_output, (grad_residual + grad).astype(BF16), gain_part
 
@@ -1583,13 +1658,10 @@
     def gather_rows(values):
         return lax.all_gather(values, "row", axis=0, tiled=False)
 
-    mix_mine = mine(mix_weight, 1, heads * PER_HEAD)
-    decay_mine = mine(decay_weight, 1, heads * 2)
-    decay_pad = jnp.pad(decay_mine, ((0, 0), (0, 128 - heads * 2)))
-    splits = [0, PER_HEAD + 128]
+    places = [(0, PER_HEAD + DECAY_ROWS)]
     for head in range(1, heads):
-        splits.append(splits[-1] + PER_HEAD)
-    mix_pad = jnp.concatenate([mix_mine[:, :PER_HEAD], decay_pad, mix_mine[:, PER_HEAD:]], axis=1)
+        places.append((sum(places[-1]), PER_HEAD))
+    mix_mine = own_mix(lay, heads, mix_weight, decay_weight)
     out_all = gather_rows(mine(out_weight, 0, heads * DV))
     cuts = [0, min(units, 320), units]
     unit_blocks = own_units(lay, cuts, gate_weight, up_weight, down_weight)
@@ -1598,25 +1670,23 @@
 
     gains = jnp.stack([attn_gain, ffn_gain])
     stored, attn_all, out_grads, out_grads_all, gains, segments, mix_all = enter(
-        lay, block_input, cotangent, gains, segment_ids.reshape(1, -1), after(mix_pad, *unit_blocks)
+        lay, block_input, cotangent, gains, segment_ids.reshape(1, -1), after(mix_mine, *unit_blocks)
     )
-    mix_all = mix_all.reshape(lay.rows * width, -1)
     gain_one, gain_two = gains[:, 0].reshape(1, -1), gains[:, 1].reshape(1, -1)
     seg_row = segments.reshape(-1, 1, SEQ)
     waiting = lax.optimization_barrier((*unit_blocks, attn_all))[:-1]
     stacks = [gather_rows(values) for values in waiting]
     tokens = attn_all.shape[0]
-    head_weights = [mix_all[:, start:end] for start, end in zip(splits[:-1], splits[1:])]
-    shared, mixed, solves, projs = (), [], [], []
+    shared = (seg_row, conv_mine, log_mine, bias_mine, out_gain.reshape(1, -1))
+    mixed, solves, projs, extra = [], [], [], None
     for head in range(heads):
-        projs.append(project(after(attn_all, *mixed), head_weights[head]))
-        if not head:
-            shared = (
-                projs[0], PER_HEAD // 128, seg_row, conv_mine, log_mine, bias_mine, out_gain.reshape(1, -1),
-            )
-        values, solve = mixer_forward(head, heads, projs[head], *shared)
+        values, solve, proj, *made = mixer_forward(
+            head, places[head][0], after(attn_all, *mixed), mix_all, extra, *shared
+        )
+        extra = made[0] if made else extra
         mixed.append(values)
         solves.append(solve)
+        projs.append(proj)
     residual, ffn_all = mid_step(lay, mixed, out_all, stored, gain_two)
 
     def sum_rows(grads):
@@ -1641,12 +1711,12 @@
     other = jnp.zeros((tokens, 128), BF16)
     proj_grads, mix_grads, conv_parts, small_parts = [], [], [], []
     for head in reversed(range(heads)):
-        common = (head, heads, projs[head], *shared, solves[head], branch, out_all)
+        common = (head, projs[head], extra, *shared, solves[head], branch, out_all)
         if head:
-            grad, extra, conv_part, small_part = mixer_backward(*common, None)
+            grad, passed, conv_part, small_part = mixer_backward(*common, None)
             if lay.native:
                 grad = after(grad, crossed[0])
-            other = other + extra
+            other = other + passed
         else:
             grad, conv_part, small_part = mixer_backward(*common, other)
             if lay.native:
@@ -1666,7 +1736,7 @@
         ffn_pieces = [[ffn_grads[0], crossed[0], link(lay, ffn_grads[0]), link(lay, crossed[0])]]
         hidden[0] = after(hidden[0], *ffn_pieces[0])
     block_output, input_grad, attn_gain_part = finish_step(
-        lay, hidden, stacks, proj_grads, mix_all, splits[:-1], residual, stored, grad_residual, gain_one
+        lay, hidden, stacks, proj_grads, mix_all, places, residual, stored, grad_residual, gain_one
     )
 
     conv_part = jnp.concatenate(conv_parts, axis=1)

time: 770 us -> 768 us (level)
  matrix products: 23.4 us -> 0 us
  Pallas kernels: 678 us -> 690 us
  waiting for transfers between devices: 21.9 us -> 29.7 us
    dot_general x2 -> x0, matrix products: 23.4 us -> none  [project(): return jnp.dot(left, right, preferred_element_type=F32)]
    pallas_call x2 -> x3, Pallas kernels: 30 us -> 50.6 us  [the longest x2 46.7 us: mixer_forward(): pl.pallas_call(functools.partial(forward_kernel, head, start), grid=(coun...]
    pallas_call x1, Pallas kernels: 188 us -> 179 us  [enter_call(): pl.pallas_call(functools.partial(enter_kernel, lay.part), in_specs=[VMEM_...]
    all_gather x3, waiting for transfers between devices: 0.26 us -> 8.35 us  [gather_rows(): return lax.all_gather(values, 'row', axis=0, tiled=False)]
  transfers between devices with their start and end apart: 16 -> 16, of which waited for: 6 -> 7; matrix products, arithmetic and copies ran while one was open for 5% -> 1% of each run, Pallas kernels for 81% -> 83%
where the time goes in v5:
time: 768 us; the launch traced here: 760 us
  Pallas kernels  690 us (90%)
  waiting for transfers between devices  29.7 us (4%)
  between operations  14.9 us (2%)
  local copies, waits for them, and re-layouts  12.2 us (2%)
  starting transfers between devices  8.92 us (1%)
    pallas_call x1, Pallas kernels, enter_call(): pl.pallas_call(functools.partial(enter_kernel, lay.part), in_specs=[VMEM_...  179 us
    pallas_call x1, Pallas kernels, branch_call(): pl.pallas_call(functools.partial(branch_kernel, lay.part, len(lefts)), in...  83.3 us
    pallas_call x1, Pallas kernels, mid_call(): pl.pallas_call(functools.partial(mid_kernel, lay.part, starts), in_specs=...  76.8 us
    pallas_call x1, Pallas kernels, finish_call(): pl.pallas_call(functools.partial(finish_kernel, lay.part, len(hidden), st...  73.8 us
    pallas_call x4, Pallas kernels, stack_call(): pl.pallas_call(functools.partial(stack_kernel, counts), grid=(rows_n,), i...  54.7 us
    pallas_call x1, Pallas kernels, leave_call(): pl.pallas_call(functools.partial(leave_kernel, lay.part), in_specs=[VMEM_...  52.6 us
    pallas_call x2, Pallas kernels, mixer_backward(): pl.pallas_call(functools.partial(backward_kernel, head, last), grid=(coun...  51.3 us
    pallas_call x2, Pallas kernels, mixer_forward(): pl.pallas_call(functools.partial(forward_kernel, head, start), grid=(coun...  46.7 us
  transfers between devices with their start and end apart: 16, of which 7 were waited for; matrix products, arithmetic and copies ran while one was open for 1% of the time, Pallas kernels for 83%

profile of v5, /device:TPU:13, one launch (start us, length us, event | category | flops | bytes accessed | tf_op | source)
XLA Modules:
  0.0 759.5 jit_solution(1120900271017947422)
XLA Ops:
  11.2 3.9 own_mix.1.refs_4_
  15.0 6.0 own_units.1
  21.7 179.1 %enter.1 = (bf16[224,2048]{1,0:T(8,128)(2,1)}, bf16[8,224,2048]{2,1,0:T(8,128)(2,1)}, bf16[224,2048]{1,0:T(8,128)(2,1)}, bf16[8,224,2048]{2,1,0:T(8,128)(2,1)}, ...) custom-call(bf16[4,224,512]{2,1,0:T(8,128)(2,1)} %bitcast.63, ...), custom_call_target="tpu_custom_call" | custom-call | flops 1073741824 | bytes 419430400 | tf_op jit(solution)/shard_map/enter/pallas_call | solution.py:638
  204.1 23.5 %mixer_forward.2 = (bf16[1792,256]{1,0:T(8,128)(2,1)}, bf16[4,448,448]{2,1,0:T(8,128)(2,1)}, f32[1792,768]{1,0:T(8,128)}, f32[1792,16]{1,0:T(8,128)}) custom-call(bf16[1792,2048]{1,0:T(8,128)(2,1)} %bitcast.77, bf16[4,1552,512]{2,1,0:T(8,128)(2,1)} %get-tuple-element.91.refs_1_.refs_6_, s32[4,1,448]{2,1,0:T(1,128)} %get-tuple-element.92.refs_2_.refs_3_, ...), custom_call_target="tpu_custom_call" | custom-call | flops 12884901888 | bytes 33554432 | tf_op jit(solution)/shard_map/mixer_forward/pallas_call | solution.py:263
  228.2 23.3 %mixer_forward.3 = (bf16[1792,256]{1,0:T(8,128)(2,1)}, bf16[4,448,448]{2,1,0:T(8,128)(2,1)}, f32[1792,768]{1,0:T(8,128)}) custom-call(bf16[1792,2048]{1,0:T(8,128)(2,1)} %bitcast.78, bf16[4,1552,512]{2,1,0:T(8,128)(2,1)} %get-tuple-element.91.refs_1_.refs_6_, f32[1792,16]{1,0:T(8,128)} %get-tuple-element.95.refs_2_.refs_1_, ...), custom_call_target="tpu_custom_call" | custom-call | flops 12884901888 | bytes 33554432 | tf_op jit(solution)/shard_map/mixer_forward/pallas_call | solution.py:263
  251.5 76.8 %team_mid.1 = (f32[224,2048]{1,0:T(8,128)}, bf16[8,224,2048]{2,1,0:T(8,128)(2,1)}) custom-call(bf16[1792,256]{1,0:T(8,128)(2,1)} %get-tuple-element.93.refs_0_.refs_1_, bf16[1792,256]{1,0:T(8,128)(2,1)} %get-tuple-element.96.refs_1_.refs_2_, bf16[4,512,512]{2,1,0:T(8,128)(2,1)} %bitcast.60, bf16[224,2048]{1,0:T(8,128)(2,1)} %get-tuple-element.97.refs_3_.refs_8_, ...), custom_call_target="tpu_custom_call" | custom-call | flops 34359738368 | bytes 209715200 | tf_op jit(solution)/shard_map/team_mid/pallas_call | solution.py:862
  328.4 15.5 %ffn.2 = (bf16[1792,320]{1,0:T(8,128)(2,1)}, bf16[1792,640]{1,0:T(8,128)(2,1)}) custom-call(bf16[1792,2048]{1,0:T(8,128)(2,1)} %bitcast.89, bf16[1792,2048]{1,0:T(8,128)(2,1)} %bitcast.81, bf16[4,960,512]{2,1,0:T(8,128)(2,1)} %bitcast.57), custom_call_target="tpu_custom_call" | custom-call | flops 7046430720 | bytes 31457280 | tf_op jit(solution)/shard_map/ffn/pallas_call | solution.py:1445
  343.8 13.1 %weight_grads.4 = bf16[4,960,512]{2,1,0:T(8,128)(2,1)} custom-call(bf16[1792,640]{1,0:T(8,128)(2,1)} %get-tuple-element.111.refs_0_, bf16[1792,320]{1,0:T(8,128)(2,1)} %get-tuple-element.105.refs_1_.refs_0_, bf16[1792,2048]{1,0:T(8,128)(2,1)} %bitcast.90, bf16[1792,2048]{1,0:T(8,128)(2,1)} %bitcast.82), custom_call_target="tpu_custom_call" | custom-call | flops 7046430720 | bytes 41943040 | tf_op jit(solution)/shard_map/weight_grads/pallas_call | solution.py:1341
  357.0 8.3 %all-gather.11.cloned.1.call-done = bf16[4608,512]{1,0:T(8,128)(2,1)} async-done(((bf16[1152,512]{1,0:T(8,128)(2,1)}), bf16[4608,512]{1,0:T(8,128)(2,1)}) %all-gather.11.cloned.1.call-update) | async-done | bytes 4718608 | tf_op jit(solution)/shard_map/all_gather | solution.py:1659
  365.3 15.9 %ffn.3 = (bf16[1792,384]{1,0:T(8,128)(2,1)}, bf16[1792,768]{1,0:T(8,128)(2,1)}) custom-call(bf16[1792,2048]{1,0:T(8,128)(2,1)} %bitcast.91, bf16[1792,2048]{1,0:T(8,128)(2,1)} %bitcast.83, bf16[4,1152,512]{2,1,0:T(8,128)(2,1)} %bitcast.54), custom_call_target="tpu_custom_call" | custom-call | flops 8455716864 | bytes 31457280 | tf_op jit(solution)/shard_map/ffn/pallas_call | solution.py:1445
  381.2 14.0 %weight_grads.5 = bf16[4,1152,512]{2,1,0:T(8,128)(2,1)} custom-call(bf16[1792,768]{1,0:T(8,128)(2,1)} %get-tuple-element.112.refs_0_.refs_1_, bf16[1792,384]{1,0:T(8,128)(2,1)} %get-tuple-element.110.refs_1_, bf16[1792,2048]{1,0:T(8,128)(2,1)} %bitcast.92, bf16[1792,2048]{1,0:T(8,128)(2,1)} %bitcast.84), custom_call_target="tpu_custom_call" | custom-call | flops 8455716864 | bytes 41943040 | tf_op jit(solution)/shard_map/weight_grads/pallas_call | solution.py:1341
  395.3 83.3 %team_branch.1 = (f32[224,2048]{1,0:T(8,128)}, bf16[8,224,2048]{2,1,0:T(8,128)(2,1)}, f32[1,2048]{1,0:T(1,128)}) custom-call(bf16[1792,640]{1,0:T(8,128)(2,1)} %get-tuple-element.111.refs_0_, bf16[1792,768]{1,0:T(8,128)(2,1)} %get-tuple-element.112.refs_0_.refs_1_, bf16[4,960,512]{2,1,0:T(8,128)(2,1)} %bitcast.58, bf16[4,1152,512]{2,1,0:T(8,128)(2,1)} %bitcast.55, ...), custom_call_target="tpu_custom_call" | custom-call | flops 34359738368 | bytes 262144000 | tf_op jit(solution)/shard_map/team_branch/pallas_call | solution.py:910
  478.9 25.5 %mixer_backward.2 = (bf16[1792,768]{1,0:T(8,128)(2,1)}, bf16[1792,128]{1,0:T(8,128)(2,1)}, f32[4,4,512]{2,1,0:T(4,128)}, f32[4,1,384]{2,1,0:T(1,128)}) custom-call(f32[1792,768]{1,0:T(8,128)} %get-tuple-element.117.refs_0_, f32[1792,16]{1,0:T(8,128)} %get-tuple-element.95.refs_2_.refs_1_, s32[4,1,448]{2,1,0:T(1,128)} %get-tuple-element.92.refs_2_.refs_3_, ...), custom_call_target="tpu_custom_call" | custom-call | flops 25769803776 | bytes 67108864 | tf_op jit(solution)/shard_map/mixer_backward/pallas_call | solution.py:321
  504.4 16.8 %weight_grads.6 = bf16[4,1280,512]{2,1,0:T(8,128)(2,1)} custom-call(bf16[1792,768]{1,0:T(8,128)(2,1)} %get-tuple-element.129.refs_0_.refs_5_, bf16[1792,256]{1,0:T(8,128)(2,1)} %get-tuple-element.93.refs_0_.refs_1_, bf16[1792,256]{1,0:T(8,128)(2,1)} %get-tuple-element.96.refs_1_.refs_2_, bf16[1792,2048]{1,0:T(8,128)(2,1)} %bitcast.79, ...), custom_call_target="tpu_custom_call" | custom-call | flops 9395240960 | bytes 41943040 | tf_op jit(solution)/shard_map/weight_grads/pallas_call | solution.py:1341
  523.0 7.2 reduce-scatter.7.cloned.1.call-done
  531.4 25.7 %mixer_backward.3 = (bf16[1792,896]{1,0:T(8,128)(2,1)}, f32[4,4,512]{2,1,0:T(4,128)}, f32[4,1,384]{2,1,0:T(1,128)}) custom-call(f32[1792,768]{1,0:T(8,128)} %get-tuple-element.123.refs_0_, f32[1792,16]{1,0:T(8,128)} %get-tuple-element.95.refs_2_.refs_1_, s32[4,1,448]{2,1,0:T(1,128)} %get-tuple-element.92.refs_2_.refs_3_, ...), custom_call_target="tpu_custom_call" | custom-call | flops 25769803776 | bytes 67108864 | tf_op jit(solution)/shard_map/mixer_backward/pallas_call | solution.py:321
  557.4 10.8 %weight_grads.7 = bf16[4,784,512]{2,1,0:T(8,128)(2,1)} custom-call(bf16[1792,896]{1,0:T(8,128)(2,1)} %get-tuple-element.128.refs_0_.refs_4_, bf16[1792,2048]{1,0:T(8,128)(2,1)} %bitcast.80), custom_call_target="tpu_custom_call" | custom-call | flops 6576668672 | bytes 41943040 | tf_op jit(solution)/shard_map/weight_grads/pallas_call | solution.py:1341
  568.2 73.8 %team_finish.1 = (bf16[4,224,512]{2,1,0:T(8,128)(2,1)}, bf16[4,224,512]{2,1,0:T(8,128)(2,1)}, f32[1,2048]{1,0:T(1,128)}) custom-call(bf16[1792,320]{1,0:T(8,128)(2,1)} %get-tuple-element.105.refs_1_.refs_0_, bf16[1792,384]{1,0:T(8,128)(2,1)} %get-tuple-element.110.refs_1_, bf16[4,960,512]{2,1,0:T(8,128)(2,1)} %bitcast.59, bf16[4,1152,512]{2,1,0:T(8,128)(2,1)} %bitcast.56, ...), custom_call_target="tpu_custom_call" | custom-call | flops 34359738368 | bytes 262144000 | tf_op jit(solution)/shard_map/team_finish/pallas_call | solution.py:977
  650.0 11.4 %place_ffn.1 = (f32[512,2816]{1,0:T(8,128)}, f32[512,2816]{1,0:T(8,128)}, f32[2816,512]{1,0:T(8,128)}) custom-call(s32[4]{0:T(128)} %pad_add_fusion.order, bf16[960,512]{1,0:T(8,128)(2,1)} %bitcast.43, bf16[960,512]{1,0:T(8,128)(2,1)} %copy-done.5, bf16[960,512]{1,0:T(8,128)(2,1)} %copy-done.6, bf16[960,512]{1,0:T(8,128)(2,1)} %collective-permute-done.2.refs_3_.refs_11_, ...), custom_call_target="tpu_custom_call" | custom-call | flops 1073741824 | bytes 31457280 | tf_op jit(solution)/shard_map/place_ffn/pallas_call | solution.py:1303
  661.9 8.8 %collective-permute-done.4.refs_1_ = bf16[1280,512]{1,0:T(8,128)(2,1)S(1)} collective-permute-done((bf16[1280,512]{1,0:T(8,128)(2,1)}, bf16[1280,512]{1,0:T(8,128)(2,1)S(1)}, u32[]{:S(2)}, u32[]{:S(2)}) %collective-permute-start.4) | collective-permute-done | bytes 1310752 | tf_op jit(solution)/shard_map/ppermute | solution.py:1132
  678.4 6.2 place_rows.1
  684.6 5.9 place_late_head.1._
  690.9 52.6 %leave.1 = (bf16[4,224,512]{2,1,0:T(8,128)(2,1)}, bf16[4,224,512]{2,1,0:T(8,128)(2,1)}, bf16[4,784,512]{2,1,0:T(8,128)(2,1)}, f32[8,72,128]{2,1,0:T(8,128)}) custom-call(bf16[4,224,512]{2,1,0:T(8,128)(2,1)} %get-tuple-element.131.refs_0_, bf16[4,224,512]{2,1,0:T(8,128)(2,1)} %get-tuple-element.132.refs_1_, bf16[784,512]{1,0:T(8,128)(2,1)} %bitcast.67, ...), custom_call_target="tpu_custom_call" | custom-call | flops 1073741824 | bytes 125829120 | tf_op jit(solution)/shard_map/leave/pallas_call | solution.py:1109
  743.6 6.7 close.1
  (97 shorter events, 30.5 us)
Async XLA Ops:
  7.2 244.3 %all-gather.7.cloned.1.call-start = ((), (), s32[]{:S(2)}) async-start(), calls=%async_computation.8 | async-start | bytes 2621440 | tf_op jit(solution)/shard_map/all_gather | solution.py:1659
  9.6 318.7 %all-gather.9.cloned.1.call-start = ((), (), s32[]{:S(2)}) async-start(), calls=%async_computation.9 | async-start | bytes 4915200 | tf_op jit(solution)/shard_map/all_gather | solution.py:1659
  21.7 179.9 %copy-start.16 = (f32[8]{0:T(128)S(1)}, f32[8]{0:T(128)}, u32[]{:S(2)}) copy-start(f32[8]{0:T(128)} %param.21) | copy-start | bytes 100
  21.7 180.5 %copy-start.17 = (f32[8]{0:T(128)S(1)}, f32[8]{0:T(128)}, u32[]{:S(2)}) copy-start(f32[8]{0:T(128)} %param.22) | copy-start | bytes 100
  200.8 164.5 %all-gather.11.cloned.1.call-start = ((), (), s32[]{:S(2)}) async-start(), calls=%async_computation.10 | async-start | bytes 5898240 | tf_op jit(solution)/shard_map/all_gather | solution.py:1659
  201.6 277.0 %reduce-scatter.5.cloned.1.call-start = ((), (), s32[]{:S(2)}) async-start(), calls=%async_computation.4 | async-start | bytes 4915200 | tf_op jit(solution)/shard_map/reduce_scatter | solution.py:1693
  356.9 173.2 %reduce-scatter.7.cloned.1.call-start = ((), (), s32[]{:S(2)}) async-start(), calls=%async_computation.5 | async-start | bytes 5898240 | tf_op jit(solution)/shard_map/reduce_scatter | solution.py:1693
  395.2 246.8 %reduce-scatter.11.cloned.1.call-start = ((), (), s32[]{:S(2)}) async-start(), calls=%async_computation.7 | async-start | bytes 6553600 | tf_op jit(solution)/shard_map/reduce_scatter | solution.py:1693
  478.6 25.8 %collective-permute-start = (bf16[960,512]{1,0:T(8,128)(2,1)}, bf16[960,512]{1,0:T(8,128)(2,1)S(1)}, u32[]{:S(2)}, u32[]{:S(2)}) collective-permute-start(bf16[960,512]{1,0:T(8,128)(2,1)} %bitcast.42), channel_id=1, source_target_pairs={{0,16},{16,0},{8,24},{24,8},{1,17},{17,1},{9,25},{25,9},{2,18},{18... | collective-permute-start | bytes 2949128 | tf_op jit(solution)/shard_map/ppermute | solution.py:1132
  521.3 169.6 %reduce-scatter.9.cloned.1.call-start = ((), (), s32[]{:S(2)}) async-start(), calls=%async_computation.6 | async-start | bytes 4014080 | tf_op jit(solution)/shard_map/reduce_scatter | solution.py:1693
  522.5 45.7 %collective-permute-start.1 = (bf16[960,512]{1,0:T(8,128)(2,1)S(1)}, bf16[960,512]{1,0:T(8,128)(2,1)S(1)}, u32[]{:S(2)}, u32[]{:S(2)}) collective-permute-start(bf16[960,512]{1,0:T(8,128)(2,1)S(1)} %bitcast.45), channel_id=1, source_target_pairs={{0,8},{8,0},{16,24},{24,16},{1,9},{9,1},{17,25},{25,17},{2,10},{10... | collective-permute-start | bytes 2949128 | tf_op jit(solution)/shard_map/ppermute | solution.py:1136
  522.9 45.3 %collective-permute-start.2 = (bf16[960,512]{1,0:T(8,128)(2,1)S(1)}, bf16[960,512]{1,0:T(8,128)(2,1)}, u32[]{:S(2)}, u32[]{:S(2)}) collective-permute-start(bf16[960,512]{1,0:T(8,128)(2,1)S(1)} %collective-permute-done.refs_1_.refs_9_), channel_id=1, source_target_pairs={{0,8},{8,0},{16,24},{24,16},{1,9},{9,1},{17,25},{25,17},{2,10},{10... | collective-permute-start | bytes 2949128 | tf_op jit(solution)/shard_map/ppermute | solution.py:1136
  530.2 27.2 %collective-permute-start.3 = (bf16[1152,512]{1,0:T(8,128)(2,1)}, bf16[1152,512]{1,0:T(8,128)(2,1)}, u32[]{:S(2)}, u32[]{:S(2)}) collective-permute-start(bf16[1152,512]{1,0:T(8,128)(2,1)} %bitcast.16.refs_4_.refs_12_), channel_id=1, source_target_pairs={{0,16},{16,0},{8,24},{24,8},{1,17},{17,1},{9,25},{25,9},{2,18},{18... | collective-permute-start | bytes 3538952 | tf_op jit(solution)/shard_map/ppermute | solution.py:1132
  568.2 73.8 %copy-start.6 = (bf16[960,512]{1,0:T(8,128)(2,1)}, bf16[960,512]{1,0:T(8,128)(2,1)S(1)}, u32[]{:S(2)}) copy-start(bf16[960,512]{1,0:T(8,128)(2,1)S(1)} %collective-permute-done.1.refs_2_.refs_10_) | copy-start | bytes 2949124
  642.0 28.7 %collective-permute-start.4 = (bf16[1280,512]{1,0:T(8,128)(2,1)}, bf16[1280,512]{1,0:T(8,128)(2,1)S(1)}, u32[]{:S(2)}, u32[]{:S(2)}) collective-permute-start(bf16[1280,512]{1,0:T(8,128)(2,1)} %bitcast.38), channel_id=1, source_target_pairs={{0,16},{16,0},{8,24},{24,8},{1,17},{17,1},{9,25},{25,9},{2,18},{18... | collective-permute-start | bytes 3932168 | tf_op jit(solution)/shard_map/ppermute | solution.py:1132
  643.3 5.0 collective-permute-start.5
  645.5 4.5 collective-permute-start.6
  646.1 27.4 %copy-start.7 = (f32[4,4,512]{2,1,0:T(4,128)S(1)}, f32[4,4,512]{2,1,0:T(4,128)}, u32[]{:S(2)}) copy-start(f32[4,4,512]{2,1,0:T(4,128)} %get-tuple-element.139) | copy-start | bytes 98308
  646.1 28.0 %copy-start.13 = (f32[4,1,384]{2,1,0:T(1,128)S(1)}, f32[4,1,384]{2,1,0:T(1,128)}, u32[]{:S(2)}) copy-start(f32[4,1,384]{2,1,0:T(1,128)} %get-tuple-element.140) | copy-start | bytes 18436
  646.1 28.1 %copy-start.8 = (f32[4,4,512]{2,1,0:T(4,128)S(1)}, f32[4,4,512]{2,1,0:T(4,128)}, u32[]{:S(2)}) copy-start(f32[4,4,512]{2,1,0:T(4,128)} %get-tuple-element.138) | copy-start | bytes 98308
  646.1 31.4 %copy-start.10 = (f32[1,2048]{1,0:T(1,128)S(1)}, f32[1,2048]{1,0:T(1,128)}, u32[]{:S(2)}) copy-start(f32[1,2048]{1,0:T(1,128)} %get-tuple-element.143) | copy-start | bytes 24580
  646.1 31.4 %copy-start.11 = (f32[1,2048]{1,0:T(1,128)S(1)}, f32[1,2048]{1,0:T(1,128)}, u32[]{:S(2)}) copy-start(f32[1,2048]{1,0:T(1,128)} %get-tuple-element.142) | copy-start | bytes 24580
  661.5 16.9 %collective-permute-start.7 = (bf16[1280,512]{1,0:T(8,128)(2,1)S(1)}, bf16[1280,512]{1,0:T(8,128)(2,1)}, u32[]{:S(2)}, u32[]{:S(2)}) collective-permute-start(bf16[1280,512]{1,0:T(8,128)(2,1)S(1)} %bitcast.41), channel_id=1, source_target_pairs={{0,8},{8,0},{16,24},{24,16},{1,9},{9,1},{17,25},{25,17},{2,10},{10... | collective-permute-start | bytes 3932168 | tf_op jit(solution)/shard_map/ppermute | solution.py:1136
  670.7 7.7 %collective-permute-start.8 = (bf16[1280,512]{1,0:T(8,128)(2,1)S(1)}, bf16[1280,512]{1,0:T(8,128)(2,1)}, u32[]{:S(2)}, u32[]{:S(2)}) collective-permute-start(bf16[1280,512]{1,0:T(8,128)(2,1)S(1)} %collective-permute-done.4.refs_1_), channel_id=1, source_target_pairs={{0,8},{8,0},{16,24},{24,16},{1,9},{9,1},{17,25},{25,17},{2,10},{10... | collective-permute-start | bytes 3932168 | tf_op jit(solution)/shard_map/ppermute | solution.py:1136
  (10 other events, 116.0 us)
Sparse Core Ops, SparseCore 0:
  9.8 71.0 all-gather.6
  200.9 74.2 all-gather.8
  277.4 87.8 all-gather.10
  368.0 73.5 reduce-scatter.4
  444.4 85.7 reduce-scatter.6
  532.9 94.3 reduce-scatter.10
  629.5 61.3 reduce-scatter.8

commit v6 on v5

--- a/solution.py
+++ b/solution.py
@@ -257,7 +257,7 @@
     size = 64
     while size < length:
         size *= 2
-    group = 2 if count % 2 == 0 else 1
+    group = 1
     extra_spec = pl.BlockSpec((group * length, DECAY_ROWS), lambda s: (s, 0))
     extra_shape = jax.ShapeDtypeStruct((tokens, DECAY_ROWS), F32)
     return pl.pallas_call(
@@ -1368,20 +1368,6 @@
                 out[2 * (end - start) :, :] = down[base + start : base + end, :]
 
 
-def units_call(lay, cuts, gate, up, down):
-    features, wide = gate.shape
-    rows = [3 * (end - start) for start, end in zip(cuts[:-1], cuts[1:])]
-    return pl.pallas_call(
-        functools.partial(units_kernel, lay.part, cuts),
-        grid=(features // 128,),
-        in_specs=[pl.BlockSpec((128, wide), lambda i: (i, 0))] * 2 + [pl.BlockSpec((wide, 128), lambda i: (0, i))],
-        out_specs=[pl.BlockSpec((count, 128), lambda i: (0, i)) for count in rows],
-        out_shape=[jax.ShapeDtypeStruct((count, features), BF16) for count in rows],
-        compiler_params=pltpu.CompilerParams(vmem_limit_bytes=60 << 20),
-        name="own_units",
-    )(gate, up, down)
-
-
 def own_mix_kernel(heads, ways, part, mix, decay, out):
     turned = mix[...].T
     out[:PER_HEAD, :] = turned[:PER_HEAD]
@@ -1397,25 +1383,33 @@
             out[PER_HEAD : PER_HEAD + DECAY_ROWS, :] = jnp.concatenate([rows, empty]).astype(BF16)
 
 
-def own_mix_call(lay, heads, mix, decay):
-    features = mix.shape[0]
-    rows = heads * PER_HEAD + DECAY_ROWS
+def own_kernel(part_name, cuts, heads, ways, part, mix, decay, gate, up, down, mix_out, *outs):
+    own_mix_kernel(heads, ways, part, mix, decay, mix_out)
+    units_kernel(part_name, cuts, gate, up, down, *outs)
+
+
+def own_call(lay, cuts, heads, mix, decay, gate, up, down):
+    features, wide = gate.shape
+    rows = [heads * PER_HEAD + DECAY_ROWS] + [3 * (end - start) for start, end in zip(cuts[:-1], cuts[1:])]
     part = lax.axis_index(lay.part).astype(jnp.int32).reshape(1)
     return pl.pallas_call(
-        functools.partial(own_mix_kernel, heads, lay.ways),
+        functools.partial(own_kernel, lay.part, cuts, heads, lay.ways),
         grid_spec=pltpu.PrefetchScalarGridSpec(
             num_scalar_prefetch=1,
             grid=(features // 128,),
             in_specs=[
                 pl.BlockSpec((128, heads * PER_HEAD), lambda i, part: (i, part[0])),
                 pl.BlockSpec((128, decay.shape[1]), lambda i, part: (i, 0)),
+                pl.BlockSpec((128, wide), lambda i, part: (i, 0)),
+                pl.BlockSpec((128, wide), lambda i, part: (i, 0)),
+                pl.BlockSpec((wide, 128), lambda i, part: (0, i)),
             ],
-            out_specs=pl.BlockSpec((rows, 128), lambda i, part: (0, i)),
+            out_specs=[pl.BlockSpec((count, 128), lambda i, part: (0, i)) for count in rows],
         ),
-        out_shape=jax.ShapeDtypeStruct((rows, features), BF16),
+        out_shape=[jax.ShapeDtypeStruct((count, features), BF16) for count in rows],
         compiler_params=pltpu.CompilerParams(vmem_limit_bytes=60 << 20),
-        name="own_mix",
-    )(part, mix, decay)
+        name="own_weights",
+    )(part, mix, decay, gate, up, down)
 
 
 def ffn_kernel(values, grads, stack, hidden, both_grad):
@@ -1561,8 +1555,6 @@
 
 
 def own_mix(lay, heads, mix, decay):
-    if lay.native:
-        return own_mix_call(lay, heads, mix, decay)
     part = lax.axis_index(lay.part)
     mix = lax.dynamic_slice_in_dim(mix, part * heads * PER_HEAD, heads * PER_HEAD, 1).T
     decay = lax.dynamic_slice_in_dim(decay, part * 2 * heads, 2 * heads, 1).T
@@ -1571,8 +1563,6 @@
 
 
 def own_units(lay, cuts, gate, up, down):
-    if lay.native:
-        return units_call(lay, cuts, gate, up, down)
     start, size = lax.axis_index(lay.part) * cuts[-1], cuts[-1]
     gate, up = (lax.dynamic_slice_in_dim(values, start, size, 1).T for values in (gate, up))
     down = lax.dynamic_slice_in_dim(down, start, size, 0)
@@ -1661,10 +1651,15 @@
     places = [(0, PER_HEAD + DECAY_ROWS)]
     for head in range(1, heads):
         places.append((sum(places[-1]), PER_HEAD))
-    mix_mine = own_mix(lay, heads, mix_weight, decay_weight)
     out_all = gather_rows(mine(out_weight, 0, heads * DV))
     cuts = [0, min(units, 320), units]
-    unit_blocks = own_units(lay, cuts, gate_weight, up_weight, down_weight)
+    if lay.native:
+        mix_mine, *unit_blocks = own_call(
+            lay, cuts, heads, mix_weight, decay_weight, gate_weight, up_weight, down_weight
+        )
+    else:
+        mix_mine = own_mix(lay, heads, mix_weight, decay_weight)
+        unit_blocks = own_units(lay, cuts, gate_weight, up_weight, down_weight)
     conv_mine = mine(conv_weight, 1, heads * INNER)
     log_mine, bias_mine = mine(decay_log, 0, heads), mine(decay_bias, 0, heads)
 

time: 768 us -> 763 us (level)
  waiting for transfers between devices: 29.7 us -> 19.3 us
  Pallas kernels: 690 us -> 699 us
    pallas_call x2, Pallas kernels: 46.7 us -> 55.9 us  [mixer_forward(): pl.pallas_call(functools.partial(forward_kernel, head, start), grid=(coun...]
    all_gather x3, waiting for transfers between devices: 8.35 us -> 0.06 us  [gather_rows(): return lax.all_gather(values, 'row', axis=0, tiled=False)]
  transfers between devices with their start and end apart: 16 -> 16, of which waited for: 7 -> 6; matrix products, arithmetic and copies ran while one was open for 1% -> 1% of each run, Pallas kernels for 83% -> 84%
where the time goes in v6:
time: 763 us; the launch traced here: 759 us
  Pallas kernels  699 us (92%)
  waiting for transfers between devices  19.3 us (3%)
  between operations  14.6 us (2%)
  local copies, waits for them, and re-layouts  12.3 us (2%)
  starting transfers between devices  10.4 us (1%)
    pallas_call x1, Pallas kernels, enter_call(): pl.pallas_call(functools.partial(enter_kernel, lay.part), in_specs=[VMEM_...  182 us
    pallas_call x1, Pallas kernels, branch_call(): pl.pallas_call(functools.partial(branch_kernel, lay.part, len(lefts)), in...  82.5 us
    pallas_call x1, Pallas kernels, mid_call(): pl.pallas_call(functools.partial(mid_kernel, lay.part, starts), in_specs=...  77 us
    pallas_call x1, Pallas kernels, finish_call(): pl.pallas_call(functools.partial(finish_kernel, lay.part, len(hidden), st...  73.8 us
    pallas_call x2, Pallas kernels, mixer_forward(): pl.pallas_call(functools.partial(forward_kernel, head, start), grid=(coun...  55.9 us
    pallas_call x4, Pallas kernels, stack_call(): pl.pallas_call(functools.partial(stack_kernel, counts), grid=(rows_n,), i...  55.2 us
    pallas_call x1, Pallas kernels, leave_call(): pl.pallas_call(functools.partial(leave_kernel, lay.part), in_specs=[VMEM_...  52.6 us
    pallas_call x2, Pallas kernels, mixer_backward(): pl.pallas_call(functools.partial(backward_kernel, head, last), grid=(coun...  51.2 us
  transfers between devices with their start and end apart: 16, of which 6 were waited for; matrix products, arithmetic and copies ran while one was open for 1% of the time, Pallas kernels for 84%

profile of v6, /device:TPU:13, one launch (start us, length us, event | category | flops | bytes accessed | tf_op | source)
XLA Modules:
  0.0 759.2 jit_solution(2641910015704186553)
XLA Ops:
  11.2 7.0 own_weights.1
  18.8 182.0 %enter.1 = (bf16[224,2048]{1,0:T(8,128)(2,1)}, bf16[8,224,2048]{2,1,0:T(8,128)(2,1)}, bf16[224,2048]{1,0:T(8,128)(2,1)}, bf16[8,224,2048]{2,1,0:T(8,128)(2,1)}, ...) custom-call(bf16[4,224,512]{2,1,0:T(8,128)(2,1)} %bitcast.63, ...), custom_call_target="tpu_custom_call" | custom-call | flops 1073741824 | bytes 419430400 | tf_op jit(solution)/shard_map/enter/pallas_call | solution.py:638
  204.3 27.8 %mixer_forward.2 = (bf16[1792,256]{1,0:T(8,128)(2,1)}, bf16[4,448,448]{2,1,0:T(8,128)(2,1)}, f32[1792,768]{1,0:T(8,128)}, f32[1792,16]{1,0:T(8,128)}) custom-call(bf16[1792,2048]{1,0:T(8,128)(2,1)} %bitcast.77, bf16[4,1552,512]{2,1,0:T(8,128)(2,1)} %get-tuple-element.90.refs_1_.refs_6_, s32[4,1,448]{2,1,0:T(1,128)} %get-tuple-element.91.refs_2_.refs_3_, ...), custom_call_target="tpu_custom_call" | custom-call | flops 12884901888 | bytes 33554432 | tf_op jit(solution)/shard_map/mixer_forward/pallas_call | solution.py:263
  232.7 28.1 %mixer_forward.3 = (bf16[1792,256]{1,0:T(8,128)(2,1)}, bf16[4,448,448]{2,1,0:T(8,128)(2,1)}, f32[1792,768]{1,0:T(8,128)}) custom-call(bf16[1792,2048]{1,0:T(8,128)(2,1)} %bitcast.78, bf16[4,1552,512]{2,1,0:T(8,128)(2,1)} %get-tuple-element.90.refs_1_.refs_6_, f32[1792,16]{1,0:T(8,128)} %get-tuple-element.94.refs_2_.refs_1_, ...), custom_call_target="tpu_custom_call" | custom-call | flops 12884901888 | bytes 33554432 | tf_op jit(solution)/shard_map/mixer_forward/pallas_call | solution.py:263
  260.8 77.0 %team_mid.1 = (f32[224,2048]{1,0:T(8,128)}, bf16[8,224,2048]{2,1,0:T(8,128)(2,1)}) custom-call(bf16[1792,256]{1,0:T(8,128)(2,1)} %get-tuple-element.92.refs_0_.refs_1_, bf16[1792,256]{1,0:T(8,128)(2,1)} %get-tuple-element.95.refs_1_.refs_2_, bf16[4,512,512]{2,1,0:T(8,128)(2,1)} %bitcast.60, bf16[224,2048]{1,0:T(8,128)(2,1)} %get-tuple-element.96.refs_3_.refs_8_, ...), custom_call_target="tpu_custom_call" | custom-call | flops 34359738368 | bytes 209715200 | tf_op jit(solution)/shard_map/team_mid/pallas_call | solution.py:862
  337.9 15.4 %ffn.2 = (bf16[1792,320]{1,0:T(8,128)(2,1)}, bf16[1792,640]{1,0:T(8,128)(2,1)}) custom-call(bf16[1792,2048]{1,0:T(8,128)(2,1)} %bitcast.89, bf16[1792,2048]{1,0:T(8,128)(2,1)} %bitcast.81, bf16[4,960,512]{2,1,0:T(8,128)(2,1)} %bitcast.57), custom_call_target="tpu_custom_call" | custom-call | flops 7046430720 | bytes 31457280 | tf_op jit(solution)/shard_map/ffn/pallas_call | solution.py:1439
  353.3 13.5 %weight_grads.4 = bf16[4,960,512]{2,1,0:T(8,128)(2,1)} custom-call(bf16[1792,640]{1,0:T(8,128)(2,1)} %get-tuple-element.112.refs_0_, bf16[1792,320]{1,0:T(8,128)(2,1)} %get-tuple-element.106.refs_1_.refs_0_, bf16[1792,2048]{1,0:T(8,128)(2,1)} %bitcast.90, bf16[1792,2048]{1,0:T(8,128)(2,1)} %bitcast.82), custom_call_target="tpu_custom_call" | custom-call | flops 7046430720 | bytes 41943040 | tf_op jit(solution)/shard_map/weight_grads/pallas_call | solution.py:1341
  366.9 15.9 %ffn.3 = (bf16[1792,384]{1,0:T(8,128)(2,1)}, bf16[1792,768]{1,0:T(8,128)(2,1)}) custom-call(bf16[1792,2048]{1,0:T(8,128)(2,1)} %bitcast.91, bf16[1792,2048]{1,0:T(8,128)(2,1)} %bitcast.83, bf16[4,1152,512]{2,1,0:T(8,128)(2,1)} %bitcast.54), custom_call_target="tpu_custom_call" | custom-call | flops 8455716864 | bytes 31457280 | tf_op jit(solution)/shard_map/ffn/pallas_call | solution.py:1439
  382.8 14.0 %weight_grads.5 = bf16[4,1152,512]{2,1,0:T(8,128)(2,1)} custom-call(bf16[1792,768]{1,0:T(8,128)(2,1)} %get-tuple-element.113.refs_0_.refs_1_, bf16[1792,384]{1,0:T(8,128)(2,1)} %get-tuple-element.111.refs_1_, bf16[1792,2048]{1,0:T(8,128)(2,1)} %bitcast.92, bf16[1792,2048]{1,0:T(8,128)(2,1)} %bitcast.84), custom_call_target="tpu_custom_call" | custom-call | flops 8455716864 | bytes 41943040 | tf_op jit(solution)/shard_map/weight_grads/pallas_call | solution.py:1341
  396.8 82.5 %team_branch.1 = (f32[224,2048]{1,0:T(8,128)}, bf16[8,224,2048]{2,1,0:T(8,128)(2,1)}, f32[1,2048]{1,0:T(1,128)}) custom-call(bf16[1792,640]{1,0:T(8,128)(2,1)} %get-tuple-element.112.refs_0_, bf16[1792,768]{1,0:T(8,128)(2,1)} %get-tuple-element.113.refs_0_.refs_1_, bf16[4,960,512]{2,1,0:T(8,128)(2,1)} %bitcast.58, bf16[4,1152,512]{2,1,0:T(8,128)(2,1)} %bitcast.55, ...), custom_call_target="tpu_custom_call" | custom-call | flops 34359738368 | bytes 262144000 | tf_op jit(solution)/shard_map/team_branch/pallas_call | solution.py:910
  480.9 25.6 %mixer_backward.2 = (bf16[1792,768]{1,0:T(8,128)(2,1)}, bf16[1792,128]{1,0:T(8,128)(2,1)}, f32[4,4,512]{2,1,0:T(4,128)}, f32[4,1,384]{2,1,0:T(1,128)}) custom-call(f32[1792,768]{1,0:T(8,128)} %get-tuple-element.118.refs_0_, f32[1792,16]{1,0:T(8,128)} %get-tuple-element.94.refs_2_.refs_1_, s32[4,1,448]{2,1,0:T(1,128)} %get-tuple-element.91.refs_2_.refs_3_, ...), custom_call_target="tpu_custom_call" | custom-call | flops 25769803776 | bytes 67108864 | tf_op jit(solution)/shard_map/mixer_backward/pallas_call | solution.py:321
  506.5 16.9 %weight_grads.6 = bf16[4,1280,512]{2,1,0:T(8,128)(2,1)} custom-call(bf16[1792,768]{1,0:T(8,128)(2,1)} %get-tuple-element.130.refs_0_.refs_5_, bf16[1792,256]{1,0:T(8,128)(2,1)} %get-tuple-element.92.refs_0_.refs_1_, bf16[1792,256]{1,0:T(8,128)(2,1)} %get-tuple-element.95.refs_1_.refs_2_, bf16[1792,2048]{1,0:T(8,128)(2,1)} %bitcast.79, ...), custom_call_target="tpu_custom_call" | custom-call | flops 9395240960 | bytes 41943040 | tf_op jit(solution)/shard_map/weight_grads/pallas_call | solution.py:1341
  525.1 5.0 reduce-scatter.7.cloned.1.call-done
  531.3 25.7 %mixer_backward.3 = (bf16[1792,896]{1,0:T(8,128)(2,1)}, f32[4,4,512]{2,1,0:T(4,128)}, f32[4,1,384]{2,1,0:T(1,128)}) custom-call(f32[1792,768]{1,0:T(8,128)} %get-tuple-element.124.refs_0_, f32[1792,16]{1,0:T(8,128)} %get-tuple-element.94.refs_2_.refs_1_, s32[4,1,448]{2,1,0:T(1,128)} %get-tuple-element.91.refs_2_.refs_3_, ...), custom_call_target="tpu_custom_call" | custom-call | flops 25769803776 | bytes 67108864 | tf_op jit(solution)/shard_map/mixer_backward/pallas_call | solution.py:321
  557.3 10.8 %weight_grads.7 = bf16[4,784,512]{2,1,0:T(8,128)(2,1)} custom-call(bf16[1792,896]{1,0:T(8,128)(2,1)} %get-tuple-element.129.refs_0_.refs_4_, bf16[1792,2048]{1,0:T(8,128)(2,1)} %bitcast.80), custom_call_target="tpu_custom_call" | custom-call | flops 6576668672 | bytes 41943040 | tf_op jit(solution)/shard_map/weight_grads/pallas_call | solution.py:1341
  568.1 73.8 %team_finish.1 = (bf16[4,224,512]{2,1,0:T(8,128)(2,1)}, bf16[4,224,512]{2,1,0:T(8,128)(2,1)}, f32[1,2048]{1,0:T(1,128)}) custom-call(bf16[1792,320]{1,0:T(8,128)(2,1)} %get-tuple-element.106.refs_1_.refs_0_, bf16[1792,384]{1,0:T(8,128)(2,1)} %get-tuple-element.111.refs_1_, bf16[4,960,512]{2,1,0:T(8,128)(2,1)} %bitcast.59, bf16[4,1152,512]{2,1,0:T(8,128)(2,1)} %bitcast.56, ...), custom_call_target="tpu_custom_call" | custom-call | flops 34359738368 | bytes 262144000 | tf_op jit(solution)/shard_map/team_finish/pallas_call | solution.py:977
  649.9 11.4 %place_ffn.1 = (f32[512,2816]{1,0:T(8,128)}, f32[512,2816]{1,0:T(8,128)}, f32[2816,512]{1,0:T(8,128)}) custom-call(s32[4]{0:T(128)} %pad_add_fusion.order, bf16[960,512]{1,0:T(8,128)(2,1)} %bitcast.43, bf16[960,512]{1,0:T(8,128)(2,1)} %copy-done.5, bf16[960,512]{1,0:T(8,128)(2,1)} %copy-done.6, bf16[960,512]{1,0:T(8,128)(2,1)} %collective-permute-done.2.refs_3_.refs_11_, ...), custom_call_target="tpu_custom_call" | custom-call | flops 1073741824 | bytes 31457280 | tf_op jit(solution)/shard_map/place_ffn/pallas_call | solution.py:1303
  661.8 8.9 %collective-permute-done.4.refs_1_ = bf16[1280,512]{1,0:T(8,128)(2,1)S(1)} collective-permute-done((bf16[1280,512]{1,0:T(8,128)(2,1)}, bf16[1280,512]{1,0:T(8,128)(2,1)S(1)}, u32[]{:S(2)}, u32[]{:S(2)}) %collective-permute-start.4) | collective-permute-done | bytes 1310752 | tf_op jit(solution)/shard_map/ppermute | solution.py:1132
  670.7 2.8 collective-permute-start.8
  674.7 2.7 fusion
  678.3 6.2 place_rows.1
  684.6 5.9 place_late_head.1._
  690.8 52.6 %leave.1 = (bf16[4,224,512]{2,1,0:T(8,128)(2,1)}, bf16[4,224,512]{2,1,0:T(8,128)(2,1)}, bf16[4,784,512]{2,1,0:T(8,128)(2,1)}, f32[8,72,128]{2,1,0:T(8,128)}) custom-call(bf16[4,224,512]{2,1,0:T(8,128)(2,1)} %get-tuple-element.132.refs_0_, bf16[4,224,512]{2,1,0:T(8,128)(2,1)} %get-tuple-element.133.refs_1_, bf16[784,512]{1,0:T(8,128)(2,1)} %bitcast.67, ...), custom_call_target="tpu_custom_call" | custom-call | flops 1073741824 | bytes 125829120 | tf_op jit(solution)/shard_map/leave/pallas_call | solution.py:1109
  743.4 6.7 close.1
  (96 shorter events, 26.6 us)
Async XLA Ops:
  7.2 253.6 %all-gather.7.cloned.1.call-start = ((), (), s32[]{:S(2)}) async-start(), calls=%async_computation.8 | async-start | bytes 2621440 | tf_op jit(solution)/shard_map/all_gather | solution.py:1649
  9.6 328.2 %all-gather.9.cloned.1.call-start = ((), (), s32[]{:S(2)}) async-start(), calls=%async_computation.9 | async-start | bytes 4915200 | tf_op jit(solution)/shard_map/all_gather | solution.py:1649
  18.8 183.0 %copy-start.16 = (f32[8]{0:T(128)S(1)}, f32[8]{0:T(128)}, u32[]{:S(2)}) copy-start(f32[8]{0:T(128)} %param.21) | copy-start | bytes 100
  18.8 183.6 %copy-start.17 = (f32[8]{0:T(128)S(1)}, f32[8]{0:T(128)}, u32[]{:S(2)}) copy-start(f32[8]{0:T(128)} %param.22) | copy-start | bytes 100
  200.8 166.1 %all-gather.11.cloned.1.call-start = ((), (), s32[]{:S(2)}) async-start(), calls=%async_computation.10 | async-start | bytes 5898240 | tf_op jit(solution)/shard_map/all_gather | solution.py:1649
  201.5 277.8 %reduce-scatter.5.cloned.1.call-start = ((), (), s32[]{:S(2)}) async-start(), calls=%async_computation.4 | async-start | bytes 4915200 | tf_op jit(solution)/shard_map/reduce_scatter | solution.py:1688
  204.3 27.8 %copy-start.9 = (f32[4,2,512]{2,1,0:T(2,128)S(1)}, f32[4,2,512]{2,1,0:T(2,128)}, u32[]{:S(2)}) copy-start(f32[4,2,512]{2,1,0:T(2,128)} %get-tuple-element.97) | copy-start | bytes 49156
  366.8 163.3 %reduce-scatter.7.cloned.1.call-start = ((), (), s32[]{:S(2)}) async-start(), calls=%async_computation.5 | async-start | bytes 5898240 | tf_op jit(solution)/shard_map/reduce_scatter | solution.py:1688
  396.8 245.2 %reduce-scatter.11.cloned.1.call-start = ((), (), s32[]{:S(2)}) async-start(), calls=%async_computation.7 | async-start | bytes 6553600 | tf_op jit(solution)/shard_map/reduce_scatter | solution.py:1688
  479.3 27.1 %collective-permute-start = (bf16[960,512]{1,0:T(8,128)(2,1)}, bf16[960,512]{1,0:T(8,128)(2,1)S(1)}, u32[]{:S(2)}, u32[]{:S(2)}) collective-permute-start(bf16[960,512]{1,0:T(8,128)(2,1)} %bitcast.42), channel_id=1, source_target_pairs={{0,16},{16,0},{8,24},{24,8},{1,17},{17,1},{9,25},{25,9},{2,18},{18... | collective-permute-start | bytes 2949128 | tf_op jit(solution)/shard_map/ppermute | solution.py:1132
  523.4 167.4 %reduce-scatter.9.cloned.1.call-start = ((), (), s32[]{:S(2)}) async-start(), calls=%async_computation.6 | async-start | bytes 4014080 | tf_op jit(solution)/shard_map/reduce_scatter | solution.py:1688
  524.6 43.5 %collective-permute-start.1 = (bf16[960,512]{1,0:T(8,128)(2,1)S(1)}, bf16[960,512]{1,0:T(8,128)(2,1)S(1)}, u32[]{:S(2)}, u32[]{:S(2)}) collective-permute-start(bf16[960,512]{1,0:T(8,128)(2,1)S(1)} %bitcast.45), channel_id=1, source_target_pairs={{0,8},{8,0},{16,24},{24,16},{1,9},{9,1},{17,25},{25,17},{2,10},{10... | collective-permute-start | bytes 2949128 | tf_op jit(solution)/shard_map/ppermute | solution.py:1136
  525.0 43.1 %collective-permute-start.2 = (bf16[960,512]{1,0:T(8,128)(2,1)S(1)}, bf16[960,512]{1,0:T(8,128)(2,1)}, u32[]{:S(2)}, u32[]{:S(2)}) collective-permute-start(bf16[960,512]{1,0:T(8,128)(2,1)S(1)} %collective-permute-done.refs_1_.refs_9_), channel_id=1, source_target_pairs={{0,8},{8,0},{16,24},{24,16},{1,9},{9,1},{17,25},{25,17},{2,10},{10... | collective-permute-start | bytes 2949128 | tf_op jit(solution)/shard_map/ppermute | solution.py:1136
  530.1 27.2 %collective-permute-start.3 = (bf16[1152,512]{1,0:T(8,128)(2,1)}, bf16[1152,512]{1,0:T(8,128)(2,1)}, u32[]{:S(2)}, u32[]{:S(2)}) collective-permute-start(bf16[1152,512]{1,0:T(8,128)(2,1)} %bitcast.16.refs_4_.refs_12_), channel_id=1, source_target_pairs={{0,16},{16,0},{8,24},{24,8},{1,17},{17,1},{9,25},{25,9},{2,18},{18... | collective-permute-start | bytes 3538952 | tf_op jit(solution)/shard_map/ppermute | solution.py:1132
  568.1 73.8 %copy-start.6 = (bf16[960,512]{1,0:T(8,128)(2,1)}, bf16[960,512]{1,0:T(8,128)(2,1)S(1)}, u32[]{:S(2)}) copy-start(bf16[960,512]{1,0:T(8,128)(2,1)S(1)} %collective-permute-done.1.refs_2_.refs_10_) | copy-start | bytes 2949124
  641.9 28.7 %collective-permute-start.4 = (bf16[1280,512]{1,0:T(8,128)(2,1)}, bf16[1280,512]{1,0:T(8,128)(2,1)S(1)}, u32[]{:S(2)}, u32[]{:S(2)}) collective-permute-start(bf16[1280,512]{1,0:T(8,128)(2,1)} %bitcast.38), channel_id=1, source_target_pairs={{0,16},{16,0},{8,24},{24,8},{1,17},{17,1},{9,25},{25,9},{2,18},{18... | collective-permute-start | bytes 3932168 | tf_op jit(solution)/shard_map/ppermute | solution.py:1132
  643.2 5.0 collective-permute-start.5
  645.4 4.5 collective-permute-start.6
  646.0 28.1 %copy-start.13 = (f32[4,1,384]{2,1,0:T(1,128)S(1)}, f32[4,1,384]{2,1,0:T(1,128)}, u32[]{:S(2)}) copy-start(f32[4,1,384]{2,1,0:T(1,128)} %get-tuple-element.141) | copy-start | bytes 18436
  646.0 28.1 %copy-start.8 = (f32[4,4,512]{2,1,0:T(4,128)S(1)}, f32[4,4,512]{2,1,0:T(4,128)}, u32[]{:S(2)}) copy-start(f32[4,4,512]{2,1,0:T(4,128)} %get-tuple-element.139) | copy-start | bytes 98308
  646.0 31.4 %copy-start.10 = (f32[1,2048]{1,0:T(1,128)S(1)}, f32[1,2048]{1,0:T(1,128)}, u32[]{:S(2)}) copy-start(f32[1,2048]{1,0:T(1,128)} %get-tuple-element.144) | copy-start | bytes 24580
  646.0 31.4 %copy-start.11 = (f32[1,2048]{1,0:T(1,128)S(1)}, f32[1,2048]{1,0:T(1,128)}, u32[]{:S(2)}) copy-start(f32[1,2048]{1,0:T(1,128)} %get-tuple-element.143) | copy-start | bytes 24580
  661.4 17.0 %collective-permute-start.7 = (bf16[1280,512]{1,0:T(8,128)(2,1)S(1)}, bf16[1280,512]{1,0:T(8,128)(2,1)}, u32[]{:S(2)}, u32[]{:S(2)}) collective-permute-start(bf16[1280,512]{1,0:T(8,128)(2,1)S(1)} %bitcast.41), channel_id=1, source_target_pairs={{0,8},{8,0},{16,24},{24,16},{1,9},{9,1},{17,25},{25,17},{2,10},{10... | collective-permute-start | bytes 3932168 | tf_op jit(solution)/shard_map/ppermute | solution.py:1136
  670.7 7.7 %collective-permute-start.8 = (bf16[1280,512]{1,0:T(8,128)(2,1)S(1)}, bf16[1280,512]{1,0:T(8,128)(2,1)}, u32[]{:S(2)}, u32[]{:S(2)}) collective-permute-start(bf16[1280,512]{1,0:T(8,128)(2,1)S(1)} %collective-permute-done.4.refs_1_), channel_id=1, source_target_pairs={{0,8},{8,0},{16,24},{24,16},{1,9},{9,1},{17,25},{25,17},{2,10},{10... | collective-permute-start | bytes 3932168 | tf_op jit(solution)/shard_map/ppermute | solution.py:1136
  (10 other events, 122.0 us)
Sparse Core Ops, SparseCore 0:
  9.8 73.6 all-gather.6
  200.9 74.2 all-gather.8
  277.3 87.8 all-gather.10
  368.0 73.5 reduce-scatter.4
  444.3 85.7 reduce-scatter.6
  532.8 94.2 reduce-scatter.10
  629.4 61.3 reduce-scatter.8
